TPU v7x, 256 devices: a whole 4x4x8 slice. The times are simulated.
256 devices in a mesh: sub: 32 (over y, x, core), coarse: 8 (over z).
Axes of the slice: x: 4, y: 4, z: 8, core: 2. Of those that a mesh axis runs over, the one named last changes fastest.
Arguments:
- deflation: float32 [32, 64, 128, 512], P('sub', None, 'coarse')
- conductivity: float32 [32, 128, 512], P('sub', 'coarse'), may hold values from 0.1 to 10
- storage: float32 [32, 128, 512], P('sub', 'coarse'), may hold values from 0.5 to 4
- interface_rows: int32 [32, 8, 8, 512], P('sub', 'coarse'), may hold values from 0 to 8191, as said below
- interface_counts: int32 [32, 8, 8], P('sub', 'coarse'), may hold values from 0 to 512, as said below
Outputs:
- coarse_factor: float32 [32, 512, 512], P('sub')
- panel_rows: float32 [32, 8, 512, 512], P('sub', 'coarse')
Inputs may be any that keep to these rules, and one draw needn't show every extreme that they name: Slot j of a subdomain names the column offset o = j - 4 for j < 4 and j - 3 otherwise; interface_counts[a, c, slot of o] equals interface_counts[a + o, c, slot of -o], and is 0 where a + o lies outside 0 to 31. The most, 512, is reached in every draw. `interface_rows`: slots j < 4 hold cells with x = 0, the others cells with x = 15. Entries past a slot's count are also such cells and carry no edge.
All inputs are finite; a program needn't handle non-finite values.
Results may differ from a plain program's by a relative error of at most 0.0003.
Values sent between devices are 32-bit elements; how exact they have to be, the bound alone decides.
No kernel may reach another device: no remote copies, remote signals or barrier semaphores. Data moves between devices by JAX's collectives and lax.ppermute only.
A program may use at most 64 MiB of HBM per device.

v0:
```python
import jax
import jax.numpy as jnp
from jax import lax
from jax.sharding import PartitionSpec as P

K = 64
CX = 16
REACH = 4


highest = lax.Precision.HIGHEST


def passed_along(block, axis, distance):
    devices = range(lax.axis_size(axis))
    route = [(i - distance, i) for i in devices if i - distance in devices]
    return lax.ppermute(block, axis, route)


def extended_2(cells, sides, width):
    for axis, dim in sides:
        count = lax.axis_size(axis)
        ends = count - 1
        head = lax.slice_in_dim(cells, 0, width, axis=dim)
        tail = lax.slice_in_dim(cells, cells.shape[dim] - width, cells.shape[dim], axis=dim)
        cells = jnp.concatenate(
            [
                lax.ppermute(tail, axis, [(i, (i + 1) % count) for i in range(ends)]),
                cells,
                lax.ppermute(head, axis, [((i + 1) % count, i) for i in range(ends)]),
            ],
            axis=dim,
        )
    return cells


def harmonic(first, second):
    return 2.0 * first * second / (first + second)


def slot_of(offset):
    return offset + REACH if offset < 0 else offset + REACH - 1


def interior(vectors, sigma_cells, storage_cells):
    width_xy = sigma_cells.shape[1]
    layers = sigma_cells.shape[0]
    position = jnp.arange(width_xy)
    result = storage_cells[None] * vectors
    for stride, at_edge in ((1, position % CX == CX - 1), (CX, position >= width_xy - CX)):
        weights = jnp.where(
            at_edge[None, :], 0.0, harmonic(sigma_cells, jnp.roll(sigma_cells, -stride, axis=1))
        )
        flow_term = weights[None] * (jnp.roll(vectors, -stride, axis=2) - vectors)
        result = result - flow_term + jnp.roll(flow_term, stride, axis=2)
    top_layer = (jnp.arange(layers) == layers - 1)[:, None]
    weights = jnp.where(top_layer, 0.0, harmonic(sigma_cells, jnp.roll(sigma_cells, -1, axis=0)))
    flow_term = weights[None] * (jnp.roll(vectors, -1, axis=1) - vectors)
    return result - flow_term + jnp.roll(flow_term, 1, axis=1)


def pair_gram(left, right):
    return jnp.einsum("kp,lp->kl", left, right, precision=highest)


def lateral_both(payload, offset):
    return passed_along((payload[0], payload[1]), "sub", -offset)


def body(deflation, conductivity, storage, interface_rows, interface_counts):
    vectors = deflation[0]
    sigma_cells = conductivity[0]
    storage_cells = storage[0]
    row_index = interface_rows[0, 0]
    live_counts = interface_counts[0, 0]
    groups = lax.axis_size("coarse")
    level = lax.axis_index("coarse")
    layers = vectors.shape[1]
    cells = layers * vectors.shape[2]
    pad_rows = row_index.shape[1]
    applied = interior(vectors, sigma_cells, storage_cells)
    own_block = jnp.einsum("kzx,lzx->kl", vectors, applied, precision=highest)
    flat = vectors.reshape(K, cells)
    flat_sigma = sigma_cells.reshape(cells)
    picked = jnp.take(flat, row_index.reshape(-1), axis=1).reshape(K, 2 * REACH, pad_rows)
    picked_sigma = jnp.take(flat_sigma, row_index.reshape(-1)).reshape(2 * REACH, pad_rows)
    position = jnp.arange(pad_rows)
    lateral = [None] * (2 * REACH)
    top_face = vectors[:, layers - 1]
    bottom_face = vectors[:, 0]
    for offset in list(range(-REACH, 0)) + list(range(1, REACH + 1)):
        slot = slot_of(offset)
        mirror = slot_of(-offset)
        partner, partner_sigma = lateral_both((picked[:, mirror], picked_sigma[mirror]), offset)
        weights = jnp.where(
            position < live_counts[slot], harmonic(picked_sigma[slot], partner_sigma), 0.0
        )
        own_rows = picked[:, slot]
        own_block = own_block + pair_gram(own_rows * weights[None], own_rows)
        lateral[slot] = -pair_gram(own_rows * weights[None], partner)
    stacked = jnp.concatenate([vectors, sigma_cells[None]], axis=0)
    extended = extended_2(stacked, (("coarse", 1),), 1)
    above = extended[:K, layers + 1]
    above_sigma = extended[K, layers + 1]
    below = extended[:K, 0]
    below_sigma = extended[K, 0]
    upper_weight = harmonic(sigma_cells[layers - 1], above_sigma)[None]
    lower_weight = harmonic(sigma_cells[0], below_sigma)[None]
    own_block = own_block + pair_gram(top_face * upper_weight, top_face)
    own_block = own_block + pair_gram(bottom_face * lower_weight, bottom_face)
    upper_block = -pair_gram(top_face * upper_weight, above)
    lower_block = -pair_gram(bottom_face * lower_weight, below)
    bands = jnp.stack([lower_block, own_block, upper_block]).reshape(-1)
    collected = lax.all_gather(bands, "coarse", axis=0, tiled=True).reshape(groups, 3, K, K)
    zero_block = jnp.zeros((K, K), jnp.float32)
    row_list = []
    for target in range(groups):
        pieces = []
        for source in range(groups):
            if source == target - 1:
                pieces.append(collected[target, 0])
            elif source == target:
                pieces.append(collected[target, 1])
            elif source == target + 1:
                pieces.append(collected[target, 2])
            else:
                pieces.append(zero_block)
        row_list.append(jnp.concatenate(pieces, axis=1))
    coarse = jnp.concatenate(row_list, axis=0)
    factor = jnp.linalg.cholesky(coarse)
    lateral_cols = jnp.stack(lateral, axis=0).transpose(1, 0, 2).reshape(K, 2 * REACH * K)
    row_block = (jnp.arange(groups * K) // K)[:, None]
    right_side = jnp.where(row_block == level, jnp.tile(lateral_cols, (groups, 1)), 0.0)
    panel = lax.linalg.triangular_solve(factor, right_side, left_side=True, lower=True)
    return (factor[None], panel[None, None])


def solution(mesh):
    placed = (
        P("sub", None, "coarse", None),
        P("sub", "coarse", None),
        P("sub", "coarse", None),
        P("sub", "coarse", None, None),
        P("sub", "coarse", None),
    )
    return jax.shard_map(
        body,
        mesh=mesh,
        in_specs=placed,
        out_specs=(P("sub", None, None), P("sub", "coarse", None, None)),
        check_vma=False,
    )
```

profile of v0, /device:TPU:2, one launch (start us, length us, event | category | flops | bytes accessed | tf_op | source)
XLA Modules:
  0.0 363.8 jit_solution(2878827101648777609)
XLA Ops:
  2.9 23.0 %gather_fusion.1 = f32[4096]{0:T(1024)S(1)} fusion(f32[8192]{0:T(1024)S(1)} %bitcast.286, s32[4096]{0:T(1024)S(1)} %broadcast_clamp_fusion), kind=kCustom, calls=%fused_computation.1 | custom fusion | bytes 49152 | tf_op jit(solution)/shard_map/jit(_take)/gather | solution.py:86
  30.0 2.8 copy.46
  33.7 16.3 %gather_fusion = f32[4096,64]{1,0:T(8,128)} fusion(f32[64,8192]{0,1:T(8,128)} %bitcast.295, s32[4096]{0:T(1024)S(1)} %broadcast_clamp_fusion), kind=kCustom, calls=%fused_computation | custom fusion | bytes 2113536 | tf_op jit(solution)/shard_map/jit(_take)/gather | solution.py:85
  57.6 6.0 %collective-permute-start.1 = (f32[512]{0:T(512)S(1)}, f32[512]{0:T(512)S(1)}, u32[]{:S(2)}, u32[]{:S(2)}) collective-permute-start(f32[512]{0:T(512)S(1)} %get-tuple-element.93), channel_id=1, source_target_pairs={{0,32},{8,40},{16,48},{24,56},{32,64},{40,72},{48,80},{56,88},{64,... | collective-permute-start | bytes 6152 | tf_op jit(solution)/shard_map/ppermute | solution.py:17
  63.6 3.8 %collective-permute-start.2 = (f32[512]{0:T(512)S(1)}, f32[512]{0:T(512)S(1)}, u32[]{:S(2)}, u32[]{:S(2)}) collective-permute-start(f32[512]{0:T(512)S(1)} %get-tuple-element.91), channel_id=1, source_target_pairs={{0,24},{8,32},{16,40},{24,48},{32,56},{40,64},{48,72},{56,80},{64,... | collective-permute-start | bytes 6152 | tf_op jit(solution)/shard_map/ppermute | solution.py:17
  68.8 6.2 %collective-permute-start.3 = (f32[512]{0:T(512)S(1)}, f32[512]{0:T(512)S(1)}, u32[]{:S(2)}, u32[]{:S(2)}) collective-permute-start(f32[512]{0:T(512)S(1)} %get-tuple-element.89), channel_id=1, source_target_pairs={{0,16},{8,24},{16,32},{24,40},{32,48},{40,56},{48,64},{56,72},{64,... | collective-permute-start | bytes 6152 | tf_op jit(solution)/shard_map/ppermute | solution.py:17
  78.8 5.2 %collective-permute-start = (f32[65,1,512]{2,1,0:T(1,128)}, f32[65,1,512]{2,1,0:T(1,128)}, u32[]{:S(2)}, u32[]{:S(2)}) collective-permute-start(f32[65,1,512]{2,1,0:T(1,128)} %get-tuple-element.20), channel_id=1, source_target_pairs={{0,1},{1,2},{2,3},{3,4},{4,5},{5,6},{6,7},{8,9},{9,10},{10,11},{11... | collective-permute-start | bytes 399368 | tf_op jit(solution)/shard_map/ppermute | solution.py:28
  84.0 6.8 %collective-permute-start.10 = (f32[64,512]{0,1:T(8,128)S(1)}, f32[64,512]{0,1:T(8,128)}, u32[]{:S(2)}, u32[]{:S(2)}) collective-permute-start(f32[64,512]{0,1:T(8,128)S(1)} %get-tuple-element.29), channel_id=1, source_target_pairs={{0,32},{8,40},{16,48},{24,56},{32,64},{40,72},{48,80},{56,88},{64,... | collective-permute-start | bytes 393224 | tf_op jit(solution)/shard_map/ppermute | solution.py:17
  92.8 3.8 %fusion.141 = (f32[512]{0:T(512)S(1)}, f32[512]{0:T(512)S(1)}, f32[512]{0:T(512)S(1)}, f32[512]{0:T(512)S(1)}, f32[512]{0:T(512)S(1)}, /*index=5*/f32[512]{0:T(512)S(1)}, f32[512]{0:T(512)S(1)}) fusion(f32[512]{0:T(512)S(1)} %collective-permute-done.8, s32[]{:T(128)} %bitcast.41, f32[4096]{0:T(1024)S(1)} %and_select_fusion, ...), kind=kLoop, calls=%fused_computation.270 | loop fusion | flops 18432 | bytes 40984 | tf_op jit(solution)/shard_map/jit(_where)/select_n | solution.py:95
  96.6 2.8 collective-permute-start.4
  103.6 2.0 slice.472
  107.4 4.1 %collective-permute-start.12 = (f32[64,512]{0,1:T(8,128)}, f32[64,512]{0,1:T(8,128)S(1)}, u32[]{:S(2)}, u32[]{:S(2)}) collective-permute-start(f32[64,512]{0,1:T(8,128)} %get-tuple-element.27), channel_id=1, source_target_pairs={{0,16},{8,24},{16,32},{24,40},{32,48},{40,56},{48,64},{56,72},{64,... | collective-permute-start | bytes 393224 | tf_op jit(solution)/shard_map/ppermute | solution.py:17
  115.7 3.7 %collective-permute-start.14 = (f32[64,512]{0,1:T(8,128)}, f32[64,512]{0,1:T(8,128)S(1)}, u32[]{:S(2)}, u32[]{:S(2)}) collective-permute-start(f32[64,512]{0,1:T(8,128)} %get-tuple-element.25), channel_id=1, source_target_pairs={{8,0},{16,8},{24,16},{32,24},{40,32},{48,40},{56,48},{64,56},{72,6... | collective-permute-start | bytes 393224 | tf_op jit(solution)/shard_map/ppermute | solution.py:17
  131.5 3.5 collective-permute-done.16
  135.7 10.3 %collective-permute-done.17 = f32[64,512]{0,1:T(8,128)S(1)} collective-permute-done((f32[64,512]{0,1:T(8,128)S(1)}, f32[64,512]{0,1:T(8,128)S(1)}, u32[]{:S(2)}, u32[]{:S(2)}) %collective-permute-start.17) | collective-permute-done | bytes 131104 | tf_op jit(solution)/shard_map/ppermute | solution.py:17
  150.0 4.5 %fusion = (f32[64,16,512]{2,1,0:T(8,128)S(1)}, f32[64,16,512]{2,1,0:T(8,128)S(1)}, f32[64,16,512]{2,1,0:T(8,128)S(1)}) fusion(f32[64,16,1]{2,1,0:T(8,128)} %slice.467, f32[64,16,511]{2,1,0:T(8,128)} %slice.466, f32[16,512]{1,0:T(8,128)} %get-tuple-element.75, f32[1,64,16,512]{3,2,1,0:T(8,128)S(1)} %copy-done, f32[64,16,16]{2,1,0:T(8,128)} %slice.473, ...), kind=kLoop, calls=%fused_computation.5 | loop fusion | flops 4718592 | bytes 14778368 | tf_op jit(solution)/shard_map/mul | solution.py:54
  155.3 2.2 fusion.4
  157.5 4.1 %fusion.10 = f32[64,64]{1,0:T(8,128)S(1)} fusion(f32[64,16,512]{2,1,0:T(8,128)S(1)} %bitcast.294, f32[64,16,512]{2,1,0:T(8,128)S(1)} %fusion.4), kind=kOutput, calls=%fused_computation.26 | convolution fusion | flops 402653184 | bytes 4210688 | tf_op jit(solution)/shard_map/kzx,lzx->kl/dot_general | solution.py:82
  162.4 12.9 %convolution_add_fusion.8 = f32[64,64]{1,0:T(8,128)S(1)} fusion(f32[64,64]{1,0:T(8,128)S(1)} %convolution_add_fusion.9, f32[64,8,512]{0,2,1:T(8,128)S(1)} %copy-done.3, f32[512]{0:T(512)S(1)} %copy-done.15), kind=kOutput, calls=%fused_computation.64 | convolution fusion | flops 25202688 | bytes 575488 | tf_op jit(solution)/shard_map/kp,lp->kl/dot_general | solution.py:63
  182.5 28.9 %all_gather.3 = f32[98304]{0:T(1024)S(1)} all-gather(f32[12288]{0:T(1024)S(1)} %reshape.308), channel_id=1, replica_groups=mesh['sub'=32,'coarse'=8] {'coarse'}, dimensions={0}, use_global_device_ids=true | all-gather | bytes 442368 | tf_op jit(solution)/shard_map/all_gather | solution.py:114
  219.5 11.7 %cholesky.104 = f32[128,128]{1,0:T(8,128)S(1)} custom-call(f32[128,128]{1,0:T(8,128)S(1)} %cholesky.266), custom_call_target="Cholesky" | custom-call | tf_op jit(solution)/shard_map/jit(cholesky)/cholesky | solution.py:130
  231.4 9.8 %custom-call.30 = f32[1,128,128]{1,2,0:T(8,128)S(1)} custom-call(f32[1,128,128]{2,1,0:T(8,128)S(1)} %get-tuple-element.74), custom_call_target="InvertDiagBlocksLowerTriangular" | custom-call | tf_op jit(solution)/shard_map/jit(cholesky)/cholesky | solution.py:130
  243.7 11.7 %cholesky.217 = f32[128,128]{1,0:T(8,128)S(1)} custom-call(f32[128,128]{1,0:T(8,128)S(1)} %cholesky.270), custom_call_target="Cholesky" | custom-call | tf_op jit(solution)/shard_map/jit(cholesky)/cholesky | solution.py:130
  255.5 10.0 %custom-call.31 = f32[1,128,128]{1,2,0:T(8,128)S(1)} custom-call(f32[1,128,128]{2,1,0:T(8,128)S(1)} %get-tuple-element.71), custom_call_target="InvertDiagBlocksLowerTriangular" | custom-call | tf_op jit(solution)/shard_map/jit(cholesky)/cholesky | solution.py:130
  267.1 11.7 %cholesky.238 = f32[128,128]{1,0:T(8,128)S(1)} custom-call(f32[128,128]{1,0:T(8,128)S(1)} %cholesky.275), custom_call_target="Cholesky" | custom-call | tf_op jit(solution)/shard_map/jit(cholesky)/cholesky | solution.py:130
  278.8 9.8 %custom-call.32 = f32[1,128,128]{1,2,0:T(8,128)S(1)} custom-call(f32[1,128,128]{2,1,0:T(8,128)S(1)} %get-tuple-element.68), custom_call_target="InvertDiagBlocksLowerTriangular" | custom-call | tf_op jit(solution)/shard_map/jit(cholesky)/cholesky | solution.py:130
  290.1 11.7 %cholesky.255 = f32[128,128]{1,0:T(8,128)S(1)} custom-call(f32[128,128]{1,0:T(8,128)S(1)} %convolution_subtract_fusion.5), custom_call_target="Cholesky" | custom-call | tf_op jit(solution)/shard_map/jit(cholesky)/cholesky | solution.py:130
  308.6 10.5 %while.1 = (s32[]{:T(128)}, f32[512,512]{1,0:T(8,128)S(1)}, s32[4,2]{0,1:T(2,128)S(1)}, f32[4,128,128]{2,1,0:T(8,128)}, s32[]{:T(128)}) while((s32[]{:T(128)}, f32[512,512]{1,0:T(8,128)S(1)}, s32[4,2]{0,1:T(2,128)S(1)}, f32[4,128,128]{2,1,0:T(8,128)}, s32[]{:T(128)}) %tuple.90), condition=%wide.while_cond, body=%wide.while_body.sunk | while | flops 2 | bytes 132205 | solution.py:134
  309.2 2.0 bitcast_dynamic-update-slice_fusion.2
  314.4 2.0 bitcast_dynamic-update-slice_fusion.2
  317.1 2.0 bitcast_dynamic-update-slice_fusion.2
  319.0 40.1 %custom-call.33 = f32[4,128,128]{1,2,0:T(8,128)S(1)} custom-call(f32[4,128,128]{2,1,0:T(8,128)} %get-tuple-element.9), custom_call_target="InvertDiagBlocksLowerTriangular" | custom-call | tf_op jit(solution)/shard_map/triangular_solve | solution.py:134
  (226 shorter events, 83.5 us)
Async XLA Ops:
  2.9 25.0 %copy-start.5 = (f32[1,16,512]{2,1,0:T(8,128)S(1)}, f32[1,16,512]{2,1,0:T(8,128)}, u32[]{:S(2)}) copy-start(f32[1,16,512]{2,1,0:T(8,128)} %param.6) | copy-start | bytes 98308
  2.9 25.8 %copy-start.11 = (s32[1,1,8,512]{3,2,1,0:T(8,128)S(1)}, s32[1,1,8,512]{3,2,1,0:T(8,128)}, u32[]{:S(2)}) copy-start(s32[1,1,8,512]{3,2,1,0:T(8,128)} %param.8) | copy-start | bytes 49156
  2.9 27.1 %copy-start = (f32[1,64,16,512]{3,2,1,0:T(8,128)S(1)}, f32[1,64,16,512]{3,2,1,0:T(8,128)}, u32[]{:S(2)}) copy-start(f32[1,64,16,512]{3,2,1,0:T(8,128)} %param.5) | copy-start | bytes 6291460
  26.0 29.1 %collective-permute-start.5 = (f32[512]{0:T(512)S(1)}, f32[512]{0:T(512)S(1)}, u32[]{:S(2)}, u32[]{:S(2)}) collective-permute-start(f32[512]{0:T(512)S(1)} %slice.489), channel_id=1, source_target_pairs={{8,0},{16,8},{24,16},{32,24},{40,32},{48,40},{56,48},{64,56},{72,6... | collective-permute-start | bytes 6152 | tf_op jit(solution)/shard_map/ppermute | solution.py:17
  28.5 25.3 %copy-start.22 = (f32[1,1,512]{2,1,0:T(1,128)}, f32[1,1,512]{2,1,0:T(1,128)S(1)}, u32[]{:S(2)}) copy-start(f32[1,1,512]{2,1,0:T(1,128)S(1)} %get-tuple-element.78) | copy-start | bytes 6148
  55.7 73.6 %copy-start.20 = (f32[512]{0:T(512)}, f32[512]{0:T(512)S(1)}, u32[]{:S(2)}) copy-start(f32[512]{0:T(512)S(1)} %get-tuple-element.88) | copy-start | bytes 6148
  55.7 19.3 %collective-permute-start.8 = (f32[512]{0:T(512)S(1)}, f32[512]{0:T(512)S(1)}, u32[]{:S(2)}, u32[]{:S(2)}) collective-permute-start(f32[512]{0:T(512)S(1)} %get-tuple-element.87), channel_id=1, source_target_pairs={{32,0},{40,8},{48,16},{56,24},{64,32},{72,40},{80,48},{88,56},{96,... | collective-permute-start | bytes 6152 | tf_op jit(solution)/shard_map/ppermute | solution.py:17
  57.6 19.9 %collective-permute-start.1 = (f32[512]{0:T(512)S(1)}, f32[512]{0:T(512)S(1)}, u32[]{:S(2)}, u32[]{:S(2)}) collective-permute-start(f32[512]{0:T(512)S(1)} %get-tuple-element.93), channel_id=1, source_target_pairs={{0,32},{8,40},{16,48},{24,56},{32,64},{40,72},{48,80},{56,88},{64,... | collective-permute-start | bytes 6152 | tf_op jit(solution)/shard_map/ppermute | solution.py:17
  63.6 15.2 %collective-permute-start.2 = (f32[512]{0:T(512)S(1)}, f32[512]{0:T(512)S(1)}, u32[]{:S(2)}, u32[]{:S(2)}) collective-permute-start(f32[512]{0:T(512)S(1)} %get-tuple-element.91), channel_id=1, source_target_pairs={{0,24},{8,32},{16,40},{24,48},{32,56},{40,64},{48,72},{56,80},{64,... | collective-permute-start | bytes 6152 | tf_op jit(solution)/shard_map/ppermute | solution.py:17
  67.5 16.5 %collective-permute-start.7 = (f32[512]{0:T(512)S(1)}, f32[512]{0:T(512)S(1)}, u32[]{:S(2)}, u32[]{:S(2)}) collective-permute-start(f32[512]{0:T(512)S(1)} %get-tuple-element.92), channel_id=1, source_target_pairs={{24,0},{32,8},{40,16},{48,24},{56,32},{64,40},{72,48},{80,56},{88,... | collective-permute-start | bytes 6152 | tf_op jit(solution)/shard_map/ppermute | solution.py:17
  68.8 22.0 %collective-permute-start.3 = (f32[512]{0:T(512)S(1)}, f32[512]{0:T(512)S(1)}, u32[]{:S(2)}, u32[]{:S(2)}) collective-permute-start(f32[512]{0:T(512)S(1)} %get-tuple-element.89), channel_id=1, source_target_pairs={{0,16},{8,24},{16,32},{24,40},{32,48},{40,56},{48,64},{56,72},{64,... | collective-permute-start | bytes 6152 | tf_op jit(solution)/shard_map/ppermute | solution.py:17
  75.0 17.8 %collective-permute-start.6 = (f32[512]{0:T(512)S(1)}, f32[512]{0:T(512)S(1)}, u32[]{:S(2)}, u32[]{:S(2)}) collective-permute-start(f32[512]{0:T(512)S(1)} %get-tuple-element.90), channel_id=1, source_target_pairs={{16,0},{24,8},{32,16},{40,24},{48,32},{56,40},{64,48},{72,56},{80,... | collective-permute-start | bytes 6152 | tf_op jit(solution)/shard_map/ppermute | solution.py:17
  77.5 70.2 %collective-permute-start.9 = (f32[65,1,512]{2,1,0:T(1,128)}, f32[65,1,512]{2,1,0:T(1,128)}, u32[]{:S(2)}, u32[]{:S(2)}) collective-permute-start(f32[65,1,512]{2,1,0:T(1,128)} %get-tuple-element.21), channel_id=1, source_target_pairs={{1,0},{2,1},{3,2},{4,3},{5,4},{6,5},{7,6},{9,8},{10,9},{11,10},{12... | collective-permute-start | bytes 399368 | tf_op jit(solution)/shard_map/ppermute | solution.py:30
  78.8 69.6 %collective-permute-start = (f32[65,1,512]{2,1,0:T(1,128)}, f32[65,1,512]{2,1,0:T(1,128)}, u32[]{:S(2)}, u32[]{:S(2)}) collective-permute-start(f32[65,1,512]{2,1,0:T(1,128)} %get-tuple-element.20), channel_id=1, source_target_pairs={{0,1},{1,2},{2,3},{3,4},{4,5},{5,6},{6,7},{8,9},{9,10},{10,11},{11... | collective-permute-start | bytes 399368 | tf_op jit(solution)/shard_map/ppermute | solution.py:28
  84.0 28.0 %collective-permute-start.10 = (f32[64,512]{0,1:T(8,128)S(1)}, f32[64,512]{0,1:T(8,128)}, u32[]{:S(2)}, u32[]{:S(2)}) collective-permute-start(f32[64,512]{0,1:T(8,128)S(1)} %get-tuple-element.29), channel_id=1, source_target_pairs={{0,32},{8,40},{16,48},{24,56},{32,64},{40,72},{48,80},{56,88},{64,... | collective-permute-start | bytes 393224 | tf_op jit(solution)/shard_map/ppermute | solution.py:17
  90.8 24.9 %collective-permute-start.11 = (f32[64,512]{0,1:T(8,128)}, f32[64,512]{0,1:T(8,128)}, u32[]{:S(2)}, u32[]{:S(2)}) collective-permute-start(f32[64,512]{0,1:T(8,128)} %get-tuple-element.28), channel_id=1, source_target_pairs={{0,24},{8,32},{16,40},{24,48},{32,56},{40,64},{48,72},{56,80},{64,... | collective-permute-start | bytes 393224 | tf_op jit(solution)/shard_map/ppermute | solution.py:17
  96.6 17.4 %copy-start.16 = (f32[512]{0:T(512)}, f32[512]{0:T(512)S(1)}, u32[]{:S(2)}) copy-start(f32[512]{0:T(512)S(1)} %get-tuple-element.81) | copy-start | bytes 6148
  96.6 22.8 %copy-start.14 = (f32[512]{0:T(512)}, f32[512]{0:T(512)S(1)}, u32[]{:S(2)}) copy-start(f32[512]{0:T(512)S(1)} %get-tuple-element.82) | copy-start | bytes 6148
  96.6 10.7 %collective-permute-start.4 = (f32[512]{0:T(512)S(1)}, f32[512]{0:T(512)S(1)}, u32[]{:S(2)}, u32[]{:S(2)}) collective-permute-start(f32[512]{0:T(512)S(1)} %get-tuple-element.86), channel_id=1, source_target_pairs={{0,8},{8,16},{16,24},{24,32},{32,40},{40,48},{48,56},{56,64},{64,7... | collective-permute-start | bytes 6152 | tf_op jit(solution)/shard_map/ppermute | solution.py:17
  105.6 15.6 %copy-start.10 = (f32[64,512]{0,1:T(8,128)S(1)}, f32[64,512]{0,1:T(8,128)}, u32[]{:S(2)}) copy-start(f32[64,512]{0,1:T(8,128)} %get-tuple-element.24) | copy-start | bytes 393220
  107.4 21.9 %copy-start.2 = (f32[64,8,512]{0,2,1:T(8,128)S(1)}, f32[64,8,512]{0,2,1:T(8,128)}, u32[]{:S(2)}) copy-start(f32[64,8,512]{0,2,1:T(8,128)} %copy-done.1) | copy-start | bytes 3145732
  107.4 13.7 %collective-permute-start.12 = (f32[64,512]{0,1:T(8,128)}, f32[64,512]{0,1:T(8,128)S(1)}, u32[]{:S(2)}, u32[]{:S(2)}) collective-permute-start(f32[64,512]{0,1:T(8,128)} %get-tuple-element.27), channel_id=1, source_target_pairs={{0,16},{8,24},{16,32},{24,40},{32,48},{40,56},{48,64},{56,72},{64,... | collective-permute-start | bytes 393224 | tf_op jit(solution)/shard_map/ppermute | solution.py:17
  112.1 34.6 %copy-start.18 = (f32[512]{0:T(512)}, f32[512]{0:T(512)S(1)}, u32[]{:S(2)}) copy-start(f32[512]{0:T(512)S(1)} %fusion.137) | copy-start | bytes 6148
  112.1 12.7 %collective-permute-start.13 = (f32[64,512]{0,1:T(8,128)}, f32[64,512]{0,1:T(8,128)S(1)}, u32[]{:S(2)}, u32[]{:S(2)}) collective-permute-start(f32[64,512]{0,1:T(8,128)} %get-tuple-element.26), channel_id=1, source_target_pairs={{0,8},{8,16},{16,24},{24,32},{32,40},{40,48},{48,56},{56,64},{64,7... | collective-permute-start | bytes 393224 | tf_op jit(solution)/shard_map/ppermute | solution.py:17
  115.7 11.9 %collective-permute-start.14 = (f32[64,512]{0,1:T(8,128)}, f32[64,512]{0,1:T(8,128)S(1)}, u32[]{:S(2)}, u32[]{:S(2)}) collective-permute-start(f32[64,512]{0,1:T(8,128)} %get-tuple-element.25), channel_id=1, source_target_pairs={{8,0},{16,8},{24,16},{32,24},{40,32},{48,40},{56,48},{64,56},{72,6... | collective-permute-start | bytes 393224 | tf_op jit(solution)/shard_map/ppermute | solution.py:17
  121.2 9.7 %collective-permute-start.15 = (f32[64,512]{0,1:T(8,128)S(1)}, f32[64,512]{0,1:T(8,128)S(1)}, u32[]{:S(2)}, u32[]{:S(2)}) collective-permute-start(f32[64,512]{0,1:T(8,128)S(1)} %copy-done.10), channel_id=1, source_target_pairs={{16,0},{24,8},{32,16},{40,24},{48,32},{56,40},{64,48},{72,56},{80,... | collective-permute-start | bytes 393224 | tf_op jit(solution)/shard_map/ppermute | solution.py:17
  124.7 10.3 %collective-permute-start.16 = (f32[64,512]{0,1:T(8,128)S(1)}, f32[64,512]{0,1:T(8,128)S(1)}, u32[]{:S(2)}, u32[]{:S(2)}) collective-permute-start(f32[64,512]{0,1:T(8,128)S(1)} %get-tuple-element.23), channel_id=1, source_target_pairs={{24,0},{32,8},{40,16},{48,24},{56,32},{64,40},{72,48},{80,56},{88,... | collective-permute-start | bytes 393224 | tf_op jit(solution)/shard_map/ppermute | solution.py:17
  127.7 18.3 %collective-permute-start.17 = (f32[64,512]{0,1:T(8,128)S(1)}, f32[64,512]{0,1:T(8,128)S(1)}, u32[]{:S(2)}, u32[]{:S(2)}) collective-permute-start(f32[64,512]{0,1:T(8,128)S(1)} %get-tuple-element.22), channel_id=1, source_target_pairs={{32,0},{40,8},{48,16},{56,24},{64,32},{72,40},{80,48},{88,56},{96,... | collective-permute-start | bytes 393224 | tf_op jit(solution)/shard_map/ppermute | solution.py:17
  157.5 18.5 %copy-start.19 = (f32[512]{0:T(512)S(1)}, f32[512]{0:T(512)}, u32[]{:S(2)}) copy-start(f32[512]{0:T(512)} %copy-done.18) | copy-start | bytes 6148
  161.6 15.0 %copy-start.21 = (f32[512]{0:T(512)S(1)}, f32[512]{0:T(512)}, u32[]{:S(2)}) copy-start(f32[512]{0:T(512)} %copy-done.20) | copy-start | bytes 6148
  182.3 30.4 %copy-start.8 = (f32[64,512]{0,1:T(8,128)S(1)}, f32[64,512]{0,1:T(8,128)}, u32[]{:S(2)}) copy-start(f32[64,512]{0,1:T(8,128)} %constant_dynamic-update-slice_fusion.3) | copy-start | bytes 393220
  267.1 41.5 %copy-start.23 = (s32[4]{0:T(128)S(1)}, s32[4]{0:T(128)}, u32[]{:S(2)}) copy-start(s32[4]{0:T(128)} %iota_multiply_fusion) | copy-start | bytes 52
  (10 other events, 27.3 us)
where the time goes:
time: 371 us; the launch traced here: 364 us
  other arithmetic  140 us (38%)
  local copies, waits for them, and re-layouts  79.3 us (21%)
  starting transfers between devices  55 us (15%)
  matrix products  40.9 us (11%)
  blocking collectives  28.9 us (8%)
  waiting for transfers between devices  14.7 us (4%)
  between operations  4.82 us (1%)
    another operation x15, other arithmetic, body(): factor = jnp.linalg.cholesky(coarse)  79.3 us
    ppermute x16, starting transfers between devices, passed_along(): return lax.ppermute(block, axis, route)  48.5 us
    another operation x3, other arithmetic, body(): lax.linalg.triangular_solve(factor, right_side, left_side=True, lower=True)  42.1 us
    all_gather x1, blocking collectives, body(): lax.all_gather(bands, 'coarse', axis=0, tiled=True).reshape(groups, 3, K, K)  28.9 us
    dot_general x20, matrix products, pair_gram(): return jnp.einsum('kp,lp->kl', left, right, precision=highest)  28.2 us
    gather x1, local copies, waits for them, and re-layouts, body(): jnp.take(flat_sigma, row_index.reshape(-1)).reshape(2 * REACH, pad_rows)  23 us
    gather x1, local copies, waits for them, and re-layouts, body(): jnp.take(flat, row_index.reshape(-1), axis=1)  16.3 us
    ppermute x16, waiting for transfers between devices, passed_along(): return lax.ppermute(block, axis, route)  14.7 us
  transfers between devices with their start and end apart: 18, of which 3 were waited for; matrix products, arithmetic and copies ran while one was open for 14% of the time, Pallas kernels for 0%

commit v1 on v0

v1 whole, which is shorter than its diff:
```python
import jax
import jax.numpy as jnp
from jax import lax
from jax.experimental import pallas as pl
from jax.experimental.pallas import tpu as pltpu
from jax.sharding import PartitionSpec as P

K = 64
CX = 16
CY = 32
CZ = 16
FACE = 512
REACH = 4
ROWS = K + 8

f32 = jnp.float32
bf16 = jnp.bfloat16
VMEM = pl.BlockSpec(memory_space=pltpu.VMEM)
SMEM = pl.BlockSpec(memory_space=pltpu.SMEM)
MATRIX = (((1,), (0,)), ((), ()))
GRAM = (((1,), (1,)), ((), ()))


def product(left, right, dims):
    return lax.dot_general(left, right, dims, preferred_element_type=f32)


def harmonic(first, second):
    return 2.0 * first * second / (first + second)


def halves(x):
    high = x.astype(bf16)
    return high, (x - high.astype(f32)).astype(bf16)


def stacked(x):
    return jnp.concatenate(halves(x), axis=0)


def quadrants(square):
    half = square[:K] + square[K:]
    return half[:, :K] + half[:, K:]


def rows_of(vectors, sigma):
    high, low = halves(sigma)
    tail = jnp.concatenate([high.astype(f32), low.astype(f32)], axis=0).astype(bf16)
    return jnp.concatenate([*halves(vectors), tail], axis=0)


def joined(found):
    return jnp.concatenate(
        [found[:K] + found[K : 2 * K], found[2 * K : 2 * K + 8] + found[2 * K + 8 :]], axis=0
    )


def fetch(source, strips, sems):
    copies = [
        pltpu.make_async_copy(source.at[:, pl.ds(128 * q, 128)], strips.at[q], sems.at[q])
        for q in range(4)
    ]
    for copy in copies:
        copy.start()
    return copies


def layer_of(strips, z):
    return jnp.concatenate([strips[q, pl.ds(z, K, stride=CZ), :] for q in range(4)], axis=1)


def pick_kernel(vectors_ref, sigma_ref, index_ref, *outs):
    picked, top_ref, bottom_ref, strips, sems = outs[:8], *outs[8:]
    copies = fetch(vectors_ref, strips, sems)
    lane = lax.broadcasted_iota(jnp.int32, (1, 256), 1)
    within = lane % 128
    cell_of_lane = (within % CY) * CX + jnp.where(lane >= 128, CX - 1, 0)
    cell = lax.broadcasted_iota(jnp.int32, (FACE, 256), 0)
    faces = jnp.zeros((4 * 144, 256), f32)
    for copy in copies:
        copy.wait()
    for step in range(4):
        groups = []
        for group in range(4):
            z = 4 * group + step
            layer = layer_of(strips, z)
            sigma = jnp.broadcast_to(sigma_ref[z : z + 1, :], (8, FACE))
            groups.append(rows_of(layer, sigma))
            if z == 0:
                bottom_ref[...] = jnp.concatenate([layer, sigma], axis=0)
            if z == CZ - 1:
                top_ref[...] = jnp.concatenate([layer, sigma], axis=0)
        chosen = jnp.where(within // CY == step, cell_of_lane, -1)
        select = jnp.where(cell == chosen, 1.0, 0.0).astype(bf16)
        faces = faces + product(jnp.concatenate(groups, axis=0), select, MATRIX)
    place = lax.broadcasted_iota(jnp.int32, (FACE, FACE), 0)
    for side in range(2):
        table = jnp.concatenate(
            [
                faces[144 * group : 144 * (group + 1), 128 * side : 128 * (side + 1)]
                for group in range(4)
            ],
            axis=1,
        ).astype(bf16)
        for slot in range(REACH * side, REACH * (side + 1)):
            cell_index = index_ref[slot : slot + 1, :]
            wanted = (cell_index >> 9) * CY + ((cell_index >> 4) & (CY - 1))
            select = jnp.where(place == wanted, 1.0, 0.0).astype(bf16)
            picked[slot][...] = joined(product(table, select, MATRIX))


def own_kernel(vectors_ref, sigma_ref, storage_ref, own_ref, strips, sems):
    copies = fetch(vectors_ref, strips, sems)
    sigma = sigma_ref[...]
    lane = lax.broadcasted_iota(jnp.int32, (CZ, FACE), 1)
    layer = lax.broadcasted_iota(jnp.int32, (CZ, FACE), 0)
    along_x = jnp.where(
        lane % CX == CX - 1, 0.0, harmonic(sigma, pltpu.roll(sigma, FACE - 1, 1))
    )
    along_y = jnp.where(
        lane >= FACE - CX, 0.0, harmonic(sigma, pltpu.roll(sigma, FACE - CX, 1))
    )
    along_z = jnp.where(layer == CZ - 1, 0.0, harmonic(sigma, pltpu.roll(sigma, CZ - 1, 0)))
    half = 0.5 * (
        storage_ref[...]
        + along_x
        + pltpu.roll(along_x, 1, 1)
        + along_y
        + pltpu.roll(along_y, CX, 1)
        + along_z
        + pltpu.roll(along_z, 1, 0)
    )
    total = jnp.zeros((2 * K, 2 * K), f32)
    for copy in copies:
        copy.wait()
    below = layer_of(strips, 0)
    for z in range(CZ):
        now = below
        applied = half[z : z + 1] * now
        applied = applied - along_x[z : z + 1] * pltpu.roll(now, FACE - 1, 1)
        applied = applied - along_y[z : z + 1] * pltpu.roll(now, FACE - CX, 1)
        if z < CZ - 1:
            below = layer_of(strips, z + 1)
            applied = applied - along_z[z : z + 1] * below
        total = total + product(stacked(now), stacked(applied), GRAM)
    own = quadrants(total)
    own_ref[...] = own + own.T


def weights_of(counts_ref, own_refs, partner_refs):
    place = lax.broadcasted_iota(jnp.int32, (1, FACE), 1)
    result = []
    for slot in range(2 * REACH):
        pair = harmonic(own_refs[slot][K : K + 1, :], partner_refs[slot][K : K + 1, :])
        result.append(jnp.where(place < counts_ref[slot], pair, 0.0))
    return result


def block_kernel(counts_ref, level_ref, own_ref, *refs):
    own_refs, partner_refs = refs[:8], refs[8:16]
    top_ref, bottom_ref, below_ref, above_ref, out_ref = refs[16:]
    weights = weights_of(counts_ref, own_refs, partner_refs)
    total = jnp.zeros((2 * K, 2 * K), f32)
    for slot in range(2 * REACH):
        rows = own_refs[slot][:K, :]
        total = total + product(stacked(rows * weights[slot]), stacked(rows), GRAM)
    top = top_ref[:K, :]
    upward = harmonic(top_ref[K : K + 1, :], above_ref[:1, :])
    total = total + product(stacked(top * upward), stacked(top), GRAM)
    bottom = bottom_ref[:K, :]
    downward = harmonic(bottom_ref[K : K + 1, :], below_ref[K : K + 1, :])
    weighted = stacked(bottom * downward)
    total = total + product(weighted, stacked(bottom), GRAM)
    own = own_ref[...] + quadrants(total)
    own = 0.5 * (own + own.T)
    lower = -quadrants(product(weighted, stacked(below_ref[:K, :]), GRAM))
    even = level_ref[0] % 2 == 0
    payload = jnp.where(
        even, jnp.concatenate([own, lower], axis=1), jnp.concatenate([lower, own], axis=1)
    )
    for copy in range(8):
        out_ref[copy] = payload


def lateral_kernel(counts_ref, *refs):
    own_refs, partner_refs, out_ref = refs[:8], refs[8:16], refs[16]
    weights = weights_of(counts_ref, own_refs, partner_refs)
    blocks = []
    for slot in range(2 * REACH):
        rows = own_refs[slot][:K, :] * -weights[slot]
        blocks.append(quadrants(product(stacked(rows), stacked(partner_refs[slot][:K, :]), GRAM)))
    out_ref[...] = jnp.concatenate(blocks, axis=1)


def eliminate(rows, right, offset, lane, sub):
    factor_rows, inverse_rows = [], []
    wide = (8, 128)
    for panel in range(8):
        first = offset + 8 * panel
        column = [[None] * 16 for _ in range(8)]
        for k in range(8):
            for g in range(panel, 16):
                column[k][g] = jnp.broadcast_to(rows[g][:, first + k : first + k + 1], wide)
        pivot = [[None] * 8 for _ in range(8)]
        for i in range(8):
            for k in range(i, 8):
                pivot[i][k] = jnp.broadcast_to(column[i][panel][k : k + 1, :], wide)
        left_row = [jnp.broadcast_to(rows[panel][k : k + 1, :], wide) for k in range(8)]
        right_row = [jnp.broadcast_to(right[panel][k : k + 1, :], wide) for k in range(8)]
        kept = jnp.zeros(wide, f32)
        kept_right = jnp.zeros(wide, f32)
        for i in range(8):
            scale = lax.rsqrt(pivot[i][i])
            inverse = 1.0 / pivot[i][i]
            kept = jnp.where(sub == i, jnp.where(lane >= first + i, left_row[i], 0.0) * scale if offset == 0 else jnp.where((lane >= first + i) | (lane < 64), left_row[i], 0.0) * scale, kept)
            kept_right = jnp.where(sub == i, right_row[i] * scale, kept_right)
            left_row[i] = left_row[i] * inverse
            right_row[i] = right_row[i] * inverse
            scaled = [None] * 8
            for l in range(i + 1, 8):
                scaled[l] = pivot[i][l] * inverse
            for k in range(8):
                if k == i:
                    continue
                by = pivot[i][k] if k > i else pivot[k][i]
                left_row[k] = left_row[k] - by * left_row[i]
                right_row[k] = right_row[k] - by * right_row[i]
                for l in range(max(i + 1, k), 8):
                    pivot[k][l] = pivot[k][l] - by * scaled[l]
            pivot[i] = scaled
        for g in range(panel + 1, 16):
            for k in range(8):
                rows[g] = rows[g] - column[k][g] * left_row[k]
                right[g] = right[g] - column[k][g] * right_row[k]
        factor_rows.append(kept)
        inverse_rows.append(kept_right)
    return factor_rows, inverse_rows

def chol_kernel(level_ref, blocks_ref, lateral_ref, factor_ref, panel_ref, cross, top, top_right, inverse):
    lane = lax.broadcasted_iota(jnp.int32, (8, 128), 1)
    sub = lax.broadcasted_iota(jnp.int32, (8, 128), 0)
    level = level_ref[0]
    zero = jnp.zeros((64, 128), f32)
    factor_ref[...] = jnp.zeros((512, 512), f32)
    for c in range(1, 8):
        block = blocks_ref[c]
        if c % 2 == 1:
            cross[c - 1] = jnp.concatenate([zero, block], axis=0).T[:64]
        else:
            cross[c - 1] = jnp.concatenate([block, zero], axis=0).T[64:]
    cross[7] = zero
    def unit(g, c):
        return jnp.where((lane == sub + 8 * g) & (level == c), 1.0, 0.0)
    for g in range(8):
        top[pl.ds(8 * g, 8), :] = blocks_ref[0, pl.ds(8 * g, 8), :]
        top_right[pl.ds(8 * g, 8), :] = unit(g, 0)

    @pl.loop(0, 4)
    def _(q):
        c = 2 * q
        last = q == 3
        at = [pl.ds(8 * g, 8) for g in range(8)]
        rows = [jnp.where(lane < 64, top[at[g], :], cross[c, at[g], :]) for g in range(8)]
        rows += [blocks_ref[c + 1, at[g], :] for g in range(8)]
        right = [top_right[at[g], :] for g in range(8)] + [unit(g, c + 1) for g in range(8)]
        even, even_right = eliminate(rows, right, 0, lane, sub)
        nxt = jnp.minimum(c + 2, 7)
        middle = [jnp.where(lane < 64, cross[c + 1, at[g], :], rows[8 + g]) for g in range(8)]
        middle += [jnp.where(last, 0.0, blocks_ref[nxt, at[g], :]) for g in range(8)]
        middle_right = right[8:] + [unit(g, c + 2) for g in range(8)]
        odd, odd_right = eliminate(middle, middle_right, 64, lane, sub)
        for g in range(8):
            top[at[g], :] = middle[8 + g]
            top_right[at[g], :] = middle_right[8 + g]
            inverse[pl.ds(pl.multiple_of(128 * q, 128) + 8 * g, 8), :] = even_right[g]
            inverse[pl.ds(pl.multiple_of(128 * q, 128) + 64 + 8 * g, 8), :] = odd_right[g]
        both = jnp.concatenate(even + odd, axis=0).T
        wide_lane = lax.broadcasted_iota(jnp.int32, (64, 128), 1)
        start = pl.multiple_of(128 * q, 128)
        cols = pl.ds(start, 128)
        factor_ref[pl.ds(start, 64), cols] = jnp.where(wide_lane < 64, both[:64], 0.0)
        factor_ref[pl.ds(start + 64, 64), cols] = both[64:]
        @pl.when(q < 3)
        def _():
            factor_ref[pl.ds(start + 128, 64), cols] = jnp.where(wide_lane < 64, 0.0, both[:64])
    gh, gm = halves(inverse[:, :64])
    bh, bm = halves(lateral_ref[...])
    left = jnp.concatenate([gh, gm, gh], axis=1)
    down = jnp.concatenate([bh, bh, bm], axis=0)
    panel_ref[...] = jnp.dot(left, down, preferred_element_type=f32)


ANYWHERE = pl.BlockSpec(memory_space=pl.ANY)
STRIPS = (pltpu.VMEM((4, K * CZ, 128), f32), pltpu.SemaphoreType.DMA((4,)))


def call(kernel, name, outs, operands, smem=0, anywhere=0, flops=10**8, scratch=()):
    return pl.pallas_call(
        kernel,
        out_shape=outs,
        in_specs=[SMEM] * smem + [ANYWHERE] * anywhere + [VMEM] * (len(operands) - smem - anywhere),
        out_specs=jax.tree.map(lambda _: VMEM, outs),
        scratch_shapes=scratch,
        compiler_params=pltpu.CompilerParams(vmem_limit_bytes=40 * 2**20),
        cost_estimate=pl.CostEstimate(flops=flops, bytes_accessed=2 * 10**6, transcendentals=1000),
        name=name,
    )(*operands)


def array(*shape):
    return jax.ShapeDtypeStruct(shape, f32)


def passed_along(block, axis, distance):
    devices = range(lax.axis_size(axis))
    route = [(i - distance, i) for i in devices if i - distance in devices]
    return lax.ppermute(block, axis, route)


def body(deflation, conductivity, storage, interface_rows, interface_counts):
    vectors = deflation[0].reshape(K * CZ, FACE)
    sigma = conductivity[0]
    counts = interface_counts.reshape(2 * REACH)
    level = lax.axis_index("coarse").reshape(1)
    *picked, top, bottom = call(
        pick_kernel,
        "pick",
        (array(ROWS, FACE),) * 10,
        (vectors, sigma, interface_rows[0, 0]),
        anywhere=1,
        scratch=STRIPS,
    )
    partners = [None] * (2 * REACH)
    for distance in (4, 3, 2, 1):
        ahead, behind = REACH + distance - 1, REACH - distance
        partners[behind] = passed_along(picked[ahead], "sub", distance)
        partners[ahead] = passed_along(picked[behind], "sub", -distance)
    below = passed_along(top, "coarse", 1)
    above = passed_along(bottom[K:], "coarse", -1)
    own = call(own_kernel, "own", array(K, K), (vectors, sigma, storage[0]), anywhere=1, scratch=STRIPS)
    payload = call(
        block_kernel,
        "block",
        array(8, K, 2 * K),
        (counts, level, own, *picked, *partners, top, bottom, below, above),
        smem=2,
    )
    blocks = lax.all_to_all(payload, "coarse", 0, 0)
    lateral = call(
        lateral_kernel, "lateral", array(K, 8 * K), (counts, *picked, *partners), smem=1
    )
    factor, panel = call(
        chol_kernel,
        "factor",
        (array(8 * K, 8 * K), array(8 * K, 8 * K)),
        (level, blocks, lateral),
        smem=1,
        flops=10**9,
        scratch=(
            pltpu.VMEM((8, K, 2 * K), f32),
            pltpu.VMEM((K, 2 * K), f32),
            pltpu.VMEM((K, 2 * K), f32),
            pltpu.VMEM((8 * K, 2 * K), f32),
        ),
    )
    return (factor[None], panel[None, None])


def solution(mesh):
    placed = (
        P("sub", None, "coarse", None),
        P("sub", "coarse", None),
        P("sub", "coarse", None),
        P("sub", "coarse", None, None),
        P("sub", "coarse", None),
    )
    return jax.shard_map(
        body,
        mesh=mesh,
        in_specs=placed,
        out_specs=(P("sub", None, None), P("sub", "coarse", None, None)),
        check_vma=False,
    )
```

time: 371 us -> 99 us (0.27)
  the two profiles are of different devices: /device:TPU:2 before, /device:TPU:10 now
where the time goes in v1:
time: 99 us; the launch traced here: 98.4 us
  starting transfers between devices  38.4 us (39%)
  Pallas kernels  33.4 us (34%)
  waiting for transfers between devices  19.2 us (19%)
  local copies, waits for them, and re-layouts  6.38 us (6%)
    pallas_call x5, Pallas kernels, call(): pl.pallas_call(kernel, out_shape=outs, in_specs=[SMEM] * smem + [ANYWHERE...  33.4 us
    ppermute x10, starting transfers between devices, passed_along(): return lax.ppermute(block, axis, route)  30.1 us
    all_to_all x1, waiting for transfers between devices, body(): blocks = lax.all_to_all(payload, 'coarse', 0, 0)  10.1 us
    ppermute x10, waiting for transfers between devices, passed_along(): return lax.ppermute(block, axis, route)  9.19 us
    all_to_all x1, starting transfers between devices, body(): blocks = lax.all_to_all(payload, 'coarse', 0, 0)  8.32 us
    unnamed x38, local copies, waits for them, and re-layouts  6.37 us
  transfers between devices with their start and end apart: 11, of which 3 were waited for; matrix products, arithmetic and copies ran while one was open for 0% of the time, Pallas kernels for 5%

profile of v1, /device:TPU:10, one launch (start us, length us, event | category | flops | bytes accessed | tf_op | source)
XLA Modules:
  0.0 98.4 jit_solution(4495214834456929156)
XLA Ops:
  0.6 1.6 %copy-done = f32[1,64,16,512]{3,2,1,0:T(8,128)S(1)} copy-done((f32[1,64,16,512]{3,2,1,0:T(8,128)S(1)}, f32[1,64,16,512]{3,2,1,0:T(8,128)}, u32[]{:S(2)}) %copy-start) | copy-done | bytes 2097176
  2.2 0.8 copy-done.14
  3.0 0.7 copy-done.17
  3.7 3.0 %pick.1 = (f32[72,512]{1,0:T(8,128)S(1)}, f32[72,512]{1,0:T(8,128)S(1)}, f32[72,512]{1,0:T(8,128)S(1)}, f32[72,512]{1,0:T(8,128)S(1)}, f32[72,512]{1,0:T(8,128)S...) custom-call(f32[1024,512]{1,0:T(8,128)S(1)} %bitcast.8, ...), custom_call_target="tpu_custom_call" | custom-call | flops 100000000 | bytes 2000000 | tf_op jit(solution)/shard_map/pick/pallas_call | solution.py:298
  6.7 3.8 %collective-permute-start.8 = (f32[72,512]{1,0:T(8,128)S(1)}, f32[72,512]{1,0:T(8,128)S(1)}, u32[]{:S(2)}, u32[]{:S(2)}) collective-permute-start(f32[72,512]{1,0:T(8,128)S(1)} %get-tuple-element.22.refs_16_), channel_id=1, source_target_pairs={{0,1},{1,2},{2,3},{3,4},{4,5},{5,6},{6,7},{8,9},{9,10},{10,11},{11... | collective-permute-start | bytes 442376 | tf_op jit(solution)/shard_map/ppermute | solution.py:317
  10.5 0.0 copy-start.10
  10.5 0.7 copy-done.10
  11.2 3.9 %collective-permute-start.7 = (f32[72,512]{1,0:T(8,128)S(1)}, f32[72,512]{1,0:T(8,128)S(1)}, u32[]{:S(2)}, u32[]{:S(2)}) collective-permute-start(f32[72,512]{1,0:T(8,128)S(1)} %get-tuple-element.14.refs_0_), channel_id=1, source_target_pairs={{32,0},{40,8},{48,16},{56,24},{64,32},{72,40},{80,48},{88,56},{96,... | collective-permute-start | bytes 442376 | tf_op jit(solution)/shard_map/ppermute | solution.py:317
  15.1 2.2 %collective-permute-start.6 = (f32[72,512]{1,0:T(8,128)S(1)}, f32[72,512]{1,0:T(8,128)S(1)}, u32[]{:S(2)}, u32[]{:S(2)}) collective-permute-start(f32[72,512]{1,0:T(8,128)S(1)} %get-tuple-element.15.refs_1_), channel_id=1, source_target_pairs={{24,0},{32,8},{40,16},{48,24},{56,32},{64,40},{72,48},{80,56},{88,... | collective-permute-start | bytes 442376 | tf_op jit(solution)/shard_map/ppermute | solution.py:317
  17.3 3.1 %collective-permute-start.5 = (f32[72,512]{1,0:T(8,128)S(1)}, f32[72,512]{1,0:T(8,128)S(1)}, u32[]{:S(2)}, u32[]{:S(2)}) collective-permute-start(f32[72,512]{1,0:T(8,128)S(1)} %get-tuple-element.16.refs_2_), channel_id=1, source_target_pairs={{16,0},{24,8},{32,16},{40,24},{48,32},{56,40},{64,48},{72,56},{80,... | collective-permute-start | bytes 442376 | tf_op jit(solution)/shard_map/ppermute | solution.py:317
  20.4 0.7 copy-done.8
  21.1 1.3 %collective-permute-start.9 = (f32[8,512]{1,0:T(8,128)S(1)}, f32[8,512]{1,0:T(8,128)S(1)}, u32[]{:S(2)}, u32[]{:S(2)}) collective-permute-start(f32[8,512]{1,0:T(8,128)S(1)} %slice.3), channel_id=1, source_target_pairs={{1,0},{2,1},{3,2},{4,3},{5,4},{6,5},{7,6},{9,8},{10,9},{11,10},{12... | collective-permute-start | bytes 49160 | tf_op jit(solution)/shard_map/ppermute | solution.py:317
  22.4 4.3 %collective-permute-done.9.refs_19_ = f32[8,512]{1,0:T(8,128)S(1)} collective-permute-done((f32[8,512]{1,0:T(8,128)S(1)}, f32[8,512]{1,0:T(8,128)S(1)}, u32[]{:S(2)}, u32[]{:S(2)}) %collective-permute-start.9) | collective-permute-done | bytes 16416 | tf_op jit(solution)/shard_map/ppermute | solution.py:317
  26.7 1.9 %collective-permute-start.4 = (f32[72,512]{1,0:T(8,128)S(1)}, f32[72,512]{1,0:T(8,128)}, u32[]{:S(2)}, u32[]{:S(2)}) collective-permute-start(f32[72,512]{1,0:T(8,128)S(1)} %get-tuple-element.17.refs_3_), channel_id=1, source_target_pairs={{8,0},{16,8},{24,16},{32,24},{40,32},{48,40},{56,48},{64,56},{72,6... | collective-permute-start | bytes 442376 | tf_op jit(solution)/shard_map/ppermute | solution.py:317
  28.6 0.7 copy-done.12
  29.3 2.4 %collective-permute-start.3 = (f32[72,512]{1,0:T(8,128)S(1)}, f32[72,512]{1,0:T(8,128)}, u32[]{:S(2)}, u32[]{:S(2)}) collective-permute-start(f32[72,512]{1,0:T(8,128)S(1)} %get-tuple-element.18.refs_4_), channel_id=1, source_target_pairs={{0,8},{8,16},{16,24},{24,32},{32,40},{40,48},{48,56},{56,64},{64,7... | collective-permute-start | bytes 442376 | tf_op jit(solution)/shard_map/ppermute | solution.py:317
  31.7 3.2 %collective-permute-start.2 = (f32[72,512]{1,0:T(8,128)S(1)}, f32[72,512]{1,0:T(8,128)}, u32[]{:S(2)}, u32[]{:S(2)}) collective-permute-start(f32[72,512]{1,0:T(8,128)S(1)} %get-tuple-element.19.refs_5_), channel_id=1, source_target_pairs={{0,16},{8,24},{16,32},{24,40},{32,48},{40,56},{48,64},{56,72},{64,... | collective-permute-start | bytes 442376 | tf_op jit(solution)/shard_map/ppermute | solution.py:317
  34.9 0.6 copy-done.2
  35.5 5.3 %collective-permute-start.1 = (f32[72,512]{1,0:T(8,128)S(1)}, f32[72,512]{1,0:T(8,128)}, u32[]{:S(2)}, u32[]{:S(2)}) collective-permute-start(f32[72,512]{1,0:T(8,128)S(1)} %get-tuple-element.20.refs_6_), channel_id=1, source_target_pairs={{0,24},{8,32},{16,40},{24,48},{32,56},{40,64},{48,72},{56,80},{64,... | collective-permute-start | bytes 442376 | tf_op jit(solution)/shard_map/ppermute | solution.py:317
  40.8 0.0 copy-start.5
  40.8 0.7 copy-done.5
  41.5 3.1 %collective-permute-start = (f32[72,512]{1,0:T(8,128)S(1)}, f32[72,512]{1,0:T(8,128)}, u32[]{:S(2)}, u32[]{:S(2)}) collective-permute-start(f32[72,512]{1,0:T(8,128)S(1)} %get-tuple-element.21.refs_7_), channel_id=1, source_target_pairs={{0,32},{8,40},{16,48},{24,56},{32,64},{40,72},{48,80},{56,88},{64,... | collective-permute-start | bytes 442376 | tf_op jit(solution)/shard_map/ppermute | solution.py:317
  44.6 0.0 copy-start.6
  44.6 0.0 copy-start.11
  44.6 2.7 %own.1.own_ref = f32[64,64]{1,0:T(8,128)S(1)} custom-call(f32[1024,512]{1,0:T(8,128)S(1)} %bitcast.9, f32[16,512]{1,0:T(8,128)S(1)} %bitcast.11, f32[16,512]{1,0:T(8,128)S(1)} %bitcast.12), custom_call_target="tpu_custom_call" | custom-call | flops 100000000 | bytes 2000000 | tf_op jit(solution)/shard_map/own/pallas_call | solution.py:298
  47.3 0.0 copy-start.7
  47.4 4.8 %collective-permute-done.refs_8_ = f32[72,512]{1,0:T(8,128)} collective-permute-done((f32[72,512]{1,0:T(8,128)S(1)}, f32[72,512]{1,0:T(8,128)}, u32[]{:S(2)}, u32[]{:S(2)}) %collective-permute-start) | collective-permute-done | bytes 147488 | tf_op jit(solution)/shard_map/ppermute | solution.py:317
  52.2 2.7 %block.1 = f32[8,64,128]{2,1,0:T(8,128)} custom-call(s32[8]{0:T(128)S(1)} %bitcast.14, s32[1]{0:T(128)} %bitcast.level_ref, f32[64,64]{1,0:T(8,128)S(1)} %own.1.own_ref, f32[72,512]{1,0:T(8,128)S(1)} %get-tuple-element.14.refs_0_, f32[72,512]{1,0:T(8,128)S(1)} %get-tuple-element.15.refs_1_, f32[72,512]{1,0:T(8,128)S(1)} %get-tuple-element.16.refs_2_, ...), custom_call_target="tpu_custom_call" | custom-call | flops 100000000 | bytes 2000000 | tf_op jit(solution)/shard_map/block/pallas_call | solution.py:298
  55.0 8.3 %all-to-all-start = ((f32[8,64,128]{2,1,0:T(8,128)}), f32[8,64,128]{2,1,0:T(8,128)S(1)}, u32[]{:S(2)}, u32[]{:S(2)}) async-start(f32[8,64,128]{2,1,0:T(8,128)} %block.1), calls=%async_computation | async-start | bytes 524288 | tf_op jit(solution)/shard_map/all_to_all | solution.py:348
  63.3 1.8 %lateral.1.lateral_ref = f32[64,512]{1,0:T(8,128)S(1)} custom-call(s32[8]{0:T(128)S(1)} %bitcast.15, f32[72,512]{1,0:T(8,128)S(1)} %get-tuple-element.14.refs_0_, f32[72,512]{1,0:T(8,128)S(1)} %get-tuple-element.15.refs_1_, f32[72,512]{1,0:T(8,128)S(1)} %get-tuple-element.16.refs_2_, f32[72,512]{1,0:T(8,128)S(1)} %get-tuple-element.17.refs_3_, ...), custom_call_target="tpu_custom_call" | custom-call | flops 100000000 | bytes 2000000 | tf_op jit(solution)/shard_map/lateral/pallas_call | solution.py:298
  65.1 10.1 %all-to-all-done.blocks_ref = f32[8,64,128]{2,1,0:T(8,128)S(1)} async-done(((f32[8,64,128]{2,1,0:T(8,128)}), f32[8,64,128]{2,1,0:T(8,128)S(1)}, u32[]{:S(2)}, u32[]{:S(2)}) %all-to-all-start) | async-done | bytes 262176 | tf_op jit(solution)/shard_map/all_to_all | solution.py:348
  75.2 23.2 %factor.1 = (f32[512,512]{1,0:T(8,128)}, f32[512,512]{1,0:T(8,128)}) custom-call(s32[1]{0:T(128)} %bitcast.level_ref, f32[8,64,128]{2,1,0:T(8,128)S(1)} %all-to-all-done.blocks_ref, f32[64,512]{1,0:T(8,128)S(1)} %lateral.1.lateral_ref), custom_call_target="tpu_custom_call" | custom-call | flops 1000000000 | bytes 2000000 | tf_op jit(solution)/shard_map/factor/pallas_call | solution.py:298
  (34 shorter events, 0.1 us)
Async XLA Ops:
  0.6 1.6 %copy-start = (f32[1,64,16,512]{3,2,1,0:T(8,128)S(1)}, f32[1,64,16,512]{3,2,1,0:T(8,128)}, u32[]{:S(2)}) copy-start(f32[1,64,16,512]{3,2,1,0:T(8,128)} %param.5) | copy-start | bytes 6291460
  2.2 0.8 copy-start.14
  3.0 0.7 copy-start.17
  3.7 40.9 %copy-start.1 = (f32[1,64,16,512]{3,2,1,0:T(8,128)S(1)}, f32[1,64,16,512]{3,2,1,0:T(8,128)}, u32[]{:S(2)}) copy-start(f32[1,64,16,512]{3,2,1,0:T(8,128)} %param.5) | copy-start | bytes 6291460
  3.7 40.9 %copy-start.15 = (f32[1,16,512]{2,1,0:T(8,128)S(1)}, f32[1,16,512]{2,1,0:T(8,128)}, u32[]{:S(2)}) copy-start(f32[1,16,512]{2,1,0:T(8,128)} %param.6) | copy-start | bytes 98308
  3.7 40.9 %copy-start.16 = (f32[1,16,512]{2,1,0:T(8,128)S(1)}, f32[1,16,512]{2,1,0:T(8,128)}, u32[]{:S(2)}) copy-start(f32[1,16,512]{2,1,0:T(8,128)} %param.7) | copy-start | bytes 98308
  3.7 48.5 %copy-start.18 = (s32[1,1,8]{2,1,0:T(1,128)S(1)}, s32[1,1,8]{2,1,0:T(1,128)}, u32[]{:S(2)}) copy-start(s32[1,1,8]{2,1,0:T(1,128)} %param.9) | copy-start | bytes 100
  6.7 21.9 %collective-permute-start.8 = (f32[72,512]{1,0:T(8,128)S(1)}, f32[72,512]{1,0:T(8,128)S(1)}, u32[]{:S(2)}, u32[]{:S(2)}) collective-permute-start(f32[72,512]{1,0:T(8,128)S(1)} %get-tuple-element.22.refs_16_), channel_id=1, source_target_pairs={{0,1},{1,2},{2,3},{3,4},{4,5},{5,6},{6,7},{8,9},{9,10},{10,11},{11... | collective-permute-start | bytes 442376 | tf_op jit(solution)/shard_map/ppermute | solution.py:317
  10.5 0.7 copy-start.10
  11.2 20.5 %collective-permute-start.7 = (f32[72,512]{1,0:T(8,128)S(1)}, f32[72,512]{1,0:T(8,128)S(1)}, u32[]{:S(2)}, u32[]{:S(2)}) collective-permute-start(f32[72,512]{1,0:T(8,128)S(1)} %get-tuple-element.14.refs_0_), channel_id=1, source_target_pairs={{32,0},{40,8},{48,16},{56,24},{64,32},{72,40},{80,48},{88,56},{96,... | collective-permute-start | bytes 442376 | tf_op jit(solution)/shard_map/ppermute | solution.py:317
  15.1 19.7 %collective-permute-start.6 = (f32[72,512]{1,0:T(8,128)S(1)}, f32[72,512]{1,0:T(8,128)S(1)}, u32[]{:S(2)}, u32[]{:S(2)}) collective-permute-start(f32[72,512]{1,0:T(8,128)S(1)} %get-tuple-element.15.refs_1_), channel_id=1, source_target_pairs={{24,0},{32,8},{40,16},{48,24},{56,32},{64,40},{72,48},{80,56},{88,... | collective-permute-start | bytes 442376 | tf_op jit(solution)/shard_map/ppermute | solution.py:317
  17.3 23.5 %collective-permute-start.5 = (f32[72,512]{1,0:T(8,128)S(1)}, f32[72,512]{1,0:T(8,128)S(1)}, u32[]{:S(2)}, u32[]{:S(2)}) collective-permute-start(f32[72,512]{1,0:T(8,128)S(1)} %get-tuple-element.16.refs_2_), channel_id=1, source_target_pairs={{16,0},{24,8},{32,16},{40,24},{48,32},{56,40},{64,48},{72,56},{80,... | collective-permute-start | bytes 442376 | tf_op jit(solution)/shard_map/ppermute | solution.py:317
  20.4 0.7 copy-start.8
  21.1 5.6 %collective-permute-start.9 = (f32[8,512]{1,0:T(8,128)S(1)}, f32[8,512]{1,0:T(8,128)S(1)}, u32[]{:S(2)}, u32[]{:S(2)}) collective-permute-start(f32[8,512]{1,0:T(8,128)S(1)} %slice.3), channel_id=1, source_target_pairs={{1,0},{2,1},{3,2},{4,3},{5,4},{6,5},{7,6},{9,8},{10,9},{11,10},{12... | collective-permute-start | bytes 49160 | tf_op jit(solution)/shard_map/ppermute | solution.py:317
  26.7 20.6 %collective-permute-start.4 = (f32[72,512]{1,0:T(8,128)S(1)}, f32[72,512]{1,0:T(8,128)}, u32[]{:S(2)}, u32[]{:S(2)}) collective-permute-start(f32[72,512]{1,0:T(8,128)S(1)} %get-tuple-element.17.refs_3_), channel_id=1, source_target_pairs={{8,0},{16,8},{24,16},{32,24},{40,32},{48,40},{56,48},{64,56},{72,6... | collective-permute-start | bytes 442376 | tf_op jit(solution)/shard_map/ppermute | solution.py:317
  28.6 0.7 copy-start.12
  29.3 18.1 %collective-permute-start.3 = (f32[72,512]{1,0:T(8,128)S(1)}, f32[72,512]{1,0:T(8,128)}, u32[]{:S(2)}, u32[]{:S(2)}) collective-permute-start(f32[72,512]{1,0:T(8,128)S(1)} %get-tuple-element.18.refs_4_), channel_id=1, source_target_pairs={{0,8},{8,16},{16,24},{24,32},{32,40},{40,48},{48,56},{56,64},{64,7... | collective-permute-start | bytes 442376 | tf_op jit(solution)/shard_map/ppermute | solution.py:317
  31.7 15.7 %collective-permute-start.2 = (f32[72,512]{1,0:T(8,128)S(1)}, f32[72,512]{1,0:T(8,128)}, u32[]{:S(2)}, u32[]{:S(2)}) collective-permute-start(f32[72,512]{1,0:T(8,128)S(1)} %get-tuple-element.19.refs_5_), channel_id=1, source_target_pairs={{0,16},{8,24},{16,32},{24,40},{32,48},{40,56},{48,64},{56,72},{64,... | collective-permute-start | bytes 442376 | tf_op jit(solution)/shard_map/ppermute | solution.py:317
  34.9 0.7 copy-start.2
  35.5 11.8 %collective-permute-start.1 = (f32[72,512]{1,0:T(8,128)S(1)}, f32[72,512]{1,0:T(8,128)}, u32[]{:S(2)}, u32[]{:S(2)}) collective-permute-start(f32[72,512]{1,0:T(8,128)S(1)} %get-tuple-element.20.refs_6_), channel_id=1, source_target_pairs={{0,24},{8,32},{16,40},{24,48},{32,56},{40,64},{48,72},{56,80},{64,... | collective-permute-start | bytes 442376 | tf_op jit(solution)/shard_map/ppermute | solution.py:317
  40.8 0.7 copy-start.5
  41.5 10.8 %collective-permute-start = (f32[72,512]{1,0:T(8,128)S(1)}, f32[72,512]{1,0:T(8,128)}, u32[]{:S(2)}, u32[]{:S(2)}) collective-permute-start(f32[72,512]{1,0:T(8,128)S(1)} %get-tuple-element.21.refs_7_), channel_id=1, source_target_pairs={{0,32},{8,40},{16,48},{24,56},{32,64},{40,72},{48,80},{56,88},{64,... | collective-permute-start | bytes 442376 | tf_op jit(solution)/shard_map/ppermute | solution.py:317
  44.5 7.7 %copy-start.3 = (f32[72,512]{1,0:T(8,128)S(1)}, f32[72,512]{1,0:T(8,128)}, u32[]{:S(2)}) copy-start(f32[72,512]{1,0:T(8,128)} %copy-done.2) | copy-start | bytes 442372
  44.6 7.7 %copy-start.6 = (f32[72,512]{1,0:T(8,128)S(1)}, f32[72,512]{1,0:T(8,128)}, u32[]{:S(2)}) copy-start(f32[72,512]{1,0:T(8,128)} %copy-done.5) | copy-start | bytes 442372
  44.6 7.7 %copy-start.9 = (f32[72,512]{1,0:T(8,128)S(1)}, f32[72,512]{1,0:T(8,128)}, u32[]{:S(2)}) copy-start(f32[72,512]{1,0:T(8,128)} %copy-done.8) | copy-start | bytes 442372
  44.6 7.7 %copy-start.11 = (f32[72,512]{1,0:T(8,128)S(1)}, f32[72,512]{1,0:T(8,128)}, u32[]{:S(2)}) copy-start(f32[72,512]{1,0:T(8,128)} %copy-done.10) | copy-start | bytes 442372
  44.6 7.7 %copy-start.13 = (f32[72,512]{1,0:T(8,128)S(1)}, f32[72,512]{1,0:T(8,128)}, u32[]{:S(2)}) copy-start(f32[72,512]{1,0:T(8,128)} %copy-done.12) | copy-start | bytes 442372
  47.3 16.0 %copy-start.4 = (f32[72,512]{1,0:T(8,128)S(1)}, f32[72,512]{1,0:T(8,128)}, u32[]{:S(2)}) copy-start(f32[72,512]{1,0:T(8,128)} %copy-done.2) | copy-start | bytes 442372
  47.3 16.0 %copy-start.7 = (f32[72,512]{1,0:T(8,128)S(1)}, f32[72,512]{1,0:T(8,128)}, u32[]{:S(2)}) copy-start(f32[72,512]{1,0:T(8,128)} %copy-done.5) | copy-start | bytes 442372
  55.0 20.2 %all-to-all-start = ((f32[8,64,128]{2,1,0:T(8,128)}), f32[8,64,128]{2,1,0:T(8,128)S(1)}, u32[]{:S(2)}, u32[]{:S(2)}) async-start(f32[8,64,128]{2,1,0:T(8,128)} %block.1), calls=%async_computation | async-start | bytes 524288 | tf_op jit(solution)/shard_map/all_to_all | solution.py:348

commit v2 on v1

--- a/solution.py
+++ b/solution.py
@@ -1,3 +1,5 @@
+import functools
+
 import jax
 import jax.numpy as jnp
 from jax import lax
@@ -55,23 +57,19 @@
     )
 
 
-def fetch(source, strips, sems):
+def layer_of(strips, z):
+    return jnp.concatenate([strips[q, pl.ds(z, K, stride=CZ), :] for q in range(4)], axis=1)
+
+
+def pick_kernel(vectors_hbm, sigma_hbm, index_hbm, strips, own_ref, ahead_ref, behind_ref, top_ref, bottom_ref, first_ref, sigma_ref, index_ref, sems):
     copies = [
-        pltpu.make_async_copy(source.at[:, pl.ds(128 * q, 128)], strips.at[q], sems.at[q])
+        pltpu.make_async_copy(vectors_hbm.at[:, pl.ds(128 * q, 128)], strips.at[q], sems.at[q])
         for q in range(4)
     ]
+    copies.append(pltpu.make_async_copy(sigma_hbm, sigma_ref, sems.at[4]))
+    copies.append(pltpu.make_async_copy(index_hbm, index_ref, sems.at[5]))
     for copy in copies:
         copy.start()
-    return copies
-
-
-def layer_of(strips, z):
-    return jnp.concatenate([strips[q, pl.ds(z, K, stride=CZ), :] for q in range(4)], axis=1)
-
-
-def pick_kernel(vectors_ref, sigma_ref, index_ref, *outs):
-    picked, top_ref, bottom_ref, strips, sems = outs[:8], *outs[8:]
-    copies = fetch(vectors_ref, strips, sems)
     lane = lax.broadcasted_iota(jnp.int32, (1, 256), 1)
     within = lane % 128
     cell_of_lane = (within % CY) * CX + jnp.where(lane >= 128, CX - 1, 0)
@@ -88,6 +86,7 @@
             groups.append(rows_of(layer, sigma))
             if z == 0:
                 bottom_ref[...] = jnp.concatenate([layer, sigma], axis=0)
+                first_ref[...] = sigma
             if z == CZ - 1:
                 top_ref[...] = jnp.concatenate([layer, sigma], axis=0)
         chosen = jnp.where(within // CY == step, cell_of_lane, -1)
@@ -95,22 +94,28 @@
         faces = faces + product(jnp.concatenate(groups, axis=0), select, MATRIX)
     place = lax.broadcasted_iota(jnp.int32, (FACE, FACE), 0)
     for side in range(2):
-        table = jnp.concatenate(
+        wide = jnp.concatenate(
             [
                 faces[144 * group : 144 * (group + 1), 128 * side : 128 * (side + 1)]
                 for group in range(4)
             ],
             axis=1,
-        ).astype(bf16)
+        )
+        table = wide.astype(bf16)
+        out_ref = ahead_ref if side else behind_ref
+        out_ref[:K] = wide[:K] + wide[K : 2 * K]
         for slot in range(REACH * side, REACH * (side + 1)):
             cell_index = index_ref[slot : slot + 1, :]
             wanted = (cell_index >> 9) * CY + ((cell_index >> 4) & (CY - 1))
             select = jnp.where(place == wanted, 1.0, 0.0).astype(bf16)
-            picked[slot][...] = joined(product(table, select, MATRIX))
-
-
-def own_kernel(vectors_ref, sigma_ref, storage_ref, own_ref, strips, sems):
-    copies = fetch(vectors_ref, strips, sems)
+            found = product(table, select, MATRIX)
+            own_ref[slot] = found[: 2 * K].astype(bf16)
+            reach = slot - REACH if side else REACH - 1 - slot
+            out_ref[K + reach : K + reach + 1] = found[2 * K : 2 * K + 1] + found[2 * K + 8 : 2 * K + 9]
+            out_ref[K + 4 + reach : K + 5 + reach] = wanted.astype(f32)
+
+
+def own_kernel(strips, sigma_ref, storage_ref, top_ref, bottom_ref, below_ref, above_ref, own_ref, lower_ref):
     sigma = sigma_ref[...]
     lane = lax.broadcasted_iota(jnp.int32, (CZ, FACE), 1)
     layer = lax.broadcasted_iota(jnp.int32, (CZ, FACE), 0)
@@ -121,6 +126,8 @@
         lane >= FACE - CX, 0.0, harmonic(sigma, pltpu.roll(sigma, FACE - CX, 1))
     )
     along_z = jnp.where(layer == CZ - 1, 0.0, harmonic(sigma, pltpu.roll(sigma, CZ - 1, 0)))
+    downward = harmonic(bottom_ref[K : K + 1, :], below_ref[K : K + 1, :])
+    upward = harmonic(top_ref[K : K + 1, :], above_ref[:1, :])
     half = 0.5 * (
         storage_ref[...]
         + along_x
@@ -129,10 +136,10 @@
         + pltpu.roll(along_y, CX, 1)
         + along_z
         + pltpu.roll(along_z, 1, 0)
+        + jnp.where(layer == 0, downward, 0.0)
+        + jnp.where(layer == CZ - 1, upward, 0.0)
     )
     total = jnp.zeros((2 * K, 2 * K), f32)
-    for copy in copies:
-        copy.wait()
     below = layer_of(strips, 0)
     for z in range(CZ):
         now = below
@@ -145,35 +152,61 @@
         total = total + product(stacked(now), stacked(applied), GRAM)
     own = quadrants(total)
     own_ref[...] = own + own.T
-
-
-def weights_of(counts_ref, own_refs, partner_refs):
+    weighted = stacked(bottom_ref[:K, :] * downward)
+    lower_ref[...] = -quadrants(product(weighted, stacked(below_ref[:K, :]), GRAM))
+
+
+def pack_kernel(core_ref, ahead, behind, ahead2, behind2, ahead4, behind4, out_ref, *, rows):
+    count = rows.stop - rows.start
+    for core, chosen in ((0, (ahead, ahead2, behind2, behind4)), (1, (ahead2, ahead4, behind, behind2))):
+        @pl.when(core_ref[0] == core)
+        def _(chosen=chosen):
+            for at, ref in enumerate(chosen):
+                out_ref[count * at : count * (at + 1)] = ref[rows]
+
+
+def partner_tail(refs, offset):
+    ahead2, behind2, ahead4, behind4, tails = refs
+    if offset % 2:
+        at = {-1: 0, -3: 1, 1: 2, 3: 3}[offset]
+        return tails[8 * at : 8 * at + 8]
+    return {-2: ahead2, -4: ahead4, 2: behind2, 4: behind4}[offset][K : K + 8]
+
+
+def partner_face(refs, offset):
+    ahead2, behind2, ahead4, behind4, faces = refs
+    if offset % 2:
+        at = {-1: 0, -3: 1, 1: 2, 3: 3}[offset]
+        return faces[K * at : K * at + K]
+    return {-2: ahead2, -4: ahead4, 2: behind2, 4: behind4}[offset][:K]
+
+
+OFFSETS = (-4, -3, -2, -1, 1, 2, 3, 4)
+
+
+def weight_of(counts_ref, ahead, behind, slot, tail):
+    offset = OFFSETS[slot]
+    reach = abs(offset) - 1
     place = lax.broadcasted_iota(jnp.int32, (1, FACE), 1)
-    result = []
-    for slot in range(2 * REACH):
-        pair = harmonic(own_refs[slot][K : K + 1, :], partner_refs[slot][K : K + 1, :])
-        result.append(jnp.where(place < counts_ref[slot], pair, 0.0))
-    return result
-
-
-def block_kernel(counts_ref, level_ref, own_ref, *refs):
-    own_refs, partner_refs = refs[:8], refs[8:16]
-    top_ref, bottom_ref, below_ref, above_ref, out_ref = refs[16:]
-    weights = weights_of(counts_ref, own_refs, partner_refs)
+    mine = (ahead if offset > 0 else behind)[K + reach : K + reach + 1]
+    pair = harmonic(mine, tail[reach : reach + 1])
+    return jnp.where(place < counts_ref[slot], pair, 0.0)
+
+
+def weighted_rows(own_ref, slot, weight):
+    rows = own_ref[slot]
+    return stacked((rows[:K].astype(f32) + rows[K:].astype(f32)) * weight)
+
+
+def block_kernel(counts_ref, level_ref, own_block, lower_block, own_ref, ahead, behind, *refs):
+    *partners, out_ref = refs
     total = jnp.zeros((2 * K, 2 * K), f32)
-    for slot in range(2 * REACH):
-        rows = own_refs[slot][:K, :]
-        total = total + product(stacked(rows * weights[slot]), stacked(rows), GRAM)
-    top = top_ref[:K, :]
-    upward = harmonic(top_ref[K : K + 1, :], above_ref[:1, :])
-    total = total + product(stacked(top * upward), stacked(top), GRAM)
-    bottom = bottom_ref[:K, :]
-    downward = harmonic(bottom_ref[K : K + 1, :], below_ref[K : K + 1, :])
-    weighted = stacked(bottom * downward)
-    total = total + product(weighted, stacked(bottom), GRAM)
-    own = own_ref[...] + quadrants(total)
-    own = 0.5 * (own + own.T)
-    lower = -quadrants(product(weighted, stacked(below_ref[:K, :]), GRAM))
+    for slot, offset in enumerate(OFFSETS):
+        weight = weight_of(counts_ref, ahead, behind, slot, partner_tail(partners, offset))
+        total = total + product(weighted_rows(own_ref, slot, weight), own_ref[slot], GRAM)
+    extra = quadrants(total)
+    own = own_block[...] + 0.5 * (extra + extra.T)
+    lower = lower_block[...]
     even = level_ref[0] % 2 == 0
     payload = jnp.where(
         even, jnp.concatenate([own, lower], axis=1), jnp.concatenate([lower, own], axis=1)
@@ -182,13 +215,17 @@
         out_ref[copy] = payload
 
 
-def lateral_kernel(counts_ref, *refs):
-    own_refs, partner_refs, out_ref = refs[:8], refs[8:16], refs[16]
-    weights = weights_of(counts_ref, own_refs, partner_refs)
+def lateral_kernel(counts_ref, own_ref, ahead, behind, ahead2, behind2, ahead4, behind4, tails, faces, out_ref):
+    place = lax.broadcasted_iota(jnp.int32, (FACE, FACE), 0).astype(f32)
     blocks = []
-    for slot in range(2 * REACH):
-        rows = own_refs[slot][:K, :] * -weights[slot]
-        blocks.append(quadrants(product(stacked(rows), stacked(partner_refs[slot][:K, :]), GRAM)))
+    for slot, offset in enumerate(OFFSETS):
+        tail = partner_tail((ahead2, behind2, ahead4, behind4, tails), offset)
+        face = partner_face((ahead2, behind2, ahead4, behind4, faces), offset)
+        weight = weight_of(counts_ref, ahead, behind, slot, tail)
+        reach = abs(offset) - 1
+        select = jnp.where(place == tail[4 + reach : 5 + reach], 1.0, 0.0).astype(bf16)
+        found = product(stacked(face), select, MATRIX).astype(bf16)
+        blocks.append(quadrants(product(weighted_rows(own_ref, slot, -weight), found, GRAM)))
     out_ref[...] = jnp.concatenate(blocks, axis=1)
 
 
@@ -290,25 +327,24 @@
     panel_ref[...] = jnp.dot(left, down, preferred_element_type=f32)
 
 
-ANYWHERE = pl.BlockSpec(memory_space=pl.ANY)
-STRIPS = (pltpu.VMEM((4, K * CZ, 128), f32), pltpu.SemaphoreType.DMA((4,)))
-
-
-def call(kernel, name, outs, operands, smem=0, anywhere=0, flops=10**8, scratch=()):
+HBM = pl.BlockSpec(memory_space=pltpu.HBM)
+
+
+def call(kernel, name, outs, operands, smem=0, hbm=0, flops=10**8, scratch=(), limit=16):
     return pl.pallas_call(
         kernel,
         out_shape=outs,
-        in_specs=[SMEM] * smem + [ANYWHERE] * anywhere + [VMEM] * (len(operands) - smem - anywhere),
+        in_specs=[SMEM] * smem + [HBM] * hbm + [VMEM] * (len(operands) - smem - hbm),
         out_specs=jax.tree.map(lambda _: VMEM, outs),
         scratch_shapes=scratch,
-        compiler_params=pltpu.CompilerParams(vmem_limit_bytes=40 * 2**20),
+        compiler_params=pltpu.CompilerParams(vmem_limit_bytes=limit * 2**20),
         cost_estimate=pl.CostEstimate(flops=flops, bytes_accessed=2 * 10**6, transcendentals=1000),
         name=name,
     )(*operands)
 
 
-def array(*shape):
-    return jax.ShapeDtypeStruct(shape, f32)
+def array(*shape, dtype=f32):
+    return jax.ShapeDtypeStruct(shape, dtype)
 
 
 def passed_along(block, axis, distance):
@@ -322,32 +358,69 @@
     sigma = conductivity[0]
     counts = interface_counts.reshape(2 * REACH)
     level = lax.axis_index("coarse").reshape(1)
-    *picked, top, bottom = call(
+    core = (lax.axis_index("sub") % 2).reshape(1)
+    strips, mine, ahead, behind, top, bottom, first = call(
         pick_kernel,
         "pick",
-        (array(ROWS, FACE),) * 10,
-        (vectors, sigma, interface_rows[0, 0]),
-        anywhere=1,
-        scratch=STRIPS,
-    )
-    partners = [None] * (2 * REACH)
-    for distance in (4, 3, 2, 1):
-        ahead, behind = REACH + distance - 1, REACH - distance
-        partners[behind] = passed_along(picked[ahead], "sub", distance)
-        partners[ahead] = passed_along(picked[behind], "sub", -distance)
+        (
+            array(4, K * CZ, 128),
+            array(8, 2 * K, FACE, dtype=bf16),
+            array(ROWS, FACE),
+            array(ROWS, FACE),
+            array(ROWS, FACE),
+            array(ROWS, FACE),
+            array(8, FACE),
+        ),
+        tuple(
+            pltpu.with_memory_space_constraint(x, pltpu.HBM)
+            for x in (vectors, sigma, interface_rows[0, 0])
+        ),
+        hbm=3,
+        scratch=(
+            pltpu.VMEM((CZ, FACE), f32),
+            pltpu.VMEM((2 * REACH, FACE), jnp.int32),
+            pltpu.SemaphoreType.DMA((6,)),
+        ),
+    )
     below = passed_along(top, "coarse", 1)
-    above = passed_along(bottom[K:], "coarse", -1)
-    own = call(own_kernel, "own", array(K, K), (vectors, sigma, storage[0]), anywhere=1, scratch=STRIPS)
+    above = passed_along(first, "coarse", -1)
+    ahead4 = passed_along(ahead, "sub", 4)
+    behind4 = passed_along(behind, "sub", -4)
+    ahead2 = passed_along(ahead, "sub", 2)
+    behind2 = passed_along(behind, "sub", -2)
+    own, lower = call(
+        own_kernel,
+        "own",
+        (array(K, K), array(K, K)),
+        (strips, sigma, storage[0], top, bottom, below, above),
+    )
+    direct = (ahead2, behind2, ahead4, behind4)
+
+    def swapped(name, rows, after):
+        kernel = functools.partial(pack_kernel, rows=rows)
+        sent, after = lax.optimization_barrier(((core, ahead, behind, *direct), after))
+        packed = call(
+            kernel, name, array(4 * (rows.stop - rows.start), FACE), sent, smem=1, flops=10**6
+        )
+        route = [(i, i ^ 1) for i in range(lax.axis_size("sub"))]
+        return lax.ppermute(packed, "sub", route), after
+
+    tails, (own, lower) = swapped("tails", slice(K, ROWS), (own, lower))
     payload = call(
         block_kernel,
         "block",
         array(8, K, 2 * K),
-        (counts, level, own, *picked, *partners, top, bottom, below, above),
+        (counts, level, own, lower, mine, ahead, behind, *direct, tails),
         smem=2,
     )
+    faces, payload = swapped("faces", slice(0, K), payload)
     blocks = lax.all_to_all(payload, "coarse", 0, 0)
     lateral = call(
-        lateral_kernel, "lateral", array(K, 8 * K), (counts, *picked, *partners), smem=1
+        lateral_kernel,
+        "lateral",
+        array(K, 8 * K),
+        (counts, mine, ahead, behind, *direct, tails, faces),
+        smem=1,
     )
     factor, panel = call(
         chol_kernel,

time: 99 us -> 80.7 us (0.82)
  the two profiles are of different devices: /device:TPU:10 before, /device:TPU:15 now
where the time goes in v2:
time: 80.7 us; the launch traced here: 80.3 us
  Pallas kernels  34.3 us (43%)
  starting transfers between devices  27.3 us (34%)
  waiting for transfers between devices  14.9 us (18%)
  local copies, waits for them, and re-layouts  2.93 us (4%)
    pallas_call x7, Pallas kernels, call(): pl.pallas_call(kernel, out_shape=outs, in_specs=[SMEM] * smem + [HBM] * h...  34.3 us
    ppermute x6, starting transfers between devices, passed_along(): return lax.ppermute(block, axis, route)  17.2 us
    all_to_all x1, waiting for transfers between devices, body(): blocks = lax.all_to_all(payload, 'coarse', 0, 0)  9.58 us
    all_to_all x1, starting transfers between devices, body(): blocks = lax.all_to_all(payload, 'coarse', 0, 0)  8 us
    ppermute x6, waiting for transfers between devices, passed_along(): return lax.ppermute(block, axis, route)  4.44 us
    unnamed x10, local copies, waits for them, and re-layouts  2.93 us
    ppermute x2, starting transfers between devices, swapped(): return (lax.ppermute(packed, 'sub', route), after)  2.11 us
  transfers between devices with their start and end apart: 9, of which 4 were waited for; matrix products, arithmetic and copies ran while one was open for 0% of the time, Pallas kernels for 6%

profile of v2, /device:TPU:15, one launch (start us, length us, event | category | flops | bytes accessed | tf_op | source)
XLA Modules:
  0.0 80.3 jit_solution(16630875755281533864)
XLA Ops:
  0.6 0.0 copy-start.2
  0.6 0.0 copy-start.3
  0.7 4.3 %pick.1 = (f32[4,1024,128]{2,1,0:T(8,128)S(1)}, bf16[8,128,512]{2,1,0:T(8,128)(2,1)S(1)}, f32[72,512]{1,0:T(8,128)S(1)}, f32[72,512]{1,0:T(8,128)S(1)}, f32[72,5...) custom-call(f32[1024,512]{1,0:T(8,128)} %bitcast.14, f32[16,512]{1,0:T(8,128)} %bitcast.9, ...), custom_call_target="tpu_custom_call" | custom-call | flops 100000000 | bytes 2000000 | tf_op jit(solution)/shard_map/pick/pallas_call | solution.py:334
  4.9 0.0 copy-start
  4.9 1.3 %copy-done = f32[4,1024,128]{2,1,0:T(8,128)} copy-done((f32[4,1024,128]{2,1,0:T(8,128)}, f32[4,1024,128]{2,1,0:T(8,128)S(1)}, u32[]{:S(2)}) %copy-start) | copy-done | bytes 2097176
  6.3 1.4 %collective-permute-start.5 = (f32[8,512]{1,0:T(8,128)S(1)}, f32[8,512]{1,0:T(8,128)S(1)}, u32[]{:S(2)}, u32[]{:S(2)}) collective-permute-start(f32[8,512]{1,0:T(8,128)S(1)} %get-tuple-element.35), channel_id=1, source_target_pairs={{1,0},{2,1},{3,2},{4,3},{5,4},{6,5},{7,6},{9,8},{10,9},{11,10},{12... | collective-permute-start | bytes 49160 | tf_op jit(solution)/shard_map/ppermute | solution.py:353
  7.7 4.2 %collective-permute-start.4 = (f32[72,512]{1,0:T(8,128)S(1)}, f32[72,512]{1,0:T(8,128)S(1)}, u32[]{:S(2)}, u32[]{:S(2)}) collective-permute-start(f32[72,512]{1,0:T(8,128)S(1)} %get-tuple-element.33.top_ref), channel_id=1, source_target_pairs={{0,1},{1,2},{2,3},{3,4},{4,5},{5,6},{6,7},{8,9},{9,10},{10,11},{11... | collective-permute-start | bytes 442376 | tf_op jit(solution)/shard_map/ppermute | solution.py:353
  11.9 4.0 %collective-permute-start.2 = (f32[72,512]{1,0:T(8,128)S(1)}, f32[72,512]{1,0:T(8,128)S(1)}, u32[]{:S(2)}, u32[]{:S(2)}) collective-permute-start(f32[72,512]{1,0:T(8,128)S(1)} %get-tuple-element.50.ahead), channel_id=1, source_target_pairs={{0,32},{8,40},{16,48},{24,56},{32,64},{40,72},{48,80},{56,88},{64,... | collective-permute-start | bytes 442376 | tf_op jit(solution)/shard_map/ppermute | solution.py:353
  15.9 3.7 %collective-permute-start = (f32[72,512]{1,0:T(8,128)S(1)}, f32[72,512]{1,0:T(8,128)S(1)}, u32[]{:S(2)}, u32[]{:S(2)}) collective-permute-start(f32[72,512]{1,0:T(8,128)S(1)} %get-tuple-element.50.ahead), channel_id=1, source_target_pairs={{0,16},{8,24},{16,32},{24,40},{32,48},{40,56},{48,64},{56,72},{64,... | collective-permute-start | bytes 442376 | tf_op jit(solution)/shard_map/ppermute | solution.py:353
  19.7 1.9 %collective-permute-start.3 = (f32[72,512]{1,0:T(8,128)S(1)}, f32[72,512]{1,0:T(8,128)S(1)}, u32[]{:S(2)}, u32[]{:S(2)}) collective-permute-start(f32[72,512]{1,0:T(8,128)S(1)} %get-tuple-element.51.behind), channel_id=1, source_target_pairs={{32,0},{40,8},{48,16},{56,24},{64,32},{72,40},{80,48},{88,56},{96,... | collective-permute-start | bytes 442376 | tf_op jit(solution)/shard_map/ppermute | solution.py:353
  21.6 0.0 collective-permute-done.5.above_ref
  21.6 1.9 %collective-permute-start.1 = (f32[72,512]{1,0:T(8,128)S(1)}, f32[72,512]{1,0:T(8,128)S(1)}, u32[]{:S(2)}, u32[]{:S(2)}) collective-permute-start(f32[72,512]{1,0:T(8,128)S(1)} %get-tuple-element.51.behind), channel_id=1, source_target_pairs={{16,0},{24,8},{32,16},{40,24},{48,32},{56,40},{64,48},{72,56},{80,... | collective-permute-start | bytes 442376 | tf_op jit(solution)/shard_map/ppermute | solution.py:353
  23.5 0.0 collective-permute-done.4.below_ref
  23.5 0.0 copy-done.2
  23.6 0.0 copy-done.3
  23.6 0.0 copy-start.1
  23.6 1.6 %copy-done.1 = f32[4,1024,128]{2,1,0:T(8,128)S(1)} copy-done((f32[4,1024,128]{2,1,0:T(8,128)S(1)}, f32[4,1024,128]{2,1,0:T(8,128)}, u32[]{:S(2)}) %copy-start.1) | copy-done | bytes 2097176
  25.2 2.2 %own.1 = (f32[64,64]{1,0:T(8,128)S(1)}, f32[64,64]{1,0:T(8,128)S(1)}) custom-call(f32[4,1024,128]{2,1,0:T(8,128)S(1)} %copy-done.1, f32[16,512]{1,0:T(8,128)S(1)} %bitcast.10, f32[16,512]{1,0:T(8,128)S(1)} %bitcast.11, f32[72,512]{1,0:T(8,128)S(1)} %get-tuple-element.33.top_ref, f32[72,512]{1,0:T(8,128)S(1)} %get-tuple-element.34.bottom_ref, ...), custom_call_target="tpu_custom_call" | custom-call | flops 100000000 | bytes 2000000 | tf_op jit(solution)/shard_map/own/pallas_call | solution.py:334
  27.3 0.0 collective-permute-done.2.ahead4.refs_2_
  27.3 0.0 collective-permute-done.ahead2.refs_0_
  27.3 0.6 collective-permute-done.3.behind4.refs_3_
  27.9 3.8 %collective-permute-done.1.behind2.refs_1_ = f32[72,512]{1,0:T(8,128)S(1)} collective-permute-done((f32[72,512]{1,0:T(8,128)S(1)}, f32[72,512]{1,0:T(8,128)S(1)}, u32[]{:S(2)}, u32[]{:S(2)}) %collective-permute-start.1) | collective-permute-done | bytes 147488 | tf_op jit(solution)/shard_map/ppermute | solution.py:353
  31.8 1.7 %collective-permute-start.6 = (f32[32,512]{1,0:T(8,128)S(1)}, f32[32,512]{1,0:T(8,128)S(1)}, u32[]{:S(2)}, u32[]{:S(2)}) collective-permute-start(f32[32,512]{1,0:T(8,128)S(1)} %tails.1), channel_id=1, source_target_pairs={{0,8},{8,0},{16,24},{24,16},{32,40},{40,32},{48,56},{56,48},{64,72... | collective-permute-start | bytes 196616 | tf_op jit(solution)/shard_map/ppermute | solution.py:406
  33.4 0.9 %collective-permute-done.6.refs_4_.tails = f32[32,512]{1,0:T(8,128)S(1)} collective-permute-done((f32[32,512]{1,0:T(8,128)S(1)}, f32[32,512]{1,0:T(8,128)S(1)}, u32[]{:S(2)}, u32[]{:S(2)}) %collective-permute-start.6) | collective-permute-done | bytes 65568 | tf_op jit(solution)/shard_map/ppermute | solution.py:406
  34.4 0.0 copy-done.4
  34.4 1.9 %block.1 = f32[8,64,128]{2,1,0:T(8,128)} custom-call(s32[8]{0:T(128)S(1)} %bitcast.12, s32[1]{0:T(128)} %bitcast.level_ref, f32[64,64]{1,0:T(8,128)S(1)} %get-tuple-element.38.own_block, f32[64,64]{1,0:T(8,128)S(1)} %get-tuple-element.39.lower_block, bf16[8,128,512]{2,1,0:T(8,128)(2,1)S(1)} %get-tuple-element.40.own_ref, ...), custom_call_target="tpu_custom_call" | custom-call | flops 100000000 | bytes 2000000 | tf_op jit(solution)/shard_map/block/pallas_call | solution.py:334
  36.3 0.4 collective-permute-start.7
  36.8 8.0 %all-to-all-start = ((f32[8,64,128]{2,1,0:T(8,128)}), f32[8,64,128]{2,1,0:T(8,128)S(1)}, u32[]{:S(2)}, u32[]{:S(2)}) async-start(f32[8,64,128]{2,1,0:T(8,128)} %block.1), calls=%async_computation | async-start | bytes 524288 | tf_op jit(solution)/shard_map/all_to_all | solution.py:417
  44.8 0.0 collective-permute-done.7.faces
  44.8 2.7 %lateral.1.lateral_ref = f32[64,512]{1,0:T(8,128)S(1)} custom-call(s32[8]{0:T(128)S(1)} %bitcast.13, bf16[8,128,512]{2,1,0:T(8,128)(2,1)S(1)} %get-tuple-element.40.own_ref, f32[72,512]{1,0:T(8,128)S(1)} %get-tuple-element.50.ahead, f32[72,512]{1,0:T(8,128)S(1)} %get-tuple-element.51.behind, f32[72,512]{1,0:T(8,128)S(1)} %collective-permute-done.ahead2.refs_0_, ...), custom_call_target="tpu_custom_call" | custom-call | flops 100000000 | bytes 2000000 | tf_op jit(solution)/shard_map/lateral/pallas_call | solution.py:334
  47.5 9.6 %all-to-all-done.blocks_ref = f32[8,64,128]{2,1,0:T(8,128)S(1)} async-done(((f32[8,64,128]{2,1,0:T(8,128)}), f32[8,64,128]{2,1,0:T(8,128)S(1)}, u32[]{:S(2)}, u32[]{:S(2)}) %all-to-all-start) | async-done | bytes 262176 | tf_op jit(solution)/shard_map/all_to_all | solution.py:417
  57.0 23.2 %factor.1 = (f32[512,512]{1,0:T(8,128)}, f32[512,512]{1,0:T(8,128)}) custom-call(s32[1]{0:T(128)} %bitcast.level_ref, f32[8,64,128]{2,1,0:T(8,128)S(1)} %all-to-all-done.blocks_ref, f32[64,512]{1,0:T(8,128)S(1)} %lateral.1.lateral_ref), custom_call_target="tpu_custom_call" | custom-call | flops 1000000000 | bytes 2000000 | tf_op jit(solution)/shard_map/factor/pallas_call | solution.py:334
  (3 shorter events, 0.0 us)
Async XLA Ops:
  0.6 22.9 %copy-start.2 = (f32[1,16,512]{2,1,0:T(8,128)S(1)}, f32[1,16,512]{2,1,0:T(8,128)}, u32[]{:S(2)}) copy-start(f32[1,16,512]{2,1,0:T(8,128)} %param.6) | copy-start | bytes 98308
  0.6 22.9 %copy-start.3 = (f32[1,16,512]{2,1,0:T(8,128)S(1)}, f32[1,16,512]{2,1,0:T(8,128)}, u32[]{:S(2)}) copy-start(f32[1,16,512]{2,1,0:T(8,128)} %param.7) | copy-start | bytes 98308
  4.9 1.3 %copy-start = (f32[4,1024,128]{2,1,0:T(8,128)}, f32[4,1024,128]{2,1,0:T(8,128)S(1)}, u32[]{:S(2)}) copy-start(f32[4,1024,128]{2,1,0:T(8,128)S(1)} %get-tuple-element.32.strips) | copy-start | bytes 6291460
  6.3 28.1 %copy-start.4 = (s32[1,1,8]{2,1,0:T(1,128)S(1)}, s32[1,1,8]{2,1,0:T(1,128)}, u32[]{:S(2)}) copy-start(s32[1,1,8]{2,1,0:T(1,128)} %param.9) | copy-start | bytes 100
  6.3 15.3 %collective-permute-start.5 = (f32[8,512]{1,0:T(8,128)S(1)}, f32[8,512]{1,0:T(8,128)S(1)}, u32[]{:S(2)}, u32[]{:S(2)}) collective-permute-start(f32[8,512]{1,0:T(8,128)S(1)} %get-tuple-element.35), channel_id=1, source_target_pairs={{1,0},{2,1},{3,2},{4,3},{5,4},{6,5},{7,6},{9,8},{10,9},{11,10},{12... | collective-permute-start | bytes 49160 | tf_op jit(solution)/shard_map/ppermute | solution.py:353
  7.7 15.9 %collective-permute-start.4 = (f32[72,512]{1,0:T(8,128)S(1)}, f32[72,512]{1,0:T(8,128)S(1)}, u32[]{:S(2)}, u32[]{:S(2)}) collective-permute-start(f32[72,512]{1,0:T(8,128)S(1)} %get-tuple-element.33.top_ref), channel_id=1, source_target_pairs={{0,1},{1,2},{2,3},{3,4},{4,5},{5,6},{6,7},{8,9},{9,10},{10,11},{11... | collective-permute-start | bytes 442376 | tf_op jit(solution)/shard_map/ppermute | solution.py:353
  11.9 15.5 %collective-permute-start.2 = (f32[72,512]{1,0:T(8,128)S(1)}, f32[72,512]{1,0:T(8,128)S(1)}, u32[]{:S(2)}, u32[]{:S(2)}) collective-permute-start(f32[72,512]{1,0:T(8,128)S(1)} %get-tuple-element.50.ahead), channel_id=1, source_target_pairs={{0,32},{8,40},{16,48},{24,56},{32,64},{40,72},{48,80},{56,88},{64,... | collective-permute-start | bytes 442376 | tf_op jit(solution)/shard_map/ppermute | solution.py:353
  15.9 11.4 %collective-permute-start = (f32[72,512]{1,0:T(8,128)S(1)}, f32[72,512]{1,0:T(8,128)S(1)}, u32[]{:S(2)}, u32[]{:S(2)}) collective-permute-start(f32[72,512]{1,0:T(8,128)S(1)} %get-tuple-element.50.ahead), channel_id=1, source_target_pairs={{0,16},{8,24},{16,32},{24,40},{32,48},{40,56},{48,64},{56,72},{64,... | collective-permute-start | bytes 442376 | tf_op jit(solution)/shard_map/ppermute | solution.py:353
  19.7 8.3 %collective-permute-start.3 = (f32[72,512]{1,0:T(8,128)S(1)}, f32[72,512]{1,0:T(8,128)S(1)}, u32[]{:S(2)}, u32[]{:S(2)}) collective-permute-start(f32[72,512]{1,0:T(8,128)S(1)} %get-tuple-element.51.behind), channel_id=1, source_target_pairs={{32,0},{40,8},{48,16},{56,24},{64,32},{72,40},{80,48},{88,56},{96,... | collective-permute-start | bytes 442376 | tf_op jit(solution)/shard_map/ppermute | solution.py:353
  21.6 10.2 %collective-permute-start.1 = (f32[72,512]{1,0:T(8,128)S(1)}, f32[72,512]{1,0:T(8,128)S(1)}, u32[]{:S(2)}, u32[]{:S(2)}) collective-permute-start(f32[72,512]{1,0:T(8,128)S(1)} %get-tuple-element.51.behind), channel_id=1, source_target_pairs={{16,0},{24,8},{32,16},{40,24},{48,32},{56,40},{64,48},{72,56},{80,... | collective-permute-start | bytes 442376 | tf_op jit(solution)/shard_map/ppermute | solution.py:353
  23.6 1.6 %copy-start.1 = (f32[4,1024,128]{2,1,0:T(8,128)S(1)}, f32[4,1024,128]{2,1,0:T(8,128)}, u32[]{:S(2)}) copy-start(f32[4,1024,128]{2,1,0:T(8,128)} %copy-done) | copy-start | bytes 6291460
  31.8 2.6 %collective-permute-start.6 = (f32[32,512]{1,0:T(8,128)S(1)}, f32[32,512]{1,0:T(8,128)S(1)}, u32[]{:S(2)}, u32[]{:S(2)}) collective-permute-start(f32[32,512]{1,0:T(8,128)S(1)} %tails.1), channel_id=1, source_target_pairs={{0,8},{8,0},{16,24},{24,16},{32,40},{40,32},{48,56},{56,48},{64,72... | collective-permute-start | bytes 196616 | tf_op jit(solution)/shard_map/ppermute | solution.py:406
  36.3 8.5 %collective-permute-start.7 = (f32[256,512]{1,0:T(8,128)S(1)}, f32[256,512]{1,0:T(8,128)S(1)}, u32[]{:S(2)}, u32[]{:S(2)}) collective-permute-start(f32[256,512]{1,0:T(8,128)S(1)} %faces.1), channel_id=1, source_target_pairs={{0,8},{8,0},{16,24},{24,16},{32,40},{40,32},{48,56},{56,48},{64,72... | collective-permute-start | bytes 1572872 | tf_op jit(solution)/shard_map/ppermute | solution.py:406
  36.8 20.3 %all-to-all-start = ((f32[8,64,128]{2,1,0:T(8,128)}), f32[8,64,128]{2,1,0:T(8,128)S(1)}, u32[]{:S(2)}, u32[]{:S(2)}) async-start(f32[8,64,128]{2,1,0:T(8,128)} %block.1), calls=%async_computation | async-start | bytes 524288 | tf_op jit(solution)/shard_map/all_to_all | solution.py:417

commit v3 on v2

v3 whole, which is shorter than its diff:
```python
import functools

import jax
import jax.numpy as jnp
from jax import lax
from jax.experimental import pallas as pl
from jax.experimental.pallas import tpu as pltpu
from jax.sharding import PartitionSpec as P

K = 64
CX = 16
CY = 32
CZ = 16
FACE = 512
REACH = 4
ROWS = K + 8

f32 = jnp.float32
bf16 = jnp.bfloat16
VMEM = pl.BlockSpec(memory_space=pltpu.VMEM)
MATRIX = (((1,), (0,)), ((), ()))
GRAM = (((1,), (1,)), ((), ()))


def product(left, right, dims):
    return lax.dot_general(left, right, dims, preferred_element_type=f32)


def harmonic(first, second):
    return 2.0 * first * second / (first + second)


def halves(x):
    high = x.astype(bf16)
    return high, (x - high.astype(f32)).astype(bf16)


def stacked(x):
    return jnp.concatenate(halves(x), axis=0)


def quadrants(square):
    half = square[:K] + square[K:]
    return half[:, :K] + half[:, K:]


def rows_of(vectors, sigma):
    high, low = halves(sigma)
    tail = jnp.concatenate([high.astype(f32), low.astype(f32)], axis=0).astype(bf16)
    return jnp.concatenate([*halves(vectors), tail], axis=0)


def joined(found):
    return jnp.concatenate(
        [found[:K] + found[K : 2 * K], found[2 * K : 2 * K + 8] + found[2 * K + 8 :]], axis=0
    )


def layer_of(strips, z):
    return jnp.concatenate([strips[q, pl.ds(z, K, stride=CZ), :] for q in range(4)], axis=1)


def pick_kernel(vectors_hbm, sigma_hbm, index_hbm, counts_hbm, strips, own_ref, ahead_ref, behind_ref, ahead_tail, behind_tail, top_ref, bottom_ref, first_ref, live_ref, sigma_ref, index_ref, counts_ref, sems):
    copies = [
        pltpu.make_async_copy(vectors_hbm.at[:, pl.ds(128 * q, 128)], strips.at[q], sems.at[q])
        for q in range(4)
    ]
    copies.append(pltpu.make_async_copy(sigma_hbm, sigma_ref, sems.at[4]))
    copies.append(pltpu.make_async_copy(index_hbm, index_ref, sems.at[5]))
    copies.append(pltpu.make_async_copy(counts_hbm, counts_ref, sems.at[6]))
    for copy in copies:
        copy.start()
    lane = lax.broadcasted_iota(jnp.int32, (1, 256), 1)
    within = lane % 128
    cell_of_lane = (within % CY) * CX + jnp.where(lane >= 128, CX - 1, 0)
    cell = lax.broadcasted_iota(jnp.int32, (FACE, 256), 0)
    faces = jnp.zeros((4 * 144, 256), f32)
    for copy in copies:
        copy.wait()
    for step in range(4):
        groups = []
        for group in range(4):
            z = 4 * group + step
            layer = layer_of(strips, z)
            sigma = jnp.broadcast_to(sigma_ref[z : z + 1, :], (8, FACE))
            groups.append(rows_of(layer, sigma))
            if z == 0:
                bottom_ref[...] = jnp.concatenate([layer, sigma], axis=0)
                first_ref[...] = sigma
            if z == CZ - 1:
                top_ref[...] = jnp.concatenate([layer, sigma], axis=0)
        chosen = jnp.where(within // CY == step, cell_of_lane, -1)
        select = jnp.where(cell == chosen, 1.0, 0.0).astype(bf16)
        faces = faces + product(jnp.concatenate(groups, axis=0), select, MATRIX)
    along = lax.broadcasted_iota(jnp.int32, (1, FACE), 1)
    for slot in range(2 * REACH):
        live_ref[slot : slot + 1] = jnp.where(along < counts_ref[slot], 1.0, 0.0)
    place = lax.broadcasted_iota(jnp.int32, (FACE, FACE), 0)
    for side in range(2):
        wide = jnp.concatenate(
            [
                faces[144 * group : 144 * (group + 1), 128 * side : 128 * (side + 1)]
                for group in range(4)
            ],
            axis=1,
        )
        table = wide.astype(bf16)
        face_ref, tail_ref = (ahead_ref, ahead_tail) if side else (behind_ref, behind_tail)
        face_ref[...] = wide[:K] + wide[K : 2 * K]
        for slot in range(REACH * side, REACH * (side + 1)):
            cell_index = index_ref[slot : slot + 1, :]
            wanted = (cell_index >> 9) * CY + ((cell_index >> 4) & (CY - 1))
            select = jnp.where(place == wanted, 1.0, 0.0).astype(bf16)
            found = product(table, select, MATRIX)
            own_ref[slot] = found[: 2 * K].astype(bf16)
            reach = slot - REACH if side else REACH - 1 - slot
            tail_ref[reach : reach + 1] = found[2 * K : 2 * K + 1] + found[2 * K + 8 : 2 * K + 9]
            tail_ref[4 + reach : 5 + reach] = wanted.astype(f32)


def own_kernel(strips, sigma_ref, storage_ref, top_ref, bottom_ref, below_ref, above_ref, own_ref, lower_ref):
    sigma = sigma_ref[...]
    lane = lax.broadcasted_iota(jnp.int32, (CZ, FACE), 1)
    layer = lax.broadcasted_iota(jnp.int32, (CZ, FACE), 0)
    along_x = jnp.where(
        lane % CX == CX - 1, 0.0, harmonic(sigma, pltpu.roll(sigma, FACE - 1, 1))
    )
    along_y = jnp.where(
        lane >= FACE - CX, 0.0, harmonic(sigma, pltpu.roll(sigma, FACE - CX, 1))
    )
    along_z = jnp.where(layer == CZ - 1, 0.0, harmonic(sigma, pltpu.roll(sigma, CZ - 1, 0)))
    downward = harmonic(bottom_ref[K : K + 1, :], below_ref[K : K + 1, :])
    upward = harmonic(top_ref[K : K + 1, :], above_ref[:1, :])
    half = 0.5 * (
        storage_ref[...]
        + along_x
        + pltpu.roll(along_x, 1, 1)
        + along_y
        + pltpu.roll(along_y, CX, 1)
        + along_z
        + pltpu.roll(along_z, 1, 0)
        + jnp.where(layer == 0, downward, 0.0)
        + jnp.where(layer == CZ - 1, upward, 0.0)
    )
    total = jnp.zeros((2 * K, 2 * K), f32)
    below = layer_of(strips, 0)
    for z in range(CZ):
        now = below
        applied = half[z : z + 1] * now
        applied = applied - along_x[z : z + 1] * pltpu.roll(now, FACE - 1, 1)
        applied = applied - along_y[z : z + 1] * pltpu.roll(now, FACE - CX, 1)
        if z < CZ - 1:
            below = layer_of(strips, z + 1)
            applied = applied - along_z[z : z + 1] * below
        total = total + product(stacked(now), stacked(applied), GRAM)
    own = quadrants(total)
    own_ref[...] = own + own.T
    weighted = stacked(bottom_ref[:K, :] * downward)
    lower_ref[...] = -quadrants(product(weighted, stacked(below_ref[:K, :]), GRAM))


def pack_kernel(ahead, behind, ahead2, behind2, ahead4, behind4, out_ref):
    count = ahead.shape[0]
    mine = lax.axis_index("sub") % 2
    for core, chosen in ((0, (ahead, ahead2, behind2, behind4)), (1, (ahead2, ahead4, behind, behind2))):
        @pl.when(mine == core)
        def _(chosen=chosen):
            for at, ref in enumerate(chosen):
                out_ref[count * at : count * (at + 1)] = ref[...]


OFFSETS = (-4, -3, -2, -1, 1, 2, 3, 4)


def partner(refs, offset):
    ahead2, behind2, ahead4, behind4, swapped = refs
    if offset % 2:
        at = {-1: 0, -3: 1, 1: 2, 3: 3}[offset]
        count = ahead2.shape[0]
        return swapped[count * at : count * at + count]
    return {-2: ahead2, -4: ahead4, 2: behind2, 4: behind4}[offset][...]


def weight_of(live_ref, ahead_tail, behind_tail, slot, tail):
    offset = OFFSETS[slot]
    reach = abs(offset) - 1
    mine = (ahead_tail if offset > 0 else behind_tail)[reach : reach + 1]
    pair = harmonic(mine, tail[reach : reach + 1])
    return jnp.where(live_ref[slot : slot + 1] > 0.0, pair, 0.0)


def weighted_rows(own_ref, slot, weight):
    rows = own_ref[slot]
    return stacked((rows[:K].astype(f32) + rows[K:].astype(f32)) * weight)


def block_kernel(live_ref, own_block, lower_block, own_ref, ahead, behind, *refs):
    *tails, out_ref = refs
    total = jnp.zeros((2 * K, 2 * K), f32)
    for slot, offset in enumerate(OFFSETS):
        weight = weight_of(live_ref, ahead, behind, slot, partner(tails, offset))
        total = total + product(weighted_rows(own_ref, slot, weight), own_ref[slot], GRAM)
    extra = quadrants(total)
    own = own_block[...] + 0.5 * (extra + extra.T)
    lower = lower_block[...]
    even = lax.axis_index("coarse") % 2 == 0
    payload = jnp.where(
        even, jnp.concatenate([own, lower], axis=1), jnp.concatenate([lower, own], axis=1)
    )
    for copy in range(8):
        out_ref[copy] = payload


def panel_kernel(live_ref, own_ref, ahead, behind, *refs):
    tails, faces, inverse, out_ref = refs[:5], refs[5:10], refs[10], refs[11]
    place = lax.broadcasted_iota(jnp.int32, (FACE, FACE), 0).astype(f32)
    blocks = []
    for slot, offset in enumerate(OFFSETS):
        tail = partner(tails, offset)
        weight = weight_of(live_ref, ahead, behind, slot, tail)
        reach = abs(offset) - 1
        select = jnp.where(place == tail[4 + reach : 5 + reach], 1.0, 0.0).astype(bf16)
        found = product(stacked(partner(faces, offset)), select, MATRIX).astype(bf16)
        blocks.append(quadrants(product(weighted_rows(own_ref, slot, -weight), found, GRAM)))
    high, low = halves(jnp.concatenate(blocks, axis=1))
    left_high, left_low = halves(inverse[:, :K])
    left = jnp.concatenate([left_high, left_low, left_high], axis=1)
    out_ref[...] = product(left, jnp.concatenate([high, high, low], axis=0), MATRIX)


def eliminate(rows, right, offset, lane, sub):
    factor_rows, inverse_rows = [], []
    wide = (8, 128)
    for panel in range(8):
        first = offset + 8 * panel
        column = [[None] * 16 for _ in range(8)]
        for k in range(8):
            for g in range(panel, 16):
                column[k][g] = jnp.broadcast_to(rows[g][:, first + k : first + k + 1], wide)
        pivot = [[None] * 8 for _ in range(8)]
        for i in range(8):
            for k in range(i, 8):
                pivot[i][k] = jnp.broadcast_to(column[i][panel][k : k + 1, :], wide)
        left_row = [jnp.broadcast_to(rows[panel][k : k + 1, :], wide) for k in range(8)]
        right_row = [jnp.broadcast_to(right[panel][k : k + 1, :], wide) for k in range(8)]
        kept = jnp.zeros(wide, f32)
        kept_right = jnp.zeros(wide, f32)
        for i in range(8):
            scale = lax.rsqrt(pivot[i][i])
            inverse = 1.0 / pivot[i][i]
            kept = jnp.where(sub == i, jnp.where(lane >= first + i, left_row[i], 0.0) * scale if offset == 0 else jnp.where((lane >= first + i) | (lane < 64), left_row[i], 0.0) * scale, kept)
            kept_right = jnp.where(sub == i, right_row[i] * scale, kept_right)
            left_row[i] = left_row[i] * inverse
            right_row[i] = right_row[i] * inverse
            scaled = [None] * 8
            for l in range(i + 1, 8):
                scaled[l] = pivot[i][l] * inverse
            for k in range(8):
                if k == i:
                    continue
                by = pivot[i][k] if k > i else pivot[k][i]
                left_row[k] = left_row[k] - by * left_row[i]
                right_row[k] = right_row[k] - by * right_row[i]
                for l in range(max(i + 1, k), 8):
                    pivot[k][l] = pivot[k][l] - by * scaled[l]
            pivot[i] = scaled
        for g in range(panel + 1, 16):
            for k in range(8):
                rows[g] = rows[g] - column[k][g] * left_row[k]
                right[g] = right[g] - column[k][g] * right_row[k]
        factor_rows.append(kept)
        inverse_rows.append(kept_right)
    return factor_rows, inverse_rows

def half_factor(begin, level, blocks_ref, factor_ref, cross, top, top_right, inverse):
    lane = lax.broadcasted_iota(jnp.int32, (8, 128), 1)
    sub = lax.broadcasted_iota(jnp.int32, (8, 128), 0)
    wide_lane = lax.broadcasted_iota(jnp.int32, (K, 2 * K), 1)
    zero = jnp.zeros((K, 2 * K), f32)
    at = [pl.ds(8 * g, 8) for g in range(8)]
    for c in range(4 * begin + 1, min(4 * begin + 5, 8)):
        block = blocks_ref[c]
        if c % 2 == 1:
            cross[c - 1] = jnp.concatenate([zero, block], axis=0).T[:K]
        else:
            cross[c - 1] = jnp.concatenate([block, zero], axis=0).T[K:]
    if begin:
        cross[7] = zero

    def unit(g, c):
        return jnp.where((lane == sub + 8 * g) & (level == c), 1.0, 0.0)

    if not begin:
        for g in range(8):
            top[at[g], :] = blocks_ref[0, at[g], :]
            top_right[at[g], :] = unit(g, 0)

    @pl.loop(2 * begin, 2 * begin + 2)
    def _(q):
        c = 2 * q
        last = q == 3
        rows = [jnp.where(lane < K, top[at[g], :], cross[c, at[g], :]) for g in range(8)]
        rows += [blocks_ref[c + 1, at[g], :] for g in range(8)]
        right = [top_right[at[g], :] for g in range(8)] + [unit(g, c + 1) for g in range(8)]
        even, even_right = eliminate(rows, right, 0, lane, sub)
        following = jnp.minimum(c + 2, 7)
        middle = [jnp.where(lane < K, cross[c + 1, at[g], :], rows[8 + g]) for g in range(8)]
        middle += [jnp.where(last, 0.0, blocks_ref[following, at[g], :]) for g in range(8)]
        middle_right = right[8:] + [unit(g, c + 2) for g in range(8)]
        odd, odd_right = eliminate(middle, middle_right, K, lane, sub)
        start = pl.multiple_of(128 * q, 128)
        for g in range(8):
            top[at[g], :] = middle[8 + g]
            top_right[at[g], :] = middle_right[8 + g]
            inverse[pl.ds(start + 8 * g, 8), :] = even_right[g]
            inverse[pl.ds(start + K + 8 * g, 8), :] = odd_right[g]
        both = jnp.concatenate(even + odd, axis=0).T
        cols = pl.ds(start, 128)
        factor_ref[pl.ds(start, K), cols] = jnp.where(wide_lane < K, both[:K], 0.0)
        factor_ref[pl.ds(start + K, K), cols] = both[K:]

        @pl.when(q < 3)
        def _():
            factor_ref[pl.ds(start + 128, K), cols] = jnp.where(wide_lane < K, 0.0, both[:K])


def first_half(blocks_ref, factor_ref, inverse, top, top_right, cross):
    factor_ref[...] = jnp.zeros((5 * K, 4 * K), f32)
    half_factor(0, lax.axis_index("coarse"), blocks_ref, factor_ref, cross, top, top_right, inverse)


def second_half(blocks_ref, part_ref, first_inverse, first_top, first_right, factor_ref, inverse, cross, top, top_right):
    factor_ref[: 5 * K, : 4 * K] = part_ref[...]
    factor_ref[5 * K :, : 4 * K] = jnp.zeros((3 * K, 4 * K), f32)
    factor_ref[:, 4 * K :] = jnp.zeros((8 * K, 4 * K), f32)
    inverse[: 4 * K, :] = first_inverse[...]
    top[...] = first_top[...]
    top_right[...] = first_right[...]
    half_factor(1, lax.axis_index("coarse"), blocks_ref, factor_ref, cross, top, top_right, inverse)


HBM = pl.BlockSpec(memory_space=pltpu.HBM)


def call(kernel, name, outs, operands, hbm=0, flops=10**8, scratch=(), limit=16):
    return pl.pallas_call(
        kernel,
        out_shape=outs,
        in_specs=[HBM] * hbm + [VMEM] * (len(operands) - hbm),
        out_specs=jax.tree.map(lambda _: VMEM, outs),
        scratch_shapes=scratch,
        compiler_params=pltpu.CompilerParams(vmem_limit_bytes=limit * 2**20),
        cost_estimate=pl.CostEstimate(flops=flops, bytes_accessed=2 * 10**6, transcendentals=1000),
        name=name,
    )(*operands)


def array(*shape, dtype=f32):
    return jax.ShapeDtypeStruct(shape, dtype)


FIRST = (array(5 * K, 4 * K), array(4 * K, 2 * K), array(K, 2 * K), array(K, 2 * K))


def passed_along(block, axis, distance):
    devices = range(lax.axis_size(axis))
    route = [(i - distance, i) for i in devices if i - distance in devices]
    return lax.ppermute(block, axis, route)


def body(deflation, conductivity, storage, interface_rows, interface_counts):
    vectors = deflation[0].reshape(K * CZ, FACE)
    sigma = conductivity[0]
    counts = interface_counts.reshape(2 * REACH)
    strips, mine, ahead, behind, ahead_tail, behind_tail, top, bottom, first, live = call(
        pick_kernel,
        "pick",
        (
            array(4, K * CZ, 128),
            array(8, 2 * K, FACE, dtype=bf16),
            array(K, FACE),
            array(K, FACE),
            array(8, FACE),
            array(8, FACE),
            array(ROWS, FACE),
            array(ROWS, FACE),
            array(8, FACE),
            array(8, FACE),
        ),
        tuple(
            pltpu.with_memory_space_constraint(x, pltpu.HBM)
            for x in (vectors, sigma, interface_rows[0, 0], counts)
        ),
        hbm=4,
        scratch=(
            pltpu.VMEM((CZ, FACE), f32),
            pltpu.VMEM((2 * REACH, FACE), jnp.int32),
            pltpu.SMEM((2 * REACH,), jnp.int32),
            pltpu.SemaphoreType.DMA((7,)),
        ),
    )
    below = passed_along(top, "coarse", 1)
    above = passed_along(first, "coarse", -1)

    def direct(ahead, behind):
        return (
            passed_along(ahead, "sub", 2),
            passed_along(behind, "sub", -2),
            passed_along(ahead, "sub", 4),
            passed_along(behind, "sub", -4),
        )

    def swapped(name, own, received):
        packed = call(
            pack_kernel,
            name,
            array(4 * own[0].shape[0], FACE),
            (*own, *received),
            flops=10**6,
        )
        return lax.ppermute(packed, "sub", [(i, i ^ 1) for i in range(lax.axis_size("sub"))])

    tails = direct(ahead_tail, behind_tail)
    own, lower = call(
        own_kernel,
        "own",
        (array(K, K), array(K, K)),
        (strips, sigma, storage[0], top, bottom, below, above),
    )
    tails, (own, lower) = lax.optimization_barrier((tails, (own, lower)))
    tails = (*tails, swapped("tails", (ahead_tail, behind_tail), tails))
    payload = call(
        block_kernel,
        "block",
        array(8, K, 2 * K),
        (live, own, lower, mine, ahead_tail, behind_tail, *tails),
    )
    (ahead, behind), payload = lax.optimization_barrier(((ahead, behind), payload))
    blocks = lax.all_to_all(payload, "coarse", 0, 0)
    faces = direct(ahead, behind)
    state = call(
        first_half,
        "factor_first",
        FIRST,
        (blocks,),
        flops=10**9,
        scratch=(pltpu.VMEM((8, K, 2 * K), f32),),
    )
    faces, state = lax.optimization_barrier((faces, state))
    faces = (*faces, swapped("faces", (ahead, behind), faces))
    factor, inverse = call(
        second_half,
        "factor_second",
        (array(8 * K, 8 * K), array(8 * K, 2 * K)),
        (blocks, *state),
        flops=10**9,
        scratch=(pltpu.VMEM((8, K, 2 * K), f32), pltpu.VMEM((K, 2 * K), f32), pltpu.VMEM((K, 2 * K), f32)),
    )
    panel = call(
        panel_kernel,
        "panel",
        array(8 * K, 8 * K),
        (live, mine, ahead_tail, behind_tail, *tails, *faces, inverse),
    )
    return (factor[None], panel[None, None])


def solution(mesh):
    placed = (
        P("sub", None, "coarse", None),
        P("sub", "coarse", None),
        P("sub", "coarse", None),
        P("sub", "coarse", None, None),
        P("sub", "coarse", None),
    )
    return jax.shard_map(
        body,
        mesh=mesh,
        in_specs=placed,
        out_specs=(P("sub", None, None), P("sub", "coarse", None, None)),
        check_vma=False,
    )
```

time: 80.7 us -> 83.7 us (1.037)
  the two profiles are of different devices: /device:TPU:15 before, /device:TPU:49 now
where the time goes in v3:
time: 83.7 us; the launch traced here: 83.2 us
  starting transfers between devices  47.2 us (56%)
  Pallas kernels  34.2 us (41%)
  waiting for transfers between devices  0.93 us (1%)
  between operations  0.87 us (1%)
    pallas_call x8, Pallas kernels, call(): pl.pallas_call(kernel, out_shape=outs, in_specs=[HBM] * hbm + [VMEM] * (l...  34.2 us
    ppermute x10, starting transfers between devices, passed_along(): return lax.ppermute(block, axis, route)  33 us
    all_to_all x1, starting transfers between devices, body(): blocks = lax.all_to_all(payload, 'coarse', 0, 0)  9.21 us
    ppermute x2, starting transfers between devices, swapped(): lax.ppermute(packed, 'sub', [(i, i ^ 1) for i in range(lax.axis_size('sub...  5 us
  transfers between devices with their start and end apart: 13, of which 1 were waited for; matrix products, arithmetic and copies ran while one was open for 0% of the time, Pallas kernels for 30%

profile of v3, /device:TPU:49, one launch (start us, length us, event | category | flops | bytes accessed | tf_op | source)
XLA Modules:
  0.0 83.2 jit_solution(15824951921690369622)
XLA Ops:
  0.7 4.3 %pick.1 = (f32[4,1024,128]{2,1,0:T(8,128)S(1)}, bf16[8,128,512]{2,1,0:T(8,128)(2,1)S(1)}, f32[64,512]{1,0:T(8,128)S(1)}, f32[64,512]{1,0:T(8,128)S(1)}, f32[8,51...) custom-call(f32[1024,512]{1,0:T(8,128)} %bitcast.10, ...), custom_call_target="tpu_custom_call" | custom-call | flops 100000000 | bytes 2000000 | tf_op jit(solution)/shard_map/pick/pallas_call | solution.py:346
  4.9 3.5 %collective-permute-start.4 = (f32[72,512]{1,0:T(8,128)S(1)}, f32[72,512]{1,0:T(8,128)S(1)}, u32[]{:S(2)}, u32[]{:S(2)}) collective-permute-start(f32[72,512]{1,0:T(8,128)S(1)} %get-tuple-element.43.top_ref), channel_id=1, source_target_pairs={{0,1},{1,2},{2,3},{3,4},{4,5},{5,6},{6,7},{8,9},{9,10},{10,11},{11... | collective-permute-start | bytes 442376 | tf_op jit(solution)/shard_map/ppermute | solution.py:368
  8.5 1.9 %collective-permute-start.5 = (f32[8,512]{1,0:T(8,128)S(1)}, f32[8,512]{1,0:T(8,128)S(1)}, u32[]{:S(2)}, u32[]{:S(2)}) collective-permute-start(f32[8,512]{1,0:T(8,128)S(1)} %get-tuple-element.45), channel_id=1, source_target_pairs={{1,0},{2,1},{3,2},{4,3},{5,4},{6,5},{7,6},{9,8},{10,9},{11,10},{12... | collective-permute-start | bytes 49160 | tf_op jit(solution)/shard_map/ppermute | solution.py:368
  10.4 4.7 %collective-permute-start.2 = (f32[8,512]{1,0:T(8,128)S(1)}, f32[8,512]{1,0:T(8,128)S(1)}, u32[]{:S(2)}, u32[]{:S(2)}) collective-permute-start(f32[8,512]{1,0:T(8,128)S(1)} %get-tuple-element.40.ahead), channel_id=1, source_target_pairs={{0,32},{8,40},{16,48},{24,56},{32,64},{40,72},{48,80},{56,88},{64,... | collective-permute-start | bytes 49160 | tf_op jit(solution)/shard_map/ppermute | solution.py:368
  15.1 2.2 %collective-permute-start = (f32[8,512]{1,0:T(8,128)S(1)}, f32[8,512]{1,0:T(8,128)S(1)}, u32[]{:S(2)}, u32[]{:S(2)}) collective-permute-start(f32[8,512]{1,0:T(8,128)S(1)} %get-tuple-element.40.ahead), channel_id=1, source_target_pairs={{0,16},{8,24},{16,32},{24,40},{32,48},{40,56},{48,64},{56,72},{64,... | collective-permute-start | bytes 49160 | tf_op jit(solution)/shard_map/ppermute | solution.py:368
  17.3 4.5 %collective-permute-start.3 = (f32[8,512]{1,0:T(8,128)S(1)}, f32[8,512]{1,0:T(8,128)S(1)}, u32[]{:S(2)}, u32[]{:S(2)}) collective-permute-start(f32[8,512]{1,0:T(8,128)S(1)} %get-tuple-element.41.behind), channel_id=1, source_target_pairs={{32,0},{40,8},{48,16},{56,24},{64,32},{72,40},{80,48},{88,56},{96,... | collective-permute-start | bytes 49160 | tf_op jit(solution)/shard_map/ppermute | solution.py:368
  21.9 0.0 collective-permute-done.5.above_ref
  21.9 2.6 %collective-permute-start.1 = (f32[8,512]{1,0:T(8,128)S(1)}, f32[8,512]{1,0:T(8,128)S(1)}, u32[]{:S(2)}, u32[]{:S(2)}) collective-permute-start(f32[8,512]{1,0:T(8,128)S(1)} %get-tuple-element.41.behind), channel_id=1, source_target_pairs={{16,0},{24,8},{32,16},{40,24},{48,32},{56,40},{64,48},{72,56},{80,... | collective-permute-start | bytes 49160 | tf_op jit(solution)/shard_map/ppermute | solution.py:368
  24.4 0.0 collective-permute-done.4.below_ref
  24.5 2.2 %own.1 = (f32[64,64]{1,0:T(8,128)S(1)}, f32[64,64]{1,0:T(8,128)S(1)}) custom-call(f32[4,1024,128]{2,1,0:T(8,128)S(1)} %get-tuple-element.42.strips, f32[16,512]{1,0:T(8,128)S(1)} %bitcast.8, f32[16,512]{1,0:T(8,128)S(1)} %bitcast.9, f32[72,512]{1,0:T(8,128)S(1)} %get-tuple-element.43.top_ref, f32[72,512]{1,0:T(8,128)S(1)} %get-tuple-element.44.bottom_ref, ...), custom_call_target="tpu_custom_call" | custom-call | flops 100000000 | bytes 2000000 | tf_op jit(solution)/shard_map/own/pallas_call | solution.py:346
  26.6 0.0 collective-permute-done.2.ahead4.refs_2_
  26.6 0.0 collective-permute-done.ahead2.refs_0_
  26.7 0.0 collective-permute-done.3.behind4.refs_3_
  26.7 0.0 collective-permute-done.1.behind2.refs_1_
  26.7 2.7 %collective-permute-start.6 = (f32[32,512]{1,0:T(8,128)S(1)}, f32[32,512]{1,0:T(8,128)S(1)}, u32[]{:S(2)}, u32[]{:S(2)}) collective-permute-start(f32[32,512]{1,0:T(8,128)S(1)} %tails.1), channel_id=1, source_target_pairs={{0,8},{8,0},{16,24},{24,16},{32,40},{40,32},{48,56},{56,48},{64,72... | collective-permute-start | bytes 196616 | tf_op jit(solution)/shard_map/ppermute | solution.py:421
  29.4 0.9 %collective-permute-done.6.refs_4_ = f32[32,512]{1,0:T(8,128)S(1)} collective-permute-done((f32[32,512]{1,0:T(8,128)S(1)}, f32[32,512]{1,0:T(8,128)S(1)}, u32[]{:S(2)}, u32[]{:S(2)}) %collective-permute-start.6) | collective-permute-done | bytes 65568 | tf_op jit(solution)/shard_map/ppermute | solution.py:421
  30.3 1.4 %block.1 = f32[8,64,128]{2,1,0:T(8,128)} custom-call(f32[8,512]{1,0:T(8,128)S(1)} %get-tuple-element.39.live_ref, f32[64,64]{1,0:T(8,128)S(1)} %get-tuple-element.48.own_block, f32[64,64]{1,0:T(8,128)S(1)} %get-tuple-element.49.lower_block, bf16[8,128,512]{2,1,0:T(8,128)(2,1)S(1)} %get-tuple-element.50.own_ref, f32[8,512]{1,0:T(8,128)S(1)} %get-tuple-element.40.ahead, ...), custom_call_target="tpu_custom_call" | custom-call | flops 100000000 | bytes 2000000 | tf_op jit(solution)/shard_map/block/pallas_call | solution.py:346
  31.7 9.2 %all-to-all-start = ((f32[8,64,128]{2,1,0:T(8,128)}), f32[8,64,128]{2,1,0:T(8,128)S(1)}, u32[]{:S(2)}, u32[]{:S(2)}) async-start(f32[8,64,128]{2,1,0:T(8,128)} %block.1), calls=%async_computation | async-start | bytes 524288 | tf_op jit(solution)/shard_map/all_to_all | solution.py:439
  40.9 3.8 %collective-permute-start.9 = (f32[64,512]{1,0:T(8,128)S(1)}, f32[64,512]{1,0:T(8,128)S(1)}, u32[]{:S(2)}, u32[]{:S(2)}) collective-permute-start(f32[64,512]{1,0:T(8,128)S(1)} %get-tuple-element.56.ahead), channel_id=1, source_target_pairs={{0,32},{8,40},{16,48},{24,56},{32,64},{40,72},{48,80},{56,88},{64,... | collective-permute-start | bytes 393224 | tf_op jit(solution)/shard_map/ppermute | solution.py:368
  44.7 2.9 %collective-permute-start.7 = (f32[64,512]{1,0:T(8,128)S(1)}, f32[64,512]{1,0:T(8,128)S(1)}, u32[]{:S(2)}, u32[]{:S(2)}) collective-permute-start(f32[64,512]{1,0:T(8,128)S(1)} %get-tuple-element.56.ahead), channel_id=1, source_target_pairs={{0,16},{8,24},{16,32},{24,40},{32,48},{40,56},{48,64},{56,72},{64,... | collective-permute-start | bytes 393224 | tf_op jit(solution)/shard_map/ppermute | solution.py:368
  47.6 4.7 %collective-permute-start.10 = (f32[64,512]{1,0:T(8,128)S(1)}, f32[64,512]{1,0:T(8,128)S(1)}, u32[]{:S(2)}, u32[]{:S(2)}) collective-permute-start(f32[64,512]{1,0:T(8,128)S(1)} %get-tuple-element.57.behind), channel_id=1, source_target_pairs={{32,0},{40,8},{48,16},{56,24},{64,32},{72,40},{80,48},{88,56},{96,... | collective-permute-start | bytes 393224 | tf_op jit(solution)/shard_map/ppermute | solution.py:368
  52.3 2.2 %collective-permute-start.8 = (f32[64,512]{1,0:T(8,128)S(1)}, f32[64,512]{1,0:T(8,128)S(1)}, u32[]{:S(2)}, u32[]{:S(2)}) collective-permute-start(f32[64,512]{1,0:T(8,128)S(1)} %get-tuple-element.57.behind), channel_id=1, source_target_pairs={{16,0},{24,8},{32,16},{40,24},{48,32},{56,40},{64,48},{72,56},{80,... | collective-permute-start | bytes 393224 | tf_op jit(solution)/shard_map/ppermute | solution.py:368
  54.5 0.0 all-to-all-done.blocks_ref
  54.5 10.9 %factor_first.1 = (f32[320,256]{1,0:T(8,128)S(1)}, f32[256,128]{1,0:T(8,128)S(1)}, f32[64,128]{1,0:T(8,128)S(1)}, f32[64,128]{1,0:T(8,128)S(1)}) custom-call(f32[8,64,128]{2,1,0:T(8,128)S(1)} %all-to-all-done.blocks_ref), custom_call_target="tpu_custom_call" | custom-call | flops 1000000000 | bytes 2000000 | tf_op jit(solution)/shard_map/factor_first/pallas_call | solution.py:346
  65.4 0.0 collective-permute-done.9.ahead4.refs_7_
  65.4 0.0 collective-permute-done.7.ahead2.refs_5_
  65.5 0.0 collective-permute-done.8.behind2.refs_6_
  65.5 0.1 faces.1
  65.5 2.3 %collective-permute-start.11 = (f32[256,512]{1,0:T(8,128)S(1)}, f32[256,512]{1,0:T(8,128)S(1)}, u32[]{:S(2)}, u32[]{:S(2)}) collective-permute-start(f32[256,512]{1,0:T(8,128)S(1)} %faces.1), channel_id=1, source_target_pairs={{0,8},{8,0},{16,24},{24,16},{32,40},{40,32},{48,56},{56,48},{64,72... | collective-permute-start | bytes 1572872 | tf_op jit(solution)/shard_map/ppermute | solution.py:421
  67.8 11.9 %factor_second.1 = (f32[512,512]{1,0:T(8,128)}, f32[512,128]{1,0:T(8,128)S(1)}) custom-call(f32[8,64,128]{2,1,0:T(8,128)S(1)} %all-to-all-done.blocks_ref, f32[320,256]{1,0:T(8,128)S(1)} %get-tuple-element.62.part_ref, f32[256,128]{1,0:T(8,128)S(1)} %get-tuple-element.63.first_inverse, f32[64,128]{1,0:T(8,128)S(1)} %get-tuple-element.64.first_top, ...), custom_call_target="tpu_custom_call" | custom-call | flops 1000000000 | bytes 2000000 | tf_op jit(solution)/shard_map/factor_second/pallas_call | solution.py:346
  79.8 0.0 collective-permute-done.11.refs_9_
  79.8 3.4 %panel.1 = f32[512,512]{1,0:T(8,128)} custom-call(f32[8,512]{1,0:T(8,128)S(1)} %get-tuple-element.39.live_ref, bf16[8,128,512]{2,1,0:T(8,128)(2,1)S(1)} %get-tuple-element.50.own_ref, f32[8,512]{1,0:T(8,128)S(1)} %get-tuple-element.40.ahead, f32[8,512]{1,0:T(8,128)S(1)} %get-tuple-element.41.behind, f32[8,512]{1,0:T(8,128)S(1)} %collective-permute-done.ahead2.refs_0_, ...), custom_call_target="tpu_custom_call" | custom-call | flops 100000000 | bytes 2000000 | tf_op jit(solution)/shard_map/panel/pallas_call | solution.py:346
  (6 shorter events, 0.0 us)
Async XLA Ops:
  0.6 23.8 %copy-start = (f32[1,16,512]{2,1,0:T(8,128)S(1)}, f32[1,16,512]{2,1,0:T(8,128)}, u32[]{:S(2)}) copy-start(f32[1,16,512]{2,1,0:T(8,128)} %param.6) | copy-start | bytes 98308
  0.6 23.8 %copy-start.1 = (f32[1,16,512]{2,1,0:T(8,128)S(1)}, f32[1,16,512]{2,1,0:T(8,128)}, u32[]{:S(2)}) copy-start(f32[1,16,512]{2,1,0:T(8,128)} %param.7) | copy-start | bytes 98308
  4.9 19.5 %collective-permute-start.4 = (f32[72,512]{1,0:T(8,128)S(1)}, f32[72,512]{1,0:T(8,128)S(1)}, u32[]{:S(2)}, u32[]{:S(2)}) collective-permute-start(f32[72,512]{1,0:T(8,128)S(1)} %get-tuple-element.43.top_ref), channel_id=1, source_target_pairs={{0,1},{1,2},{2,3},{3,4},{4,5},{5,6},{6,7},{8,9},{9,10},{10,11},{11... | collective-permute-start | bytes 442376 | tf_op jit(solution)/shard_map/ppermute | solution.py:368
  8.5 13.4 %collective-permute-start.5 = (f32[8,512]{1,0:T(8,128)S(1)}, f32[8,512]{1,0:T(8,128)S(1)}, u32[]{:S(2)}, u32[]{:S(2)}) collective-permute-start(f32[8,512]{1,0:T(8,128)S(1)} %get-tuple-element.45), channel_id=1, source_target_pairs={{1,0},{2,1},{3,2},{4,3},{5,4},{6,5},{7,6},{9,8},{10,9},{11,10},{12... | collective-permute-start | bytes 49160 | tf_op jit(solution)/shard_map/ppermute | solution.py:368
  10.4 16.2 %collective-permute-start.2 = (f32[8,512]{1,0:T(8,128)S(1)}, f32[8,512]{1,0:T(8,128)S(1)}, u32[]{:S(2)}, u32[]{:S(2)}) collective-permute-start(f32[8,512]{1,0:T(8,128)S(1)} %get-tuple-element.40.ahead), channel_id=1, source_target_pairs={{0,32},{8,40},{16,48},{24,56},{32,64},{40,72},{48,80},{56,88},{64,... | collective-permute-start | bytes 49160 | tf_op jit(solution)/shard_map/ppermute | solution.py:368
  15.1 11.6 %collective-permute-start = (f32[8,512]{1,0:T(8,128)S(1)}, f32[8,512]{1,0:T(8,128)S(1)}, u32[]{:S(2)}, u32[]{:S(2)}) collective-permute-start(f32[8,512]{1,0:T(8,128)S(1)} %get-tuple-element.40.ahead), channel_id=1, source_target_pairs={{0,16},{8,24},{16,32},{24,40},{32,48},{40,56},{48,64},{56,72},{64,... | collective-permute-start | bytes 49160 | tf_op jit(solution)/shard_map/ppermute | solution.py:368
  17.3 9.3 %collective-permute-start.3 = (f32[8,512]{1,0:T(8,128)S(1)}, f32[8,512]{1,0:T(8,128)S(1)}, u32[]{:S(2)}, u32[]{:S(2)}) collective-permute-start(f32[8,512]{1,0:T(8,128)S(1)} %get-tuple-element.41.behind), channel_id=1, source_target_pairs={{32,0},{40,8},{48,16},{56,24},{64,32},{72,40},{80,48},{88,56},{96,... | collective-permute-start | bytes 49160 | tf_op jit(solution)/shard_map/ppermute | solution.py:368
  21.9 4.8 %collective-permute-start.1 = (f32[8,512]{1,0:T(8,128)S(1)}, f32[8,512]{1,0:T(8,128)S(1)}, u32[]{:S(2)}, u32[]{:S(2)}) collective-permute-start(f32[8,512]{1,0:T(8,128)S(1)} %get-tuple-element.41.behind), channel_id=1, source_target_pairs={{16,0},{24,8},{32,16},{40,24},{48,32},{56,40},{64,48},{72,56},{80,... | collective-permute-start | bytes 49160 | tf_op jit(solution)/shard_map/ppermute | solution.py:368
  26.7 3.6 %collective-permute-start.6 = (f32[32,512]{1,0:T(8,128)S(1)}, f32[32,512]{1,0:T(8,128)S(1)}, u32[]{:S(2)}, u32[]{:S(2)}) collective-permute-start(f32[32,512]{1,0:T(8,128)S(1)} %tails.1), channel_id=1, source_target_pairs={{0,8},{8,0},{16,24},{24,16},{32,40},{40,32},{48,56},{56,48},{64,72... | collective-permute-start | bytes 196616 | tf_op jit(solution)/shard_map/ppermute | solution.py:421
  31.7 22.8 %all-to-all-start = ((f32[8,64,128]{2,1,0:T(8,128)}), f32[8,64,128]{2,1,0:T(8,128)S(1)}, u32[]{:S(2)}, u32[]{:S(2)}) async-start(f32[8,64,128]{2,1,0:T(8,128)} %block.1), calls=%async_computation | async-start | bytes 524288 | tf_op jit(solution)/shard_map/all_to_all | solution.py:439
  40.9 24.5 %collective-permute-start.9 = (f32[64,512]{1,0:T(8,128)S(1)}, f32[64,512]{1,0:T(8,128)S(1)}, u32[]{:S(2)}, u32[]{:S(2)}) collective-permute-start(f32[64,512]{1,0:T(8,128)S(1)} %get-tuple-element.56.ahead), channel_id=1, source_target_pairs={{0,32},{8,40},{16,48},{24,56},{32,64},{40,72},{48,80},{56,88},{64,... | collective-permute-start | bytes 393224 | tf_op jit(solution)/shard_map/ppermute | solution.py:368
  44.7 20.7 %collective-permute-start.7 = (f32[64,512]{1,0:T(8,128)S(1)}, f32[64,512]{1,0:T(8,128)S(1)}, u32[]{:S(2)}, u32[]{:S(2)}) collective-permute-start(f32[64,512]{1,0:T(8,128)S(1)} %get-tuple-element.56.ahead), channel_id=1, source_target_pairs={{0,16},{8,24},{16,32},{24,40},{32,48},{40,56},{48,64},{56,72},{64,... | collective-permute-start | bytes 393224 | tf_op jit(solution)/shard_map/ppermute | solution.py:368
  47.6 17.9 %collective-permute-start.10 = (f32[64,512]{1,0:T(8,128)S(1)}, f32[64,512]{1,0:T(8,128)S(1)}, u32[]{:S(2)}, u32[]{:S(2)}) collective-permute-start(f32[64,512]{1,0:T(8,128)S(1)} %get-tuple-element.57.behind), channel_id=1, source_target_pairs={{32,0},{40,8},{48,16},{56,24},{64,32},{72,40},{80,48},{88,56},{96,... | collective-permute-start | bytes 393224 | tf_op jit(solution)/shard_map/ppermute | solution.py:368
  52.3 13.2 %collective-permute-start.8 = (f32[64,512]{1,0:T(8,128)S(1)}, f32[64,512]{1,0:T(8,128)S(1)}, u32[]{:S(2)}, u32[]{:S(2)}) collective-permute-start(f32[64,512]{1,0:T(8,128)S(1)} %get-tuple-element.57.behind), channel_id=1, source_target_pairs={{16,0},{24,8},{32,16},{40,24},{48,32},{56,40},{64,48},{72,56},{80,... | collective-permute-start | bytes 393224 | tf_op jit(solution)/shard_map/ppermute | solution.py:368
  65.5 14.2 %collective-permute-start.11 = (f32[256,512]{1,0:T(8,128)S(1)}, f32[256,512]{1,0:T(8,128)S(1)}, u32[]{:S(2)}, u32[]{:S(2)}) collective-permute-start(f32[256,512]{1,0:T(8,128)S(1)} %faces.1), channel_id=1, source_target_pairs={{0,8},{8,0},{16,24},{24,16},{32,40},{40,32},{48,56},{56,48},{64,72... | collective-permute-start | bytes 1572872 | tf_op jit(solution)/shard_map/ppermute | solution.py:421

commit v4 on v3

--- a/solution.py
+++ b/solution.py
@@ -129,8 +129,11 @@
         lane >= FACE - CX, 0.0, harmonic(sigma, pltpu.roll(sigma, FACE - CX, 1))
     )
     along_z = jnp.where(layer == CZ - 1, 0.0, harmonic(sigma, pltpu.roll(sigma, CZ - 1, 0)))
+    level = lax.axis_index("coarse")
     downward = harmonic(bottom_ref[K : K + 1, :], below_ref[K : K + 1, :])
+    downward = jnp.where(level == 0, 0.0, downward)
     upward = harmonic(top_ref[K : K + 1, :], above_ref[:1, :])
+    upward = jnp.where(level == lax.axis_size("coarse") - 1, 0.0, upward)
     half = 0.5 * (
         storage_ref[...]
         + along_x
@@ -363,9 +366,8 @@
 
 
 def passed_along(block, axis, distance):
-    devices = range(lax.axis_size(axis))
-    route = [(i - distance, i) for i in devices if i - distance in devices]
-    return lax.ppermute(block, axis, route)
+    count = lax.axis_size(axis)
+    return lax.ppermute(block, axis, [(i, (i + distance) % count) for i in range(count)])
 
 
 def body(deflation, conductivity, storage, interface_rows, interface_counts):

time: 83.7 us -> 71.4 us (0.85)
  the two profiles are of different devices: /device:TPU:49 before, /device:TPU:1 now
where the time goes in v4:
time: 71.4 us; the launch traced here: 71.2 us
  Pallas kernels  34.2 us (48%)
  starting transfers between devices  31.3 us (44%)
  waiting for transfers between devices  4.94 us (7%)
  between operations  0.76 us (1%)
    pallas_call x8, Pallas kernels, call(): pl.pallas_call(kernel, out_shape=outs, in_specs=[HBM] * hbm + [VMEM] * (l...  34.2 us
    ppermute x10, starting transfers between devices, passed_along(): lax.ppermute(block, axis, [(i, (i + distance) % count) for i in range(cou...  21.6 us
    all_to_all x1, starting transfers between devices, body(): blocks = lax.all_to_all(payload, 'coarse', 0, 0)  5.48 us
    ppermute x2, starting transfers between devices, swapped(): lax.ppermute(packed, 'sub', [(i, i ^ 1) for i in range(lax.axis_size('sub...  4.24 us
    all_to_all x1, waiting for transfers between devices, body(): blocks = lax.all_to_all(payload, 'coarse', 0, 0)  4.01 us
  transfers between devices with their start and end apart: 13, of which 2 were waited for; matrix products, arithmetic and copies ran while one was open for 0% of the time, Pallas kernels for 35%

profile of v4, /device:TPU:1, one launch (start us, length us, event | category | flops | bytes accessed | tf_op | source)
XLA Modules:
  0.0 71.2 jit_solution(9121044252251551132)
XLA Ops:
  0.7 4.3 %pick.1 = (f32[4,1024,128]{2,1,0:T(8,128)S(1)}, bf16[8,128,512]{2,1,0:T(8,128)(2,1)S(1)}, f32[64,512]{1,0:T(8,128)S(1)}, f32[64,512]{1,0:T(8,128)S(1)}, f32[8,51...) custom-call(f32[1024,512]{1,0:T(8,128)} %bitcast.10, ...), custom_call_target="tpu_custom_call" | custom-call | flops 100000000 | bytes 2000000 | tf_op jit(solution)/shard_map/pick/pallas_call | solution.py:349
  4.9 2.5 %collective-permute-start.4 = (f32[72,512]{1,0:T(8,128)S(1)}, f32[72,512]{1,0:T(8,128)S(1)}, u32[]{:S(2)}, u32[]{:S(2)}) collective-permute-start(f32[72,512]{1,0:T(8,128)S(1)} %get-tuple-element.43.top_ref), channel_id=1, source_target_pairs={{0,1},{1,2},{2,3},{3,4},{4,5},{5,6},{6,7},{7,0},{8,9},{9,10},{10,1... | collective-permute-start | bytes 442376 | tf_op jit(solution)/shard_map/ppermute | solution.py:370
  7.5 4.0 %collective-permute-start.5 = (f32[8,512]{1,0:T(8,128)S(1)}, f32[8,512]{1,0:T(8,128)S(1)}, u32[]{:S(2)}, u32[]{:S(2)}) collective-permute-start(f32[8,512]{1,0:T(8,128)S(1)} %get-tuple-element.45), channel_id=1, source_target_pairs={{0,7},{1,0},{2,1},{3,2},{4,3},{5,4},{6,5},{7,6},{8,15},{9,8},{10,9... | collective-permute-start | bytes 49160 | tf_op jit(solution)/shard_map/ppermute | solution.py:370
  11.5 2.7 %collective-permute-start.2 = (f32[8,512]{1,0:T(8,128)S(1)}, f32[8,512]{1,0:T(8,128)S(1)}, u32[]{:S(2)}, u32[]{:S(2)}) collective-permute-start(f32[8,512]{1,0:T(8,128)S(1)} %get-tuple-element.40.ahead), channel_id=1, source_target_pairs={{0,32},{8,40},{16,48},{24,56},{32,64},{40,72},{48,80},{56,88},{64,... | collective-permute-start | bytes 49160 | tf_op jit(solution)/shard_map/ppermute | solution.py:370
  14.3 0.3 collective-permute-start
  14.6 3.8 %collective-permute-start.3 = (f32[8,512]{1,0:T(8,128)S(1)}, f32[8,512]{1,0:T(8,128)S(1)}, u32[]{:S(2)}, u32[]{:S(2)}) collective-permute-start(f32[8,512]{1,0:T(8,128)S(1)} %get-tuple-element.41.behind), channel_id=1, source_target_pairs={{0,224},{8,232},{16,240},{24,248},{32,0},{40,8},{48,16},{56,24},{6... | collective-permute-start | bytes 49160 | tf_op jit(solution)/shard_map/ppermute | solution.py:370
  18.4 0.0 collective-permute-done.5.above_ref
  18.4 1.0 %collective-permute-start.1 = (f32[8,512]{1,0:T(8,128)S(1)}, f32[8,512]{1,0:T(8,128)S(1)}, u32[]{:S(2)}, u32[]{:S(2)}) collective-permute-start(f32[8,512]{1,0:T(8,128)S(1)} %get-tuple-element.41.behind), channel_id=1, source_target_pairs={{0,240},{8,248},{16,0},{24,8},{32,16},{40,24},{48,32},{56,40},{64,... | collective-permute-start | bytes 49160 | tf_op jit(solution)/shard_map/ppermute | solution.py:370
  19.4 0.0 collective-permute-done.4.below_ref
  19.4 2.2 %own.1 = (f32[64,64]{1,0:T(8,128)S(1)}, f32[64,64]{1,0:T(8,128)S(1)}) custom-call(f32[4,1024,128]{2,1,0:T(8,128)S(1)} %get-tuple-element.42.strips, f32[16,512]{1,0:T(8,128)S(1)} %bitcast.8, f32[16,512]{1,0:T(8,128)S(1)} %bitcast.9, f32[72,512]{1,0:T(8,128)S(1)} %get-tuple-element.43.top_ref, f32[72,512]{1,0:T(8,128)S(1)} %get-tuple-element.44.bottom_ref, ...), custom_call_target="tpu_custom_call" | custom-call | flops 100000000 | bytes 2000000 | tf_op jit(solution)/shard_map/own/pallas_call | solution.py:349
  21.6 0.0 collective-permute-done.2.ahead4.refs_2_
  21.6 0.0 collective-permute-done.ahead2.refs_0_
  21.6 0.0 collective-permute-done.3.behind4.refs_3_
  21.7 0.0 collective-permute-done.1.behind2.refs_1_
  21.7 2.3 %collective-permute-start.6 = (f32[32,512]{1,0:T(8,128)S(1)}, f32[32,512]{1,0:T(8,128)S(1)}, u32[]{:S(2)}, u32[]{:S(2)}) collective-permute-start(f32[32,512]{1,0:T(8,128)S(1)} %tails.1), channel_id=1, source_target_pairs={{0,8},{8,0},{16,24},{24,16},{32,40},{40,32},{48,56},{56,48},{64,72... | collective-permute-start | bytes 196616 | tf_op jit(solution)/shard_map/ppermute | solution.py:423
  24.0 0.9 %collective-permute-done.6.refs_4_ = f32[32,512]{1,0:T(8,128)S(1)} collective-permute-done((f32[32,512]{1,0:T(8,128)S(1)}, f32[32,512]{1,0:T(8,128)S(1)}, u32[]{:S(2)}, u32[]{:S(2)}) %collective-permute-start.6) | collective-permute-done | bytes 65568 | tf_op jit(solution)/shard_map/ppermute | solution.py:423
  24.9 1.4 %block.1 = f32[8,64,128]{2,1,0:T(8,128)} custom-call(f32[8,512]{1,0:T(8,128)S(1)} %get-tuple-element.39.live_ref, f32[64,64]{1,0:T(8,128)S(1)} %get-tuple-element.48.own_block, f32[64,64]{1,0:T(8,128)S(1)} %get-tuple-element.49.lower_block, bf16[8,128,512]{2,1,0:T(8,128)(2,1)S(1)} %get-tuple-element.50.own_ref, f32[8,512]{1,0:T(8,128)S(1)} %get-tuple-element.40.ahead, ...), custom_call_target="tpu_custom_call" | custom-call | flops 100000000 | bytes 2000000 | tf_op jit(solution)/shard_map/block/pallas_call | solution.py:349
  26.2 5.5 %all-to-all-start = ((f32[8,64,128]{2,1,0:T(8,128)}), f32[8,64,128]{2,1,0:T(8,128)S(1)}, u32[]{:S(2)}, u32[]{:S(2)}) async-start(f32[8,64,128]{2,1,0:T(8,128)} %block.1), calls=%async_computation | async-start | bytes 524288 | tf_op jit(solution)/shard_map/all_to_all | solution.py:441
  31.7 1.9 %collective-permute-start.9 = (f32[64,512]{1,0:T(8,128)S(1)}, f32[64,512]{1,0:T(8,128)S(1)}, u32[]{:S(2)}, u32[]{:S(2)}) collective-permute-start(f32[64,512]{1,0:T(8,128)S(1)} %get-tuple-element.56.ahead), channel_id=1, source_target_pairs={{0,32},{8,40},{16,48},{24,56},{32,64},{40,72},{48,80},{56,88},{64,... | collective-permute-start | bytes 393224 | tf_op jit(solution)/shard_map/ppermute | solution.py:370
  33.6 0.4 collective-permute-start.7
  34.0 4.6 %collective-permute-start.10 = (f32[64,512]{1,0:T(8,128)S(1)}, f32[64,512]{1,0:T(8,128)S(1)}, u32[]{:S(2)}, u32[]{:S(2)}) collective-permute-start(f32[64,512]{1,0:T(8,128)S(1)} %get-tuple-element.57.behind), channel_id=1, source_target_pairs={{0,224},{8,232},{16,240},{24,248},{32,0},{40,8},{48,16},{56,24},{6... | collective-permute-start | bytes 393224 | tf_op jit(solution)/shard_map/ppermute | solution.py:370
  38.6 0.3 collective-permute-start.8
  38.9 4.0 %all-to-all-done.blocks_ref = f32[8,64,128]{2,1,0:T(8,128)S(1)} async-done(((f32[8,64,128]{2,1,0:T(8,128)}), f32[8,64,128]{2,1,0:T(8,128)S(1)}, u32[]{:S(2)}, u32[]{:S(2)}) %all-to-all-start) | async-done | bytes 262176 | tf_op jit(solution)/shard_map/all_to_all | solution.py:441
  42.9 10.9 %factor_first.1 = (f32[320,256]{1,0:T(8,128)S(1)}, f32[256,128]{1,0:T(8,128)S(1)}, f32[64,128]{1,0:T(8,128)S(1)}, f32[64,128]{1,0:T(8,128)S(1)}) custom-call(f32[8,64,128]{2,1,0:T(8,128)S(1)} %all-to-all-done.blocks_ref), custom_call_target="tpu_custom_call" | custom-call | flops 1000000000 | bytes 2000000 | tf_op jit(solution)/shard_map/factor_first/pallas_call | solution.py:349
  53.8 0.0 collective-permute-done.9.ahead4.refs_7_
  53.8 0.0 collective-permute-done.10.behind4.refs_8_
  53.8 0.0 collective-permute-done.8.behind2.refs_6_
  53.8 0.1 faces.1
  53.9 2.0 %collective-permute-start.11 = (f32[256,512]{1,0:T(8,128)S(1)}, f32[256,512]{1,0:T(8,128)S(1)}, u32[]{:S(2)}, u32[]{:S(2)}) collective-permute-start(f32[256,512]{1,0:T(8,128)S(1)} %faces.1), channel_id=1, source_target_pairs={{0,8},{8,0},{16,24},{24,16},{32,40},{40,32},{48,56},{56,48},{64,72... | collective-permute-start | bytes 1572872 | tf_op jit(solution)/shard_map/ppermute | solution.py:423
  55.9 11.9 %factor_second.1 = (f32[512,512]{1,0:T(8,128)}, f32[512,128]{1,0:T(8,128)S(1)}) custom-call(f32[8,64,128]{2,1,0:T(8,128)S(1)} %all-to-all-done.blocks_ref, f32[320,256]{1,0:T(8,128)S(1)} %get-tuple-element.62.part_ref, f32[256,128]{1,0:T(8,128)S(1)} %get-tuple-element.63.first_inverse, f32[64,128]{1,0:T(8,128)S(1)} %get-tuple-element.64.first_top, ...), custom_call_target="tpu_custom_call" | custom-call | flops 1000000000 | bytes 2000000 | tf_op jit(solution)/shard_map/factor_second/pallas_call | solution.py:349
  67.8 0.0 collective-permute-done.11.refs_9_
  67.8 3.4 %panel.1 = f32[512,512]{1,0:T(8,128)} custom-call(f32[8,512]{1,0:T(8,128)S(1)} %get-tuple-element.39.live_ref, bf16[8,128,512]{2,1,0:T(8,128)(2,1)S(1)} %get-tuple-element.50.own_ref, f32[8,512]{1,0:T(8,128)S(1)} %get-tuple-element.40.ahead, f32[8,512]{1,0:T(8,128)S(1)} %get-tuple-element.41.behind, f32[8,512]{1,0:T(8,128)S(1)} %collective-permute-done.ahead2.refs_0_, ...), custom_call_target="tpu_custom_call" | custom-call | flops 100000000 | bytes 2000000 | tf_op jit(solution)/shard_map/panel/pallas_call | solution.py:349
  (6 shorter events, 0.0 us)
Async XLA Ops:
  0.6 18.8 %copy-start = (f32[1,16,512]{2,1,0:T(8,128)S(1)}, f32[1,16,512]{2,1,0:T(8,128)}, u32[]{:S(2)}) copy-start(f32[1,16,512]{2,1,0:T(8,128)} %param.6) | copy-start | bytes 98308
  0.6 18.8 %copy-start.1 = (f32[1,16,512]{2,1,0:T(8,128)S(1)}, f32[1,16,512]{2,1,0:T(8,128)}, u32[]{:S(2)}) copy-start(f32[1,16,512]{2,1,0:T(8,128)} %param.7) | copy-start | bytes 98308
  4.9 14.5 %collective-permute-start.4 = (f32[72,512]{1,0:T(8,128)S(1)}, f32[72,512]{1,0:T(8,128)S(1)}, u32[]{:S(2)}, u32[]{:S(2)}) collective-permute-start(f32[72,512]{1,0:T(8,128)S(1)} %get-tuple-element.43.top_ref), channel_id=1, source_target_pairs={{0,1},{1,2},{2,3},{3,4},{4,5},{5,6},{6,7},{7,0},{8,9},{9,10},{10,1... | collective-permute-start | bytes 442376 | tf_op jit(solution)/shard_map/ppermute | solution.py:370
  7.5 10.9 %collective-permute-start.5 = (f32[8,512]{1,0:T(8,128)S(1)}, f32[8,512]{1,0:T(8,128)S(1)}, u32[]{:S(2)}, u32[]{:S(2)}) collective-permute-start(f32[8,512]{1,0:T(8,128)S(1)} %get-tuple-element.45), channel_id=1, source_target_pairs={{0,7},{1,0},{2,1},{3,2},{4,3},{5,4},{6,5},{7,6},{8,15},{9,8},{10,9... | collective-permute-start | bytes 49160 | tf_op jit(solution)/shard_map/ppermute | solution.py:370
  11.5 10.1 %collective-permute-start.2 = (f32[8,512]{1,0:T(8,128)S(1)}, f32[8,512]{1,0:T(8,128)S(1)}, u32[]{:S(2)}, u32[]{:S(2)}) collective-permute-start(f32[8,512]{1,0:T(8,128)S(1)} %get-tuple-element.40.ahead), channel_id=1, source_target_pairs={{0,32},{8,40},{16,48},{24,56},{32,64},{40,72},{48,80},{56,88},{64,... | collective-permute-start | bytes 49160 | tf_op jit(solution)/shard_map/ppermute | solution.py:370
  14.3 7.4 %collective-permute-start = (f32[8,512]{1,0:T(8,128)S(1)}, f32[8,512]{1,0:T(8,128)S(1)}, u32[]{:S(2)}, u32[]{:S(2)}) collective-permute-start(f32[8,512]{1,0:T(8,128)S(1)} %get-tuple-element.40.ahead), channel_id=1, source_target_pairs={{0,16},{8,24},{16,32},{24,40},{32,48},{40,56},{48,64},{56,72},{64,... | collective-permute-start | bytes 49160 | tf_op jit(solution)/shard_map/ppermute | solution.py:370
  14.6 7.1 %collective-permute-start.3 = (f32[8,512]{1,0:T(8,128)S(1)}, f32[8,512]{1,0:T(8,128)S(1)}, u32[]{:S(2)}, u32[]{:S(2)}) collective-permute-start(f32[8,512]{1,0:T(8,128)S(1)} %get-tuple-element.41.behind), channel_id=1, source_target_pairs={{0,224},{8,232},{16,240},{24,248},{32,0},{40,8},{48,16},{56,24},{6... | collective-permute-start | bytes 49160 | tf_op jit(solution)/shard_map/ppermute | solution.py:370
  18.4 3.2 %collective-permute-start.1 = (f32[8,512]{1,0:T(8,128)S(1)}, f32[8,512]{1,0:T(8,128)S(1)}, u32[]{:S(2)}, u32[]{:S(2)}) collective-permute-start(f32[8,512]{1,0:T(8,128)S(1)} %get-tuple-element.41.behind), channel_id=1, source_target_pairs={{0,240},{8,248},{16,0},{24,8},{32,16},{40,24},{48,32},{56,40},{64,... | collective-permute-start | bytes 49160 | tf_op jit(solution)/shard_map/ppermute | solution.py:370
  21.7 3.2 %collective-permute-start.6 = (f32[32,512]{1,0:T(8,128)S(1)}, f32[32,512]{1,0:T(8,128)S(1)}, u32[]{:S(2)}, u32[]{:S(2)}) collective-permute-start(f32[32,512]{1,0:T(8,128)S(1)} %tails.1), channel_id=1, source_target_pairs={{0,8},{8,0},{16,24},{24,16},{32,40},{40,32},{48,56},{56,48},{64,72... | collective-permute-start | bytes 196616 | tf_op jit(solution)/shard_map/ppermute | solution.py:423
  26.2 16.6 %all-to-all-start = ((f32[8,64,128]{2,1,0:T(8,128)}), f32[8,64,128]{2,1,0:T(8,128)S(1)}, u32[]{:S(2)}, u32[]{:S(2)}) async-start(f32[8,64,128]{2,1,0:T(8,128)} %block.1), calls=%async_computation | async-start | bytes 524288 | tf_op jit(solution)/shard_map/all_to_all | solution.py:441
  31.7 22.1 %collective-permute-start.9 = (f32[64,512]{1,0:T(8,128)S(1)}, f32[64,512]{1,0:T(8,128)S(1)}, u32[]{:S(2)}, u32[]{:S(2)}) collective-permute-start(f32[64,512]{1,0:T(8,128)S(1)} %get-tuple-element.56.ahead), channel_id=1, source_target_pairs={{0,32},{8,40},{16,48},{24,56},{32,64},{40,72},{48,80},{56,88},{64,... | collective-permute-start | bytes 393224 | tf_op jit(solution)/shard_map/ppermute | solution.py:370
  33.6 20.2 %collective-permute-start.7 = (f32[64,512]{1,0:T(8,128)S(1)}, f32[64,512]{1,0:T(8,128)S(1)}, u32[]{:S(2)}, u32[]{:S(2)}) collective-permute-start(f32[64,512]{1,0:T(8,128)S(1)} %get-tuple-element.56.ahead), channel_id=1, source_target_pairs={{0,16},{8,24},{16,32},{24,40},{32,48},{40,56},{48,64},{56,72},{64,... | collective-permute-start | bytes 393224 | tf_op jit(solution)/shard_map/ppermute | solution.py:370
  34.0 19.8 %collective-permute-start.10 = (f32[64,512]{1,0:T(8,128)S(1)}, f32[64,512]{1,0:T(8,128)S(1)}, u32[]{:S(2)}, u32[]{:S(2)}) collective-permute-start(f32[64,512]{1,0:T(8,128)S(1)} %get-tuple-element.57.behind), channel_id=1, source_target_pairs={{0,224},{8,232},{16,240},{24,248},{32,0},{40,8},{48,16},{56,24},{6... | collective-permute-start | bytes 393224 | tf_op jit(solution)/shard_map/ppermute | solution.py:370
  38.6 15.2 %collective-permute-start.8 = (f32[64,512]{1,0:T(8,128)S(1)}, f32[64,512]{1,0:T(8,128)S(1)}, u32[]{:S(2)}, u32[]{:S(2)}) collective-permute-start(f32[64,512]{1,0:T(8,128)S(1)} %get-tuple-element.57.behind), channel_id=1, source_target_pairs={{0,240},{8,248},{16,0},{24,8},{32,16},{40,24},{48,32},{56,40},{64,... | collective-permute-start | bytes 393224 | tf_op jit(solution)/shard_map/ppermute | solution.py:370
  53.9 13.9 %collective-permute-start.11 = (f32[256,512]{1,0:T(8,128)S(1)}, f32[256,512]{1,0:T(8,128)S(1)}, u32[]{:S(2)}, u32[]{:S(2)}) collective-permute-start(f32[256,512]{1,0:T(8,128)S(1)} %faces.1), channel_id=1, source_target_pairs={{0,8},{8,0},{16,24},{24,16},{32,40},{40,32},{48,56},{56,48},{64,72... | collective-permute-start | bytes 1572872 | tf_op jit(solution)/shard_map/ppermute | solution.py:423

commit v5 on v4

--- a/solution.py
+++ b/solution.py
@@ -231,27 +231,56 @@
     out_ref[...] = product(left, jnp.concatenate([high, high, low], axis=0), MATRIX)
 
 
+def thirds(x):
+    high = x.astype(bf16)
+    rest = x - high.astype(f32)
+    middle = rest.astype(bf16)
+    return high, middle, (rest - middle.astype(f32)).astype(bf16)
+
+
+def fine_product(left, right):
+    a, b, c = thirds(left)
+    p, q, r = thirds(right)
+    first = product(jnp.concatenate([a, b, c], axis=0), p, MATRIX)
+    second = product(jnp.concatenate([a, b], axis=0), q, MATRIX)
+    small = product(a, r, MATRIX) + first[2 * K :] + second[K:]
+    return first[:K] + (first[K : 2 * K] + second[:K] + small)
+
+
+def lane_of(x, lane):
+    index = jnp.full(x.shape, lane, jnp.int32)
+    return jnp.take_along_axis(x, index, axis=1, mode="promise_in_bounds")
+
+
+def sublane_of(x, sublane):
+    index = jnp.full(x.shape, sublane, jnp.int32)
+    return jnp.take_along_axis(x, index, axis=0, mode="promise_in_bounds")
+
+
 def eliminate(rows, right, offset, lane, sub):
-    factor_rows, inverse_rows = [], []
     wide = (8, 128)
+    kept_rows, kept_right_rows = [], []
     for panel in range(8):
         first = offset + 8 * panel
-        column = [[None] * 16 for _ in range(8)]
-        for k in range(8):
-            for g in range(panel, 16):
-                column[k][g] = jnp.broadcast_to(rows[g][:, first + k : first + k + 1], wide)
+        column = [
+            {
+                g: lane_of(rows[g], first + k)
+                for g in range(panel, 8)
+            }
+            for k in range(8)
+        ]
         pivot = [[None] * 8 for _ in range(8)]
         for i in range(8):
             for k in range(i, 8):
-                pivot[i][k] = jnp.broadcast_to(column[i][panel][k : k + 1, :], wide)
-        left_row = [jnp.broadcast_to(rows[panel][k : k + 1, :], wide) for k in range(8)]
-        right_row = [jnp.broadcast_to(right[panel][k : k + 1, :], wide) for k in range(8)]
+                pivot[i][k] = sublane_of(column[i][panel], k)
+        left_row = [sublane_of(rows[panel], k) for k in range(8)]
+        right_row = [sublane_of(right[panel], k) for k in range(8)]
         kept = jnp.zeros(wide, f32)
         kept_right = jnp.zeros(wide, f32)
         for i in range(8):
             scale = lax.rsqrt(pivot[i][i])
             inverse = 1.0 / pivot[i][i]
-            kept = jnp.where(sub == i, jnp.where(lane >= first + i, left_row[i], 0.0) * scale if offset == 0 else jnp.where((lane >= first + i) | (lane < 64), left_row[i], 0.0) * scale, kept)
+            kept = jnp.where(sub == i, left_row[i] * scale, kept)
             kept_right = jnp.where(sub == i, right_row[i] * scale, kept_right)
             left_row[i] = left_row[i] * inverse
             right_row[i] = right_row[i] * inverse
@@ -267,18 +296,23 @@
                 for l in range(max(i + 1, k), 8):
                     pivot[k][l] = pivot[k][l] - by * scaled[l]
             pivot[i] = scaled
-        for g in range(panel + 1, 16):
+        for g in range(panel + 1, 8):
             for k in range(8):
                 rows[g] = rows[g] - column[k][g] * left_row[k]
                 right[g] = right[g] - column[k][g] * right_row[k]
-        factor_rows.append(kept)
-        inverse_rows.append(kept_right)
-    return factor_rows, inverse_rows
+        live = (lane >= first + sub) if offset else ((lane >= first + sub) | (lane >= K))
+        if offset:
+            live = live | (lane < K)
+        kept_rows.append(jnp.where(live, kept, 0.0))
+        kept_right_rows.append(kept_right)
+    return jnp.concatenate(kept_rows, axis=0), jnp.concatenate(kept_right_rows, axis=0)
+
 
 def half_factor(begin, level, blocks_ref, factor_ref, cross, top, top_right, inverse):
     lane = lax.broadcasted_iota(jnp.int32, (8, 128), 1)
     sub = lax.broadcasted_iota(jnp.int32, (8, 128), 0)
     wide_lane = lax.broadcasted_iota(jnp.int32, (K, 2 * K), 1)
+    wide_sub = lax.broadcasted_iota(jnp.int32, (K, 2 * K), 0)
     zero = jnp.zeros((K, 2 * K), f32)
     at = [pl.ds(8 * g, 8) for g in range(8)]
     for c in range(4 * begin + 1, min(4 * begin + 5, 8)):
@@ -290,34 +324,35 @@
     if begin:
         cross[7] = zero
 
-    def unit(g, c):
-        return jnp.where((lane == sub + 8 * g) & (level == c), 1.0, 0.0)
+    def unit(c):
+        return jnp.where((wide_lane == wide_sub) & (level == c), 1.0, 0.0)
 
     if not begin:
-        for g in range(8):
-            top[at[g], :] = blocks_ref[0, at[g], :]
-            top_right[at[g], :] = unit(g, 0)
+        top[...] = blocks_ref[0]
+        top_right[...] = unit(0)
 
     @pl.loop(2 * begin, 2 * begin + 2)
     def _(q):
         c = 2 * q
         last = q == 3
         rows = [jnp.where(lane < K, top[at[g], :], cross[c, at[g], :]) for g in range(8)]
-        rows += [blocks_ref[c + 1, at[g], :] for g in range(8)]
-        right = [top_right[at[g], :] for g in range(8)] + [unit(g, c + 1) for g in range(8)]
+        right = [top_right[at[g], :] for g in range(8)]
         even, even_right = eliminate(rows, right, 0, lane, sub)
-        following = jnp.minimum(c + 2, 7)
-        middle = [jnp.where(lane < K, cross[c + 1, at[g], :], rows[8 + g]) for g in range(8)]
-        middle += [jnp.where(last, 0.0, blocks_ref[following, at[g], :]) for g in range(8)]
-        middle_right = right[8:] + [unit(g, c + 2) for g in range(8)]
-        odd, odd_right = eliminate(middle, middle_right, K, lane, sub)
+        even_turned = even.T
+        taken = fine_product(even_turned[K:], jnp.concatenate([even, even_right], axis=1))
+        under = blocks_ref[c + 1] - taken[:, : 2 * K]
+        under_right = unit(c + 1) - taken[:, 2 * K :]
+        rows = [jnp.where(lane < K, cross[c + 1, at[g], :], under[8 * g : 8 * g + 8]) for g in range(8)]
+        right = [under_right[8 * g : 8 * g + 8] for g in range(8)]
+        odd, odd_right = eliminate(rows, right, K, lane, sub)
+        odd_turned = odd.T
+        taken = fine_product(odd_turned[:K], jnp.concatenate([odd, odd_right], axis=1))
+        top[...] = jnp.where(last, 0.0, blocks_ref[jnp.minimum(c + 2, 7)]) - taken[:, : 2 * K]
+        top_right[...] = unit(c + 2) - taken[:, 2 * K :]
         start = pl.multiple_of(128 * q, 128)
-        for g in range(8):
-            top[at[g], :] = middle[8 + g]
-            top_right[at[g], :] = middle_right[8 + g]
-            inverse[pl.ds(start + 8 * g, 8), :] = even_right[g]
-            inverse[pl.ds(start + K + 8 * g, 8), :] = odd_right[g]
-        both = jnp.concatenate(even + odd, axis=0).T
+        inverse[pl.ds(start, K), :] = even_right
+        inverse[pl.ds(start + K, K), :] = odd_right
+        both = jnp.concatenate([even_turned, odd_turned], axis=1)
         cols = pl.ds(start, 128)
         factor_ref[pl.ds(start, K), cols] = jnp.where(wide_lane < K, both[:K], 0.0)
         factor_ref[pl.ds(start + K, K), cols] = both[K:]

time: 71.4 us -> 64.2 us (0.90)
  Pallas kernels: 34.2 us -> 27.1 us
    pallas_call x8, Pallas kernels: 34.2 us -> 27.1 us  [call(): pl.pallas_call(kernel, out_shape=outs, in_specs=[HBM] * hbm + [VMEM] * (l...]
  transfers between devices with their start and end apart: 13 -> 13, of which waited for: 2 -> 2; matrix products, arithmetic and copies ran while one was open for 0% -> 0% of each run, Pallas kernels for 35% -> 28%
where the time goes in v5:
time: 64.2 us; the launch traced here: 64 us
  starting transfers between devices  31.1 us (48%)
  Pallas kernels  27.1 us (42%)
  waiting for transfers between devices  4.94 us (8%)
  between operations  0.76 us (1%)
    pallas_call x8, Pallas kernels, call(): pl.pallas_call(kernel, out_shape=outs, in_specs=[HBM] * hbm + [VMEM] * (l...  27.1 us
    ppermute x10, starting transfers between devices, passed_along(): lax.ppermute(block, axis, [(i, (i + distance) % count) for i in range(cou...  21.6 us
    all_to_all x1, starting transfers between devices, body(): blocks = lax.all_to_all(payload, 'coarse', 0, 0)  5.48 us
    ppermute x2, starting transfers between devices, swapped(): lax.ppermute(packed, 'sub', [(i, i ^ 1) for i in range(lax.axis_size('sub...  4.02 us
    all_to_all x1, waiting for transfers between devices, body(): blocks = lax.all_to_all(payload, 'coarse', 0, 0)  4.01 us
  transfers between devices with their start and end apart: 13, of which 2 were waited for; matrix products, arithmetic and copies ran while one was open for 0% of the time, Pallas kernels for 28%

profile of v5, /device:TPU:1, one launch (start us, length us, event | category | flops | bytes accessed | tf_op | source)
XLA Modules:
  0.0 64.0 jit_solution(16135492377601016147)
XLA Ops:
  0.7 4.3 %pick.1 = (f32[4,1024,128]{2,1,0:T(8,128)S(1)}, bf16[8,128,512]{2,1,0:T(8,128)(2,1)S(1)}, f32[64,512]{1,0:T(8,128)S(1)}, f32[64,512]{1,0:T(8,128)S(1)}, f32[8,51...) custom-call(f32[1024,512]{1,0:T(8,128)} %bitcast.10, ...), custom_call_target="tpu_custom_call" | custom-call | flops 100000000 | bytes 2000000 | tf_op jit(solution)/shard_map/pick/pallas_call | solution.py:384
  4.9 2.5 %collective-permute-start.4 = (f32[72,512]{1,0:T(8,128)S(1)}, f32[72,512]{1,0:T(8,128)S(1)}, u32[]{:S(2)}, u32[]{:S(2)}) collective-permute-start(f32[72,512]{1,0:T(8,128)S(1)} %get-tuple-element.43.top_ref), channel_id=1, source_target_pairs={{0,1},{1,2},{2,3},{3,4},{4,5},{5,6},{6,7},{7,0},{8,9},{9,10},{10,1... | collective-permute-start | bytes 442376 | tf_op jit(solution)/shard_map/ppermute | solution.py:405
  7.5 4.0 %collective-permute-start.5 = (f32[8,512]{1,0:T(8,128)S(1)}, f32[8,512]{1,0:T(8,128)S(1)}, u32[]{:S(2)}, u32[]{:S(2)}) collective-permute-start(f32[8,512]{1,0:T(8,128)S(1)} %get-tuple-element.45), channel_id=1, source_target_pairs={{0,7},{1,0},{2,1},{3,2},{4,3},{5,4},{6,5},{7,6},{8,15},{9,8},{10,9... | collective-permute-start | bytes 49160 | tf_op jit(solution)/shard_map/ppermute | solution.py:405
  11.5 2.7 %collective-permute-start.2 = (f32[8,512]{1,0:T(8,128)S(1)}, f32[8,512]{1,0:T(8,128)S(1)}, u32[]{:S(2)}, u32[]{:S(2)}) collective-permute-start(f32[8,512]{1,0:T(8,128)S(1)} %get-tuple-element.40.ahead), channel_id=1, source_target_pairs={{0,32},{8,40},{16,48},{24,56},{32,64},{40,72},{48,80},{56,88},{64,... | collective-permute-start | bytes 49160 | tf_op jit(solution)/shard_map/ppermute | solution.py:405
  14.3 0.3 collective-permute-start
  14.6 3.8 %collective-permute-start.3 = (f32[8,512]{1,0:T(8,128)S(1)}, f32[8,512]{1,0:T(8,128)S(1)}, u32[]{:S(2)}, u32[]{:S(2)}) collective-permute-start(f32[8,512]{1,0:T(8,128)S(1)} %get-tuple-element.41.behind), channel_id=1, source_target_pairs={{0,224},{8,232},{16,240},{24,248},{32,0},{40,8},{48,16},{56,24},{6... | collective-permute-start | bytes 49160 | tf_op jit(solution)/shard_map/ppermute | solution.py:405
  18.4 0.0 collective-permute-done.5.above_ref
  18.4 1.0 %collective-permute-start.1 = (f32[8,512]{1,0:T(8,128)S(1)}, f32[8,512]{1,0:T(8,128)S(1)}, u32[]{:S(2)}, u32[]{:S(2)}) collective-permute-start(f32[8,512]{1,0:T(8,128)S(1)} %get-tuple-element.41.behind), channel_id=1, source_target_pairs={{0,240},{8,248},{16,0},{24,8},{32,16},{40,24},{48,32},{56,40},{64,... | collective-permute-start | bytes 49160 | tf_op jit(solution)/shard_map/ppermute | solution.py:405
  19.4 0.0 collective-permute-done.4.below_ref
  19.4 2.2 %own.1 = (f32[64,64]{1,0:T(8,128)S(1)}, f32[64,64]{1,0:T(8,128)S(1)}) custom-call(f32[4,1024,128]{2,1,0:T(8,128)S(1)} %get-tuple-element.42.strips, f32[16,512]{1,0:T(8,128)S(1)} %bitcast.8, f32[16,512]{1,0:T(8,128)S(1)} %bitcast.9, f32[72,512]{1,0:T(8,128)S(1)} %get-tuple-element.43.top_ref, f32[72,512]{1,0:T(8,128)S(1)} %get-tuple-element.44.bottom_ref, ...), custom_call_target="tpu_custom_call" | custom-call | flops 100000000 | bytes 2000000 | tf_op jit(solution)/shard_map/own/pallas_call | solution.py:384
  21.6 0.0 collective-permute-done.2.ahead4.refs_2_
  21.6 0.0 collective-permute-done.ahead2.refs_0_
  21.6 0.0 collective-permute-done.3.behind4.refs_3_
  21.7 0.0 collective-permute-done.1.behind2.refs_1_
  21.7 2.3 %collective-permute-start.6 = (f32[32,512]{1,0:T(8,128)S(1)}, f32[32,512]{1,0:T(8,128)S(1)}, u32[]{:S(2)}, u32[]{:S(2)}) collective-permute-start(f32[32,512]{1,0:T(8,128)S(1)} %tails.1), channel_id=1, source_target_pairs={{0,8},{8,0},{16,24},{24,16},{32,40},{40,32},{48,56},{56,48},{64,72... | collective-permute-start | bytes 196616 | tf_op jit(solution)/shard_map/ppermute | solution.py:458
  24.0 0.9 %collective-permute-done.6.refs_4_ = f32[32,512]{1,0:T(8,128)S(1)} collective-permute-done((f32[32,512]{1,0:T(8,128)S(1)}, f32[32,512]{1,0:T(8,128)S(1)}, u32[]{:S(2)}, u32[]{:S(2)}) %collective-permute-start.6) | collective-permute-done | bytes 65568 | tf_op jit(solution)/shard_map/ppermute | solution.py:458
  24.9 1.4 %block.1 = f32[8,64,128]{2,1,0:T(8,128)} custom-call(f32[8,512]{1,0:T(8,128)S(1)} %get-tuple-element.39.live_ref, f32[64,64]{1,0:T(8,128)S(1)} %get-tuple-element.48.own_block, f32[64,64]{1,0:T(8,128)S(1)} %get-tuple-element.49.lower_block, bf16[8,128,512]{2,1,0:T(8,128)(2,1)S(1)} %get-tuple-element.50.own_ref, f32[8,512]{1,0:T(8,128)S(1)} %get-tuple-element.40.ahead, ...), custom_call_target="tpu_custom_call" | custom-call | flops 100000000 | bytes 2000000 | tf_op jit(solution)/shard_map/block/pallas_call | solution.py:384
  26.2 5.5 %all-to-all-start = ((f32[8,64,128]{2,1,0:T(8,128)}), f32[8,64,128]{2,1,0:T(8,128)S(1)}, u32[]{:S(2)}, u32[]{:S(2)}) async-start(f32[8,64,128]{2,1,0:T(8,128)} %block.1), calls=%async_computation | async-start | bytes 524288 | tf_op jit(solution)/shard_map/all_to_all | solution.py:476
  31.7 1.9 %collective-permute-start.9 = (f32[64,512]{1,0:T(8,128)S(1)}, f32[64,512]{1,0:T(8,128)S(1)}, u32[]{:S(2)}, u32[]{:S(2)}) collective-permute-start(f32[64,512]{1,0:T(8,128)S(1)} %get-tuple-element.56.ahead), channel_id=1, source_target_pairs={{0,32},{8,40},{16,48},{24,56},{32,64},{40,72},{48,80},{56,88},{64,... | collective-permute-start | bytes 393224 | tf_op jit(solution)/shard_map/ppermute | solution.py:405
  33.6 0.4 collective-permute-start.7
  34.0 4.6 %collective-permute-start.10 = (f32[64,512]{1,0:T(8,128)S(1)}, f32[64,512]{1,0:T(8,128)S(1)}, u32[]{:S(2)}, u32[]{:S(2)}) collective-permute-start(f32[64,512]{1,0:T(8,128)S(1)} %get-tuple-element.57.behind), channel_id=1, source_target_pairs={{0,224},{8,232},{16,240},{24,248},{32,0},{40,8},{48,16},{56,24},{6... | collective-permute-start | bytes 393224 | tf_op jit(solution)/shard_map/ppermute | solution.py:405
  38.6 0.3 collective-permute-start.8
  38.9 4.0 %all-to-all-done.blocks_ref = f32[8,64,128]{2,1,0:T(8,128)S(1)} async-done(((f32[8,64,128]{2,1,0:T(8,128)}), f32[8,64,128]{2,1,0:T(8,128)S(1)}, u32[]{:S(2)}, u32[]{:S(2)}) %all-to-all-start) | async-done | bytes 262176 | tf_op jit(solution)/shard_map/all_to_all | solution.py:476
  42.9 7.4 %factor_first.1 = (f32[320,256]{1,0:T(8,128)S(1)}, f32[256,128]{1,0:T(8,128)S(1)}, f32[64,128]{1,0:T(8,128)S(1)}, f32[64,128]{1,0:T(8,128)S(1)}) custom-call(f32[8,64,128]{2,1,0:T(8,128)S(1)} %all-to-all-done.blocks_ref), custom_call_target="tpu_custom_call" | custom-call | flops 1000000000 | bytes 2000000 | tf_op jit(solution)/shard_map/factor_first/pallas_call | solution.py:384
  50.3 0.0 collective-permute-done.9.ahead4.refs_7_
  50.3 0.0 collective-permute-done.7.ahead2.refs_5_
  50.3 0.0 collective-permute-done.10.behind4.refs_8_
  50.3 0.0 collective-permute-done.8.behind2.refs_6_
  50.3 0.1 faces.1
  50.4 1.8 %collective-permute-start.11 = (f32[256,512]{1,0:T(8,128)S(1)}, f32[256,512]{1,0:T(8,128)S(1)}, u32[]{:S(2)}, u32[]{:S(2)}) collective-permute-start(f32[256,512]{1,0:T(8,128)S(1)} %faces.1), channel_id=1, source_target_pairs={{0,8},{8,0},{16,24},{24,16},{32,40},{40,32},{48,56},{56,48},{64,72... | collective-permute-start | bytes 1572872 | tf_op jit(solution)/shard_map/ppermute | solution.py:458
  52.1 8.4 %factor_second.1 = (f32[512,512]{1,0:T(8,128)}, f32[512,128]{1,0:T(8,128)S(1)}) custom-call(f32[8,64,128]{2,1,0:T(8,128)S(1)} %all-to-all-done.blocks_ref, f32[320,256]{1,0:T(8,128)S(1)} %get-tuple-element.62.part_ref, f32[256,128]{1,0:T(8,128)S(1)} %get-tuple-element.63.first_inverse, f32[64,128]{1,0:T(8,128)S(1)} %get-tuple-element.64.first_top, ...), custom_call_target="tpu_custom_call" | custom-call | flops 1000000000 | bytes 2000000 | tf_op jit(solution)/shard_map/factor_second/pallas_call | solution.py:384
  60.6 3.4 %panel.1 = f32[512,512]{1,0:T(8,128)} custom-call(f32[8,512]{1,0:T(8,128)S(1)} %get-tuple-element.39.live_ref, bf16[8,128,512]{2,1,0:T(8,128)(2,1)S(1)} %get-tuple-element.50.own_ref, f32[8,512]{1,0:T(8,128)S(1)} %get-tuple-element.40.ahead, f32[8,512]{1,0:T(8,128)S(1)} %get-tuple-element.41.behind, f32[8,512]{1,0:T(8,128)S(1)} %collective-permute-done.ahead2.refs_0_, ...), custom_call_target="tpu_custom_call" | custom-call | flops 100000000 | bytes 2000000 | tf_op jit(solution)/shard_map/panel/pallas_call | solution.py:384
  (6 shorter events, 0.0 us)
Async XLA Ops:
  0.6 18.8 %copy-start = (f32[1,16,512]{2,1,0:T(8,128)S(1)}, f32[1,16,512]{2,1,0:T(8,128)}, u32[]{:S(2)}) copy-start(f32[1,16,512]{2,1,0:T(8,128)} %param.6) | copy-start | bytes 98308
  0.6 18.8 %copy-start.1 = (f32[1,16,512]{2,1,0:T(8,128)S(1)}, f32[1,16,512]{2,1,0:T(8,128)}, u32[]{:S(2)}) copy-start(f32[1,16,512]{2,1,0:T(8,128)} %param.7) | copy-start | bytes 98308
  4.9 14.5 %collective-permute-start.4 = (f32[72,512]{1,0:T(8,128)S(1)}, f32[72,512]{1,0:T(8,128)S(1)}, u32[]{:S(2)}, u32[]{:S(2)}) collective-permute-start(f32[72,512]{1,0:T(8,128)S(1)} %get-tuple-element.43.top_ref), channel_id=1, source_target_pairs={{0,1},{1,2},{2,3},{3,4},{4,5},{5,6},{6,7},{7,0},{8,9},{9,10},{10,1... | collective-permute-start | bytes 442376 | tf_op jit(solution)/shard_map/ppermute | solution.py:405
  7.5 10.9 %collective-permute-start.5 = (f32[8,512]{1,0:T(8,128)S(1)}, f32[8,512]{1,0:T(8,128)S(1)}, u32[]{:S(2)}, u32[]{:S(2)}) collective-permute-start(f32[8,512]{1,0:T(8,128)S(1)} %get-tuple-element.45), channel_id=1, source_target_pairs={{0,7},{1,0},{2,1},{3,2},{4,3},{5,4},{6,5},{7,6},{8,15},{9,8},{10,9... | collective-permute-start | bytes 49160 | tf_op jit(solution)/shard_map/ppermute | solution.py:405
  11.5 10.1 %collective-permute-start.2 = (f32[8,512]{1,0:T(8,128)S(1)}, f32[8,512]{1,0:T(8,128)S(1)}, u32[]{:S(2)}, u32[]{:S(2)}) collective-permute-start(f32[8,512]{1,0:T(8,128)S(1)} %get-tuple-element.40.ahead), channel_id=1, source_target_pairs={{0,32},{8,40},{16,48},{24,56},{32,64},{40,72},{48,80},{56,88},{64,... | collective-permute-start | bytes 49160 | tf_op jit(solution)/shard_map/ppermute | solution.py:405
  14.3 7.4 %collective-permute-start = (f32[8,512]{1,0:T(8,128)S(1)}, f32[8,512]{1,0:T(8,128)S(1)}, u32[]{:S(2)}, u32[]{:S(2)}) collective-permute-start(f32[8,512]{1,0:T(8,128)S(1)} %get-tuple-element.40.ahead), channel_id=1, source_target_pairs={{0,16},{8,24},{16,32},{24,40},{32,48},{40,56},{48,64},{56,72},{64,... | collective-permute-start | bytes 49160 | tf_op jit(solution)/shard_map/ppermute | solution.py:405
  14.6 7.1 %collective-permute-start.3 = (f32[8,512]{1,0:T(8,128)S(1)}, f32[8,512]{1,0:T(8,128)S(1)}, u32[]{:S(2)}, u32[]{:S(2)}) collective-permute-start(f32[8,512]{1,0:T(8,128)S(1)} %get-tuple-element.41.behind), channel_id=1, source_target_pairs={{0,224},{8,232},{16,240},{24,248},{32,0},{40,8},{48,16},{56,24},{6... | collective-permute-start | bytes 49160 | tf_op jit(solution)/shard_map/ppermute | solution.py:405
  18.4 3.2 %collective-permute-start.1 = (f32[8,512]{1,0:T(8,128)S(1)}, f32[8,512]{1,0:T(8,128)S(1)}, u32[]{:S(2)}, u32[]{:S(2)}) collective-permute-start(f32[8,512]{1,0:T(8,128)S(1)} %get-tuple-element.41.behind), channel_id=1, source_target_pairs={{0,240},{8,248},{16,0},{24,8},{32,16},{40,24},{48,32},{56,40},{64,... | collective-permute-start | bytes 49160 | tf_op jit(solution)/shard_map/ppermute | solution.py:405
  21.7 3.2 %collective-permute-start.6 = (f32[32,512]{1,0:T(8,128)S(1)}, f32[32,512]{1,0:T(8,128)S(1)}, u32[]{:S(2)}, u32[]{:S(2)}) collective-permute-start(f32[32,512]{1,0:T(8,128)S(1)} %tails.1), channel_id=1, source_target_pairs={{0,8},{8,0},{16,24},{24,16},{32,40},{40,32},{48,56},{56,48},{64,72... | collective-permute-start | bytes 196616 | tf_op jit(solution)/shard_map/ppermute | solution.py:458
  26.2 16.6 %all-to-all-start = ((f32[8,64,128]{2,1,0:T(8,128)}), f32[8,64,128]{2,1,0:T(8,128)S(1)}, u32[]{:S(2)}, u32[]{:S(2)}) async-start(f32[8,64,128]{2,1,0:T(8,128)} %block.1), calls=%async_computation | async-start | bytes 524288 | tf_op jit(solution)/shard_map/all_to_all | solution.py:476
  31.7 18.6 %collective-permute-start.9 = (f32[64,512]{1,0:T(8,128)S(1)}, f32[64,512]{1,0:T(8,128)S(1)}, u32[]{:S(2)}, u32[]{:S(2)}) collective-permute-start(f32[64,512]{1,0:T(8,128)S(1)} %get-tuple-element.56.ahead), channel_id=1, source_target_pairs={{0,32},{8,40},{16,48},{24,56},{32,64},{40,72},{48,80},{56,88},{64,... | collective-permute-start | bytes 393224 | tf_op jit(solution)/shard_map/ppermute | solution.py:405
  33.6 16.7 %collective-permute-start.7 = (f32[64,512]{1,0:T(8,128)S(1)}, f32[64,512]{1,0:T(8,128)S(1)}, u32[]{:S(2)}, u32[]{:S(2)}) collective-permute-start(f32[64,512]{1,0:T(8,128)S(1)} %get-tuple-element.56.ahead), channel_id=1, source_target_pairs={{0,16},{8,24},{16,32},{24,40},{32,48},{40,56},{48,64},{56,72},{64,... | collective-permute-start | bytes 393224 | tf_op jit(solution)/shard_map/ppermute | solution.py:405
  34.0 16.3 %collective-permute-start.10 = (f32[64,512]{1,0:T(8,128)S(1)}, f32[64,512]{1,0:T(8,128)S(1)}, u32[]{:S(2)}, u32[]{:S(2)}) collective-permute-start(f32[64,512]{1,0:T(8,128)S(1)} %get-tuple-element.57.behind), channel_id=1, source_target_pairs={{0,224},{8,232},{16,240},{24,248},{32,0},{40,8},{48,16},{56,24},{6... | collective-permute-start | bytes 393224 | tf_op jit(solution)/shard_map/ppermute | solution.py:405
  38.6 11.7 %collective-permute-start.8 = (f32[64,512]{1,0:T(8,128)S(1)}, f32[64,512]{1,0:T(8,128)S(1)}, u32[]{:S(2)}, u32[]{:S(2)}) collective-permute-start(f32[64,512]{1,0:T(8,128)S(1)} %get-tuple-element.57.behind), channel_id=1, source_target_pairs={{0,240},{8,248},{16,0},{24,8},{32,16},{40,24},{48,32},{56,40},{64,... | collective-permute-start | bytes 393224 | tf_op jit(solution)/shard_map/ppermute | solution.py:405
  50.4 10.2 %collective-permute-start.11 = (f32[256,512]{1,0:T(8,128)S(1)}, f32[256,512]{1,0:T(8,128)S(1)}, u32[]{:S(2)}, u32[]{:S(2)}) collective-permute-start(f32[256,512]{1,0:T(8,128)S(1)} %faces.1), channel_id=1, source_target_pairs={{0,8},{8,0},{16,24},{24,16},{32,40},{40,32},{48,56},{56,48},{64,72... | collective-permute-start | bytes 1572872 | tf_op jit(solution)/shard_map/ppermute | solution.py:458

commit v6 on v5

--- a/solution.py
+++ b/solution.py
@@ -44,6 +44,27 @@
     return half[:, :K] + half[:, K:]
 
 
+def gathered(table, index):
+    strips = []
+    for q in range(4):
+        wanted = jnp.broadcast_to(index[:, 128 * q : 128 * (q + 1)], (8, 128))
+        within, which = wanted & 127, wanted >> 7
+        groups = []
+        for g in range(0, table.shape[0], 8):
+            found = None
+            for strip in range(4):
+                part = jnp.take_along_axis(
+                    table[g : g + 8, 128 * strip : 128 * (strip + 1)],
+                    within,
+                    axis=1,
+                    mode="promise_in_bounds",
+                )
+                found = part if strip == 0 else jnp.where(which == strip, part, found)
+            groups.append(found)
+        strips.append(jnp.concatenate(groups, axis=0))
+    return jnp.concatenate(strips, axis=1)
+
+
 def rows_of(vectors, sigma):
     high, low = halves(sigma)
     tail = jnp.concatenate([high.astype(f32), low.astype(f32)], axis=0).astype(bf16)
@@ -60,7 +81,7 @@
     return jnp.concatenate([strips[q, pl.ds(z, K, stride=CZ), :] for q in range(4)], axis=1)
 
 
-def pick_kernel(vectors_hbm, sigma_hbm, index_hbm, counts_hbm, strips, own_ref, ahead_ref, behind_ref, ahead_tail, behind_tail, top_ref, bottom_ref, first_ref, live_ref, sigma_ref, index_ref, counts_ref, sems):
+def pick_kernel(vectors_hbm, sigma_hbm, index_hbm, counts_hbm, strips, own_ref, ahead_ref, behind_ref, tails_ref, top_ref, bottom_ref, first_ref, live_ref, sigma_ref, index_ref, counts_ref, sems):
     copies = [
         pltpu.make_async_copy(vectors_hbm.at[:, pl.ds(128 * q, 128)], strips.at[q], sems.at[q])
         for q in range(4)
@@ -95,7 +116,6 @@
     along = lax.broadcasted_iota(jnp.int32, (1, FACE), 1)
     for slot in range(2 * REACH):
         live_ref[slot : slot + 1] = jnp.where(along < counts_ref[slot], 1.0, 0.0)
-    place = lax.broadcasted_iota(jnp.int32, (FACE, FACE), 0)
     for side in range(2):
         wide = jnp.concatenate(
             [
@@ -104,18 +124,17 @@
             ],
             axis=1,
         )
-        table = wide.astype(bf16)
-        face_ref, tail_ref = (ahead_ref, ahead_tail) if side else (behind_ref, behind_tail)
-        face_ref[...] = wide[:K] + wide[K : 2 * K]
+        face_ref = ahead_ref if side else behind_ref
+        table = joined(wide)
+        face_ref[...] = table[:K]
         for slot in range(REACH * side, REACH * (side + 1)):
             cell_index = index_ref[slot : slot + 1, :]
             wanted = (cell_index >> 9) * CY + ((cell_index >> 4) & (CY - 1))
-            select = jnp.where(place == wanted, 1.0, 0.0).astype(bf16)
-            found = product(table, select, MATRIX)
-            own_ref[slot] = found[: 2 * K].astype(bf16)
-            reach = slot - REACH if side else REACH - 1 - slot
-            tail_ref[reach : reach + 1] = found[2 * K : 2 * K + 1] + found[2 * K + 8 : 2 * K + 9]
-            tail_ref[4 + reach : 5 + reach] = wanted.astype(f32)
+            found = gathered(table, wanted)
+            own_ref[slot] = stacked(found[:K])
+            row = slot - REACH if side else 8 + REACH - 1 - slot
+            tails_ref[row : row + 1] = found[K : K + 1]
+            tails_ref[4 + row : 5 + row] = wanted.astype(f32)
 
 
 def own_kernel(strips, sigma_ref, storage_ref, top_ref, bottom_ref, below_ref, above_ref, own_ref, lower_ref):
@@ -163,33 +182,47 @@
 
 
 def pack_kernel(ahead, behind, ahead2, behind2, ahead4, behind4, out_ref):
-    count = ahead.shape[0]
     mine = lax.axis_index("sub") % 2
     for core, chosen in ((0, (ahead, ahead2, behind2, behind4)), (1, (ahead2, ahead4, behind, behind2))):
         @pl.when(mine == core)
         def _(chosen=chosen):
             for at, ref in enumerate(chosen):
-                out_ref[count * at : count * (at + 1)] = ref[...]
+                out_ref[K * at : K * (at + 1)] = ref[...]
+
+
+def pair_kernel(own, other, ahead_ref, behind_ref):
+    ahead_ref[:8] = own[:8]
+    ahead_ref[8:] = other[:8]
+    behind_ref[:8] = own[8:]
+    behind_ref[8:] = other[8:]
+
+
+def join_kernel(first, second, out_ref):
+    out_ref[:16] = first[...]
+    out_ref[16:] = second[...]
 
 
 OFFSETS = (-4, -3, -2, -1, 1, 2, 3, 4)
 
 
-def partner(refs, offset):
+def tails_by_slot(other, before, after, swapped):
+    even = lax.axis_index("sub") % 2 == 0
+    low, high = slice(0, 8), slice(8, 16)
+    before1 = jnp.where(even, before[...], swapped[:16])
+    before2 = jnp.where(even, swapped[:16], before[...])
+    after1 = jnp.where(even, after[...], swapped[16:])
+    after2 = jnp.where(even, swapped[16:], after[...])
+    on_even = (before2[high], before2[low], before1[low], before1[high], other[high], after1[low], after1[high], after2[high])
+    on_odd = (before2[low], before1[low], before1[high], other[low], after1[low], after1[high], after2[high], after2[low])
+    return [jnp.where(even, x, y) for x, y in zip(on_even, on_odd, strict=True)]
+
+
+def partner_face(refs, offset):
     ahead2, behind2, ahead4, behind4, swapped = refs
     if offset % 2:
         at = {-1: 0, -3: 1, 1: 2, 3: 3}[offset]
-        count = ahead2.shape[0]
-        return swapped[count * at : count * at + count]
+        return swapped[K * at : K * at + K]
     return {-2: ahead2, -4: ahead4, 2: behind2, 4: behind4}[offset][...]
-
-
-def weight_of(live_ref, ahead_tail, behind_tail, slot, tail):
-    offset = OFFSETS[slot]
-    reach = abs(offset) - 1
-    mine = (ahead_tail if offset > 0 else behind_tail)[reach : reach + 1]
-    pair = harmonic(mine, tail[reach : reach + 1])
-    return jnp.where(live_ref[slot : slot + 1] > 0.0, pair, 0.0)
 
 
 def weighted_rows(own_ref, slot, weight):
@@ -197,11 +230,17 @@
     return stacked((rows[:K].astype(f32) + rows[K:].astype(f32)) * weight)
 
 
-def block_kernel(live_ref, own_block, lower_block, own_ref, ahead, behind, *refs):
-    *tails, out_ref = refs
+def block_kernel(live_ref, own_block, lower_block, own_ref, own_tails, *refs):
+    *tails, out_ref, weight_ref, index_ref = refs
     total = jnp.zeros((2 * K, 2 * K), f32)
+    found = tails_by_slot(*tails)
     for slot, offset in enumerate(OFFSETS):
-        weight = weight_of(live_ref, ahead, behind, slot, partner(tails, offset))
+        reach = abs(offset) - 1
+        row = reach if offset > 0 else 8 + reach
+        pair = harmonic(own_tails[row : row + 1], found[slot][reach : reach + 1])
+        weight = jnp.where(live_ref[slot : slot + 1] > 0.0, pair, 0.0)
+        weight_ref[slot : slot + 1] = weight
+        index_ref[slot : slot + 1] = found[slot][4 + reach : 5 + reach].astype(jnp.int32)
         total = total + product(weighted_rows(own_ref, slot, weight), own_ref[slot], GRAM)
     extra = quadrants(total)
     own = own_block[...] + 0.5 * (extra + extra.T)
@@ -214,17 +253,13 @@
         out_ref[copy] = payload
 
 
-def panel_kernel(live_ref, own_ref, ahead, behind, *refs):
-    tails, faces, inverse, out_ref = refs[:5], refs[5:10], refs[10], refs[11]
-    place = lax.broadcasted_iota(jnp.int32, (FACE, FACE), 0).astype(f32)
+def panel_kernel(weight_ref, index_ref, own_ref, *refs):
+    faces, inverse, out_ref = refs[:5], refs[5], refs[6]
     blocks = []
     for slot, offset in enumerate(OFFSETS):
-        tail = partner(tails, offset)
-        weight = weight_of(live_ref, ahead, behind, slot, tail)
-        reach = abs(offset) - 1
-        select = jnp.where(place == tail[4 + reach : 5 + reach], 1.0, 0.0).astype(bf16)
-        found = product(stacked(partner(faces, offset)), select, MATRIX).astype(bf16)
-        blocks.append(quadrants(product(weighted_rows(own_ref, slot, -weight), found, GRAM)))
+        found = gathered(partner_face(faces, offset), index_ref[slot : slot + 1, :])
+        weighted = weighted_rows(own_ref, slot, -weight_ref[slot : slot + 1])
+        blocks.append(quadrants(product(weighted, stacked(found), GRAM)))
     high, low = halves(jnp.concatenate(blocks, axis=1))
     left_high, left_low = halves(inverse[:, :K])
     left = jnp.concatenate([left_high, left_low, left_high], axis=1)
@@ -409,7 +444,7 @@
     vectors = deflation[0].reshape(K * CZ, FACE)
     sigma = conductivity[0]
     counts = interface_counts.reshape(2 * REACH)
-    strips, mine, ahead, behind, ahead_tail, behind_tail, top, bottom, first, live = call(
+    strips, mine, ahead, behind, own_tails, top, bottom, first, live = call(
         pick_kernel,
         "pick",
         (
@@ -417,8 +452,7 @@
             array(8, 2 * K, FACE, dtype=bf16),
             array(K, FACE),
             array(K, FACE),
-            array(8, FACE),
-            array(8, FACE),
+            array(16, FACE),
             array(ROWS, FACE),
             array(ROWS, FACE),
             array(8, FACE),
@@ -436,45 +470,40 @@
             pltpu.SemaphoreType.DMA((7,)),
         ),
     )
+    count = lax.axis_size("sub")
+    swap = [(i, i ^ 1) for i in range(count)]
+    other_tails = lax.ppermute(own_tails, "sub", swap)
     below = passed_along(top, "coarse", 1)
     above = passed_along(first, "coarse", -1)
-
-    def direct(ahead, behind):
-        return (
-            passed_along(ahead, "sub", 2),
-            passed_along(behind, "sub", -2),
-            passed_along(ahead, "sub", 4),
-            passed_along(behind, "sub", -4),
-        )
-
-    def swapped(name, own, received):
-        packed = call(
-            pack_kernel,
-            name,
-            array(4 * own[0].shape[0], FACE),
-            (*own, *received),
-            flops=10**6,
-        )
-        return lax.ppermute(packed, "sub", [(i, i ^ 1) for i in range(lax.axis_size("sub"))])
-
-    tails = direct(ahead_tail, behind_tail)
+    go_ahead, go_behind = call(
+        pair_kernel, "pair", (array(16, FACE), array(16, FACE)), (own_tails, other_tails), flops=10**6
+    )
+    far = [(i, (i + 2 + 2 * (i % 2)) % count) for i in range(count)]
+    before = lax.ppermute(go_ahead, "sub", far)
+    after = lax.ppermute(go_behind, "sub", [(j, i) for i, j in far])
     own, lower = call(
         own_kernel,
         "own",
         (array(K, K), array(K, K)),
         (strips, sigma, storage[0], top, bottom, below, above),
     )
-    tails, (own, lower) = lax.optimization_barrier((tails, (own, lower)))
-    tails = (*tails, swapped("tails", (ahead_tail, behind_tail), tails))
-    payload = call(
+    (before, after), (own, lower) = lax.optimization_barrier(((before, after), (own, lower)))
+    both = call(join_kernel, "join", array(32, FACE), (before, after), flops=10**6)
+    swapped_tails = lax.ppermute(both, "sub", swap)
+    payload, weight, index = call(
         block_kernel,
         "block",
-        array(8, K, 2 * K),
-        (live, own, lower, mine, ahead_tail, behind_tail, *tails),
+        (array(8, K, 2 * K), array(8, FACE), array(8, FACE, dtype=jnp.int32)),
+        (live, own, lower, mine, own_tails, other_tails, before, after, swapped_tails),
     )
     (ahead, behind), payload = lax.optimization_barrier(((ahead, behind), payload))
     blocks = lax.all_to_all(payload, "coarse", 0, 0)
-    faces = direct(ahead, behind)
+    faces = (
+        passed_along(ahead, "sub", 2),
+        passed_along(behind, "sub", -2),
+        passed_along(ahead, "sub", 4),
+        passed_along(behind, "sub", -4),
+    )
     state = call(
         first_half,
         "factor_first",
@@ -484,7 +513,8 @@
         scratch=(pltpu.VMEM((8, K, 2 * K), f32),),
     )
     faces, state = lax.optimization_barrier((faces, state))
-    faces = (*faces, swapped("faces", (ahead, behind), faces))
+    packed = call(pack_kernel, "faces", array(4 * K, FACE), (ahead, behind, *faces), flops=10**6)
+    faces = (*faces, lax.ppermute(packed, "sub", swap))
     factor, inverse = call(
         second_half,
         "factor_second",
@@ -497,7 +527,7 @@
         panel_kernel,
         "panel",
         array(8 * K, 8 * K),
-        (live, mine, ahead_tail, behind_tail, *tails, *faces, inverse),
+        (weight, index, mine, *faces, inverse),
     )
     return (factor[None], panel[None, None])
 

time: 64.2 us -> 65.1 us (1.014)
  starting transfers between devices: 31.1 us -> 29.1 us
  waiting for transfers between devices: 4.94 us -> 6.66 us
  Pallas kernels: 27.1 us -> 28.4 us
    ppermute x10 -> x6, starting transfers between devices: 21.6 us -> 13.4 us  [passed_along(): lax.ppermute(block, axis, [(i, (i + distance) % count) for i in range(cou...]
    ppermute x2 -> x5, starting transfers between devices: 4.02 us -> 9.34 us  [the longest x1 2.74 us: body(): before = lax.ppermute(go_ahead, 'sub', far)]
    pallas_call x8 -> x9, Pallas kernels: 27.1 us -> 28.4 us  [call(): pl.pallas_call(kernel, out_shape=outs, in_specs=[HBM] * hbm + [VMEM] * (l...]
    ppermute x2 -> x5, waiting for transfers between devices: 0.9 us -> 1.77 us  [the longest x1 0.9 us: body(): swapped_tails = lax.ppermute(both, 'sub', swap)]
    ppermute x10 -> x6, waiting for transfers between devices: 0.03 us -> 0.88 us  [passed_along(): lax.ppermute(block, axis, [(i, (i + distance) % count) for i in range(cou...]
    all_to_all x1, starting transfers between devices: 5.48 us -> 6.31 us  [body(): blocks = lax.all_to_all(payload, 'coarse', 0, 0)]
  transfers between devices with their start and end apart: 13 -> 12, of which waited for: 2 -> 4; matrix products, arithmetic and copies ran while one was open for 0% -> 0% of each run, Pallas kernels for 28% -> 28%
where the time goes in v6:
time: 65.1 us; the launch traced here: 64.9 us
  starting transfers between devices  29.1 us (45%)
  Pallas kernels  28.4 us (44%)
  waiting for transfers between devices  6.66 us (10%)
  between operations  0.76 us (1%)
    pallas_call x9, Pallas kernels, call(): pl.pallas_call(kernel, out_shape=outs, in_specs=[HBM] * hbm + [VMEM] * (l...  28.4 us
    ppermute x6, starting transfers between devices, passed_along(): lax.ppermute(block, axis, [(i, (i + distance) % count) for i in range(cou...  13.4 us
    all_to_all x1, starting transfers between devices, body(): blocks = lax.all_to_all(payload, 'coarse', 0, 0)  6.31 us
    all_to_all x1, waiting for transfers between devices, body(): blocks = lax.all_to_all(payload, 'coarse', 0, 0)  4.01 us
    ppermute x1, starting transfers between devices, body(): before = lax.ppermute(go_ahead, 'sub', far)  2.74 us
    ppermute x1, starting transfers between devices, body(): after = lax.ppermute(go_behind, 'sub', [(j, i) for i, j in far])  2.53 us
    ppermute x1, starting transfers between devices, body(): faces = (*faces, lax.ppermute(packed, 'sub', swap))  1.76 us
    ppermute x1, starting transfers between devices, body(): swapped_tails = lax.ppermute(both, 'sub', swap)  1.36 us
  transfers between devices with their start and end apart: 12, of which 4 were waited for; matrix products, arithmetic and copies ran while one was open for 0% of the time, Pallas kernels for 28%

profile of v6, /device:TPU:1, one launch (start us, length us, event | category | flops | bytes accessed | tf_op | source)
XLA Modules:
  0.0 64.9 jit_solution(1552697411518183788)
XLA Ops:
  0.7 4.6 %pick.1 = (f32[4,1024,128]{2,1,0:T(8,128)S(1)}, bf16[8,128,512]{2,1,0:T(8,128)(2,1)S(1)}, f32[64,512]{1,0:T(8,128)S(1)}, f32[64,512]{1,0:T(8,128)S(1)}, f32[16,5...) custom-call(f32[1024,512]{1,0:T(8,128)} %bitcast.10, ...), custom_call_target="tpu_custom_call" | custom-call | flops 100000000 | bytes 2000000 | tf_op jit(solution)/shard_map/pick/pallas_call | solution.py:419
  5.3 2.5 %collective-permute-start.3 = (f32[72,512]{1,0:T(8,128)S(1)}, f32[72,512]{1,0:T(8,128)S(1)}, u32[]{:S(2)}, u32[]{:S(2)}) collective-permute-start(f32[72,512]{1,0:T(8,128)S(1)} %get-tuple-element.46.top_ref), channel_id=1, source_target_pairs={{0,1},{1,2},{2,3},{3,4},{4,5},{5,6},{6,7},{7,0},{8,9},{9,10},{10,1... | collective-permute-start | bytes 442376 | tf_op jit(solution)/shard_map/ppermute | solution.py:440
  7.8 1.0 %collective-permute-start = (f32[16,512]{1,0:T(8,128)S(1)}, f32[16,512]{1,0:T(8,128)S(1)}, u32[]{:S(2)}, u32[]{:S(2)}) collective-permute-start(f32[16,512]{1,0:T(8,128)S(1)} %get-tuple-element.42.own.own_tails), channel_id=1, source_target_pairs={{0,8},{8,0},{16,24},{24,16},{32,40},{40,32},{48,56},{56,48},{64,72... | collective-permute-start | bytes 98312 | tf_op jit(solution)/shard_map/ppermute | solution.py:475
  8.8 0.9 %collective-permute-done.other.refs_0_ = f32[16,512]{1,0:T(8,128)S(1)} collective-permute-done((f32[16,512]{1,0:T(8,128)S(1)}, f32[16,512]{1,0:T(8,128)S(1)}, u32[]{:S(2)}, u32[]{:S(2)}) %collective-permute-start) | collective-permute-done | bytes 32800 | tf_op jit(solution)/shard_map/ppermute | solution.py:475
  9.6 2.7 %collective-permute-start.1 = (f32[16,512]{1,0:T(8,128)S(1)}, f32[16,512]{1,0:T(8,128)S(1)}, u32[]{:S(2)}, u32[]{:S(2)}) collective-permute-start(f32[16,512]{1,0:T(8,128)S(1)} %get-tuple-element.43), channel_id=1, source_target_pairs={{0,16},{8,40},{16,32},{24,56},{32,48},{40,72},{48,64},{56,88},{64,... | collective-permute-start | bytes 98312 | tf_op jit(solution)/shard_map/ppermute | solution.py:482
  12.4 2.5 %collective-permute-start.2 = (f32[16,512]{1,0:T(8,128)S(1)}, f32[16,512]{1,0:T(8,128)S(1)}, u32[]{:S(2)}, u32[]{:S(2)}) collective-permute-start(f32[16,512]{1,0:T(8,128)S(1)} %get-tuple-element.44), channel_id=1, source_target_pairs={{16,0},{40,8},{32,16},{56,24},{48,32},{72,40},{64,48},{88,56},{80,... | collective-permute-start | bytes 98312 | tf_op jit(solution)/shard_map/ppermute | solution.py:483
  14.9 3.8 %collective-permute-start.4 = (f32[8,512]{1,0:T(8,128)S(1)}, f32[8,512]{1,0:T(8,128)S(1)}, u32[]{:S(2)}, u32[]{:S(2)}) collective-permute-start(f32[8,512]{1,0:T(8,128)S(1)} %get-tuple-element.48), channel_id=1, source_target_pairs={{0,7},{1,0},{2,1},{3,2},{4,3},{5,4},{6,5},{7,6},{8,15},{9,8},{10,9... | collective-permute-start | bytes 49160 | tf_op jit(solution)/shard_map/ppermute | solution.py:440
  18.7 0.9 %collective-permute-done.4.above_ref = f32[8,512]{1,0:T(8,128)S(1)} collective-permute-done((f32[8,512]{1,0:T(8,128)S(1)}, f32[8,512]{1,0:T(8,128)S(1)}, u32[]{:S(2)}, u32[]{:S(2)}) %collective-permute-start.4) | collective-permute-done | bytes 16416 | tf_op jit(solution)/shard_map/ppermute | solution.py:440
  19.5 0.0 collective-permute-done.3.below_ref
  19.5 0.0 copy-done
  19.5 2.2 %own.1 = (f32[64,64]{1,0:T(8,128)S(1)}, f32[64,64]{1,0:T(8,128)S(1)}) custom-call(f32[4,1024,128]{2,1,0:T(8,128)S(1)} %get-tuple-element.45.strips, f32[16,512]{1,0:T(8,128)S(1)} %bitcast.8, f32[16,512]{1,0:T(8,128)S(1)} %bitcast.9, f32[72,512]{1,0:T(8,128)S(1)} %get-tuple-element.46.top_ref, f32[72,512]{1,0:T(8,128)S(1)} %get-tuple-element.47.bottom_ref, ...), custom_call_target="tpu_custom_call" | custom-call | flops 100000000 | bytes 2000000 | tf_op jit(solution)/shard_map/own/pallas_call | solution.py:419
  21.7 0.0 collective-permute-done.1.first.refs_1_
  21.7 0.0 collective-permute-done.2.second.refs_2_
  21.8 1.4 %collective-permute-start.5 = (f32[32,512]{1,0:T(8,128)S(1)}, f32[32,512]{1,0:T(8,128)S(1)}, u32[]{:S(2)}, u32[]{:S(2)}) collective-permute-start(f32[32,512]{1,0:T(8,128)S(1)} %join.1), channel_id=1, source_target_pairs={{0,8},{8,0},{16,24},{24,16},{32,40},{40,32},{48,56},{56,48},{64,72... | collective-permute-start | bytes 196616 | tf_op jit(solution)/shard_map/ppermute | solution.py:492
  23.1 0.9 %collective-permute-done.5.refs_3_ = f32[32,512]{1,0:T(8,128)S(1)} collective-permute-done((f32[32,512]{1,0:T(8,128)S(1)}, f32[32,512]{1,0:T(8,128)S(1)}, u32[]{:S(2)}, u32[]{:S(2)}) %collective-permute-start.5) | collective-permute-done | bytes 65568 | tf_op jit(solution)/shard_map/ppermute | solution.py:492
  24.0 1.4 %block.1 = (f32[8,64,128]{2,1,0:T(8,128)}, f32[8,512]{1,0:T(8,128)S(1)}, s32[8,512]{1,0:T(8,128)S(1)}) custom-call(f32[8,512]{1,0:T(8,128)S(1)} %get-tuple-element.41.live_ref, f32[64,64]{1,0:T(8,128)S(1)} %get-tuple-element.51.own_block, f32[64,64]{1,0:T(8,128)S(1)} %get-tuple-element.52.lower_block, bf16[8,128,512]{2,1,0:T(8,128)(2,1)S(1)} %get-tuple-element.53.own_ref, ...), custom_call_target="tpu_custom_call" | custom-call | flops 100000000 | bytes 2000000 | tf_op jit(solution)/shard_map/block/pallas_call | solution.py:419
  25.4 6.3 %all-to-all-start = ((f32[8,64,128]{2,1,0:T(8,128)}), f32[8,64,128]{2,1,0:T(8,128)S(1)}, u32[]{:S(2)}, u32[]{:S(2)}) async-start(f32[8,64,128]{2,1,0:T(8,128)} %get-tuple-element.57), calls=%async_computation | async-start | bytes 524288 | tf_op jit(solution)/shard_map/all_to_all | solution.py:500
  31.7 0.0 collective-permute-start.8
  31.7 0.1 collective-permute-start.6
  31.8 5.4 %collective-permute-start.9 = (f32[64,512]{1,0:T(8,128)S(1)}, f32[64,512]{1,0:T(8,128)S(1)}, u32[]{:S(2)}, u32[]{:S(2)}) collective-permute-start(f32[64,512]{1,0:T(8,128)S(1)} %get-tuple-element.59.behind), channel_id=1, source_target_pairs={{0,224},{8,232},{16,240},{24,248},{32,0},{40,8},{48,16},{56,24},{6... | collective-permute-start | bytes 393224 | tf_op jit(solution)/shard_map/ppermute | solution.py:440
  37.2 1.7 %collective-permute-start.7 = (f32[64,512]{1,0:T(8,128)S(1)}, f32[64,512]{1,0:T(8,128)S(1)}, u32[]{:S(2)}, u32[]{:S(2)}) collective-permute-start(f32[64,512]{1,0:T(8,128)S(1)} %get-tuple-element.59.behind), channel_id=1, source_target_pairs={{0,240},{8,248},{16,0},{24,8},{32,16},{40,24},{48,32},{56,40},{64,... | collective-permute-start | bytes 393224 | tf_op jit(solution)/shard_map/ppermute | solution.py:440
  38.9 4.0 %all-to-all-done.blocks_ref = f32[8,64,128]{2,1,0:T(8,128)S(1)} async-done(((f32[8,64,128]{2,1,0:T(8,128)}), f32[8,64,128]{2,1,0:T(8,128)S(1)}, u32[]{:S(2)}, u32[]{:S(2)}) %all-to-all-start) | async-done | bytes 262176 | tf_op jit(solution)/shard_map/all_to_all | solution.py:500
  42.9 7.4 %factor_first.1 = (f32[320,256]{1,0:T(8,128)S(1)}, f32[256,128]{1,0:T(8,128)S(1)}, f32[64,128]{1,0:T(8,128)S(1)}, f32[64,128]{1,0:T(8,128)S(1)}) custom-call(f32[8,64,128]{2,1,0:T(8,128)S(1)} %all-to-all-done.blocks_ref), custom_call_target="tpu_custom_call" | custom-call | flops 1000000000 | bytes 2000000 | tf_op jit(solution)/shard_map/factor_first/pallas_call | solution.py:419
  50.3 0.0 collective-permute-done.8.ahead4.refs_2_
  50.3 0.0 collective-permute-done.6.ahead2.refs_0_
  50.3 0.0 collective-permute-done.9.behind4.refs_3_
  50.4 0.0 collective-permute-done.7.behind2.refs_1_
  50.4 0.1 faces.1
  50.4 1.8 %collective-permute-start.10 = (f32[256,512]{1,0:T(8,128)S(1)}, f32[256,512]{1,0:T(8,128)S(1)}, u32[]{:S(2)}, u32[]{:S(2)}) collective-permute-start(f32[256,512]{1,0:T(8,128)S(1)} %faces.1), channel_id=1, source_target_pairs={{0,8},{8,0},{16,24},{24,16},{32,40},{40,32},{48,56},{56,48},{64,72... | collective-permute-start | bytes 1572872 | tf_op jit(solution)/shard_map/ppermute | solution.py:517
  52.2 8.4 %factor_second.1 = (f32[512,512]{1,0:T(8,128)}, f32[512,128]{1,0:T(8,128)S(1)}) custom-call(f32[8,64,128]{2,1,0:T(8,128)S(1)} %all-to-all-done.blocks_ref, f32[320,256]{1,0:T(8,128)S(1)} %get-tuple-element.64.part_ref, f32[256,128]{1,0:T(8,128)S(1)} %get-tuple-element.65.first_inverse, f32[64,128]{1,0:T(8,128)S(1)} %get-tuple-element.66.first_top, ...), custom_call_target="tpu_custom_call" | custom-call | flops 1000000000 | bytes 2000000 | tf_op jit(solution)/shard_map/factor_second/pallas_call | solution.py:419
  60.6 0.0 collective-permute-done.10.refs_4_
  60.6 4.3 %panel.1 = f32[512,512]{1,0:T(8,128)} custom-call(f32[8,512]{1,0:T(8,128)S(1)} %get-tuple-element.69.weight_ref, s32[8,512]{1,0:T(8,128)S(1)} %get-tuple-element.70.index_ref, bf16[8,128,512]{2,1,0:T(8,128)(2,1)S(1)} %get-tuple-element.53.own_ref, f32[64,512]{1,0:T(8,128)S(1)} %collective-permute-done.6.ahead2.refs_0_, ...), custom_call_target="tpu_custom_call" | custom-call | flops 100000000 | bytes 2000000 | tf_op jit(solution)/shard_map/panel/pallas_call | solution.py:419
  (5 shorter events, 0.0 us)
Async XLA Ops:
  0.6 18.9 %copy-start = (f32[1,16,512]{2,1,0:T(8,128)S(1)}, f32[1,16,512]{2,1,0:T(8,128)}, u32[]{:S(2)}) copy-start(f32[1,16,512]{2,1,0:T(8,128)} %param.6) | copy-start | bytes 98308
  0.6 18.9 %copy-start.1 = (f32[1,16,512]{2,1,0:T(8,128)S(1)}, f32[1,16,512]{2,1,0:T(8,128)}, u32[]{:S(2)}) copy-start(f32[1,16,512]{2,1,0:T(8,128)} %param.7) | copy-start | bytes 98308
  5.3 14.3 %collective-permute-start.3 = (f32[72,512]{1,0:T(8,128)S(1)}, f32[72,512]{1,0:T(8,128)S(1)}, u32[]{:S(2)}, u32[]{:S(2)}) collective-permute-start(f32[72,512]{1,0:T(8,128)S(1)} %get-tuple-element.46.top_ref), channel_id=1, source_target_pairs={{0,1},{1,2},{2,3},{3,4},{4,5},{5,6},{6,7},{7,0},{8,9},{9,10},{10,1... | collective-permute-start | bytes 442376 | tf_op jit(solution)/shard_map/ppermute | solution.py:440
  7.8 1.8 %collective-permute-start = (f32[16,512]{1,0:T(8,128)S(1)}, f32[16,512]{1,0:T(8,128)S(1)}, u32[]{:S(2)}, u32[]{:S(2)}) collective-permute-start(f32[16,512]{1,0:T(8,128)S(1)} %get-tuple-element.42.own.own_tails), channel_id=1, source_target_pairs={{0,8},{8,0},{16,24},{24,16},{32,40},{40,32},{48,56},{56,48},{64,72... | collective-permute-start | bytes 98312 | tf_op jit(solution)/shard_map/ppermute | solution.py:475
  9.6 12.1 %collective-permute-start.1 = (f32[16,512]{1,0:T(8,128)S(1)}, f32[16,512]{1,0:T(8,128)S(1)}, u32[]{:S(2)}, u32[]{:S(2)}) collective-permute-start(f32[16,512]{1,0:T(8,128)S(1)} %get-tuple-element.43), channel_id=1, source_target_pairs={{0,16},{8,40},{16,32},{24,56},{32,48},{40,72},{48,64},{56,88},{64,... | collective-permute-start | bytes 98312 | tf_op jit(solution)/shard_map/ppermute | solution.py:482
  12.4 9.4 %collective-permute-start.2 = (f32[16,512]{1,0:T(8,128)S(1)}, f32[16,512]{1,0:T(8,128)S(1)}, u32[]{:S(2)}, u32[]{:S(2)}) collective-permute-start(f32[16,512]{1,0:T(8,128)S(1)} %get-tuple-element.44), channel_id=1, source_target_pairs={{16,0},{40,8},{32,16},{56,24},{48,32},{72,40},{64,48},{88,56},{80,... | collective-permute-start | bytes 98312 | tf_op jit(solution)/shard_map/ppermute | solution.py:483
  14.9 4.6 %collective-permute-start.4 = (f32[8,512]{1,0:T(8,128)S(1)}, f32[8,512]{1,0:T(8,128)S(1)}, u32[]{:S(2)}, u32[]{:S(2)}) collective-permute-start(f32[8,512]{1,0:T(8,128)S(1)} %get-tuple-element.48), channel_id=1, source_target_pairs={{0,7},{1,0},{2,1},{3,2},{4,3},{5,4},{6,5},{7,6},{8,15},{9,8},{10,9... | collective-permute-start | bytes 49160 | tf_op jit(solution)/shard_map/ppermute | solution.py:440
  21.8 2.3 %collective-permute-start.5 = (f32[32,512]{1,0:T(8,128)S(1)}, f32[32,512]{1,0:T(8,128)S(1)}, u32[]{:S(2)}, u32[]{:S(2)}) collective-permute-start(f32[32,512]{1,0:T(8,128)S(1)} %join.1), channel_id=1, source_target_pairs={{0,8},{8,0},{16,24},{24,16},{32,40},{40,32},{48,56},{56,48},{64,72... | collective-permute-start | bytes 196616 | tf_op jit(solution)/shard_map/ppermute | solution.py:492
  25.4 17.5 %all-to-all-start = ((f32[8,64,128]{2,1,0:T(8,128)}), f32[8,64,128]{2,1,0:T(8,128)S(1)}, u32[]{:S(2)}, u32[]{:S(2)}) async-start(f32[8,64,128]{2,1,0:T(8,128)} %get-tuple-element.57), calls=%async_computation | async-start | bytes 524288 | tf_op jit(solution)/shard_map/all_to_all | solution.py:500
  31.7 18.6 %collective-permute-start.8 = (f32[64,512]{1,0:T(8,128)S(1)}, f32[64,512]{1,0:T(8,128)S(1)}, u32[]{:S(2)}, u32[]{:S(2)}) collective-permute-start(f32[64,512]{1,0:T(8,128)S(1)} %get-tuple-element.58.ahead), channel_id=1, source_target_pairs={{0,32},{8,40},{16,48},{24,56},{32,64},{40,72},{48,80},{56,88},{64,... | collective-permute-start | bytes 393224 | tf_op jit(solution)/shard_map/ppermute | solution.py:440
  31.7 18.6 %collective-permute-start.6 = (f32[64,512]{1,0:T(8,128)S(1)}, f32[64,512]{1,0:T(8,128)S(1)}, u32[]{:S(2)}, u32[]{:S(2)}) collective-permute-start(f32[64,512]{1,0:T(8,128)S(1)} %get-tuple-element.58.ahead), channel_id=1, source_target_pairs={{0,16},{8,24},{16,32},{24,40},{32,48},{40,56},{48,64},{56,72},{64,... | collective-permute-start | bytes 393224 | tf_op jit(solution)/shard_map/ppermute | solution.py:440
  31.8 18.5 %collective-permute-start.9 = (f32[64,512]{1,0:T(8,128)S(1)}, f32[64,512]{1,0:T(8,128)S(1)}, u32[]{:S(2)}, u32[]{:S(2)}) collective-permute-start(f32[64,512]{1,0:T(8,128)S(1)} %get-tuple-element.59.behind), channel_id=1, source_target_pairs={{0,224},{8,232},{16,240},{24,248},{32,0},{40,8},{48,16},{56,24},{6... | collective-permute-start | bytes 393224 | tf_op jit(solution)/shard_map/ppermute | solution.py:440
  37.2 13.1 %collective-permute-start.7 = (f32[64,512]{1,0:T(8,128)S(1)}, f32[64,512]{1,0:T(8,128)S(1)}, u32[]{:S(2)}, u32[]{:S(2)}) collective-permute-start(f32[64,512]{1,0:T(8,128)S(1)} %get-tuple-element.59.behind), channel_id=1, source_target_pairs={{0,240},{8,248},{16,0},{24,8},{32,16},{40,24},{48,32},{56,40},{64,... | collective-permute-start | bytes 393224 | tf_op jit(solution)/shard_map/ppermute | solution.py:440
  50.4 10.2 %collective-permute-start.10 = (f32[256,512]{1,0:T(8,128)S(1)}, f32[256,512]{1,0:T(8,128)S(1)}, u32[]{:S(2)}, u32[]{:S(2)}) collective-permute-start(f32[256,512]{1,0:T(8,128)S(1)} %faces.1), channel_id=1, source_target_pairs={{0,8},{8,0},{16,24},{24,16},{32,40},{40,32},{48,56},{56,48},{64,72... | collective-permute-start | bytes 1572872 | tf_op jit(solution)/shard_map/ppermute | solution.py:517

commit v7 on v6

--- a/solution.py
+++ b/solution.py
@@ -44,97 +44,80 @@
     return half[:, :K] + half[:, K:]
 
 
-def gathered(table, index):
-    strips = []
-    for q in range(4):
-        wanted = jnp.broadcast_to(index[:, 128 * q : 128 * (q + 1)], (8, 128))
-        within, which = wanted & 127, wanted >> 7
-        groups = []
-        for g in range(0, table.shape[0], 8):
-            found = None
-            for strip in range(4):
-                part = jnp.take_along_axis(
-                    table[g : g + 8, 128 * strip : 128 * (strip + 1)],
-                    within,
-                    axis=1,
-                    mode="promise_in_bounds",
-                )
-                found = part if strip == 0 else jnp.where(which == strip, part, found)
-            groups.append(found)
-        strips.append(jnp.concatenate(groups, axis=0))
-    return jnp.concatenate(strips, axis=1)
-
-
-def rows_of(vectors, sigma):
-    high, low = halves(sigma)
-    tail = jnp.concatenate([high.astype(f32), low.astype(f32)], axis=0).astype(bf16)
-    return jnp.concatenate([*halves(vectors), tail], axis=0)
-
-
-def joined(found):
-    return jnp.concatenate(
-        [found[:K] + found[K : 2 * K], found[2 * K : 2 * K + 8] + found[2 * K + 8 :]], axis=0
-    )
+def one_hot(index):
+    place = lax.broadcasted_iota(jnp.int32, (FACE, FACE), 0)
+    return jnp.where(place == index, 1.0, 0.0).astype(bf16)
 
 
 def layer_of(strips, z):
     return jnp.concatenate([strips[q, pl.ds(z, K, stride=CZ), :] for q in range(4)], axis=1)
 
 
-def pick_kernel(vectors_hbm, sigma_hbm, index_hbm, counts_hbm, strips, own_ref, ahead_ref, behind_ref, tails_ref, top_ref, bottom_ref, first_ref, live_ref, sigma_ref, index_ref, counts_ref, sems):
-    copies = [
+def pick_kernel(vectors_hbm, sigma_hbm, index_hbm, counts_hbm, strips, own_ref, ahead_ref, behind_ref, tails_ref, top_ref, bottom_ref, live_ref, sigma_ref, index_ref, counts_ref, choice_ref, hot_ref, sems):
+    small = [
+        pltpu.make_async_copy(sigma_hbm, sigma_ref, sems.at[4]),
+        pltpu.make_async_copy(index_hbm, index_ref, sems.at[5]),
+        pltpu.make_async_copy(counts_hbm, counts_ref, sems.at[6]),
+    ]
+    large = [
         pltpu.make_async_copy(vectors_hbm.at[:, pl.ds(128 * q, 128)], strips.at[q], sems.at[q])
         for q in range(4)
     ]
-    copies.append(pltpu.make_async_copy(sigma_hbm, sigma_ref, sems.at[4]))
-    copies.append(pltpu.make_async_copy(index_hbm, index_ref, sems.at[5]))
-    copies.append(pltpu.make_async_copy(counts_hbm, counts_ref, sems.at[6]))
-    for copy in copies:
+    for copy in small + large:
         copy.start()
     lane = lax.broadcasted_iota(jnp.int32, (1, 256), 1)
     within = lane % 128
     cell_of_lane = (within % CY) * CX + jnp.where(lane >= 128, CX - 1, 0)
     cell = lax.broadcasted_iota(jnp.int32, (FACE, 256), 0)
-    faces = jnp.zeros((4 * 144, 256), f32)
-    for copy in copies:
+    for step in range(4):
+        chosen = jnp.where(within // CY == step, cell_of_lane, -1)
+        choice_ref[step] = jnp.where(cell == chosen, 1.0, 0.0).astype(bf16)
+    for copy in small:
         copy.wait()
-    for step in range(4):
-        groups = []
-        for group in range(4):
-            z = 4 * group + step
-            layer = layer_of(strips, z)
-            sigma = jnp.broadcast_to(sigma_ref[z : z + 1, :], (8, FACE))
-            groups.append(rows_of(layer, sigma))
-            if z == 0:
-                bottom_ref[...] = jnp.concatenate([layer, sigma], axis=0)
-                first_ref[...] = sigma
-            if z == CZ - 1:
-                top_ref[...] = jnp.concatenate([layer, sigma], axis=0)
-        chosen = jnp.where(within // CY == step, cell_of_lane, -1)
-        select = jnp.where(cell == chosen, 1.0, 0.0).astype(bf16)
-        faces = faces + product(jnp.concatenate(groups, axis=0), select, MATRIX)
+
+    def faces_of(rows_of_layer, count):
+        total = jnp.zeros((4 * count, 256), f32)
+        for step in range(4):
+            groups = [rows_of_layer(4 * group + step) for group in range(4)]
+            total = total + product(jnp.concatenate(groups, axis=0), choice_ref[step], MATRIX)
+        return [
+            jnp.concatenate(
+                [
+                    total[count * group : count * (group + 1), 128 * side : 128 * (side + 1)]
+                    for group in range(4)
+                ],
+                axis=1,
+            )
+            for side in range(2)
+        ]
+
+    def sigma_rows(z):
+        high, low = halves(jnp.broadcast_to(sigma_ref[z : z + 1, :], (8, FACE)))
+        return jnp.concatenate([high.astype(f32), low.astype(f32)], axis=0).astype(bf16)
+
     along = lax.broadcasted_iota(jnp.int32, (1, FACE), 1)
+    sigma_faces = faces_of(sigma_rows, 16)
     for slot in range(2 * REACH):
+        side = slot // REACH
         live_ref[slot : slot + 1] = jnp.where(along < counts_ref[slot], 1.0, 0.0)
-    for side in range(2):
-        wide = jnp.concatenate(
-            [
-                faces[144 * group : 144 * (group + 1), 128 * side : 128 * (side + 1)]
-                for group in range(4)
-            ],
-            axis=1,
-        )
-        face_ref = ahead_ref if side else behind_ref
-        table = joined(wide)
-        face_ref[...] = table[:K]
+        cell_index = index_ref[slot : slot + 1, :]
+        wanted = (cell_index >> 9) * CY + ((cell_index >> 4) & (CY - 1))
+        hot_ref[slot] = one_hot(wanted)
+        found = product(sigma_faces[side].astype(bf16), hot_ref[slot], MATRIX)
+        row = slot - REACH if side else 8 + REACH - 1 - slot
+        tails_ref[row : row + 1] = found[:1] + found[8:9]
+        tails_ref[4 + row : 5 + row] = wanted.astype(f32)
+    for copy in large:
+        copy.wait()
+    for out_ref, z in ((bottom_ref, 0), (top_ref, CZ - 1)):
+        out_ref[:K] = layer_of(strips, z)
+        out_ref[K:] = jnp.broadcast_to(sigma_ref[z : z + 1, :], (8, FACE))
+    faces = faces_of(lambda z: stacked(layer_of(strips, z)), 2 * K)
+    for side, face_ref in ((0, behind_ref), (1, ahead_ref)):
+        face_ref[...] = faces[side][:K] + faces[side][K:]
+        table = faces[side].astype(bf16)
         for slot in range(REACH * side, REACH * (side + 1)):
-            cell_index = index_ref[slot : slot + 1, :]
-            wanted = (cell_index >> 9) * CY + ((cell_index >> 4) & (CY - 1))
-            found = gathered(table, wanted)
-            own_ref[slot] = stacked(found[:K])
-            row = slot - REACH if side else 8 + REACH - 1 - slot
-            tails_ref[row : row + 1] = found[K : K + 1]
-            tails_ref[4 + row : 5 + row] = wanted.astype(f32)
+            own_ref[slot] = product(table, hot_ref[slot], MATRIX).astype(bf16)
 
 
 def own_kernel(strips, sigma_ref, storage_ref, top_ref, bottom_ref, below_ref, above_ref, own_ref, lower_ref):
@@ -151,7 +134,7 @@
     level = lax.axis_index("coarse")
     downward = harmonic(bottom_ref[K : K + 1, :], below_ref[K : K + 1, :])
     downward = jnp.where(level == 0, 0.0, downward)
-    upward = harmonic(top_ref[K : K + 1, :], above_ref[:1, :])
+    upward = harmonic(top_ref[K : K + 1, :], above_ref[K : K + 1, :])
     upward = jnp.where(level == lax.axis_size("coarse") - 1, 0.0, upward)
     half = 0.5 * (
         storage_ref[...]
@@ -242,10 +225,11 @@
         weight_ref[slot : slot + 1] = weight
         index_ref[slot : slot + 1] = found[slot][4 + reach : 5 + reach].astype(jnp.int32)
         total = total + product(weighted_rows(own_ref, slot, weight), own_ref[slot], GRAM)
+    level = lax.axis_index("coarse")
     extra = quadrants(total)
     own = own_block[...] + 0.5 * (extra + extra.T)
     lower = lower_block[...]
-    even = lax.axis_index("coarse") % 2 == 0
+    even = level % 2 == 0
     payload = jnp.where(
         even, jnp.concatenate([own, lower], axis=1), jnp.concatenate([lower, own], axis=1)
     )
@@ -257,9 +241,10 @@
     faces, inverse, out_ref = refs[:5], refs[5], refs[6]
     blocks = []
     for slot, offset in enumerate(OFFSETS):
-        found = gathered(partner_face(faces, offset), index_ref[slot : slot + 1, :])
+        select = one_hot(index_ref[slot : slot + 1, :])
+        found = product(stacked(partner_face(faces, offset)), select, MATRIX).astype(bf16)
         weighted = weighted_rows(own_ref, slot, -weight_ref[slot : slot + 1])
-        blocks.append(quadrants(product(weighted, stacked(found), GRAM)))
+        blocks.append(quadrants(product(weighted, found, GRAM)))
     high, low = halves(jnp.concatenate(blocks, axis=1))
     left_high, left_low = halves(inverse[:, :K])
     left = jnp.concatenate([left_high, left_low, left_high], axis=1)
@@ -444,7 +429,7 @@
     vectors = deflation[0].reshape(K * CZ, FACE)
     sigma = conductivity[0]
     counts = interface_counts.reshape(2 * REACH)
-    strips, mine, ahead, behind, own_tails, top, bottom, first, live = call(
+    strips, mine, ahead, behind, own_tails, top, bottom, live = call(
         pick_kernel,
         "pick",
         (
@@ -456,7 +441,6 @@
             array(ROWS, FACE),
             array(ROWS, FACE),
             array(8, FACE),
-            array(8, FACE),
         ),
         tuple(
             pltpu.with_memory_space_constraint(x, pltpu.HBM)
@@ -467,6 +451,8 @@
             pltpu.VMEM((CZ, FACE), f32),
             pltpu.VMEM((2 * REACH, FACE), jnp.int32),
             pltpu.SMEM((2 * REACH,), jnp.int32),
+            pltpu.VMEM((4, FACE, 256), bf16),
+            pltpu.VMEM((2 * REACH, FACE, FACE), bf16),
             pltpu.SemaphoreType.DMA((7,)),
         ),
     )
@@ -474,7 +460,7 @@
     swap = [(i, i ^ 1) for i in range(count)]
     other_tails = lax.ppermute(own_tails, "sub", swap)
     below = passed_along(top, "coarse", 1)
-    above = passed_along(first, "coarse", -1)
+    above = passed_along(bottom, "coarse", -1)
     go_ahead, go_behind = call(
         pair_kernel, "pair", (array(16, FACE), array(16, FACE)), (own_tails, other_tails), flops=10**6
     )

time: 65.1 us -> 62.3 us (0.957)
  waiting for transfers between devices: 6.66 us -> 4.99 us
    ppermute x6, starting transfers between devices: 13.4 us -> 14.5 us  [passed_along(): lax.ppermute(block, axis, [(i, (i + distance) % count) for i in range(cou...]
    ppermute x6, waiting for transfers between devices: 0.88 us -> 0.02 us  [passed_along(): lax.ppermute(block, axis, [(i, (i + distance) % count) for i in range(cou...]
    ppermute x1, starting transfers between devices: 1.36 us -> 0.51 us  [body(): swapped_tails = lax.ppermute(both, 'sub', swap)]
    all_to_all x1, starting transfers between devices: 6.31 us -> 5.48 us  [body(): blocks = lax.all_to_all(payload, 'coarse', 0, 0)]
    all_to_all x1, waiting for transfers between devices: 4.01 us -> 3.2 us  [body(): blocks = lax.all_to_all(payload, 'coarse', 0, 0)]
  transfers between devices with their start and end apart: 12 -> 12, of which waited for: 4 -> 3; matrix products, arithmetic and copies ran while one was open for 0% -> 0% of each run, Pallas kernels for 28% -> 29%
where the time goes in v7:
time: 62.3 us; the launch traced here: 62.1 us
  starting transfers between devices  28.5 us (46%)
  Pallas kernels  27.9 us (45%)
  waiting for transfers between devices  4.99 us (8%)
  between operations  0.75 us (1%)
    pallas_call x9, Pallas kernels, call(): pl.pallas_call(kernel, out_shape=outs, in_specs=[HBM] * hbm + [VMEM] * (l...  27.9 us
    ppermute x6, starting transfers between devices, passed_along(): lax.ppermute(block, axis, [(i, (i + distance) % count) for i in range(cou...  14.5 us
    all_to_all x1, starting transfers between devices, body(): blocks = lax.all_to_all(payload, 'coarse', 0, 0)  5.48 us
    all_to_all x1, waiting for transfers between devices, body(): blocks = lax.all_to_all(payload, 'coarse', 0, 0)  3.2 us
    ppermute x1, starting transfers between devices, body(): before = lax.ppermute(go_ahead, 'sub', far)  2.74 us
    ppermute x1, starting transfers between devices, body(): after = lax.ppermute(go_behind, 'sub', [(j, i) for i, j in far])  2.53 us
    ppermute x1, starting transfers between devices, body(): faces = (*faces, lax.ppermute(packed, 'sub', swap))  1.76 us
  transfers between devices with their start and end apart: 12, of which 3 were waited for; matrix products, arithmetic and copies ran while one was open for 0% of the time, Pallas kernels for 29%

profile of v7, /device:TPU:1, one launch (start us, length us, event | category | flops | bytes accessed | tf_op | source)
XLA Modules:
  0.0 62.1 jit_solution(4923751473072005540)
XLA Ops:
  0.6 0.0 copy-start
  0.7 5.0 %pick.1 = (f32[4,1024,128]{2,1,0:T(8,128)S(1)}, bf16[8,128,512]{2,1,0:T(8,128)(2,1)S(1)}, f32[64,512]{1,0:T(8,128)S(1)}, f32[64,512]{1,0:T(8,128)S(1)}, f32[16,5...) custom-call(f32[1024,512]{1,0:T(8,128)} %bitcast.10, f32[16,512]{1,0:T(8,128)} %bitcast.7, ...), custom_call_target="tpu_custom_call" | custom-call | flops 100000000 | bytes 2000000 | tf_op jit(solution)/shard_map/pick/pallas_call | solution.py:404
  5.7 2.5 %collective-permute-start.3 = (f32[72,512]{1,0:T(8,128)S(1)}, f32[72,512]{1,0:T(8,128)S(1)}, u32[]{:S(2)}, u32[]{:S(2)}) collective-permute-start(f32[72,512]{1,0:T(8,128)S(1)} %get-tuple-element.45.top_ref), channel_id=1, source_target_pairs={{0,1},{1,2},{2,3},{3,4},{4,5},{5,6},{6,7},{7,0},{8,9},{9,10},{10,1... | collective-permute-start | bytes 442376 | tf_op jit(solution)/shard_map/ppermute | solution.py:425
  8.2 4.0 %collective-permute-start.4 = (f32[72,512]{1,0:T(8,128)S(1)}, f32[72,512]{1,0:T(8,128)S(1)}, u32[]{:S(2)}, u32[]{:S(2)}) collective-permute-start(f32[72,512]{1,0:T(8,128)S(1)} %get-tuple-element.46.bottom_ref), channel_id=1, source_target_pairs={{0,7},{1,0},{2,1},{3,2},{4,3},{5,4},{6,5},{7,6},{8,15},{9,8},{10,9... | collective-permute-start | bytes 442376 | tf_op jit(solution)/shard_map/ppermute | solution.py:425
  12.3 1.0 %collective-permute-start = (f32[16,512]{1,0:T(8,128)S(1)}, f32[16,512]{1,0:T(8,128)S(1)}, u32[]{:S(2)}, u32[]{:S(2)}) collective-permute-start(f32[16,512]{1,0:T(8,128)S(1)} %get-tuple-element.41.own.own_tails), channel_id=1, source_target_pairs={{0,8},{8,0},{16,24},{24,16},{32,40},{40,32},{48,56},{56,48},{64,72... | collective-permute-start | bytes 98312 | tf_op jit(solution)/shard_map/ppermute | solution.py:461
  13.2 0.9 %collective-permute-done.other.refs_0_ = f32[16,512]{1,0:T(8,128)S(1)} collective-permute-done((f32[16,512]{1,0:T(8,128)S(1)}, f32[16,512]{1,0:T(8,128)S(1)}, u32[]{:S(2)}, u32[]{:S(2)}) %collective-permute-start) | collective-permute-done | bytes 32800 | tf_op jit(solution)/shard_map/ppermute | solution.py:461
  14.1 2.7 %collective-permute-start.1 = (f32[16,512]{1,0:T(8,128)S(1)}, f32[16,512]{1,0:T(8,128)S(1)}, u32[]{:S(2)}, u32[]{:S(2)}) collective-permute-start(f32[16,512]{1,0:T(8,128)S(1)} %get-tuple-element.42), channel_id=1, source_target_pairs={{0,16},{8,40},{16,32},{24,56},{32,48},{40,72},{48,64},{56,88},{64,... | collective-permute-start | bytes 98312 | tf_op jit(solution)/shard_map/ppermute | solution.py:468
  16.8 2.5 %collective-permute-start.2 = (f32[16,512]{1,0:T(8,128)S(1)}, f32[16,512]{1,0:T(8,128)S(1)}, u32[]{:S(2)}, u32[]{:S(2)}) collective-permute-start(f32[16,512]{1,0:T(8,128)S(1)} %get-tuple-element.43), channel_id=1, source_target_pairs={{16,0},{40,8},{32,16},{56,24},{48,32},{72,40},{64,48},{88,56},{80,... | collective-permute-start | bytes 98312 | tf_op jit(solution)/shard_map/ppermute | solution.py:469
  19.4 0.0 collective-permute-done.3.below_ref
  19.4 0.0 collective-permute-done.4.above_ref
  19.4 2.2 %own.1 = (f32[64,64]{1,0:T(8,128)S(1)}, f32[64,64]{1,0:T(8,128)S(1)}) custom-call(f32[4,1024,128]{2,1,0:T(8,128)S(1)} %get-tuple-element.44.strips, f32[16,512]{1,0:T(8,128)S(1)} %bitcast.8, f32[16,512]{1,0:T(8,128)S(1)} %bitcast.9, f32[72,512]{1,0:T(8,128)S(1)} %get-tuple-element.45.top_ref, f32[72,512]{1,0:T(8,128)S(1)} %get-tuple-element.46.bottom_ref, ...), custom_call_target="tpu_custom_call" | custom-call | flops 100000000 | bytes 2000000 | tf_op jit(solution)/shard_map/own/pallas_call | solution.py:404
  21.6 0.0 collective-permute-done.1.first.refs_1_
  21.6 0.0 collective-permute-done.2.second.refs_2_
  21.6 0.5 collective-permute-start.5
  22.1 0.9 %collective-permute-done.5.refs_3_ = f32[32,512]{1,0:T(8,128)S(1)} collective-permute-done((f32[32,512]{1,0:T(8,128)S(1)}, f32[32,512]{1,0:T(8,128)S(1)}, u32[]{:S(2)}, u32[]{:S(2)}) %collective-permute-start.5) | collective-permute-done | bytes 65568 | tf_op jit(solution)/shard_map/ppermute | solution.py:478
  23.0 1.4 %block.1 = (f32[8,64,128]{2,1,0:T(8,128)}, f32[8,512]{1,0:T(8,128)S(1)}, s32[8,512]{1,0:T(8,128)S(1)}) custom-call(f32[8,512]{1,0:T(8,128)S(1)} %get-tuple-element.40.live_ref, f32[64,64]{1,0:T(8,128)S(1)} %get-tuple-element.49.own_block, f32[64,64]{1,0:T(8,128)S(1)} %get-tuple-element.50.lower_block, bf16[8,128,512]{2,1,0:T(8,128)(2,1)S(1)} %get-tuple-element.51.own_ref, ...), custom_call_target="tpu_custom_call" | custom-call | flops 100000000 | bytes 2000000 | tf_op jit(solution)/shard_map/block/pallas_call | solution.py:404
  24.4 5.5 %all-to-all-start = ((f32[8,64,128]{2,1,0:T(8,128)}), f32[8,64,128]{2,1,0:T(8,128)S(1)}, u32[]{:S(2)}, u32[]{:S(2)}) async-start(f32[8,64,128]{2,1,0:T(8,128)} %get-tuple-element.55), calls=%async_computation | async-start | bytes 524288 | tf_op jit(solution)/shard_map/all_to_all | solution.py:486
  29.9 1.5 %collective-permute-start.8 = (f32[64,512]{1,0:T(8,128)S(1)}, f32[64,512]{1,0:T(8,128)S(1)}, u32[]{:S(2)}, u32[]{:S(2)}) collective-permute-start(f32[64,512]{1,0:T(8,128)S(1)} %get-tuple-element.56.ahead), channel_id=1, source_target_pairs={{0,32},{8,40},{16,48},{24,56},{32,64},{40,72},{48,80},{56,88},{64,... | collective-permute-start | bytes 393224 | tf_op jit(solution)/shard_map/ppermute | solution.py:425
  31.4 1.8 %collective-permute-start.6 = (f32[64,512]{1,0:T(8,128)S(1)}, f32[64,512]{1,0:T(8,128)S(1)}, u32[]{:S(2)}, u32[]{:S(2)}) collective-permute-start(f32[64,512]{1,0:T(8,128)S(1)} %get-tuple-element.56.ahead), channel_id=1, source_target_pairs={{0,16},{8,24},{16,32},{24,40},{32,48},{40,56},{48,64},{56,72},{64,... | collective-permute-start | bytes 393224 | tf_op jit(solution)/shard_map/ppermute | solution.py:425
  33.2 3.4 %collective-permute-start.9 = (f32[64,512]{1,0:T(8,128)S(1)}, f32[64,512]{1,0:T(8,128)S(1)}, u32[]{:S(2)}, u32[]{:S(2)}) collective-permute-start(f32[64,512]{1,0:T(8,128)S(1)} %get-tuple-element.57.behind), channel_id=1, source_target_pairs={{0,224},{8,232},{16,240},{24,248},{32,0},{40,8},{48,16},{56,24},{6... | collective-permute-start | bytes 393224 | tf_op jit(solution)/shard_map/ppermute | solution.py:425
  36.5 1.3 %collective-permute-start.7 = (f32[64,512]{1,0:T(8,128)S(1)}, f32[64,512]{1,0:T(8,128)S(1)}, u32[]{:S(2)}, u32[]{:S(2)}) collective-permute-start(f32[64,512]{1,0:T(8,128)S(1)} %get-tuple-element.57.behind), channel_id=1, source_target_pairs={{0,240},{8,248},{16,0},{24,8},{32,16},{40,24},{48,32},{56,40},{64,... | collective-permute-start | bytes 393224 | tf_op jit(solution)/shard_map/ppermute | solution.py:425
  37.9 3.2 %all-to-all-done.blocks_ref = f32[8,64,128]{2,1,0:T(8,128)S(1)} async-done(((f32[8,64,128]{2,1,0:T(8,128)}), f32[8,64,128]{2,1,0:T(8,128)S(1)}, u32[]{:S(2)}, u32[]{:S(2)}) %all-to-all-start) | async-done | bytes 262176 | tf_op jit(solution)/shard_map/all_to_all | solution.py:486
  41.1 7.4 %factor_first.1 = (f32[320,256]{1,0:T(8,128)S(1)}, f32[256,128]{1,0:T(8,128)S(1)}, f32[64,128]{1,0:T(8,128)S(1)}, f32[64,128]{1,0:T(8,128)S(1)}) custom-call(f32[8,64,128]{2,1,0:T(8,128)S(1)} %all-to-all-done.blocks_ref), custom_call_target="tpu_custom_call" | custom-call | flops 1000000000 | bytes 2000000 | tf_op jit(solution)/shard_map/factor_first/pallas_call | solution.py:404
  48.5 0.0 collective-permute-done.8.ahead4.refs_2_
  48.5 0.0 collective-permute-done.6.ahead2.refs_0_
  48.5 0.0 collective-permute-done.9.behind4.refs_3_
  48.5 0.0 collective-permute-done.7.behind2.refs_1_
  48.5 0.1 faces.1
  48.6 1.8 %collective-permute-start.10 = (f32[256,512]{1,0:T(8,128)S(1)}, f32[256,512]{1,0:T(8,128)S(1)}, u32[]{:S(2)}, u32[]{:S(2)}) collective-permute-start(f32[256,512]{1,0:T(8,128)S(1)} %faces.1), channel_id=1, source_target_pairs={{0,8},{8,0},{16,24},{24,16},{32,40},{40,32},{48,56},{56,48},{64,72... | collective-permute-start | bytes 1572872 | tf_op jit(solution)/shard_map/ppermute | solution.py:503
  50.4 8.4 %factor_second.1 = (f32[512,512]{1,0:T(8,128)}, f32[512,128]{1,0:T(8,128)S(1)}) custom-call(f32[8,64,128]{2,1,0:T(8,128)S(1)} %all-to-all-done.blocks_ref, f32[320,256]{1,0:T(8,128)S(1)} %get-tuple-element.62.part_ref, f32[256,128]{1,0:T(8,128)S(1)} %get-tuple-element.63.first_inverse, f32[64,128]{1,0:T(8,128)S(1)} %get-tuple-element.64.first_top, ...), custom_call_target="tpu_custom_call" | custom-call | flops 1000000000 | bytes 2000000 | tf_op jit(solution)/shard_map/factor_second/pallas_call | solution.py:404
  58.8 0.0 collective-permute-done.10.refs_4_
  58.8 3.4 %panel.1 = f32[512,512]{1,0:T(8,128)} custom-call(f32[8,512]{1,0:T(8,128)S(1)} %get-tuple-element.67.weight_ref, s32[8,512]{1,0:T(8,128)S(1)} %get-tuple-element.68.index_ref, bf16[8,128,512]{2,1,0:T(8,128)(2,1)S(1)} %get-tuple-element.51.own_ref, f32[64,512]{1,0:T(8,128)S(1)} %collective-permute-done.6.ahead2.refs_0_, ...), custom_call_target="tpu_custom_call" | custom-call | flops 100000000 | bytes 2000000 | tf_op jit(solution)/shard_map/panel/pallas_call | solution.py:404
  (5 shorter events, 0.0 us)
Async XLA Ops:
  0.6 18.7 %copy-start = (f32[1,16,512]{2,1,0:T(8,128)S(1)}, f32[1,16,512]{2,1,0:T(8,128)}, u32[]{:S(2)}) copy-start(f32[1,16,512]{2,1,0:T(8,128)} %param.6) | copy-start | bytes 98308
  0.6 18.7 %copy-start.1 = (f32[1,16,512]{2,1,0:T(8,128)S(1)}, f32[1,16,512]{2,1,0:T(8,128)}, u32[]{:S(2)}) copy-start(f32[1,16,512]{2,1,0:T(8,128)} %param.7) | copy-start | bytes 98308
  5.7 13.7 %collective-permute-start.3 = (f32[72,512]{1,0:T(8,128)S(1)}, f32[72,512]{1,0:T(8,128)S(1)}, u32[]{:S(2)}, u32[]{:S(2)}) collective-permute-start(f32[72,512]{1,0:T(8,128)S(1)} %get-tuple-element.45.top_ref), channel_id=1, source_target_pairs={{0,1},{1,2},{2,3},{3,4},{4,5},{5,6},{6,7},{7,0},{8,9},{9,10},{10,1... | collective-permute-start | bytes 442376 | tf_op jit(solution)/shard_map/ppermute | solution.py:425
  8.2 11.1 %collective-permute-start.4 = (f32[72,512]{1,0:T(8,128)S(1)}, f32[72,512]{1,0:T(8,128)S(1)}, u32[]{:S(2)}, u32[]{:S(2)}) collective-permute-start(f32[72,512]{1,0:T(8,128)S(1)} %get-tuple-element.46.bottom_ref), channel_id=1, source_target_pairs={{0,7},{1,0},{2,1},{3,2},{4,3},{5,4},{6,5},{7,6},{8,15},{9,8},{10,9... | collective-permute-start | bytes 442376 | tf_op jit(solution)/shard_map/ppermute | solution.py:425
  12.3 1.8 %collective-permute-start = (f32[16,512]{1,0:T(8,128)S(1)}, f32[16,512]{1,0:T(8,128)S(1)}, u32[]{:S(2)}, u32[]{:S(2)}) collective-permute-start(f32[16,512]{1,0:T(8,128)S(1)} %get-tuple-element.41.own.own_tails), channel_id=1, source_target_pairs={{0,8},{8,0},{16,24},{24,16},{32,40},{40,32},{48,56},{56,48},{64,72... | collective-permute-start | bytes 98312 | tf_op jit(solution)/shard_map/ppermute | solution.py:461
  14.1 7.5 %collective-permute-start.1 = (f32[16,512]{1,0:T(8,128)S(1)}, f32[16,512]{1,0:T(8,128)S(1)}, u32[]{:S(2)}, u32[]{:S(2)}) collective-permute-start(f32[16,512]{1,0:T(8,128)S(1)} %get-tuple-element.42), channel_id=1, source_target_pairs={{0,16},{8,40},{16,32},{24,56},{32,48},{40,72},{48,64},{56,88},{64,... | collective-permute-start | bytes 98312 | tf_op jit(solution)/shard_map/ppermute | solution.py:468
  16.8 4.7 %collective-permute-start.2 = (f32[16,512]{1,0:T(8,128)S(1)}, f32[16,512]{1,0:T(8,128)S(1)}, u32[]{:S(2)}, u32[]{:S(2)}) collective-permute-start(f32[16,512]{1,0:T(8,128)S(1)} %get-tuple-element.43), channel_id=1, source_target_pairs={{16,0},{40,8},{32,16},{56,24},{48,32},{72,40},{64,48},{88,56},{80,... | collective-permute-start | bytes 98312 | tf_op jit(solution)/shard_map/ppermute | solution.py:469
  21.6 1.4 %collective-permute-start.5 = (f32[32,512]{1,0:T(8,128)S(1)}, f32[32,512]{1,0:T(8,128)S(1)}, u32[]{:S(2)}, u32[]{:S(2)}) collective-permute-start(f32[32,512]{1,0:T(8,128)S(1)} %join.1), channel_id=1, source_target_pairs={{0,8},{8,0},{16,24},{24,16},{32,40},{40,32},{48,56},{56,48},{64,72... | collective-permute-start | bytes 196616 | tf_op jit(solution)/shard_map/ppermute | solution.py:478
  24.4 16.6 %all-to-all-start = ((f32[8,64,128]{2,1,0:T(8,128)}), f32[8,64,128]{2,1,0:T(8,128)S(1)}, u32[]{:S(2)}, u32[]{:S(2)}) async-start(f32[8,64,128]{2,1,0:T(8,128)} %get-tuple-element.55), calls=%async_computation | async-start | bytes 524288 | tf_op jit(solution)/shard_map/all_to_all | solution.py:486
  29.9 18.6 %collective-permute-start.8 = (f32[64,512]{1,0:T(8,128)S(1)}, f32[64,512]{1,0:T(8,128)S(1)}, u32[]{:S(2)}, u32[]{:S(2)}) collective-permute-start(f32[64,512]{1,0:T(8,128)S(1)} %get-tuple-element.56.ahead), channel_id=1, source_target_pairs={{0,32},{8,40},{16,48},{24,56},{32,64},{40,72},{48,80},{56,88},{64,... | collective-permute-start | bytes 393224 | tf_op jit(solution)/shard_map/ppermute | solution.py:425
  31.4 17.1 %collective-permute-start.6 = (f32[64,512]{1,0:T(8,128)S(1)}, f32[64,512]{1,0:T(8,128)S(1)}, u32[]{:S(2)}, u32[]{:S(2)}) collective-permute-start(f32[64,512]{1,0:T(8,128)S(1)} %get-tuple-element.56.ahead), channel_id=1, source_target_pairs={{0,16},{8,24},{16,32},{24,40},{32,48},{40,56},{48,64},{56,72},{64,... | collective-permute-start | bytes 393224 | tf_op jit(solution)/shard_map/ppermute | solution.py:425
  33.2 15.3 %collective-permute-start.9 = (f32[64,512]{1,0:T(8,128)S(1)}, f32[64,512]{1,0:T(8,128)S(1)}, u32[]{:S(2)}, u32[]{:S(2)}) collective-permute-start(f32[64,512]{1,0:T(8,128)S(1)} %get-tuple-element.57.behind), channel_id=1, source_target_pairs={{0,224},{8,232},{16,240},{24,248},{32,0},{40,8},{48,16},{56,24},{6... | collective-permute-start | bytes 393224 | tf_op jit(solution)/shard_map/ppermute | solution.py:425
  36.5 12.0 %collective-permute-start.7 = (f32[64,512]{1,0:T(8,128)S(1)}, f32[64,512]{1,0:T(8,128)S(1)}, u32[]{:S(2)}, u32[]{:S(2)}) collective-permute-start(f32[64,512]{1,0:T(8,128)S(1)} %get-tuple-element.57.behind), channel_id=1, source_target_pairs={{0,240},{8,248},{16,0},{24,8},{32,16},{40,24},{48,32},{56,40},{64,... | collective-permute-start | bytes 393224 | tf_op jit(solution)/shard_map/ppermute | solution.py:425
  48.6 10.2 %collective-permute-start.10 = (f32[256,512]{1,0:T(8,128)S(1)}, f32[256,512]{1,0:T(8,128)S(1)}, u32[]{:S(2)}, u32[]{:S(2)}) collective-permute-start(f32[256,512]{1,0:T(8,128)S(1)} %faces.1), channel_id=1, source_target_pairs={{0,8},{8,0},{16,24},{24,16},{32,40},{40,32},{48,56},{56,48},{64,72... | collective-permute-start | bytes 1572872 | tf_op jit(solution)/shard_map/ppermute | solution.py:503

commit v8 on v7

--- a/solution.py
+++ b/solution.py
@@ -44,6 +44,23 @@
     return half[:, :K] + half[:, K:]
 
 
+def gathered(table, index):
+    strips = []
+    for q in range(4):
+        wanted = jnp.broadcast_to(index[:, 128 * q : 128 * (q + 1)], (8, 128))
+        found = None
+        for strip in range(4):
+            part = jnp.take_along_axis(
+                table[:, 128 * strip : 128 * (strip + 1)],
+                wanted & 127,
+                axis=1,
+                mode="promise_in_bounds",
+            )
+            found = part if strip == 0 else jnp.where(wanted >> 7 == strip, part, found)
+        strips.append(found)
+    return jnp.concatenate(strips, axis=1)
+
+
 def one_hot(index):
     place = lax.broadcasted_iota(jnp.int32, (FACE, FACE), 0)
     return jnp.where(place == index, 1.0, 0.0).astype(bf16)
@@ -53,7 +70,7 @@
     return jnp.concatenate([strips[q, pl.ds(z, K, stride=CZ), :] for q in range(4)], axis=1)
 
 
-def pick_kernel(vectors_hbm, sigma_hbm, index_hbm, counts_hbm, strips, own_ref, ahead_ref, behind_ref, tails_ref, top_ref, bottom_ref, live_ref, sigma_ref, index_ref, counts_ref, choice_ref, hot_ref, sems):
+def face_kernel(vectors_hbm, sigma_hbm, index_hbm, counts_hbm, strips, ahead_ref, behind_ref, tails_ref, top_ref, bottom_ref, live_ref, wanted_ref, sigma_ref, index_ref, counts_ref, choice_ref, sems):
     small = [
         pltpu.make_async_copy(sigma_hbm, sigma_ref, sems.at[4]),
         pltpu.make_async_copy(index_hbm, index_ref, sems.at[5]),
@@ -102,10 +119,10 @@
         live_ref[slot : slot + 1] = jnp.where(along < counts_ref[slot], 1.0, 0.0)
         cell_index = index_ref[slot : slot + 1, :]
         wanted = (cell_index >> 9) * CY + ((cell_index >> 4) & (CY - 1))
-        hot_ref[slot] = one_hot(wanted)
-        found = product(sigma_faces[side].astype(bf16), hot_ref[slot], MATRIX)
+        wanted_ref[slot : slot + 1] = wanted
+        found = gathered(sigma_faces[side][:8] + sigma_faces[side][8:], wanted)
         row = slot - REACH if side else 8 + REACH - 1 - slot
-        tails_ref[row : row + 1] = found[:1] + found[8:9]
+        tails_ref[row : row + 1] = found[:1]
         tails_ref[4 + row : 5 + row] = wanted.astype(f32)
     for copy in large:
         copy.wait()
@@ -115,12 +132,27 @@
     faces = faces_of(lambda z: stacked(layer_of(strips, z)), 2 * K)
     for side, face_ref in ((0, behind_ref), (1, ahead_ref)):
         face_ref[...] = faces[side][:K] + faces[side][K:]
-        table = faces[side].astype(bf16)
+
+
+def row_kernel(ahead_ref, behind_ref, wanted_ref, top_ref, bottom_ref, below_ref, above_ref, own_ref, square_ref, lower_ref):
+    for side, face_ref in ((0, behind_ref), (1, ahead_ref)):
+        table = stacked(face_ref[...])
         for slot in range(REACH * side, REACH * (side + 1)):
-            own_ref[slot] = product(table, hot_ref[slot], MATRIX).astype(bf16)
-
-
-def own_kernel(strips, sigma_ref, storage_ref, top_ref, bottom_ref, below_ref, above_ref, own_ref, lower_ref):
+            select = one_hot(wanted_ref[slot : slot + 1, :])
+            own_ref[slot] = product(table, select, MATRIX).astype(bf16)
+    level = lax.axis_index("coarse")
+    downward = harmonic(bottom_ref[K : K + 1, :], below_ref[K : K + 1, :])
+    downward = jnp.where(level == 0, 0.0, downward)
+    upward = harmonic(top_ref[K : K + 1, :], above_ref[K : K + 1, :])
+    upward = jnp.where(level == lax.axis_size("coarse") - 1, 0.0, upward)
+    top, bottom = top_ref[:K, :], bottom_ref[:K, :]
+    weighted = stacked(bottom * downward)
+    square = product(stacked(top * upward), stacked(top), GRAM)
+    square_ref[...] = quadrants(square + product(weighted, stacked(bottom), GRAM))
+    lower_ref[...] = -quadrants(product(weighted, stacked(below_ref[:K, :]), GRAM))
+
+
+def own_kernel(strips, sigma_ref, storage_ref, own_ref):
     sigma = sigma_ref[...]
     lane = lax.broadcasted_iota(jnp.int32, (CZ, FACE), 1)
     layer = lax.broadcasted_iota(jnp.int32, (CZ, FACE), 0)
@@ -131,11 +163,6 @@
         lane >= FACE - CX, 0.0, harmonic(sigma, pltpu.roll(sigma, FACE - CX, 1))
     )
     along_z = jnp.where(layer == CZ - 1, 0.0, harmonic(sigma, pltpu.roll(sigma, CZ - 1, 0)))
-    level = lax.axis_index("coarse")
-    downward = harmonic(bottom_ref[K : K + 1, :], below_ref[K : K + 1, :])
-    downward = jnp.where(level == 0, 0.0, downward)
-    upward = harmonic(top_ref[K : K + 1, :], above_ref[K : K + 1, :])
-    upward = jnp.where(level == lax.axis_size("coarse") - 1, 0.0, upward)
     half = 0.5 * (
         storage_ref[...]
         + along_x
@@ -144,8 +171,6 @@
         + pltpu.roll(along_y, CX, 1)
         + along_z
         + pltpu.roll(along_z, 1, 0)
-        + jnp.where(layer == 0, downward, 0.0)
-        + jnp.where(layer == CZ - 1, upward, 0.0)
     )
     total = jnp.zeros((2 * K, 2 * K), f32)
     below = layer_of(strips, 0)
@@ -160,8 +185,6 @@
         total = total + product(stacked(now), stacked(applied), GRAM)
     own = quadrants(total)
     own_ref[...] = own + own.T
-    weighted = stacked(bottom_ref[:K, :] * downward)
-    lower_ref[...] = -quadrants(product(weighted, stacked(below_ref[:K, :]), GRAM))
 
 
 def pack_kernel(ahead, behind, ahead2, behind2, ahead4, behind4, out_ref):
@@ -213,7 +236,7 @@
     return stacked((rows[:K].astype(f32) + rows[K:].astype(f32)) * weight)
 
 
-def block_kernel(live_ref, own_block, lower_block, own_ref, own_tails, *refs):
+def block_kernel(live_ref, own_block, square_block, lower_block, own_ref, own_tails, *refs):
     *tails, out_ref, weight_ref, index_ref = refs
     total = jnp.zeros((2 * K, 2 * K), f32)
     found = tails_by_slot(*tails)
@@ -226,7 +249,7 @@
         index_ref[slot : slot + 1] = found[slot][4 + reach : 5 + reach].astype(jnp.int32)
         total = total + product(weighted_rows(own_ref, slot, weight), own_ref[slot], GRAM)
     level = lax.axis_index("coarse")
-    extra = quadrants(total)
+    extra = quadrants(total) + square_block[...]
     own = own_block[...] + 0.5 * (extra + extra.T)
     lower = lower_block[...]
     even = level % 2 == 0
@@ -429,18 +452,18 @@
     vectors = deflation[0].reshape(K * CZ, FACE)
     sigma = conductivity[0]
     counts = interface_counts.reshape(2 * REACH)
-    strips, mine, ahead, behind, own_tails, top, bottom, live = call(
-        pick_kernel,
-        "pick",
+    strips, ahead, behind, own_tails, top, bottom, live, wanted = call(
+        face_kernel,
+        "face",
         (
             array(4, K * CZ, 128),
-            array(8, 2 * K, FACE, dtype=bf16),
             array(K, FACE),
             array(K, FACE),
             array(16, FACE),
             array(ROWS, FACE),
             array(ROWS, FACE),
             array(8, FACE),
+            array(8, FACE, dtype=jnp.int32),
         ),
         tuple(
             pltpu.with_memory_space_constraint(x, pltpu.HBM)
@@ -452,35 +475,36 @@
             pltpu.VMEM((2 * REACH, FACE), jnp.int32),
             pltpu.SMEM((2 * REACH,), jnp.int32),
             pltpu.VMEM((4, FACE, 256), bf16),
-            pltpu.VMEM((2 * REACH, FACE, FACE), bf16),
             pltpu.SemaphoreType.DMA((7,)),
         ),
     )
     count = lax.axis_size("sub")
     swap = [(i, i ^ 1) for i in range(count)]
-    other_tails = lax.ppermute(own_tails, "sub", swap)
     below = passed_along(top, "coarse", 1)
     above = passed_along(bottom, "coarse", -1)
+    other_tails = lax.ppermute(own_tails, "sub", swap)
+    own = call(own_kernel, "own", array(K, K), (strips, sigma, storage[0]))
+    (other_tails, below, above), own = lax.optimization_barrier(((other_tails, below, above), own))
     go_ahead, go_behind = call(
         pair_kernel, "pair", (array(16, FACE), array(16, FACE)), (own_tails, other_tails), flops=10**6
     )
     far = [(i, (i + 2 + 2 * (i % 2)) % count) for i in range(count)]
     before = lax.ppermute(go_ahead, "sub", far)
     after = lax.ppermute(go_behind, "sub", [(j, i) for i, j in far])
-    own, lower = call(
-        own_kernel,
-        "own",
-        (array(K, K), array(K, K)),
-        (strips, sigma, storage[0], top, bottom, below, above),
-    )
-    (before, after), (own, lower) = lax.optimization_barrier(((before, after), (own, lower)))
+    mine, square, lower = call(
+        row_kernel,
+        "rows",
+        (array(8, 2 * K, FACE, dtype=bf16), array(K, K), array(K, K)),
+        (ahead, behind, wanted, top, bottom, below, above),
+    )
+    (before, after), mine = lax.optimization_barrier(((before, after), mine))
     both = call(join_kernel, "join", array(32, FACE), (before, after), flops=10**6)
     swapped_tails = lax.ppermute(both, "sub", swap)
     payload, weight, index = call(
         block_kernel,
         "block",
         (array(8, K, 2 * K), array(8, FACE), array(8, FACE, dtype=jnp.int32)),
-        (live, own, lower, mine, own_tails, other_tails, before, after, swapped_tails),
+        (live, own, square, lower, mine, own_tails, other_tails, before, after, swapped_tails),
     )
     (ahead, behind), payload = lax.optimization_barrier(((ahead, behind), payload))
     blocks = lax.all_to_all(payload, "coarse", 0, 0)

time: 62.3 us -> 62.3 us (level)
  Pallas kernels: 27.9 us -> 26.6 us
  starting transfers between devices: 28.5 us -> 29.6 us
    pallas_call x9 -> x10, Pallas kernels: 27.9 us -> 26.6 us  [call(): pl.pallas_call(kernel, out_shape=outs, in_specs=[HBM] * hbm + [VMEM] * (l...]
    ppermute x1, starting transfers between devices: 0.51 us -> 1.53 us  [body(): swapped_tails = lax.ppermute(both, 'sub', swap)]
    ppermute x1, waiting for transfers between devices: 0.86 us -> 0.01 us  [body(): other_tails = lax.ppermute(own_tails, 'sub', swap)]
  transfers between devices with their start and end apart: 12 -> 12, of which waited for: 3 -> 5; matrix products, arithmetic and copies ran while one was open for 0% -> 0% of each run, Pallas kernels for 29% -> 31%
where the time goes in v8:
time: 62.3 us; the launch traced here: 62.1 us
  starting transfers between devices  29.6 us (48%)
  Pallas kernels  26.6 us (43%)
  waiting for transfers between devices  5.23 us (8%)
  between operations  0.74 us (1%)
    pallas_call x10, Pallas kernels, call(): pl.pallas_call(kernel, out_shape=outs, in_specs=[HBM] * hbm + [VMEM] * (l...  26.6 us
    ppermute x6, starting transfers between devices, passed_along(): lax.ppermute(block, axis, [(i, (i + distance) % count) for i in range(cou...  14.5 us
    all_to_all x1, starting transfers between devices, body(): blocks = lax.all_to_all(payload, 'coarse', 0, 0)  5.47 us
    all_to_all x1, waiting for transfers between devices, body(): blocks = lax.all_to_all(payload, 'coarse', 0, 0)  3.21 us
    ppermute x1, starting transfers between devices, body(): before = lax.ppermute(go_ahead, 'sub', far)  2.82 us
    ppermute x1, starting transfers between devices, body(): after = lax.ppermute(go_behind, 'sub', [(j, i) for i, j in far])  2.54 us
    ppermute x1, starting transfers between devices, body(): faces = (*faces, lax.ppermute(packed, 'sub', swap))  1.76 us
    ppermute x1, starting transfers between devices, body(): swapped_tails = lax.ppermute(both, 'sub', swap)  1.53 us
  transfers between devices with their start and end apart: 12, of which 5 were waited for; matrix products, arithmetic and copies ran while one was open for 0% of the time, Pallas kernels for 31%

profile of v8, /device:TPU:1, one launch (start us, length us, event | category | flops | bytes accessed | tf_op | source)
XLA Modules:
  0.0 62.1 jit_solution(6525464060032000425)
XLA Ops:
  0.7 2.8 %face.1 = (f32[4,1024,128]{2,1,0:T(8,128)S(1)}, f32[64,512]{1,0:T(8,128)S(1)}, f32[64,512]{1,0:T(8,128)S(1)}, f32[16,512]{1,0:T(8,128)S(1)}, f32[72,512]{1,0:T(8...) custom-call(f32[1024,512]{1,0:T(8,128)} %bitcast.10, f32[16,512]{1,0:T(8,128)} %bitcast.7, ...), custom_call_target="tpu_custom_call" | custom-call | flops 100000000 | bytes 2000000 | tf_op jit(solution)/shard_map/face/pallas_call | solution.py:427
  3.4 2.5 %collective-permute-start.1 = (f32[72,512]{1,0:T(8,128)S(1)}, f32[72,512]{1,0:T(8,128)S(1)}, u32[]{:S(2)}, u32[]{:S(2)}) collective-permute-start(f32[72,512]{1,0:T(8,128)S(1)} %get-tuple-element.46.top_ref), channel_id=1, source_target_pairs={{0,1},{1,2},{2,3},{3,4},{4,5},{5,6},{6,7},{7,0},{8,9},{9,10},{10,1... | collective-permute-start | bytes 442376 | tf_op jit(solution)/shard_map/ppermute | solution.py:448
  6.0 4.0 %collective-permute-start.2 = (f32[72,512]{1,0:T(8,128)S(1)}, f32[72,512]{1,0:T(8,128)S(1)}, u32[]{:S(2)}, u32[]{:S(2)}) collective-permute-start(f32[72,512]{1,0:T(8,128)S(1)} %get-tuple-element.47.bottom_ref), channel_id=1, source_target_pairs={{0,7},{1,0},{2,1},{3,2},{4,3},{5,4},{6,5},{7,6},{8,15},{9,8},{10,9... | collective-permute-start | bytes 442376 | tf_op jit(solution)/shard_map/ppermute | solution.py:448
  10.0 1.0 %collective-permute-start = (f32[16,512]{1,0:T(8,128)S(1)}, f32[16,512]{1,0:T(8,128)S(1)}, u32[]{:S(2)}, u32[]{:S(2)}) collective-permute-start(f32[16,512]{1,0:T(8,128)S(1)} %get-tuple-element.45.own.own_tails), channel_id=1, source_target_pairs={{0,8},{8,0},{16,24},{24,16},{32,40},{40,32},{48,56},{56,48},{64,72... | collective-permute-start | bytes 98312 | tf_op jit(solution)/shard_map/ppermute | solution.py:485
  11.0 2.2 %own.1.own_block = f32[64,64]{1,0:T(8,128)S(1)} custom-call(f32[4,1024,128]{2,1,0:T(8,128)S(1)} %get-tuple-element.48.strips, f32[16,512]{1,0:T(8,128)S(1)} %bitcast.8, f32[16,512]{1,0:T(8,128)S(1)} %bitcast.9), custom_call_target="tpu_custom_call" | custom-call | flops 100000000 | bytes 2000000 | tf_op jit(solution)/shard_map/own/pallas_call | solution.py:427
  13.2 0.0 collective-permute-done.other.refs_0_
  13.2 0.3 collective-permute-done.1.below_ref
  13.5 0.0 collective-permute-done.2.above_ref
  13.5 2.8 %collective-permute-start.3 = (f32[16,512]{1,0:T(8,128)S(1)}, f32[16,512]{1,0:T(8,128)S(1)}, u32[]{:S(2)}, u32[]{:S(2)}) collective-permute-start(f32[16,512]{1,0:T(8,128)S(1)} %get-tuple-element.56), channel_id=1, source_target_pairs={{0,16},{8,40},{16,32},{24,56},{32,48},{40,72},{48,64},{56,88},{64,... | collective-permute-start | bytes 98312 | tf_op jit(solution)/shard_map/ppermute | solution.py:492
  16.3 2.5 %collective-permute-start.4 = (f32[16,512]{1,0:T(8,128)S(1)}, f32[16,512]{1,0:T(8,128)S(1)}, u32[]{:S(2)}, u32[]{:S(2)}) collective-permute-start(f32[16,512]{1,0:T(8,128)S(1)} %get-tuple-element.57), channel_id=1, source_target_pairs={{16,0},{40,8},{32,16},{56,24},{48,32},{72,40},{64,48},{88,56},{80,... | collective-permute-start | bytes 98312 | tf_op jit(solution)/shard_map/ppermute | solution.py:493
  18.9 0.9 %rows.1 = (bf16[8,128,512]{2,1,0:T(8,128)(2,1)S(1)}, f32[64,64]{1,0:T(8,128)S(1)}, f32[64,64]{1,0:T(8,128)S(1)}) custom-call(f32[64,512]{1,0:T(8,128)S(1)} %get-tuple-element.64.ahead_ref.ahead, f32[64,512]{1,0:T(8,128)S(1)} %get-tuple-element.65.behind_ref.behind, s32[8,512]{1,0:T(8,128)S(1)} %get-tuple-element.50.wanted_ref, ...), custom_call_target="tpu_custom_call" | custom-call | flops 100000000 | bytes 2000000 | tf_op jit(solution)/shard_map/rows/pallas_call | solution.py:427
  19.8 0.3 collective-permute-done.3.first.refs_1_
  20.1 0.5 collective-permute-done.4.second.refs_2_
  20.6 1.5 %collective-permute-start.5 = (f32[32,512]{1,0:T(8,128)S(1)}, f32[32,512]{1,0:T(8,128)S(1)}, u32[]{:S(2)}, u32[]{:S(2)}) collective-permute-start(f32[32,512]{1,0:T(8,128)S(1)} %join.1), channel_id=1, source_target_pairs={{0,8},{8,0},{16,24},{24,16},{32,40},{40,32},{48,56},{56,48},{64,72... | collective-permute-start | bytes 196616 | tf_op jit(solution)/shard_map/ppermute | solution.py:502
  22.1 0.9 %collective-permute-done.5.refs_3_ = f32[32,512]{1,0:T(8,128)S(1)} collective-permute-done((f32[32,512]{1,0:T(8,128)S(1)}, f32[32,512]{1,0:T(8,128)S(1)}, u32[]{:S(2)}, u32[]{:S(2)}) %collective-permute-start.5) | collective-permute-done | bytes 65568 | tf_op jit(solution)/shard_map/ppermute | solution.py:502
  23.0 1.4 %block.1 = (f32[8,64,128]{2,1,0:T(8,128)}, f32[8,512]{1,0:T(8,128)S(1)}, s32[8,512]{1,0:T(8,128)S(1)}) custom-call(f32[8,512]{1,0:T(8,128)S(1)} %get-tuple-element.44.live_ref, f32[64,64]{1,0:T(8,128)S(1)} %own.1.own_block, f32[64,64]{1,0:T(8,128)S(1)} %get-tuple-element.53.square_block, f32[64,64]{1,0:T(8,128)S(1)} %get-tuple-element.54.lower_block, ...), custom_call_target="tpu_custom_call" | custom-call | flops 100000000 | bytes 2000000 | tf_op jit(solution)/shard_map/block/pallas_call | solution.py:427
  24.5 5.5 %all-to-all-start = ((f32[8,64,128]{2,1,0:T(8,128)}), f32[8,64,128]{2,1,0:T(8,128)S(1)}, u32[]{:S(2)}, u32[]{:S(2)}) async-start(f32[8,64,128]{2,1,0:T(8,128)} %get-tuple-element.63), calls=%async_computation | async-start | bytes 524288 | tf_op jit(solution)/shard_map/all_to_all | solution.py:510
  29.9 0.7 %collective-permute-start.8 = (f32[64,512]{1,0:T(8,128)S(1)}, f32[64,512]{1,0:T(8,128)S(1)}, u32[]{:S(2)}, u32[]{:S(2)}) collective-permute-start(f32[64,512]{1,0:T(8,128)S(1)} %get-tuple-element.64.ahead_ref.ahead), channel_id=1, source_target_pairs={{0,32},{8,40},{16,48},{24,56},{32,64},{40,72},{48,80},{56,88},{64,... | collective-permute-start | bytes 393224 | tf_op jit(solution)/shard_map/ppermute | solution.py:448
  30.6 2.6 %collective-permute-start.6 = (f32[64,512]{1,0:T(8,128)S(1)}, f32[64,512]{1,0:T(8,128)S(1)}, u32[]{:S(2)}, u32[]{:S(2)}) collective-permute-start(f32[64,512]{1,0:T(8,128)S(1)} %get-tuple-element.64.ahead_ref.ahead), channel_id=1, source_target_pairs={{0,16},{8,24},{16,32},{24,40},{32,48},{40,56},{48,64},{56,72},{64,... | collective-permute-start | bytes 393224 | tf_op jit(solution)/shard_map/ppermute | solution.py:448
  33.2 3.0 %collective-permute-start.9 = (f32[64,512]{1,0:T(8,128)S(1)}, f32[64,512]{1,0:T(8,128)S(1)}, u32[]{:S(2)}, u32[]{:S(2)}) collective-permute-start(f32[64,512]{1,0:T(8,128)S(1)} %get-tuple-element.65.behind_ref.behind), channel_id=1, source_target_pairs={{0,224},{8,232},{16,240},{24,248},{32,0},{40,8},{48,16},{56,24},{6... | collective-permute-start | bytes 393224 | tf_op jit(solution)/shard_map/ppermute | solution.py:448
  36.2 1.7 %collective-permute-start.7 = (f32[64,512]{1,0:T(8,128)S(1)}, f32[64,512]{1,0:T(8,128)S(1)}, u32[]{:S(2)}, u32[]{:S(2)}) collective-permute-start(f32[64,512]{1,0:T(8,128)S(1)} %get-tuple-element.65.behind_ref.behind), channel_id=1, source_target_pairs={{0,240},{8,248},{16,0},{24,8},{32,16},{40,24},{48,32},{56,40},{64,... | collective-permute-start | bytes 393224 | tf_op jit(solution)/shard_map/ppermute | solution.py:448
  37.9 3.2 %all-to-all-done.blocks_ref = f32[8,64,128]{2,1,0:T(8,128)S(1)} async-done(((f32[8,64,128]{2,1,0:T(8,128)}), f32[8,64,128]{2,1,0:T(8,128)S(1)}, u32[]{:S(2)}, u32[]{:S(2)}) %all-to-all-start) | async-done | bytes 262176 | tf_op jit(solution)/shard_map/all_to_all | solution.py:510
  41.1 7.4 %factor_first.1 = (f32[320,256]{1,0:T(8,128)S(1)}, f32[256,128]{1,0:T(8,128)S(1)}, f32[64,128]{1,0:T(8,128)S(1)}, f32[64,128]{1,0:T(8,128)S(1)}) custom-call(f32[8,64,128]{2,1,0:T(8,128)S(1)} %all-to-all-done.blocks_ref), custom_call_target="tpu_custom_call" | custom-call | flops 1000000000 | bytes 2000000 | tf_op jit(solution)/shard_map/factor_first/pallas_call | solution.py:427
  48.5 0.0 collective-permute-done.8.ahead4.refs_2_
  48.5 0.0 collective-permute-done.6.ahead2.refs_0_
  48.5 0.0 collective-permute-done.9.behind4.refs_3_
  48.5 0.0 collective-permute-done.7.behind2.refs_1_
  48.6 0.1 faces.1
  48.6 1.8 %collective-permute-start.10 = (f32[256,512]{1,0:T(8,128)S(1)}, f32[256,512]{1,0:T(8,128)S(1)}, u32[]{:S(2)}, u32[]{:S(2)}) collective-permute-start(f32[256,512]{1,0:T(8,128)S(1)} %faces.1), channel_id=1, source_target_pairs={{0,8},{8,0},{16,24},{24,16},{32,40},{40,32},{48,56},{56,48},{64,72... | collective-permute-start | bytes 1572872 | tf_op jit(solution)/shard_map/ppermute | solution.py:527
  50.4 8.4 %factor_second.1 = (f32[512,512]{1,0:T(8,128)}, f32[512,128]{1,0:T(8,128)S(1)}) custom-call(f32[8,64,128]{2,1,0:T(8,128)S(1)} %all-to-all-done.blocks_ref, f32[320,256]{1,0:T(8,128)S(1)} %get-tuple-element.70.part_ref, f32[256,128]{1,0:T(8,128)S(1)} %get-tuple-element.71.first_inverse, f32[64,128]{1,0:T(8,128)S(1)} %get-tuple-element.72.first_top, ...), custom_call_target="tpu_custom_call" | custom-call | flops 1000000000 | bytes 2000000 | tf_op jit(solution)/shard_map/factor_second/pallas_call | solution.py:427
  58.8 0.0 collective-permute-done.10.refs_4_
  58.8 3.4 %panel.1 = f32[512,512]{1,0:T(8,128)} custom-call(f32[8,512]{1,0:T(8,128)S(1)} %get-tuple-element.75.weight_ref, s32[8,512]{1,0:T(8,128)S(1)} %get-tuple-element.76.index_ref, bf16[8,128,512]{2,1,0:T(8,128)(2,1)S(1)} %get-tuple-element.59.own_ref, f32[64,512]{1,0:T(8,128)S(1)} %collective-permute-done.6.ahead2.refs_0_, ...), custom_call_target="tpu_custom_call" | custom-call | flops 100000000 | bytes 2000000 | tf_op jit(solution)/shard_map/panel/pallas_call | solution.py:427
  (6 shorter events, 0.0 us)
Async XLA Ops:
  0.6 10.3 %copy-start = (f32[1,16,512]{2,1,0:T(8,128)S(1)}, f32[1,16,512]{2,1,0:T(8,128)}, u32[]{:S(2)}) copy-start(f32[1,16,512]{2,1,0:T(8,128)} %param.6) | copy-start | bytes 98308
  0.6 10.3 %copy-start.1 = (f32[1,16,512]{2,1,0:T(8,128)S(1)}, f32[1,16,512]{2,1,0:T(8,128)}, u32[]{:S(2)}) copy-start(f32[1,16,512]{2,1,0:T(8,128)} %param.7) | copy-start | bytes 98308
  3.4 10.1 %collective-permute-start.1 = (f32[72,512]{1,0:T(8,128)S(1)}, f32[72,512]{1,0:T(8,128)S(1)}, u32[]{:S(2)}, u32[]{:S(2)}) collective-permute-start(f32[72,512]{1,0:T(8,128)S(1)} %get-tuple-element.46.top_ref), channel_id=1, source_target_pairs={{0,1},{1,2},{2,3},{3,4},{4,5},{5,6},{6,7},{7,0},{8,9},{9,10},{10,1... | collective-permute-start | bytes 442376 | tf_op jit(solution)/shard_map/ppermute | solution.py:448
  6.0 7.5 %collective-permute-start.2 = (f32[72,512]{1,0:T(8,128)S(1)}, f32[72,512]{1,0:T(8,128)S(1)}, u32[]{:S(2)}, u32[]{:S(2)}) collective-permute-start(f32[72,512]{1,0:T(8,128)S(1)} %get-tuple-element.47.bottom_ref), channel_id=1, source_target_pairs={{0,7},{1,0},{2,1},{3,2},{4,3},{5,4},{6,5},{7,6},{8,15},{9,8},{10,9... | collective-permute-start | bytes 442376 | tf_op jit(solution)/shard_map/ppermute | solution.py:448
  10.0 3.2 %collective-permute-start = (f32[16,512]{1,0:T(8,128)S(1)}, f32[16,512]{1,0:T(8,128)S(1)}, u32[]{:S(2)}, u32[]{:S(2)}) collective-permute-start(f32[16,512]{1,0:T(8,128)S(1)} %get-tuple-element.45.own.own_tails), channel_id=1, source_target_pairs={{0,8},{8,0},{16,24},{24,16},{32,40},{40,32},{48,56},{56,48},{64,72... | collective-permute-start | bytes 98312 | tf_op jit(solution)/shard_map/ppermute | solution.py:485
  13.5 6.6 %collective-permute-start.3 = (f32[16,512]{1,0:T(8,128)S(1)}, f32[16,512]{1,0:T(8,128)S(1)}, u32[]{:S(2)}, u32[]{:S(2)}) collective-permute-start(f32[16,512]{1,0:T(8,128)S(1)} %get-tuple-element.56), channel_id=1, source_target_pairs={{0,16},{8,40},{16,32},{24,56},{32,48},{40,72},{48,64},{56,88},{64,... | collective-permute-start | bytes 98312 | tf_op jit(solution)/shard_map/ppermute | solution.py:492
  16.3 4.3 %collective-permute-start.4 = (f32[16,512]{1,0:T(8,128)S(1)}, f32[16,512]{1,0:T(8,128)S(1)}, u32[]{:S(2)}, u32[]{:S(2)}) collective-permute-start(f32[16,512]{1,0:T(8,128)S(1)} %get-tuple-element.57), channel_id=1, source_target_pairs={{16,0},{40,8},{32,16},{56,24},{48,32},{72,40},{64,48},{88,56},{80,... | collective-permute-start | bytes 98312 | tf_op jit(solution)/shard_map/ppermute | solution.py:493
  20.6 2.4 %collective-permute-start.5 = (f32[32,512]{1,0:T(8,128)S(1)}, f32[32,512]{1,0:T(8,128)S(1)}, u32[]{:S(2)}, u32[]{:S(2)}) collective-permute-start(f32[32,512]{1,0:T(8,128)S(1)} %join.1), channel_id=1, source_target_pairs={{0,8},{8,0},{16,24},{24,16},{32,40},{40,32},{48,56},{56,48},{64,72... | collective-permute-start | bytes 196616 | tf_op jit(solution)/shard_map/ppermute | solution.py:502
  24.5 16.6 %all-to-all-start = ((f32[8,64,128]{2,1,0:T(8,128)}), f32[8,64,128]{2,1,0:T(8,128)S(1)}, u32[]{:S(2)}, u32[]{:S(2)}) async-start(f32[8,64,128]{2,1,0:T(8,128)} %get-tuple-element.63), calls=%async_computation | async-start | bytes 524288 | tf_op jit(solution)/shard_map/all_to_all | solution.py:510
  29.9 18.6 %collective-permute-start.8 = (f32[64,512]{1,0:T(8,128)S(1)}, f32[64,512]{1,0:T(8,128)S(1)}, u32[]{:S(2)}, u32[]{:S(2)}) collective-permute-start(f32[64,512]{1,0:T(8,128)S(1)} %get-tuple-element.64.ahead_ref.ahead), channel_id=1, source_target_pairs={{0,32},{8,40},{16,48},{24,56},{32,64},{40,72},{48,80},{56,88},{64,... | collective-permute-start | bytes 393224 | tf_op jit(solution)/shard_map/ppermute | solution.py:448
  30.6 17.9 %collective-permute-start.6 = (f32[64,512]{1,0:T(8,128)S(1)}, f32[64,512]{1,0:T(8,128)S(1)}, u32[]{:S(2)}, u32[]{:S(2)}) collective-permute-start(f32[64,512]{1,0:T(8,128)S(1)} %get-tuple-element.64.ahead_ref.ahead), channel_id=1, source_target_pairs={{0,16},{8,24},{16,32},{24,40},{32,48},{40,56},{48,64},{56,72},{64,... | collective-permute-start | bytes 393224 | tf_op jit(solution)/shard_map/ppermute | solution.py:448
  33.2 15.4 %collective-permute-start.9 = (f32[64,512]{1,0:T(8,128)S(1)}, f32[64,512]{1,0:T(8,128)S(1)}, u32[]{:S(2)}, u32[]{:S(2)}) collective-permute-start(f32[64,512]{1,0:T(8,128)S(1)} %get-tuple-element.65.behind_ref.behind), channel_id=1, source_target_pairs={{0,224},{8,232},{16,240},{24,248},{32,0},{40,8},{48,16},{56,24},{6... | collective-permute-start | bytes 393224 | tf_op jit(solution)/shard_map/ppermute | solution.py:448
  36.2 12.4 %collective-permute-start.7 = (f32[64,512]{1,0:T(8,128)S(1)}, f32[64,512]{1,0:T(8,128)S(1)}, u32[]{:S(2)}, u32[]{:S(2)}) collective-permute-start(f32[64,512]{1,0:T(8,128)S(1)} %get-tuple-element.65.behind_ref.behind), channel_id=1, source_target_pairs={{0,240},{8,248},{16,0},{24,8},{32,16},{40,24},{48,32},{56,40},{64,... | collective-permute-start | bytes 393224 | tf_op jit(solution)/shard_map/ppermute | solution.py:448
  48.6 10.2 %collective-permute-start.10 = (f32[256,512]{1,0:T(8,128)S(1)}, f32[256,512]{1,0:T(8,128)S(1)}, u32[]{:S(2)}, u32[]{:S(2)}) collective-permute-start(f32[256,512]{1,0:T(8,128)S(1)} %faces.1), channel_id=1, source_target_pairs={{0,8},{8,0},{16,24},{24,16},{32,40},{40,32},{48,56},{56,48},{64,72... | collective-permute-start | bytes 1572872 | tf_op jit(solution)/shard_map/ppermute | solution.py:527

commit v9 on v8

--- a/solution.py
+++ b/solution.py
@@ -134,12 +134,14 @@
         face_ref[...] = faces[side][:K] + faces[side][K:]
 
 
-def row_kernel(ahead_ref, behind_ref, wanted_ref, top_ref, bottom_ref, below_ref, above_ref, own_ref, square_ref, lower_ref):
+def row_kernel(ahead_ref, behind_ref, wanted_ref, top_ref, bottom_ref, below_ref, above_ref, own_ref, exact_ref, square_ref, lower_ref):
     for side, face_ref in ((0, behind_ref), (1, ahead_ref)):
         table = stacked(face_ref[...])
         for slot in range(REACH * side, REACH * (side + 1)):
             select = one_hot(wanted_ref[slot : slot + 1, :])
-            own_ref[slot] = product(table, select, MATRIX).astype(bf16)
+            found = product(table, select, MATRIX)
+            own_ref[slot] = found.astype(bf16)
+            exact_ref[slot] = found[:K] + found[K:]
     level = lax.axis_index("coarse")
     downward = harmonic(bottom_ref[K : K + 1, :], below_ref[K : K + 1, :])
     downward = jnp.where(level == 0, 0.0, downward)
@@ -231,13 +233,8 @@
     return {-2: ahead2, -4: ahead4, 2: behind2, 4: behind4}[offset][...]
 
 
-def weighted_rows(own_ref, slot, weight):
-    rows = own_ref[slot]
-    return stacked((rows[:K].astype(f32) + rows[K:].astype(f32)) * weight)
-
-
-def block_kernel(live_ref, own_block, square_block, lower_block, own_ref, own_tails, *refs):
-    *tails, out_ref, weight_ref, index_ref = refs
+def block_kernel(live_ref, own_block, square_block, lower_block, own_ref, exact_ref, own_tails, *refs):
+    *tails, out_ref, weighted_ref, index_ref = refs
     total = jnp.zeros((2 * K, 2 * K), f32)
     found = tails_by_slot(*tails)
     for slot, offset in enumerate(OFFSETS):
@@ -245,9 +242,10 @@
         row = reach if offset > 0 else 8 + reach
         pair = harmonic(own_tails[row : row + 1], found[slot][reach : reach + 1])
         weight = jnp.where(live_ref[slot : slot + 1] > 0.0, pair, 0.0)
-        weight_ref[slot : slot + 1] = weight
         index_ref[slot : slot + 1] = found[slot][4 + reach : 5 + reach].astype(jnp.int32)
-        total = total + product(weighted_rows(own_ref, slot, weight), own_ref[slot], GRAM)
+        weighted = stacked(exact_ref[slot] * weight)
+        weighted_ref[slot] = weighted
+        total = total + product(weighted, own_ref[slot], GRAM)
     level = lax.axis_index("coarse")
     extra = quadrants(total) + square_block[...]
     own = own_block[...] + 0.5 * (extra + extra.T)
@@ -260,18 +258,25 @@
         out_ref[copy] = payload
 
 
-def panel_kernel(weight_ref, index_ref, own_ref, *refs):
-    faces, inverse, out_ref = refs[:5], refs[5], refs[6]
+def panel_kernel(weighted_ref, index_ref, *refs):
+    faces, (inverse, out_hbm, rows_ref, sems) = refs[:5], refs[5:]
     blocks = []
     for slot, offset in enumerate(OFFSETS):
         select = one_hot(index_ref[slot : slot + 1, :])
         found = product(stacked(partner_face(faces, offset)), select, MATRIX).astype(bf16)
-        weighted = weighted_rows(own_ref, slot, -weight_ref[slot : slot + 1])
-        blocks.append(quadrants(product(weighted, found, GRAM)))
+        blocks.append(-quadrants(product(weighted_ref[slot], found, GRAM)))
     high, low = halves(jnp.concatenate(blocks, axis=1))
-    left_high, left_low = halves(inverse[:, :K])
-    left = jnp.concatenate([left_high, left_low, left_high], axis=1)
-    out_ref[...] = product(left, jnp.concatenate([high, high, low], axis=0), MATRIX)
+    down = jnp.concatenate([high, high, low], axis=0)
+    copies = []
+    for part in range(4):
+        at = slice(128 * part, 128 * (part + 1))
+        left_high, left_low = halves(inverse[at, :K])
+        left = jnp.concatenate([left_high, left_low, left_high], axis=1)
+        rows_ref[part] = product(left, down, MATRIX)
+        copies.append(pltpu.make_async_copy(rows_ref.at[part], out_hbm.at[at], sems.at[part]))
+        copies[-1].start()
+    for copy in copies:
+        copy.wait()
 
 
 def thirds(x):
@@ -396,13 +401,14 @@
         inverse[pl.ds(start, K), :] = even_right
         inverse[pl.ds(start + K, K), :] = odd_right
         both = jnp.concatenate([even_turned, odd_turned], axis=1)
-        cols = pl.ds(start, 128)
-        factor_ref[pl.ds(start, K), cols] = jnp.where(wide_lane < K, both[:K], 0.0)
-        factor_ref[pl.ds(start + K, K), cols] = both[K:]
+        within = pl.multiple_of(start - 4 * K * begin, 128)
+        cols = pl.ds(within, 128)
+        factor_ref[pl.ds(within, K), cols] = jnp.where(wide_lane < K, both[:K], 0.0)
+        factor_ref[pl.ds(within + K, K), cols] = both[K:]
 
         @pl.when(q < 3)
         def _():
-            factor_ref[pl.ds(start + 128, K), cols] = jnp.where(wide_lane < K, 0.0, both[:K])
+            factor_ref[pl.ds(within + 128, K), cols] = jnp.where(wide_lane < K, 0.0, both[:K])
 
 
 def first_half(blocks_ref, factor_ref, inverse, top, top_right, cross):
@@ -410,25 +416,35 @@
     half_factor(0, lax.axis_index("coarse"), blocks_ref, factor_ref, cross, top, top_right, inverse)
 
 
-def second_half(blocks_ref, part_ref, first_inverse, first_top, first_right, factor_ref, inverse, cross, top, top_right):
-    factor_ref[: 5 * K, : 4 * K] = part_ref[...]
-    factor_ref[5 * K :, : 4 * K] = jnp.zeros((3 * K, 4 * K), f32)
-    factor_ref[:, 4 * K :] = jnp.zeros((8 * K, 4 * K), f32)
+def second_half(blocks_ref, part_ref, first_inverse, first_top, first_right, factor_hbm, inverse, cross, top, top_right, corner, blank, sems):
+    blank[...] = jnp.zeros((4 * K, 4 * K), f32)
+    copies = [
+        pltpu.make_async_copy(part_ref, factor_hbm.at[: 5 * K, : 4 * K], sems.at[0]),
+        pltpu.make_async_copy(blank, factor_hbm.at[: 4 * K, 4 * K :], sems.at[1]),
+        pltpu.make_async_copy(blank.at[: 3 * K], factor_hbm.at[5 * K :, : 4 * K], sems.at[2]),
+    ]
+    for copy in copies:
+        copy.start()
+    corner[...] = jnp.zeros((4 * K, 4 * K), f32)
     inverse[: 4 * K, :] = first_inverse[...]
     top[...] = first_top[...]
     top_right[...] = first_right[...]
-    half_factor(1, lax.axis_index("coarse"), blocks_ref, factor_ref, cross, top, top_right, inverse)
+    half_factor(1, lax.axis_index("coarse"), blocks_ref, corner, cross, top, top_right, inverse)
+    copies.append(pltpu.make_async_copy(corner, factor_hbm.at[4 * K :, 4 * K :], sems.at[3]))
+    copies[-1].start()
+    for copy in copies:
+        copy.wait()
 
 
 HBM = pl.BlockSpec(memory_space=pltpu.HBM)
 
 
-def call(kernel, name, outs, operands, hbm=0, flops=10**8, scratch=(), limit=16):
+def call(kernel, name, outs, operands, hbm=0, out=None, flops=10**8, scratch=(), limit=16):
     return pl.pallas_call(
         kernel,
         out_shape=outs,
         in_specs=[HBM] * hbm + [VMEM] * (len(operands) - hbm),
-        out_specs=jax.tree.map(lambda _: VMEM, outs),
+        out_specs=jax.tree.map(lambda _: VMEM, outs) if out is None else out,
         scratch_shapes=scratch,
         compiler_params=pltpu.CompilerParams(vmem_limit_bytes=limit * 2**20),
         cost_estimate=pl.CostEstimate(flops=flops, bytes_accessed=2 * 10**6, transcendentals=1000),
@@ -484,27 +500,31 @@
     above = passed_along(bottom, "coarse", -1)
     other_tails = lax.ppermute(own_tails, "sub", swap)
     own = call(own_kernel, "own", array(K, K), (strips, sigma, storage[0]))
-    (other_tails, below, above), own = lax.optimization_barrier(((other_tails, below, above), own))
+    other_tails, own = lax.optimization_barrier((other_tails, own))
     go_ahead, go_behind = call(
         pair_kernel, "pair", (array(16, FACE), array(16, FACE)), (own_tails, other_tails), flops=10**6
     )
     far = [(i, (i + 2 + 2 * (i % 2)) % count) for i in range(count)]
     before = lax.ppermute(go_ahead, "sub", far)
     after = lax.ppermute(go_behind, "sub", [(j, i) for i, j in far])
-    mine, square, lower = call(
+    mine, exact, square, lower = call(
         row_kernel,
         "rows",
-        (array(8, 2 * K, FACE, dtype=bf16), array(K, K), array(K, K)),
+        (array(8, 2 * K, FACE, dtype=bf16), array(8, K, FACE), array(K, K), array(K, K)),
         (ahead, behind, wanted, top, bottom, below, above),
     )
     (before, after), mine = lax.optimization_barrier(((before, after), mine))
     both = call(join_kernel, "join", array(32, FACE), (before, after), flops=10**6)
     swapped_tails = lax.ppermute(both, "sub", swap)
-    payload, weight, index = call(
+    payload, weighted, index = call(
         block_kernel,
         "block",
-        (array(8, K, 2 * K), array(8, FACE), array(8, FACE, dtype=jnp.int32)),
-        (live, own, square, lower, mine, own_tails, other_tails, before, after, swapped_tails),
+        (
+            array(8, K, 2 * K),
+            array(8, 2 * K, FACE, dtype=bf16),
+            array(8, FACE, dtype=jnp.int32),
+        ),
+        (live, own, square, lower, mine, exact, own_tails, other_tails, before, after, swapped_tails),
     )
     (ahead, behind), payload = lax.optimization_barrier(((ahead, behind), payload))
     blocks = lax.all_to_all(payload, "coarse", 0, 0)
@@ -531,13 +551,23 @@
         (array(8 * K, 8 * K), array(8 * K, 2 * K)),
         (blocks, *state),
         flops=10**9,
-        scratch=(pltpu.VMEM((8, K, 2 * K), f32), pltpu.VMEM((K, 2 * K), f32), pltpu.VMEM((K, 2 * K), f32)),
+        out=(HBM, VMEM),
+        scratch=(
+            pltpu.VMEM((8, K, 2 * K), f32),
+            pltpu.VMEM((K, 2 * K), f32),
+            pltpu.VMEM((K, 2 * K), f32),
+            pltpu.VMEM((4 * K, 4 * K), f32),
+            pltpu.VMEM((4 * K, 4 * K), f32),
+            pltpu.SemaphoreType.DMA((4,)),
+        ),
     )
     panel = call(
         panel_kernel,
         "panel",
         array(8 * K, 8 * K),
-        (weight, index, mine, *faces, inverse),
+        (weighted, index, *faces, inverse),
+        out=HBM,
+        scratch=(pltpu.VMEM((4, 2 * K, 8 * K), f32), pltpu.SemaphoreType.DMA((4,))),
     )
     return (factor[None], panel[None, None])
 

time: 62.3 us -> 60.9 us (0.978)
  starting transfers between devices: 29.6 us -> 28.4 us
    ppermute x1, starting transfers between devices: 1.53 us -> 0.49 us  [body(): swapped_tails = lax.ppermute(both, 'sub', swap)]
  transfers between devices with their start and end apart: 12 -> 12, of which waited for: 5 -> 4; matrix products, arithmetic and copies ran while one was open for 0% -> 0% of each run, Pallas kernels for 31% -> 31%
where the time goes in v9:
time: 60.9 us; the launch traced here: 60.7 us
  starting transfers between devices  28.4 us (47%)
  Pallas kernels  26.2 us (43%)
  waiting for transfers between devices  5.18 us (9%)
  between operations  0.92 us (2%)
    pallas_call x10, Pallas kernels, call(): pl.pallas_call(kernel, out_shape=outs, in_specs=[HBM] * hbm + [VMEM] * (l...  26.2 us
    ppermute x6, starting transfers between devices, passed_along(): lax.ppermute(block, axis, [(i, (i + distance) % count) for i in range(cou...  14.4 us
    all_to_all x1, starting transfers between devices, body(): blocks = lax.all_to_all(payload, 'coarse', 0, 0)  5.48 us
    all_to_all x1, waiting for transfers between devices, body(): blocks = lax.all_to_all(payload, 'coarse', 0, 0)  3.37 us
    ppermute x1, starting transfers between devices, body(): before = lax.ppermute(go_ahead, 'sub', far)  2.82 us
    ppermute x1, starting transfers between devices, body(): after = lax.ppermute(go_behind, 'sub', [(j, i) for i, j in far])  2.54 us
    ppermute x1, starting transfers between devices, body(): faces = (*faces, lax.ppermute(packed, 'sub', swap))  1.75 us
  transfers between devices with their start and end apart: 12, of which 4 were waited for; matrix products, arithmetic and copies ran while one was open for 0% of the time, Pallas kernels for 31%

profile of v9, /device:TPU:1, one launch (start us, length us, event | category | flops | bytes accessed | tf_op | source)
XLA Modules:
  0.0 60.7 jit_solution(9696639689315912388)
XLA Ops:
  0.7 2.8 %face.1 = (f32[4,1024,128]{2,1,0:T(8,128)S(1)}, f32[64,512]{1,0:T(8,128)S(1)}, f32[64,512]{1,0:T(8,128)S(1)}, f32[16,512]{1,0:T(8,128)S(1)}, f32[72,512]{1,0:T(8...) custom-call(f32[1024,512]{1,0:T(8,128)} %bitcast.10, f32[16,512]{1,0:T(8,128)} %bitcast.7, ...), custom_call_target="tpu_custom_call" | custom-call | flops 100000000 | bytes 2000000 | tf_op jit(solution)/shard_map/face/pallas_call | solution.py:443
  3.4 2.5 %collective-permute-start.1 = (f32[72,512]{1,0:T(8,128)S(1)}, f32[72,512]{1,0:T(8,128)S(1)}, u32[]{:S(2)}, u32[]{:S(2)}) collective-permute-start(f32[72,512]{1,0:T(8,128)S(1)} %get-tuple-element.48.top_ref), channel_id=1, source_target_pairs={{0,1},{1,2},{2,3},{3,4},{4,5},{5,6},{6,7},{7,0},{8,9},{9,10},{10,1... | collective-permute-start | bytes 442376 | tf_op jit(solution)/shard_map/ppermute | solution.py:464
  6.0 4.0 %collective-permute-start.2 = (f32[72,512]{1,0:T(8,128)S(1)}, f32[72,512]{1,0:T(8,128)S(1)}, u32[]{:S(2)}, u32[]{:S(2)}) collective-permute-start(f32[72,512]{1,0:T(8,128)S(1)} %get-tuple-element.49.bottom_ref), channel_id=1, source_target_pairs={{0,7},{1,0},{2,1},{3,2},{4,3},{5,4},{6,5},{7,6},{8,15},{9,8},{10,9... | collective-permute-start | bytes 442376 | tf_op jit(solution)/shard_map/ppermute | solution.py:464
  10.0 1.0 %collective-permute-start = (f32[16,512]{1,0:T(8,128)S(1)}, f32[16,512]{1,0:T(8,128)S(1)}, u32[]{:S(2)}, u32[]{:S(2)}) collective-permute-start(f32[16,512]{1,0:T(8,128)S(1)} %get-tuple-element.44.own.own_tails), channel_id=1, source_target_pairs={{0,8},{8,0},{16,24},{24,16},{32,40},{40,32},{48,56},{56,48},{64,72... | collective-permute-start | bytes 98312 | tf_op jit(solution)/shard_map/ppermute | solution.py:501
  11.0 2.2 %own.1.own_block = f32[64,64]{1,0:T(8,128)S(1)} custom-call(f32[4,1024,128]{2,1,0:T(8,128)S(1)} %get-tuple-element.45.strips, f32[16,512]{1,0:T(8,128)S(1)} %bitcast.8, f32[16,512]{1,0:T(8,128)S(1)} %bitcast.9), custom_call_target="tpu_custom_call" | custom-call | flops 100000000 | bytes 2000000 | tf_op jit(solution)/shard_map/own/pallas_call | solution.py:443
  13.2 0.0 collective-permute-done.other.refs_0_
  13.2 2.8 %collective-permute-start.3 = (f32[16,512]{1,0:T(8,128)S(1)}, f32[16,512]{1,0:T(8,128)S(1)}, u32[]{:S(2)}, u32[]{:S(2)}) collective-permute-start(f32[16,512]{1,0:T(8,128)S(1)} %get-tuple-element.53), channel_id=1, source_target_pairs={{0,16},{8,40},{16,32},{24,56},{32,48},{40,72},{48,64},{56,88},{64,... | collective-permute-start | bytes 98312 | tf_op jit(solution)/shard_map/ppermute | solution.py:508
  16.0 2.5 %collective-permute-start.4 = (f32[16,512]{1,0:T(8,128)S(1)}, f32[16,512]{1,0:T(8,128)S(1)}, u32[]{:S(2)}, u32[]{:S(2)}) collective-permute-start(f32[16,512]{1,0:T(8,128)S(1)} %get-tuple-element.54), channel_id=1, source_target_pairs={{16,0},{40,8},{32,16},{56,24},{48,32},{72,40},{64,48},{88,56},{80,... | collective-permute-start | bytes 98312 | tf_op jit(solution)/shard_map/ppermute | solution.py:509
  18.6 0.0 collective-permute-done.1.below_ref
  18.6 0.0 collective-permute-done.2.above_ref
  18.6 1.0 %rows.1 = (bf16[8,128,512]{2,1,0:T(8,128)(2,1)S(1)}, f32[8,64,512]{2,1,0:T(8,128)S(1)}, f32[64,64]{1,0:T(8,128)S(1)}, f32[64,64]{1,0:T(8,128)S(1)}) custom-call(f32[64,512]{1,0:T(8,128)S(1)} %get-tuple-element.62.ahead_ref.ahead, f32[64,512]{1,0:T(8,128)S(1)} %get-tuple-element.63.behind_ref.behind, s32[8,512]{1,0:T(8,128)S(1)} %get-tuple-element.47.wanted_ref, ...), custom_call_target="tpu_custom_call" | custom-call | flops 100000000 | bytes 2000000 | tf_op jit(solution)/shard_map/rows/pallas_call | solution.py:443
  19.5 0.3 collective-permute-done.3.first.refs_1_
  19.8 0.6 %collective-permute-done.4.second.refs_2_ = f32[16,512]{1,0:T(8,128)S(1)} collective-permute-done((f32[16,512]{1,0:T(8,128)S(1)}, f32[16,512]{1,0:T(8,128)S(1)}, u32[]{:S(2)}, u32[]{:S(2)}) %collective-permute-start.4) | collective-permute-done | bytes 32800 | tf_op jit(solution)/shard_map/ppermute | solution.py:509
  20.4 0.5 collective-permute-start.5
  20.9 0.9 %collective-permute-done.5.refs_3_ = f32[32,512]{1,0:T(8,128)S(1)} collective-permute-done((f32[32,512]{1,0:T(8,128)S(1)}, f32[32,512]{1,0:T(8,128)S(1)}, u32[]{:S(2)}, u32[]{:S(2)}) %collective-permute-start.5) | collective-permute-done | bytes 65568 | tf_op jit(solution)/shard_map/ppermute | solution.py:518
  21.8 1.4 %block.1 = (f32[8,64,128]{2,1,0:T(8,128)}, bf16[8,128,512]{2,1,0:T(8,128)(2,1)S(1)}, s32[8,512]{1,0:T(8,128)S(1)}) custom-call(f32[8,512]{1,0:T(8,128)S(1)} %get-tuple-element.43.live_ref, f32[64,64]{1,0:T(8,128)S(1)} %own.1.own_block, f32[64,64]{1,0:T(8,128)S(1)} %get-tuple-element.50.square_block, f32[64,64]{1,0:T(8,128)S(1)} %get-tuple-element.51.lower_block, ...), custom_call_target="tpu_custom_call" | custom-call | flops 100000000 | bytes 2000000 | tf_op jit(solution)/shard_map/block/pallas_call | solution.py:443
  23.2 5.5 %all-to-all-start = ((f32[8,64,128]{2,1,0:T(8,128)}), f32[8,64,128]{2,1,0:T(8,128)S(1)}, u32[]{:S(2)}, u32[]{:S(2)}) async-start(f32[8,64,128]{2,1,0:T(8,128)} %get-tuple-element.61), calls=%async_computation | async-start | bytes 524288 | tf_op jit(solution)/shard_map/all_to_all | solution.py:530
  28.7 1.9 %collective-permute-start.8 = (f32[64,512]{1,0:T(8,128)S(1)}, f32[64,512]{1,0:T(8,128)S(1)}, u32[]{:S(2)}, u32[]{:S(2)}) collective-permute-start(f32[64,512]{1,0:T(8,128)S(1)} %get-tuple-element.62.ahead_ref.ahead), channel_id=1, source_target_pairs={{0,32},{8,40},{16,48},{24,56},{32,64},{40,72},{48,80},{56,88},{64,... | collective-permute-start | bytes 393224 | tf_op jit(solution)/shard_map/ppermute | solution.py:464
  30.6 1.2 %collective-permute-start.6 = (f32[64,512]{1,0:T(8,128)S(1)}, f32[64,512]{1,0:T(8,128)S(1)}, u32[]{:S(2)}, u32[]{:S(2)}) collective-permute-start(f32[64,512]{1,0:T(8,128)S(1)} %get-tuple-element.62.ahead_ref.ahead), channel_id=1, source_target_pairs={{0,16},{8,24},{16,32},{24,40},{32,48},{40,56},{48,64},{56,72},{64,... | collective-permute-start | bytes 393224 | tf_op jit(solution)/shard_map/ppermute | solution.py:464
  31.8 3.0 %collective-permute-start.9 = (f32[64,512]{1,0:T(8,128)S(1)}, f32[64,512]{1,0:T(8,128)S(1)}, u32[]{:S(2)}, u32[]{:S(2)}) collective-permute-start(f32[64,512]{1,0:T(8,128)S(1)} %get-tuple-element.63.behind_ref.behind), channel_id=1, source_target_pairs={{0,224},{8,232},{16,240},{24,248},{32,0},{40,8},{48,16},{56,24},{6... | collective-permute-start | bytes 393224 | tf_op jit(solution)/shard_map/ppermute | solution.py:464
  34.8 1.7 %collective-permute-start.7 = (f32[64,512]{1,0:T(8,128)S(1)}, f32[64,512]{1,0:T(8,128)S(1)}, u32[]{:S(2)}, u32[]{:S(2)}) collective-permute-start(f32[64,512]{1,0:T(8,128)S(1)} %get-tuple-element.63.behind_ref.behind), channel_id=1, source_target_pairs={{0,240},{8,248},{16,0},{24,8},{32,16},{40,24},{48,32},{56,40},{64,... | collective-permute-start | bytes 393224 | tf_op jit(solution)/shard_map/ppermute | solution.py:464
  36.5 3.4 %all-to-all-done.blocks_ref = f32[8,64,128]{2,1,0:T(8,128)S(1)} async-done(((f32[8,64,128]{2,1,0:T(8,128)}), f32[8,64,128]{2,1,0:T(8,128)S(1)}, u32[]{:S(2)}, u32[]{:S(2)}) %all-to-all-start) | async-done | bytes 262176 | tf_op jit(solution)/shard_map/all_to_all | solution.py:530
  39.8 7.4 %factor_first.1 = (f32[320,256]{1,0:T(8,128)S(1)}, f32[256,128]{1,0:T(8,128)S(1)}, f32[64,128]{1,0:T(8,128)S(1)}, f32[64,128]{1,0:T(8,128)S(1)}) custom-call(f32[8,64,128]{2,1,0:T(8,128)S(1)} %all-to-all-done.blocks_ref), custom_call_target="tpu_custom_call" | custom-call | flops 1000000000 | bytes 2000000 | tf_op jit(solution)/shard_map/factor_first/pallas_call | solution.py:443
  47.3 0.0 collective-permute-done.8.ahead4.refs_2_
  47.3 0.0 collective-permute-done.6.ahead2.refs_0_
  47.3 0.0 collective-permute-done.9.behind4.refs_3_
  47.3 0.0 collective-permute-done.7.behind2.refs_1_
  47.3 0.1 faces.1
  47.4 1.8 %collective-permute-start.10 = (f32[256,512]{1,0:T(8,128)S(1)}, f32[256,512]{1,0:T(8,128)S(1)}, u32[]{:S(2)}, u32[]{:S(2)}) collective-permute-start(f32[256,512]{1,0:T(8,128)S(1)} %faces.1), channel_id=1, source_target_pairs={{0,8},{8,0},{16,24},{24,16},{32,40},{40,32},{48,56},{56,48},{64,72... | collective-permute-start | bytes 1572872 | tf_op jit(solution)/shard_map/ppermute | solution.py:547
  49.1 8.1 %factor_second.1 = (f32[512,512]{1,0:T(8,128)}, f32[512,128]{1,0:T(8,128)S(1)}) custom-call(f32[8,64,128]{2,1,0:T(8,128)S(1)} %all-to-all-done.blocks_ref, f32[320,256]{1,0:T(8,128)S(1)} %get-tuple-element.68.part_ref, f32[256,128]{1,0:T(8,128)S(1)} %get-tuple-element.69.first_inverse, f32[64,128]{1,0:T(8,128)S(1)} %get-tuple-element.70.first_top, ...), custom_call_target="tpu_custom_call" | custom-call | flops 1000000000 | bytes 2000000 | tf_op jit(solution)/shard_map/factor_second/pallas_call | solution.py:443
  57.3 0.0 collective-permute-done.10.refs_4_
  57.3 3.3 %panel.1 = f32[512,512]{1,0:T(8,128)} custom-call(bf16[8,128,512]{2,1,0:T(8,128)(2,1)S(1)} %get-tuple-element.73.weighted_ref, s32[8,512]{1,0:T(8,128)S(1)} %get-tuple-element.74.index_ref, f32[64,512]{1,0:T(8,128)S(1)} %collective-permute-done.6.ahead2.refs_0_, f32[64,512]{1,0:T(8,128)S(1)} %collective-permute-done.7.behind2.refs_1_, ...), custom_call_target="tpu_custom_call" | custom-call | flops 100000000 | bytes 2000000 | tf_op jit(solution)/shard_map/panel/pallas_call | solution.py:443
  (6 shorter events, 0.0 us)
Async XLA Ops:
  0.6 10.3 %copy-start = (f32[1,16,512]{2,1,0:T(8,128)S(1)}, f32[1,16,512]{2,1,0:T(8,128)}, u32[]{:S(2)}) copy-start(f32[1,16,512]{2,1,0:T(8,128)} %param.6) | copy-start | bytes 98308
  0.6 10.3 %copy-start.1 = (f32[1,16,512]{2,1,0:T(8,128)S(1)}, f32[1,16,512]{2,1,0:T(8,128)}, u32[]{:S(2)}) copy-start(f32[1,16,512]{2,1,0:T(8,128)} %param.7) | copy-start | bytes 98308
  3.4 15.1 %collective-permute-start.1 = (f32[72,512]{1,0:T(8,128)S(1)}, f32[72,512]{1,0:T(8,128)S(1)}, u32[]{:S(2)}, u32[]{:S(2)}) collective-permute-start(f32[72,512]{1,0:T(8,128)S(1)} %get-tuple-element.48.top_ref), channel_id=1, source_target_pairs={{0,1},{1,2},{2,3},{3,4},{4,5},{5,6},{6,7},{7,0},{8,9},{9,10},{10,1... | collective-permute-start | bytes 442376 | tf_op jit(solution)/shard_map/ppermute | solution.py:464
  6.0 12.6 %collective-permute-start.2 = (f32[72,512]{1,0:T(8,128)S(1)}, f32[72,512]{1,0:T(8,128)S(1)}, u32[]{:S(2)}, u32[]{:S(2)}) collective-permute-start(f32[72,512]{1,0:T(8,128)S(1)} %get-tuple-element.49.bottom_ref), channel_id=1, source_target_pairs={{0,7},{1,0},{2,1},{3,2},{4,3},{5,4},{6,5},{7,6},{8,15},{9,8},{10,9... | collective-permute-start | bytes 442376 | tf_op jit(solution)/shard_map/ppermute | solution.py:464
  10.0 3.2 %collective-permute-start = (f32[16,512]{1,0:T(8,128)S(1)}, f32[16,512]{1,0:T(8,128)S(1)}, u32[]{:S(2)}, u32[]{:S(2)}) collective-permute-start(f32[16,512]{1,0:T(8,128)S(1)} %get-tuple-element.44.own.own_tails), channel_id=1, source_target_pairs={{0,8},{8,0},{16,24},{24,16},{32,40},{40,32},{48,56},{56,48},{64,72... | collective-permute-start | bytes 98312 | tf_op jit(solution)/shard_map/ppermute | solution.py:501
  13.2 6.6 %collective-permute-start.3 = (f32[16,512]{1,0:T(8,128)S(1)}, f32[16,512]{1,0:T(8,128)S(1)}, u32[]{:S(2)}, u32[]{:S(2)}) collective-permute-start(f32[16,512]{1,0:T(8,128)S(1)} %get-tuple-element.53), channel_id=1, source_target_pairs={{0,16},{8,40},{16,32},{24,56},{32,48},{40,72},{48,64},{56,88},{64,... | collective-permute-start | bytes 98312 | tf_op jit(solution)/shard_map/ppermute | solution.py:508
  16.0 4.4 %collective-permute-start.4 = (f32[16,512]{1,0:T(8,128)S(1)}, f32[16,512]{1,0:T(8,128)S(1)}, u32[]{:S(2)}, u32[]{:S(2)}) collective-permute-start(f32[16,512]{1,0:T(8,128)S(1)} %get-tuple-element.54), channel_id=1, source_target_pairs={{16,0},{40,8},{32,16},{56,24},{48,32},{72,40},{64,48},{88,56},{80,... | collective-permute-start | bytes 98312 | tf_op jit(solution)/shard_map/ppermute | solution.py:509
  20.4 1.4 %collective-permute-start.5 = (f32[32,512]{1,0:T(8,128)S(1)}, f32[32,512]{1,0:T(8,128)S(1)}, u32[]{:S(2)}, u32[]{:S(2)}) collective-permute-start(f32[32,512]{1,0:T(8,128)S(1)} %join.1), channel_id=1, source_target_pairs={{0,8},{8,0},{16,24},{24,16},{32,40},{40,32},{48,56},{56,48},{64,72... | collective-permute-start | bytes 196616 | tf_op jit(solution)/shard_map/ppermute | solution.py:518
  23.2 16.6 %all-to-all-start = ((f32[8,64,128]{2,1,0:T(8,128)}), f32[8,64,128]{2,1,0:T(8,128)S(1)}, u32[]{:S(2)}, u32[]{:S(2)}) async-start(f32[8,64,128]{2,1,0:T(8,128)} %get-tuple-element.61), calls=%async_computation | async-start | bytes 524288 | tf_op jit(solution)/shard_map/all_to_all | solution.py:530
  28.7 18.6 %collective-permute-start.8 = (f32[64,512]{1,0:T(8,128)S(1)}, f32[64,512]{1,0:T(8,128)S(1)}, u32[]{:S(2)}, u32[]{:S(2)}) collective-permute-start(f32[64,512]{1,0:T(8,128)S(1)} %get-tuple-element.62.ahead_ref.ahead), channel_id=1, source_target_pairs={{0,32},{8,40},{16,48},{24,56},{32,64},{40,72},{48,80},{56,88},{64,... | collective-permute-start | bytes 393224 | tf_op jit(solution)/shard_map/ppermute | solution.py:464
  30.6 16.7 %collective-permute-start.6 = (f32[64,512]{1,0:T(8,128)S(1)}, f32[64,512]{1,0:T(8,128)S(1)}, u32[]{:S(2)}, u32[]{:S(2)}) collective-permute-start(f32[64,512]{1,0:T(8,128)S(1)} %get-tuple-element.62.ahead_ref.ahead), channel_id=1, source_target_pairs={{0,16},{8,24},{16,32},{24,40},{32,48},{40,56},{48,64},{56,72},{64,... | collective-permute-start | bytes 393224 | tf_op jit(solution)/shard_map/ppermute | solution.py:464
  31.8 15.5 %collective-permute-start.9 = (f32[64,512]{1,0:T(8,128)S(1)}, f32[64,512]{1,0:T(8,128)S(1)}, u32[]{:S(2)}, u32[]{:S(2)}) collective-permute-start(f32[64,512]{1,0:T(8,128)S(1)} %get-tuple-element.63.behind_ref.behind), channel_id=1, source_target_pairs={{0,224},{8,232},{16,240},{24,248},{32,0},{40,8},{48,16},{56,24},{6... | collective-permute-start | bytes 393224 | tf_op jit(solution)/shard_map/ppermute | solution.py:464
  34.8 12.5 %collective-permute-start.7 = (f32[64,512]{1,0:T(8,128)S(1)}, f32[64,512]{1,0:T(8,128)S(1)}, u32[]{:S(2)}, u32[]{:S(2)}) collective-permute-start(f32[64,512]{1,0:T(8,128)S(1)} %get-tuple-element.63.behind_ref.behind), channel_id=1, source_target_pairs={{0,240},{8,248},{16,0},{24,8},{32,16},{40,24},{48,32},{56,40},{64,... | collective-permute-start | bytes 393224 | tf_op jit(solution)/shard_map/ppermute | solution.py:464
  47.4 9.9 %collective-permute-start.10 = (f32[256,512]{1,0:T(8,128)S(1)}, f32[256,512]{1,0:T(8,128)S(1)}, u32[]{:S(2)}, u32[]{:S(2)}) collective-permute-start(f32[256,512]{1,0:T(8,128)S(1)} %faces.1), channel_id=1, source_target_pairs={{0,8},{8,0},{16,24},{24,16},{32,40},{40,32},{48,56},{56,48},{64,72... | collective-permute-start | bytes 1572872 | tf_op jit(solution)/shard_map/ppermute | solution.py:547

commit v10 on v9

--- a/solution.py
+++ b/solution.py
@@ -70,7 +70,7 @@
     return jnp.concatenate([strips[q, pl.ds(z, K, stride=CZ), :] for q in range(4)], axis=1)
 
 
-def face_kernel(vectors_hbm, sigma_hbm, index_hbm, counts_hbm, strips, ahead_ref, behind_ref, tails_ref, top_ref, bottom_ref, live_ref, wanted_ref, sigma_ref, index_ref, counts_ref, choice_ref, sems):
+def face_kernel(vectors_hbm, sigma_hbm, index_hbm, counts_hbm, layers_ref, parts_ref, ahead_ref, behind_ref, tails_ref, top_ref, bottom_ref, live_ref, wanted_ref, sigma_ref, index_ref, counts_ref, choice_ref, strips, sems):
     small = [
         pltpu.make_async_copy(sigma_hbm, sigma_ref, sems.at[4]),
         pltpu.make_async_copy(index_hbm, index_ref, sems.at[5]),
@@ -126,10 +126,19 @@
         tails_ref[4 + row : 5 + row] = wanted.astype(f32)
     for copy in large:
         copy.wait()
-    for out_ref, z in ((bottom_ref, 0), (top_ref, CZ - 1)):
-        out_ref[:K] = layer_of(strips, z)
-        out_ref[K:] = jnp.broadcast_to(sigma_ref[z : z + 1, :], (8, FACE))
-    faces = faces_of(lambda z: stacked(layer_of(strips, z)), 2 * K)
+
+    def vector_rows(z):
+        layer = layer_of(strips, z)
+        layers_ref[z] = layer
+        parts = stacked(layer)
+        parts_ref[z] = parts
+        for out_ref, at in ((bottom_ref, 0), (top_ref, CZ - 1)):
+            if z == at:
+                out_ref[:K] = layer
+                out_ref[K:] = jnp.broadcast_to(sigma_ref[z : z + 1, :], (8, FACE))
+        return parts
+
+    faces = faces_of(vector_rows, 2 * K)
     for side, face_ref in ((0, behind_ref), (1, ahead_ref)):
         face_ref[...] = faces[side][:K] + faces[side][K:]
 
@@ -154,7 +163,7 @@
     lower_ref[...] = -quadrants(product(weighted, stacked(below_ref[:K, :]), GRAM))
 
 
-def own_kernel(strips, sigma_ref, storage_ref, own_ref):
+def own_kernel(layers_ref, parts_ref, sigma_ref, storage_ref, own_ref):
     sigma = sigma_ref[...]
     lane = lax.broadcasted_iota(jnp.int32, (CZ, FACE), 1)
     layer = lax.broadcasted_iota(jnp.int32, (CZ, FACE), 0)
@@ -175,16 +184,16 @@
         + pltpu.roll(along_z, 1, 0)
     )
     total = jnp.zeros((2 * K, 2 * K), f32)
-    below = layer_of(strips, 0)
+    below = layers_ref[0]
     for z in range(CZ):
         now = below
         applied = half[z : z + 1] * now
         applied = applied - along_x[z : z + 1] * pltpu.roll(now, FACE - 1, 1)
         applied = applied - along_y[z : z + 1] * pltpu.roll(now, FACE - CX, 1)
         if z < CZ - 1:
-            below = layer_of(strips, z + 1)
+            below = layers_ref[z + 1]
             applied = applied - along_z[z : z + 1] * below
-        total = total + product(stacked(now), stacked(applied), GRAM)
+        total = total + product(parts_ref[z], stacked(applied), GRAM)
     own = quadrants(total)
     own_ref[...] = own + own.T
 
@@ -243,9 +252,9 @@
         pair = harmonic(own_tails[row : row + 1], found[slot][reach : reach + 1])
         weight = jnp.where(live_ref[slot : slot + 1] > 0.0, pair, 0.0)
         index_ref[slot : slot + 1] = found[slot][4 + reach : 5 + reach].astype(jnp.int32)
-        weighted = stacked(exact_ref[slot] * weight)
-        weighted_ref[slot] = weighted
-        total = total + product(weighted, own_ref[slot], GRAM)
+        weighted_ref[slot] = stacked(exact_ref[slot] * weight)
+    for slot in range(2 * REACH):
+        total = total + product(weighted_ref[slot], own_ref[slot], GRAM)
     level = lax.axis_index("coarse")
     extra = quadrants(total) + square_block[...]
     own = own_block[...] + 0.5 * (extra + extra.T)
@@ -259,12 +268,13 @@
 
 
 def panel_kernel(weighted_ref, index_ref, *refs):
-    faces, (inverse, out_hbm, rows_ref, sems) = refs[:5], refs[5:]
-    blocks = []
+    faces, (inverse, out_hbm, found_ref, rows_ref, sems) = refs[:5], refs[5:]
     for slot, offset in enumerate(OFFSETS):
         select = one_hot(index_ref[slot : slot + 1, :])
-        found = product(stacked(partner_face(faces, offset)), select, MATRIX).astype(bf16)
-        blocks.append(-quadrants(product(weighted_ref[slot], found, GRAM)))
+        found_ref[slot] = product(stacked(partner_face(faces, offset)), select, MATRIX).astype(bf16)
+    blocks = [
+        -quadrants(product(weighted_ref[slot], found_ref[slot], GRAM)) for slot in range(2 * REACH)
+    ]
     high, low = halves(jnp.concatenate(blocks, axis=1))
     down = jnp.concatenate([high, high, low], axis=0)
     copies = []
@@ -468,11 +478,12 @@
     vectors = deflation[0].reshape(K * CZ, FACE)
     sigma = conductivity[0]
     counts = interface_counts.reshape(2 * REACH)
-    strips, ahead, behind, own_tails, top, bottom, live, wanted = call(
+    layers, parts, ahead, behind, own_tails, top, bottom, live, wanted = call(
         face_kernel,
         "face",
         (
-            array(4, K * CZ, 128),
+            array(CZ, K, FACE),
+            array(CZ, 2 * K, FACE, dtype=bf16),
             array(K, FACE),
             array(K, FACE),
             array(16, FACE),
@@ -491,6 +502,7 @@
             pltpu.VMEM((2 * REACH, FACE), jnp.int32),
             pltpu.SMEM((2 * REACH,), jnp.int32),
             pltpu.VMEM((4, FACE, 256), bf16),
+            pltpu.VMEM((4, K * CZ, 128), f32),
             pltpu.SemaphoreType.DMA((7,)),
         ),
     )
@@ -499,7 +511,7 @@
     below = passed_along(top, "coarse", 1)
     above = passed_along(bottom, "coarse", -1)
     other_tails = lax.ppermute(own_tails, "sub", swap)
-    own = call(own_kernel, "own", array(K, K), (strips, sigma, storage[0]))
+    own = call(own_kernel, "own", array(K, K), (layers, parts, sigma, storage[0]))
     other_tails, own = lax.optimization_barrier((other_tails, own))
     go_ahead, go_behind = call(
         pair_kernel, "pair", (array(16, FACE), array(16, FACE)), (own_tails, other_tails), flops=10**6
@@ -567,7 +579,11 @@
         array(8 * K, 8 * K),
         (weighted, index, *faces, inverse),
         out=HBM,
-        scratch=(pltpu.VMEM((4, 2 * K, 8 * K), f32), pltpu.SemaphoreType.DMA((4,))),
+        scratch=(
+            pltpu.VMEM((8, 2 * K, FACE), bf16),
+            pltpu.VMEM((4, 2 * K, 8 * K), f32),
+            pltpu.SemaphoreType.DMA((4,)),
+        ),
     )
     return (factor[None], panel[None, None])
 

time: 60.9 us -> 59.5 us (0.977)
  Pallas kernels: 26.2 us -> 24.8 us
    pallas_call x10, Pallas kernels: 26.2 us -> 24.8 us  [call(): pl.pallas_call(kernel, out_shape=outs, in_specs=[HBM] * hbm + [VMEM] * (l...]
where the time goes in v10:
time: 59.5 us; the launch traced here: 59.3 us
  starting transfers between devices  28.4 us (48%)
  Pallas kernels  24.8 us (42%)
  waiting for transfers between devices  5.18 us (9%)
  between operations  0.92 us (2%)
    pallas_call x10, Pallas kernels, call(): pl.pallas_call(kernel, out_shape=outs, in_specs=[HBM] * hbm + [VMEM] * (l...  24.8 us
    ppermute x6, starting transfers between devices, passed_along(): lax.ppermute(block, axis, [(i, (i + distance) % count) for i in range(cou...  14.4 us
    all_to_all x1, starting transfers between devices, body(): blocks = lax.all_to_all(payload, 'coarse', 0, 0)  5.48 us
    all_to_all x1, waiting for transfers between devices, body(): blocks = lax.all_to_all(payload, 'coarse', 0, 0)  3.37 us
    ppermute x1, starting transfers between devices, body(): before = lax.ppermute(go_ahead, 'sub', far)  2.82 us
    ppermute x1, starting transfers between devices, body(): after = lax.ppermute(go_behind, 'sub', [(j, i) for i, j in far])  2.54 us
    ppermute x1, starting transfers between devices, body(): faces = (*faces, lax.ppermute(packed, 'sub', swap))  1.76 us
  transfers between devices with their start and end apart: 12, of which 4 were waited for; matrix products, arithmetic and copies ran while one was open for 0% of the time, Pallas kernels for 31%

profile of v10, /device:TPU:1, one launch (start us, length us, event | category | flops | bytes accessed | tf_op | source)
XLA Modules:
  0.0 59.3 jit_solution(1509030795860530926)
XLA Ops:
  0.7 2.8 %face.1 = (f32[16,64,512]{2,1,0:T(8,128)S(1)}, bf16[16,128,512]{2,1,0:T(8,128)(2,1)S(1)}, f32[64,512]{1,0:T(8,128)S(1)}, f32[64,512]{1,0:T(8,128)S(1)}, f32[16,5...) custom-call(f32[1024,512]{1,0:T(8,128)} %bitcast.10, ...), custom_call_target="tpu_custom_call" | custom-call | flops 100000000 | bytes 2000000 | tf_op jit(solution)/shard_map/face/pallas_call | solution.py:453
  3.5 2.5 %collective-permute-start.1 = (f32[72,512]{1,0:T(8,128)S(1)}, f32[72,512]{1,0:T(8,128)S(1)}, u32[]{:S(2)}, u32[]{:S(2)}) collective-permute-start(f32[72,512]{1,0:T(8,128)S(1)} %get-tuple-element.50.top_ref), channel_id=1, source_target_pairs={{0,1},{1,2},{2,3},{3,4},{4,5},{5,6},{6,7},{7,0},{8,9},{9,10},{10,1... | collective-permute-start | bytes 442376 | tf_op jit(solution)/shard_map/ppermute | solution.py:474
  6.0 4.0 %collective-permute-start.2 = (f32[72,512]{1,0:T(8,128)S(1)}, f32[72,512]{1,0:T(8,128)S(1)}, u32[]{:S(2)}, u32[]{:S(2)}) collective-permute-start(f32[72,512]{1,0:T(8,128)S(1)} %get-tuple-element.51.bottom_ref), channel_id=1, source_target_pairs={{0,7},{1,0},{2,1},{3,2},{4,3},{5,4},{6,5},{7,6},{8,15},{9,8},{10,9... | collective-permute-start | bytes 442376 | tf_op jit(solution)/shard_map/ppermute | solution.py:474
  10.1 1.0 %collective-permute-start = (f32[16,512]{1,0:T(8,128)S(1)}, f32[16,512]{1,0:T(8,128)S(1)}, u32[]{:S(2)}, u32[]{:S(2)}) collective-permute-start(f32[16,512]{1,0:T(8,128)S(1)} %get-tuple-element.45.own.own_tails), channel_id=1, source_target_pairs={{0,8},{8,0},{16,24},{24,16},{32,40},{40,32},{48,56},{56,48},{64,72... | collective-permute-start | bytes 98312 | tf_op jit(solution)/shard_map/ppermute | solution.py:513
  11.0 1.7 %own.1.own_block = f32[64,64]{1,0:T(8,128)S(1)} custom-call(f32[16,64,512]{2,1,0:T(8,128)S(1)} %get-tuple-element.46.layers_ref, bf16[16,128,512]{2,1,0:T(8,128)(2,1)S(1)} %get-tuple-element.47.parts_ref, f32[16,512]{1,0:T(8,128)S(1)} %bitcast.8, f32[16,512]{1,0:T(8,128)S(1)} %bitcast.9), custom_call_target="tpu_custom_call" | custom-call | flops 100000000 | bytes 2000000 | tf_op jit(solution)/shard_map/own/pallas_call | solution.py:453
  12.7 0.0 collective-permute-done.other.refs_0_
  12.7 2.8 %collective-permute-start.3 = (f32[16,512]{1,0:T(8,128)S(1)}, f32[16,512]{1,0:T(8,128)S(1)}, u32[]{:S(2)}, u32[]{:S(2)}) collective-permute-start(f32[16,512]{1,0:T(8,128)S(1)} %get-tuple-element.55), channel_id=1, source_target_pairs={{0,16},{8,40},{16,32},{24,56},{32,48},{40,72},{48,64},{56,88},{64,... | collective-permute-start | bytes 98312 | tf_op jit(solution)/shard_map/ppermute | solution.py:520
  15.5 2.5 %collective-permute-start.4 = (f32[16,512]{1,0:T(8,128)S(1)}, f32[16,512]{1,0:T(8,128)S(1)}, u32[]{:S(2)}, u32[]{:S(2)}) collective-permute-start(f32[16,512]{1,0:T(8,128)S(1)} %get-tuple-element.56), channel_id=1, source_target_pairs={{16,0},{40,8},{32,16},{56,24},{48,32},{72,40},{64,48},{88,56},{80,... | collective-permute-start | bytes 98312 | tf_op jit(solution)/shard_map/ppermute | solution.py:521
  18.1 0.0 collective-permute-done.1.below_ref
  18.1 0.0 collective-permute-done.2.above_ref
  18.1 1.0 %rows.1 = (bf16[8,128,512]{2,1,0:T(8,128)(2,1)S(1)}, f32[8,64,512]{2,1,0:T(8,128)S(1)}, f32[64,64]{1,0:T(8,128)S(1)}, f32[64,64]{1,0:T(8,128)S(1)}) custom-call(f32[64,512]{1,0:T(8,128)S(1)} %get-tuple-element.64.ahead_ref.ahead, f32[64,512]{1,0:T(8,128)S(1)} %get-tuple-element.65.behind_ref.behind, s32[8,512]{1,0:T(8,128)S(1)} %get-tuple-element.49.wanted_ref, ...), custom_call_target="tpu_custom_call" | custom-call | flops 100000000 | bytes 2000000 | tf_op jit(solution)/shard_map/rows/pallas_call | solution.py:453
  19.1 0.3 collective-permute-done.3.first.refs_1_
  19.3 0.6 %collective-permute-done.4.second.refs_2_ = f32[16,512]{1,0:T(8,128)S(1)} collective-permute-done((f32[16,512]{1,0:T(8,128)S(1)}, f32[16,512]{1,0:T(8,128)S(1)}, u32[]{:S(2)}, u32[]{:S(2)}) %collective-permute-start.4) | collective-permute-done | bytes 32800 | tf_op jit(solution)/shard_map/ppermute | solution.py:521
  19.9 0.5 collective-permute-start.5
  20.4 0.9 %collective-permute-done.5.refs_3_ = f32[32,512]{1,0:T(8,128)S(1)} collective-permute-done((f32[32,512]{1,0:T(8,128)S(1)}, f32[32,512]{1,0:T(8,128)S(1)}, u32[]{:S(2)}, u32[]{:S(2)}) %collective-permute-start.5) | collective-permute-done | bytes 65568 | tf_op jit(solution)/shard_map/ppermute | solution.py:530
  21.3 1.4 %block.1 = (f32[8,64,128]{2,1,0:T(8,128)}, bf16[8,128,512]{2,1,0:T(8,128)(2,1)S(1)}, s32[8,512]{1,0:T(8,128)S(1)}) custom-call(f32[8,512]{1,0:T(8,128)S(1)} %get-tuple-element.44.live_ref, f32[64,64]{1,0:T(8,128)S(1)} %own.1.own_block, f32[64,64]{1,0:T(8,128)S(1)} %get-tuple-element.52.square_block, f32[64,64]{1,0:T(8,128)S(1)} %get-tuple-element.53.lower_block, ...), custom_call_target="tpu_custom_call" | custom-call | flops 100000000 | bytes 2000000 | tf_op jit(solution)/shard_map/block/pallas_call | solution.py:453
  22.7 5.5 %all-to-all-start = ((f32[8,64,128]{2,1,0:T(8,128)}), f32[8,64,128]{2,1,0:T(8,128)S(1)}, u32[]{:S(2)}, u32[]{:S(2)}) async-start(f32[8,64,128]{2,1,0:T(8,128)} %get-tuple-element.63), calls=%async_computation | async-start | bytes 524288 | tf_op jit(solution)/shard_map/all_to_all | solution.py:542
  28.2 1.9 %collective-permute-start.8 = (f32[64,512]{1,0:T(8,128)S(1)}, f32[64,512]{1,0:T(8,128)S(1)}, u32[]{:S(2)}, u32[]{:S(2)}) collective-permute-start(f32[64,512]{1,0:T(8,128)S(1)} %get-tuple-element.64.ahead_ref.ahead), channel_id=1, source_target_pairs={{0,32},{8,40},{16,48},{24,56},{32,64},{40,72},{48,80},{56,88},{64,... | collective-permute-start | bytes 393224 | tf_op jit(solution)/shard_map/ppermute | solution.py:474
  30.1 1.2 %collective-permute-start.6 = (f32[64,512]{1,0:T(8,128)S(1)}, f32[64,512]{1,0:T(8,128)S(1)}, u32[]{:S(2)}, u32[]{:S(2)}) collective-permute-start(f32[64,512]{1,0:T(8,128)S(1)} %get-tuple-element.64.ahead_ref.ahead), channel_id=1, source_target_pairs={{0,16},{8,24},{16,32},{24,40},{32,48},{40,56},{48,64},{56,72},{64,... | collective-permute-start | bytes 393224 | tf_op jit(solution)/shard_map/ppermute | solution.py:474
  31.3 3.0 %collective-permute-start.9 = (f32[64,512]{1,0:T(8,128)S(1)}, f32[64,512]{1,0:T(8,128)S(1)}, u32[]{:S(2)}, u32[]{:S(2)}) collective-permute-start(f32[64,512]{1,0:T(8,128)S(1)} %get-tuple-element.65.behind_ref.behind), channel_id=1, source_target_pairs={{0,224},{8,232},{16,240},{24,248},{32,0},{40,8},{48,16},{56,24},{6... | collective-permute-start | bytes 393224 | tf_op jit(solution)/shard_map/ppermute | solution.py:474
  34.3 1.7 %collective-permute-start.7 = (f32[64,512]{1,0:T(8,128)S(1)}, f32[64,512]{1,0:T(8,128)S(1)}, u32[]{:S(2)}, u32[]{:S(2)}) collective-permute-start(f32[64,512]{1,0:T(8,128)S(1)} %get-tuple-element.65.behind_ref.behind), channel_id=1, source_target_pairs={{0,240},{8,248},{16,0},{24,8},{32,16},{40,24},{48,32},{56,40},{64,... | collective-permute-start | bytes 393224 | tf_op jit(solution)/shard_map/ppermute | solution.py:474
  36.0 3.4 %all-to-all-done.blocks_ref = f32[8,64,128]{2,1,0:T(8,128)S(1)} async-done(((f32[8,64,128]{2,1,0:T(8,128)}), f32[8,64,128]{2,1,0:T(8,128)S(1)}, u32[]{:S(2)}, u32[]{:S(2)}) %all-to-all-start) | async-done | bytes 262176 | tf_op jit(solution)/shard_map/all_to_all | solution.py:542
  39.3 7.4 %factor_first.1 = (f32[320,256]{1,0:T(8,128)S(1)}, f32[256,128]{1,0:T(8,128)S(1)}, f32[64,128]{1,0:T(8,128)S(1)}, f32[64,128]{1,0:T(8,128)S(1)}) custom-call(f32[8,64,128]{2,1,0:T(8,128)S(1)} %all-to-all-done.blocks_ref), custom_call_target="tpu_custom_call" | custom-call | flops 1000000000 | bytes 2000000 | tf_op jit(solution)/shard_map/factor_first/pallas_call | solution.py:453
  46.8 0.0 collective-permute-done.8.ahead4.refs_2_
  46.8 0.0 collective-permute-done.6.ahead2.refs_0_
  46.8 0.0 collective-permute-done.9.behind4.refs_3_
  46.8 0.0 collective-permute-done.7.behind2.refs_1_
  46.8 0.1 faces.1
  46.9 1.8 %collective-permute-start.10 = (f32[256,512]{1,0:T(8,128)S(1)}, f32[256,512]{1,0:T(8,128)S(1)}, u32[]{:S(2)}, u32[]{:S(2)}) collective-permute-start(f32[256,512]{1,0:T(8,128)S(1)} %faces.1), channel_id=1, source_target_pairs={{0,8},{8,0},{16,24},{24,16},{32,40},{40,32},{48,56},{56,48},{64,72... | collective-permute-start | bytes 1572872 | tf_op jit(solution)/shard_map/ppermute | solution.py:559
  48.6 8.1 %factor_second.1 = (f32[512,512]{1,0:T(8,128)}, f32[512,128]{1,0:T(8,128)S(1)}) custom-call(f32[8,64,128]{2,1,0:T(8,128)S(1)} %all-to-all-done.blocks_ref, f32[320,256]{1,0:T(8,128)S(1)} %get-tuple-element.70.part_ref, f32[256,128]{1,0:T(8,128)S(1)} %get-tuple-element.71.first_inverse, f32[64,128]{1,0:T(8,128)S(1)} %get-tuple-element.72.first_top, ...), custom_call_target="tpu_custom_call" | custom-call | flops 1000000000 | bytes 2000000 | tf_op jit(solution)/shard_map/factor_second/pallas_call | solution.py:453
  56.8 0.0 collective-permute-done.10.refs_4_
  56.8 2.4 %panel.1 = f32[512,512]{1,0:T(8,128)} custom-call(bf16[8,128,512]{2,1,0:T(8,128)(2,1)S(1)} %get-tuple-element.75.weighted_ref, s32[8,512]{1,0:T(8,128)S(1)} %get-tuple-element.76.index_ref, f32[64,512]{1,0:T(8,128)S(1)} %collective-permute-done.6.ahead2.refs_0_, f32[64,512]{1,0:T(8,128)S(1)} %collective-permute-done.7.behind2.refs_1_, ...), custom_call_target="tpu_custom_call" | custom-call | flops 100000000 | bytes 2000000 | tf_op jit(solution)/shard_map/panel/pallas_call | solution.py:453
  (6 shorter events, 0.0 us)
Async XLA Ops:
  0.6 10.4 %copy-start = (f32[1,16,512]{2,1,0:T(8,128)S(1)}, f32[1,16,512]{2,1,0:T(8,128)}, u32[]{:S(2)}) copy-start(f32[1,16,512]{2,1,0:T(8,128)} %param.6) | copy-start | bytes 98308
  0.6 10.4 %copy-start.1 = (f32[1,16,512]{2,1,0:T(8,128)S(1)}, f32[1,16,512]{2,1,0:T(8,128)}, u32[]{:S(2)}) copy-start(f32[1,16,512]{2,1,0:T(8,128)} %param.7) | copy-start | bytes 98308
  3.5 14.6 %collective-permute-start.1 = (f32[72,512]{1,0:T(8,128)S(1)}, f32[72,512]{1,0:T(8,128)S(1)}, u32[]{:S(2)}, u32[]{:S(2)}) collective-permute-start(f32[72,512]{1,0:T(8,128)S(1)} %get-tuple-element.50.top_ref), channel_id=1, source_target_pairs={{0,1},{1,2},{2,3},{3,4},{4,5},{5,6},{6,7},{7,0},{8,9},{9,10},{10,1... | collective-permute-start | bytes 442376 | tf_op jit(solution)/shard_map/ppermute | solution.py:474
  6.0 12.1 %collective-permute-start.2 = (f32[72,512]{1,0:T(8,128)S(1)}, f32[72,512]{1,0:T(8,128)S(1)}, u32[]{:S(2)}, u32[]{:S(2)}) collective-permute-start(f32[72,512]{1,0:T(8,128)S(1)} %get-tuple-element.51.bottom_ref), channel_id=1, source_target_pairs={{0,7},{1,0},{2,1},{3,2},{4,3},{5,4},{6,5},{7,6},{8,15},{9,8},{10,9... | collective-permute-start | bytes 442376 | tf_op jit(solution)/shard_map/ppermute | solution.py:474
  10.1 2.6 %collective-permute-start = (f32[16,512]{1,0:T(8,128)S(1)}, f32[16,512]{1,0:T(8,128)S(1)}, u32[]{:S(2)}, u32[]{:S(2)}) collective-permute-start(f32[16,512]{1,0:T(8,128)S(1)} %get-tuple-element.45.own.own_tails), channel_id=1, source_target_pairs={{0,8},{8,0},{16,24},{24,16},{32,40},{40,32},{48,56},{56,48},{64,72... | collective-permute-start | bytes 98312 | tf_op jit(solution)/shard_map/ppermute | solution.py:513
  12.7 6.6 %collective-permute-start.3 = (f32[16,512]{1,0:T(8,128)S(1)}, f32[16,512]{1,0:T(8,128)S(1)}, u32[]{:S(2)}, u32[]{:S(2)}) collective-permute-start(f32[16,512]{1,0:T(8,128)S(1)} %get-tuple-element.55), channel_id=1, source_target_pairs={{0,16},{8,40},{16,32},{24,56},{32,48},{40,72},{48,64},{56,88},{64,... | collective-permute-start | bytes 98312 | tf_op jit(solution)/shard_map/ppermute | solution.py:520
  15.5 4.4 %collective-permute-start.4 = (f32[16,512]{1,0:T(8,128)S(1)}, f32[16,512]{1,0:T(8,128)S(1)}, u32[]{:S(2)}, u32[]{:S(2)}) collective-permute-start(f32[16,512]{1,0:T(8,128)S(1)} %get-tuple-element.56), channel_id=1, source_target_pairs={{16,0},{40,8},{32,16},{56,24},{48,32},{72,40},{64,48},{88,56},{80,... | collective-permute-start | bytes 98312 | tf_op jit(solution)/shard_map/ppermute | solution.py:521
  19.9 1.4 %collective-permute-start.5 = (f32[32,512]{1,0:T(8,128)S(1)}, f32[32,512]{1,0:T(8,128)S(1)}, u32[]{:S(2)}, u32[]{:S(2)}) collective-permute-start(f32[32,512]{1,0:T(8,128)S(1)} %join.1), channel_id=1, source_target_pairs={{0,8},{8,0},{16,24},{24,16},{32,40},{40,32},{48,56},{56,48},{64,72... | collective-permute-start | bytes 196616 | tf_op jit(solution)/shard_map/ppermute | solution.py:530
  22.7 16.6 %all-to-all-start = ((f32[8,64,128]{2,1,0:T(8,128)}), f32[8,64,128]{2,1,0:T(8,128)S(1)}, u32[]{:S(2)}, u32[]{:S(2)}) async-start(f32[8,64,128]{2,1,0:T(8,128)} %get-tuple-element.63), calls=%async_computation | async-start | bytes 524288 | tf_op jit(solution)/shard_map/all_to_all | solution.py:542
  28.2 18.6 %collective-permute-start.8 = (f32[64,512]{1,0:T(8,128)S(1)}, f32[64,512]{1,0:T(8,128)S(1)}, u32[]{:S(2)}, u32[]{:S(2)}) collective-permute-start(f32[64,512]{1,0:T(8,128)S(1)} %get-tuple-element.64.ahead_ref.ahead), channel_id=1, source_target_pairs={{0,32},{8,40},{16,48},{24,56},{32,64},{40,72},{48,80},{56,88},{64,... | collective-permute-start | bytes 393224 | tf_op jit(solution)/shard_map/ppermute | solution.py:474
  30.1 16.7 %collective-permute-start.6 = (f32[64,512]{1,0:T(8,128)S(1)}, f32[64,512]{1,0:T(8,128)S(1)}, u32[]{:S(2)}, u32[]{:S(2)}) collective-permute-start(f32[64,512]{1,0:T(8,128)S(1)} %get-tuple-element.64.ahead_ref.ahead), channel_id=1, source_target_pairs={{0,16},{8,24},{16,32},{24,40},{32,48},{40,56},{48,64},{56,72},{64,... | collective-permute-start | bytes 393224 | tf_op jit(solution)/shard_map/ppermute | solution.py:474
  31.3 15.5 %collective-permute-start.9 = (f32[64,512]{1,0:T(8,128)S(1)}, f32[64,512]{1,0:T(8,128)S(1)}, u32[]{:S(2)}, u32[]{:S(2)}) collective-permute-start(f32[64,512]{1,0:T(8,128)S(1)} %get-tuple-element.65.behind_ref.behind), channel_id=1, source_target_pairs={{0,224},{8,232},{16,240},{24,248},{32,0},{40,8},{48,16},{56,24},{6... | collective-permute-start | bytes 393224 | tf_op jit(solution)/shard_map/ppermute | solution.py:474
  34.3 12.5 %collective-permute-start.7 = (f32[64,512]{1,0:T(8,128)S(1)}, f32[64,512]{1,0:T(8,128)S(1)}, u32[]{:S(2)}, u32[]{:S(2)}) collective-permute-start(f32[64,512]{1,0:T(8,128)S(1)} %get-tuple-element.65.behind_ref.behind), channel_id=1, source_target_pairs={{0,240},{8,248},{16,0},{24,8},{32,16},{40,24},{48,32},{56,40},{64,... | collective-permute-start | bytes 393224 | tf_op jit(solution)/shard_map/ppermute | solution.py:474
  46.9 9.9 %collective-permute-start.10 = (f32[256,512]{1,0:T(8,128)S(1)}, f32[256,512]{1,0:T(8,128)S(1)}, u32[]{:S(2)}, u32[]{:S(2)}) collective-permute-start(f32[256,512]{1,0:T(8,128)S(1)} %faces.1), channel_id=1, source_target_pairs={{0,8},{8,0},{16,24},{24,16},{32,40},{40,32},{48,56},{56,48},{64,72... | collective-permute-start | bytes 1572872 | tf_op jit(solution)/shard_map/ppermute | solution.py:559

commit v11 on v10

--- a/solution.py
+++ b/solution.py
@@ -70,7 +70,7 @@
     return jnp.concatenate([strips[q, pl.ds(z, K, stride=CZ), :] for q in range(4)], axis=1)
 
 
-def face_kernel(vectors_hbm, sigma_hbm, index_hbm, counts_hbm, layers_ref, parts_ref, ahead_ref, behind_ref, tails_ref, top_ref, bottom_ref, live_ref, wanted_ref, sigma_ref, index_ref, counts_ref, choice_ref, strips, sems):
+def face_kernel(vectors_hbm, sigma_hbm, index_hbm, counts_hbm, layers_ref, parts_ref, faces_ref, tails_ref, top_ref, bottom_ref, live_ref, wanted_ref, sigma_ref, index_ref, counts_ref, choice_ref, strips, sems):
     small = [
         pltpu.make_async_copy(sigma_hbm, sigma_ref, sems.at[4]),
         pltpu.make_async_copy(index_hbm, index_ref, sems.at[5]),
@@ -139,13 +139,13 @@
         return parts
 
     faces = faces_of(vector_rows, 2 * K)
-    for side, face_ref in ((0, behind_ref), (1, ahead_ref)):
-        face_ref[...] = faces[side][:K] + faces[side][K:]
-
-
-def row_kernel(ahead_ref, behind_ref, wanted_ref, top_ref, bottom_ref, below_ref, above_ref, own_ref, exact_ref, square_ref, lower_ref):
-    for side, face_ref in ((0, behind_ref), (1, ahead_ref)):
-        table = stacked(face_ref[...])
+    for side, at in ((0, slice(K, 2 * K)), (1, slice(0, K))):
+        faces_ref[at] = faces[side][:K] + faces[side][K:]
+
+
+def row_kernel(faces_ref, wanted_ref, top_ref, bottom_ref, below_ref, above_ref, own_ref, exact_ref, square_ref, lower_ref):
+    for side, at in ((0, slice(K, 2 * K)), (1, slice(0, K))):
+        table = stacked(faces_ref[at])
         for slot in range(REACH * side, REACH * (side + 1)):
             select = one_hot(wanted_ref[slot : slot + 1, :])
             found = product(table, select, MATRIX)
@@ -198,54 +198,40 @@
     own_ref[...] = own + own.T
 
 
-def pack_kernel(ahead, behind, ahead2, behind2, ahead4, behind4, out_ref):
-    mine = lax.axis_index("sub") % 2
-    for core, chosen in ((0, (ahead, ahead2, behind2, behind4)), (1, (ahead2, ahead4, behind, behind2))):
-        @pl.when(mine == core)
-        def _(chosen=chosen):
-            for at, ref in enumerate(chosen):
-                out_ref[K * at : K * (at + 1)] = ref[...]
-
-
 def pair_kernel(own, other, ahead_ref, behind_ref):
-    ahead_ref[:8] = own[:8]
-    ahead_ref[8:] = other[:8]
-    behind_ref[:8] = own[8:]
-    behind_ref[8:] = other[8:]
+    half = own.shape[0] // 2
+    ahead_ref[:half] = own[:half]
+    ahead_ref[half:] = other[:half]
+    behind_ref[:half] = own[half:]
+    behind_ref[half:] = other[half:]
 
 
 def join_kernel(first, second, out_ref):
-    out_ref[:16] = first[...]
-    out_ref[16:] = second[...]
+    rows = first.shape[0]
+    out_ref[:rows] = first[...]
+    out_ref[rows:] = second[...]
 
 
 OFFSETS = (-4, -3, -2, -1, 1, 2, 3, 4)
 
 
-def tails_by_slot(other, before, after, swapped):
+def by_slot(other, before, after, swapped):
     even = lax.axis_index("sub") % 2 == 0
-    low, high = slice(0, 8), slice(8, 16)
-    before1 = jnp.where(even, before[...], swapped[:16])
-    before2 = jnp.where(even, swapped[:16], before[...])
-    after1 = jnp.where(even, after[...], swapped[16:])
-    after2 = jnp.where(even, swapped[16:], after[...])
+    rows = other.shape[0]
+    low, high = slice(0, rows // 2), slice(rows // 2, rows)
+    before1 = jnp.where(even, before[...], swapped[:rows])
+    before2 = jnp.where(even, swapped[:rows], before[...])
+    after1 = jnp.where(even, after[...], swapped[rows:])
+    after2 = jnp.where(even, swapped[rows:], after[...])
     on_even = (before2[high], before2[low], before1[low], before1[high], other[high], after1[low], after1[high], after2[high])
     on_odd = (before2[low], before1[low], before1[high], other[low], after1[low], after1[high], after2[high], after2[low])
     return [jnp.where(even, x, y) for x, y in zip(on_even, on_odd, strict=True)]
 
 
-def partner_face(refs, offset):
-    ahead2, behind2, ahead4, behind4, swapped = refs
-    if offset % 2:
-        at = {-1: 0, -3: 1, 1: 2, 3: 3}[offset]
-        return swapped[K * at : K * at + K]
-    return {-2: ahead2, -4: ahead4, 2: behind2, 4: behind4}[offset][...]
-
-
 def block_kernel(live_ref, own_block, square_block, lower_block, own_ref, exact_ref, own_tails, *refs):
     *tails, out_ref, weighted_ref, index_ref = refs
     total = jnp.zeros((2 * K, 2 * K), f32)
-    found = tails_by_slot(*tails)
+    found = by_slot(*tails)
     for slot, offset in enumerate(OFFSETS):
         reach = abs(offset) - 1
         row = reach if offset > 0 else 8 + reach
@@ -268,10 +254,10 @@
 
 
 def panel_kernel(weighted_ref, index_ref, *refs):
-    faces, (inverse, out_hbm, found_ref, rows_ref, sems) = refs[:5], refs[5:]
-    for slot, offset in enumerate(OFFSETS):
+    faces, (inverse, out_hbm, found_ref, rows_ref, sems) = refs[:4], refs[4:]
+    for slot, face in enumerate(by_slot(*faces)):
         select = one_hot(index_ref[slot : slot + 1, :])
-        found_ref[slot] = product(stacked(partner_face(faces, offset)), select, MATRIX).astype(bf16)
+        found_ref[slot] = product(stacked(face), select, MATRIX).astype(bf16)
     blocks = [
         -quadrants(product(weighted_ref[slot], found_ref[slot], GRAM)) for slot in range(2 * REACH)
     ]
@@ -478,14 +464,13 @@
     vectors = deflation[0].reshape(K * CZ, FACE)
     sigma = conductivity[0]
     counts = interface_counts.reshape(2 * REACH)
-    layers, parts, ahead, behind, own_tails, top, bottom, live, wanted = call(
+    layers, parts, own_faces, own_tails, top, bottom, live, wanted = call(
         face_kernel,
         "face",
         (
             array(CZ, K, FACE),
             array(CZ, 2 * K, FACE, dtype=bf16),
-            array(K, FACE),
-            array(K, FACE),
+            array(2 * K, FACE),
             array(16, FACE),
             array(ROWS, FACE),
             array(ROWS, FACE),
@@ -513,21 +498,36 @@
     other_tails = lax.ppermute(own_tails, "sub", swap)
     own = call(own_kernel, "own", array(K, K), (layers, parts, sigma, storage[0]))
     other_tails, own = lax.optimization_barrier((other_tails, own))
-    go_ahead, go_behind = call(
-        pair_kernel, "pair", (array(16, FACE), array(16, FACE)), (own_tails, other_tails), flops=10**6
-    )
     far = [(i, (i + 2 + 2 * (i % 2)) % count) for i in range(count)]
-    before = lax.ppermute(go_ahead, "sub", far)
-    after = lax.ppermute(go_behind, "sub", [(j, i) for i, j in far])
+
+    def paired(own, other):
+        half = array(own.shape[0], FACE)
+        return call(pair_kernel, "pair", (half, half), (own, other), flops=10**6)
+
+    def sent(ahead, behind):
+        return (
+            lax.ppermute(ahead, "sub", far),
+            lax.ppermute(behind, "sub", [(j, i) for i, j in far]),
+        )
+
+    def joined(before, after):
+        out = array(2 * before.shape[0], FACE)
+        return lax.ppermute(
+            call(join_kernel, "join", out, (before, after), flops=10**6), "sub", swap
+        )
+
+    before, after = sent(*paired(own_tails, other_tails))
+    other_faces = lax.ppermute(own_faces, "sub", swap)
     mine, exact, square, lower = call(
         row_kernel,
         "rows",
         (array(8, 2 * K, FACE, dtype=bf16), array(8, K, FACE), array(K, K), array(K, K)),
-        (ahead, behind, wanted, top, bottom, below, above),
-    )
-    (before, after), mine = lax.optimization_barrier(((before, after), mine))
-    both = call(join_kernel, "join", array(32, FACE), (before, after), flops=10**6)
-    swapped_tails = lax.ppermute(both, "sub", swap)
+        (own_faces, wanted, top, bottom, below, above),
+    )
+    (before, after), going, mine = lax.optimization_barrier(
+        ((before, after), paired(own_faces, other_faces), mine)
+    )
+    swapped_tails = joined(before, after)
     payload, weighted, index = call(
         block_kernel,
         "block",
@@ -538,14 +538,9 @@
         ),
         (live, own, square, lower, mine, exact, own_tails, other_tails, before, after, swapped_tails),
     )
-    (ahead, behind), payload = lax.optimization_barrier(((ahead, behind), payload))
+    going, payload = lax.optimization_barrier((going, payload))
     blocks = lax.all_to_all(payload, "coarse", 0, 0)
-    faces = (
-        passed_along(ahead, "sub", 2),
-        passed_along(behind, "sub", -2),
-        passed_along(ahead, "sub", 4),
-        passed_along(behind, "sub", -4),
-    )
+    faces = sent(*going)
     state = call(
         first_half,
         "factor_first",
@@ -555,8 +550,7 @@
         scratch=(pltpu.VMEM((8, K, 2 * K), f32),),
     )
     faces, state = lax.optimization_barrier((faces, state))
-    packed = call(pack_kernel, "faces", array(4 * K, FACE), (ahead, behind, *faces), flops=10**6)
-    faces = (*faces, lax.ppermute(packed, "sub", swap))
+    faces = (other_faces, *faces, joined(*faces))
     factor, inverse = call(
         second_half,
         "factor_second",

time: 59.5 us -> 59.8 us (level)
  waiting for transfers between devices: 5.18 us -> 7.83 us
  starting transfers between devices: 28.4 us -> 25.8 us
    ppermute x6 -> x2, starting transfers between devices: 14.4 us -> 3.84 us  [passed_along(): lax.ppermute(block, axis, [(i, (i + distance) % count) for i in range(cou...]
    ppermute x4 -> x7, starting transfers between devices: 7.6 us -> 16 us  [the longest x2 5.75 us: sent(): lax.ppermute(behind, 'sub', [(j, i) for i, j in far])]
    all_to_all x1, waiting for transfers between devices: 3.37 us -> 6.08 us  [body(): blocks = lax.all_to_all(payload, 'coarse', 0, 0)]
    pallas_call x10 -> x11, Pallas kernels: 24.8 us -> 25 us  [call(): pl.pallas_call(kernel, out_shape=outs, in_specs=[HBM] * hbm + [VMEM] * (l...]
    ppermute x4 -> x7, waiting for transfers between devices: 1.78 us -> 1.74 us  [the longest x2 0.9 us: joined(): lax.ppermute(call(join_kernel, 'join', out, (before, after), flops=10 **...]
  transfers between devices with their start and end apart: 12 -> 11, of which waited for: 4 -> 4; matrix products, arithmetic and copies ran while one was open for 0% -> 0% of each run, Pallas kernels for 31% -> 31%
where the time goes in v11:
time: 59.8 us; the launch traced here: 59.6 us
  starting transfers between devices  25.8 us (43%)
  Pallas kernels  25 us (42%)
  waiting for transfers between devices  7.83 us (13%)
  between operations  0.92 us (2%)
    pallas_call x11, Pallas kernels, call(): pl.pallas_call(kernel, out_shape=outs, in_specs=[HBM] * hbm + [VMEM] * (l...  25 us
    all_to_all x1, waiting for transfers between devices, body(): blocks = lax.all_to_all(payload, 'coarse', 0, 0)  6.08 us
    ppermute x2, starting transfers between devices, sent(): lax.ppermute(behind, 'sub', [(j, i) for i, j in far])  5.75 us
    all_to_all x1, starting transfers between devices, body(): blocks = lax.all_to_all(payload, 'coarse', 0, 0)  5.48 us
    ppermute x2, starting transfers between devices, sent(): lax.ppermute(ahead, 'sub', far)  4.69 us
    ppermute x2, starting transfers between devices, passed_along(): lax.ppermute(block, axis, [(i, (i + distance) % count) for i in range(cou...  3.84 us
    ppermute x1, starting transfers between devices, body(): other_faces = lax.ppermute(own_faces, 'sub', swap)  3.33 us
    ppermute x2, starting transfers between devices, joined(): lax.ppermute(call(join_kernel, 'join', out, (before, after), flops=10 **...  2.24 us
  transfers between devices with their start and end apart: 11, of which 4 were waited for; matrix products, arithmetic and copies ran while one was open for 0% of the time, Pallas kernels for 31%

profile of v11, /device:TPU:1, one launch (start us, length us, event | category | flops | bytes accessed | tf_op | source)
XLA Modules:
  0.0 59.6 jit_solution(13653600175547536241)
XLA Ops:
  0.6 0.0 copy-start
  0.6 0.0 copy-start.1
  0.7 2.8 %face.1 = (f32[16,64,512]{2,1,0:T(8,128)S(1)}, bf16[16,128,512]{2,1,0:T(8,128)(2,1)S(1)}, f32[128,512]{1,0:T(8,128)S(1)}, f32[16,512]{1,0:T(8,128)S(1)}, f32[72,...) custom-call(f32[1024,512]{1,0:T(8,128)} %bitcast.10, f32[16,512]{1,0:T(8,128)} %bitcast.7, ...), custom_call_target="tpu_custom_call" | custom-call | flops 100000000 | bytes 2000000 | tf_op jit(solution)/shard_map/face/pallas_call | solution.py:439
  3.5 3.3 %collective-permute-start.3 = (f32[128,512]{1,0:T(8,128)S(1)}, f32[128,512]{1,0:T(8,128)S(1)}, u32[]{:S(2)}, u32[]{:S(2)}) collective-permute-start(f32[128,512]{1,0:T(8,128)S(1)} %get-tuple-element.49.own.faces_ref), channel_id=1, source_target_pairs={{0,8},{8,0},{16,24},{24,16},{32,40},{40,32},{48,56},{56,48},{64,72... | collective-permute-start | bytes 786440 | tf_op jit(solution)/shard_map/ppermute | solution.py:520
  6.8 0.0 collective-permute-start.4
  6.8 3.8 %collective-permute-start.5 = (f32[72,512]{1,0:T(8,128)S(1)}, f32[72,512]{1,0:T(8,128)S(1)}, u32[]{:S(2)}, u32[]{:S(2)}) collective-permute-start(f32[72,512]{1,0:T(8,128)S(1)} %get-tuple-element.54.bottom_ref), channel_id=1, source_target_pairs={{0,7},{1,0},{2,1},{3,2},{4,3},{5,4},{6,5},{7,6},{8,15},{9,8},{10,9... | collective-permute-start | bytes 442376 | tf_op jit(solution)/shard_map/ppermute | solution.py:460
  10.7 0.5 collective-permute-start
  11.1 0.0 copy-done
  11.1 1.7 %own.1.own_block = f32[64,64]{1,0:T(8,128)S(1)} custom-call(f32[16,64,512]{2,1,0:T(8,128)S(1)} %get-tuple-element.44.layers_ref, bf16[16,128,512]{2,1,0:T(8,128)(2,1)S(1)} %get-tuple-element.45.parts_ref, f32[16,512]{1,0:T(8,128)S(1)} %bitcast.8, f32[16,512]{1,0:T(8,128)S(1)} %bitcast.9), custom_call_target="tpu_custom_call" | custom-call | flops 100000000 | bytes 2000000 | tf_op jit(solution)/shard_map/own/pallas_call | solution.py:439
  12.8 0.0 collective-permute-done.other.refs_0_
  12.8 2.8 %collective-permute-start.1 = (f32[16,512]{1,0:T(8,128)S(1)}, f32[16,512]{1,0:T(8,128)S(1)}, u32[]{:S(2)}, u32[]{:S(2)}) collective-permute-start(f32[16,512]{1,0:T(8,128)S(1)} %get-tuple-element.47), channel_id=1, source_target_pairs={{0,16},{8,40},{16,32},{24,56},{32,48},{40,72},{48,64},{56,88},{64,... | collective-permute-start | bytes 98312 | tf_op jit(solution)/shard_map/ppermute | solution.py:509
  15.6 2.5 %collective-permute-start.2 = (f32[16,512]{1,0:T(8,128)S(1)}, f32[16,512]{1,0:T(8,128)S(1)}, u32[]{:S(2)}, u32[]{:S(2)}) collective-permute-start(f32[16,512]{1,0:T(8,128)S(1)} %get-tuple-element.48), channel_id=1, source_target_pairs={{16,0},{40,8},{32,16},{56,24},{48,32},{72,40},{64,48},{88,56},{80,... | collective-permute-start | bytes 98312 | tf_op jit(solution)/shard_map/ppermute | solution.py:510
  18.2 0.0 collective-permute-done.4.below_ref
  18.2 0.0 collective-permute-done.5.above_ref
  18.2 1.0 %rows.1 = (bf16[8,128,512]{2,1,0:T(8,128)(2,1)S(1)}, f32[8,64,512]{2,1,0:T(8,128)S(1)}, f32[64,64]{1,0:T(8,128)S(1)}, f32[64,64]{1,0:T(8,128)S(1)}) custom-call(f32[128,512]{1,0:T(8,128)S(1)} %get-tuple-element.49.own.faces_ref, s32[8,512]{1,0:T(8,128)S(1)} %get-tuple-element.52.wanted_ref, f32[72,512]{1,0:T(8,128)S(1)} %get-tuple-element.53.top_ref, ...), custom_call_target="tpu_custom_call" | custom-call | flops 100000000 | bytes 2000000 | tf_op jit(solution)/shard_map/rows/pallas_call | solution.py:439
  19.2 0.0 collective-permute-done.3.other.refs_0_
  19.2 0.2 collective-permute-done.1.first.refs_1_
  19.4 0.6 %collective-permute-done.2.second.refs_2_ = f32[16,512]{1,0:T(8,128)S(1)} collective-permute-done((f32[16,512]{1,0:T(8,128)S(1)}, f32[16,512]{1,0:T(8,128)S(1)}, u32[]{:S(2)}, u32[]{:S(2)}) %collective-permute-start.2) | collective-permute-done | bytes 32800 | tf_op jit(solution)/shard_map/ppermute | solution.py:510
  20.0 0.5 collective-permute-start.6
  20.5 0.9 %collective-permute-done.6.refs_3_ = f32[32,512]{1,0:T(8,128)S(1)} collective-permute-done((f32[32,512]{1,0:T(8,128)S(1)}, f32[32,512]{1,0:T(8,128)S(1)}, u32[]{:S(2)}, u32[]{:S(2)}) %collective-permute-start.6) | collective-permute-done | bytes 65568 | tf_op jit(solution)/shard_map/ppermute | solution.py:515
  21.4 1.4 %block.1 = (f32[8,64,128]{2,1,0:T(8,128)}, bf16[8,128,512]{2,1,0:T(8,128)(2,1)S(1)}, s32[8,512]{1,0:T(8,128)S(1)}) custom-call(f32[8,512]{1,0:T(8,128)S(1)} %get-tuple-element.58.live_ref, f32[64,64]{1,0:T(8,128)S(1)} %own.1.own_block, f32[64,64]{1,0:T(8,128)S(1)} %get-tuple-element.60.square_block, f32[64,64]{1,0:T(8,128)S(1)} %get-tuple-element.61.lower_block, ...), custom_call_target="tpu_custom_call" | custom-call | flops 100000000 | bytes 2000000 | tf_op jit(solution)/shard_map/block/pallas_call | solution.py:439
  22.8 5.5 %all-to-all-start = ((f32[8,64,128]{2,1,0:T(8,128)}), f32[8,64,128]{2,1,0:T(8,128)S(1)}, u32[]{:S(2)}, u32[]{:S(2)}) async-start(f32[8,64,128]{2,1,0:T(8,128)} %get-tuple-element.67), calls=%async_computation | async-start | bytes 524288 | tf_op jit(solution)/shard_map/all_to_all | solution.py:542
  28.3 1.9 %collective-permute-start.7 = (f32[128,512]{1,0:T(8,128)S(1)}, f32[128,512]{1,0:T(8,128)S(1)}, u32[]{:S(2)}, u32[]{:S(2)}) collective-permute-start(f32[128,512]{1,0:T(8,128)S(1)} %get-tuple-element.68), channel_id=1, source_target_pairs={{0,16},{8,40},{16,32},{24,56},{32,48},{40,72},{48,64},{56,88},{64,... | collective-permute-start | bytes 786440 | tf_op jit(solution)/shard_map/ppermute | solution.py:509
  30.2 3.2 %collective-permute-start.8 = (f32[128,512]{1,0:T(8,128)S(1)}, f32[128,512]{1,0:T(8,128)S(1)}, u32[]{:S(2)}, u32[]{:S(2)}) collective-permute-start(f32[128,512]{1,0:T(8,128)S(1)} %get-tuple-element.69), channel_id=1, source_target_pairs={{16,0},{40,8},{32,16},{56,24},{48,32},{72,40},{64,48},{88,56},{80,... | collective-permute-start | bytes 786440 | tf_op jit(solution)/shard_map/ppermute | solution.py:510
  33.4 6.1 %all-to-all-done.blocks_ref = f32[8,64,128]{2,1,0:T(8,128)S(1)} async-done(((f32[8,64,128]{2,1,0:T(8,128)}), f32[8,64,128]{2,1,0:T(8,128)S(1)}, u32[]{:S(2)}, u32[]{:S(2)}) %all-to-all-start) | async-done | bytes 262176 | tf_op jit(solution)/shard_map/all_to_all | solution.py:542
  39.4 7.4 %factor_first.1 = (f32[320,256]{1,0:T(8,128)S(1)}, f32[256,128]{1,0:T(8,128)S(1)}, f32[64,128]{1,0:T(8,128)S(1)}, f32[64,128]{1,0:T(8,128)S(1)}) custom-call(f32[8,64,128]{2,1,0:T(8,128)S(1)} %all-to-all-done.blocks_ref), custom_call_target="tpu_custom_call" | custom-call | flops 1000000000 | bytes 2000000 | tf_op jit(solution)/shard_map/factor_first/pallas_call | solution.py:439
  46.9 0.0 collective-permute-done.7.first.refs_1_
  46.9 0.0 collective-permute-done.8.second.refs_2_
  46.9 1.8 %collective-permute-start.9 = (f32[256,512]{1,0:T(8,128)S(1)}, f32[256,512]{1,0:T(8,128)S(1)}, u32[]{:S(2)}, u32[]{:S(2)}) collective-permute-start(f32[256,512]{1,0:T(8,128)S(1)} %join.3), channel_id=1, source_target_pairs={{0,8},{8,0},{16,24},{24,16},{32,40},{40,32},{48,56},{56,48},{64,72... | collective-permute-start | bytes 1572872 | tf_op jit(solution)/shard_map/ppermute | solution.py:515
  48.7 8.1 %factor_second.1 = (f32[512,512]{1,0:T(8,128)}, f32[512,128]{1,0:T(8,128)S(1)}) custom-call(f32[8,64,128]{2,1,0:T(8,128)S(1)} %all-to-all-done.blocks_ref, f32[320,256]{1,0:T(8,128)S(1)} %get-tuple-element.74.part_ref, f32[256,128]{1,0:T(8,128)S(1)} %get-tuple-element.75.first_inverse, f32[64,128]{1,0:T(8,128)S(1)} %get-tuple-element.76.first_top, ...), custom_call_target="tpu_custom_call" | custom-call | flops 1000000000 | bytes 2000000 | tf_op jit(solution)/shard_map/factor_second/pallas_call | solution.py:439
  56.8 0.0 collective-permute-done.9.refs_3_
  56.8 2.6 %panel.1 = f32[512,512]{1,0:T(8,128)} custom-call(bf16[8,128,512]{2,1,0:T(8,128)(2,1)S(1)} %get-tuple-element.79.weighted_ref, s32[8,512]{1,0:T(8,128)S(1)} %get-tuple-element.80.index_ref, f32[128,512]{1,0:T(8,128)S(1)} %collective-permute-done.3.other.refs_0_, f32[128,512]{1,0:T(8,128)S(1)} %collective-permute-done.7.first.refs_1_, ...), custom_call_target="tpu_custom_call" | custom-call | flops 100000000 | bytes 2000000 | tf_op jit(solution)/shard_map/panel/pallas_call | solution.py:439
  (5 shorter events, 0.1 us)
Async XLA Ops:
  0.6 10.5 %copy-start = (f32[1,16,512]{2,1,0:T(8,128)S(1)}, f32[1,16,512]{2,1,0:T(8,128)}, u32[]{:S(2)}) copy-start(f32[1,16,512]{2,1,0:T(8,128)} %param.6) | copy-start | bytes 98308
  0.6 10.5 %copy-start.1 = (f32[1,16,512]{2,1,0:T(8,128)S(1)}, f32[1,16,512]{2,1,0:T(8,128)}, u32[]{:S(2)}) copy-start(f32[1,16,512]{2,1,0:T(8,128)} %param.7) | copy-start | bytes 98308
  3.5 15.7 %collective-permute-start.3 = (f32[128,512]{1,0:T(8,128)S(1)}, f32[128,512]{1,0:T(8,128)S(1)}, u32[]{:S(2)}, u32[]{:S(2)}) collective-permute-start(f32[128,512]{1,0:T(8,128)S(1)} %get-tuple-element.49.own.faces_ref), channel_id=1, source_target_pairs={{0,8},{8,0},{16,24},{24,16},{32,40},{40,32},{48,56},{56,48},{64,72... | collective-permute-start | bytes 786440 | tf_op jit(solution)/shard_map/ppermute | solution.py:520
  6.8 11.4 %collective-permute-start.4 = (f32[72,512]{1,0:T(8,128)S(1)}, f32[72,512]{1,0:T(8,128)S(1)}, u32[]{:S(2)}, u32[]{:S(2)}) collective-permute-start(f32[72,512]{1,0:T(8,128)S(1)} %get-tuple-element.53.top_ref), channel_id=1, source_target_pairs={{0,1},{1,2},{2,3},{3,4},{4,5},{5,6},{6,7},{7,0},{8,9},{9,10},{10,1... | collective-permute-start | bytes 442376 | tf_op jit(solution)/shard_map/ppermute | solution.py:460
  6.8 11.4 %collective-permute-start.5 = (f32[72,512]{1,0:T(8,128)S(1)}, f32[72,512]{1,0:T(8,128)S(1)}, u32[]{:S(2)}, u32[]{:S(2)}) collective-permute-start(f32[72,512]{1,0:T(8,128)S(1)} %get-tuple-element.54.bottom_ref), channel_id=1, source_target_pairs={{0,7},{1,0},{2,1},{3,2},{4,3},{5,4},{6,5},{7,6},{8,15},{9,8},{10,9... | collective-permute-start | bytes 442376 | tf_op jit(solution)/shard_map/ppermute | solution.py:460
  10.7 2.1 %collective-permute-start = (f32[16,512]{1,0:T(8,128)S(1)}, f32[16,512]{1,0:T(8,128)S(1)}, u32[]{:S(2)}, u32[]{:S(2)}) collective-permute-start(f32[16,512]{1,0:T(8,128)S(1)} %get-tuple-element.43.own.own_tails), channel_id=1, source_target_pairs={{0,8},{8,0},{16,24},{24,16},{32,40},{40,32},{48,56},{56,48},{64,72... | collective-permute-start | bytes 98312 | tf_op jit(solution)/shard_map/ppermute | solution.py:498
  12.8 6.6 %collective-permute-start.1 = (f32[16,512]{1,0:T(8,128)S(1)}, f32[16,512]{1,0:T(8,128)S(1)}, u32[]{:S(2)}, u32[]{:S(2)}) collective-permute-start(f32[16,512]{1,0:T(8,128)S(1)} %get-tuple-element.47), channel_id=1, source_target_pairs={{0,16},{8,40},{16,32},{24,56},{32,48},{40,72},{48,64},{56,88},{64,... | collective-permute-start | bytes 98312 | tf_op jit(solution)/shard_map/ppermute | solution.py:509
  15.6 4.4 %collective-permute-start.2 = (f32[16,512]{1,0:T(8,128)S(1)}, f32[16,512]{1,0:T(8,128)S(1)}, u32[]{:S(2)}, u32[]{:S(2)}) collective-permute-start(f32[16,512]{1,0:T(8,128)S(1)} %get-tuple-element.48), channel_id=1, source_target_pairs={{16,0},{40,8},{32,16},{56,24},{48,32},{72,40},{64,48},{88,56},{80,... | collective-permute-start | bytes 98312 | tf_op jit(solution)/shard_map/ppermute | solution.py:510
  20.0 1.4 %collective-permute-start.6 = (f32[32,512]{1,0:T(8,128)S(1)}, f32[32,512]{1,0:T(8,128)S(1)}, u32[]{:S(2)}, u32[]{:S(2)}) collective-permute-start(f32[32,512]{1,0:T(8,128)S(1)} %join.2), channel_id=1, source_target_pairs={{0,8},{8,0},{16,24},{24,16},{32,40},{40,32},{48,56},{56,48},{64,72... | collective-permute-start | bytes 196616 | tf_op jit(solution)/shard_map/ppermute | solution.py:515
  22.8 16.6 %all-to-all-start = ((f32[8,64,128]{2,1,0:T(8,128)}), f32[8,64,128]{2,1,0:T(8,128)S(1)}, u32[]{:S(2)}, u32[]{:S(2)}) async-start(f32[8,64,128]{2,1,0:T(8,128)} %get-tuple-element.67), calls=%async_computation | async-start | bytes 524288 | tf_op jit(solution)/shard_map/all_to_all | solution.py:542
  28.3 18.6 %collective-permute-start.7 = (f32[128,512]{1,0:T(8,128)S(1)}, f32[128,512]{1,0:T(8,128)S(1)}, u32[]{:S(2)}, u32[]{:S(2)}) collective-permute-start(f32[128,512]{1,0:T(8,128)S(1)} %get-tuple-element.68), channel_id=1, source_target_pairs={{0,16},{8,40},{16,32},{24,56},{32,48},{40,72},{48,64},{56,88},{64,... | collective-permute-start | bytes 786440 | tf_op jit(solution)/shard_map/ppermute | solution.py:509
  30.2 16.7 %collective-permute-start.8 = (f32[128,512]{1,0:T(8,128)S(1)}, f32[128,512]{1,0:T(8,128)S(1)}, u32[]{:S(2)}, u32[]{:S(2)}) collective-permute-start(f32[128,512]{1,0:T(8,128)S(1)} %get-tuple-element.69), channel_id=1, source_target_pairs={{16,0},{40,8},{32,16},{56,24},{48,32},{72,40},{64,48},{88,56},{80,... | collective-permute-start | bytes 786440 | tf_op jit(solution)/shard_map/ppermute | solution.py:510
  46.9 9.9 %collective-permute-start.9 = (f32[256,512]{1,0:T(8,128)S(1)}, f32[256,512]{1,0:T(8,128)S(1)}, u32[]{:S(2)}, u32[]{:S(2)}) collective-permute-start(f32[256,512]{1,0:T(8,128)S(1)} %join.3), channel_id=1, source_target_pairs={{0,8},{8,0},{16,24},{24,16},{32,40},{40,32},{48,56},{56,48},{64,72... | collective-permute-start | bytes 1572872 | tf_op jit(solution)/shard_map/ppermute | solution.py:515
